TPU v7x, 32 devices: a whole 2x2x4 slice. The times are simulated.
32 devices in a mesh: fsdp: 2 (over x), ctx: 4 (over y, core), tp: 4 (over z).
Axes of the slice: x: 2, y: 2, z: 4, core: 2. Of those that a mesh axis runs over, the one named last changes fastest.
Arguments:
- hidden: float32 [2, 2048, 1280], P('fsdp', 'ctx'), may hold values from -96 to 96
- cotangent: float32 [2, 2048, 1280], P('fsdp', 'ctx'), may hold values from -6 to 6
- lengths: int32 [2], P('fsdp'), may hold values from 1024 to 2048, as said below
- query_weight: float32 [2, 1280, 1280], P(None, 'fsdp', 'tp'), may hold values from -0.25 to 0.25
- key_weight: float32 [2, 1280, 1280], P(None, 'fsdp', 'tp'), may hold values from -0.25 to 0.25
- value_weight: float32 [2, 1280, 1280], P(None, 'fsdp', 'tp'), may hold values from -0.15625 to 0.15625
- output_weight: float32 [2, 1280, 1280], P(None, 'tp', 'fsdp'), may hold values from -1 to 1
- inner_weight: float32 [2, 1280, 5120], P(None, 'fsdp', 'tp'), may hold values from -0.15625 to 0.15625
- outer_weight: float32 [2, 5120, 1280], P(None, 'tp', 'fsdp'), may hold values from -0.078125 to 0.078125
- query_bias: float32 [2, 1280], P(None, 'tp'), may hold values from -3 to 3
- value_bias: float32 [2, 1280], P(None, 'tp'), may hold values from -3 to 3
- inner_bias: float32 [2, 5120], P(None, 'tp'), may hold values from -3 to 3
- output_bias: float32 [2, 1280], P(None, 'fsdp'), may hold values from -3 to 3
- outer_bias: float32 [2, 1280], P(None, 'fsdp'), may hold values from -3 to 3
- first_gain: float32 [2, 1280], P(None, 'fsdp'), may hold values from 0.1 to 1.9
- first_shift: float32 [2, 1280], P(None, 'fsdp'), may hold values from -3 to 3
- second_gain: float32 [2, 1280], P(None, 'fsdp'), may hold values from 0.1 to 1.9
- second_shift: float32 [2, 1280], P(None, 'fsdp'), may hold values from -3 to 3
Outputs:
- output: float32 [2, 2048, 1280], P('fsdp', 'ctx')
- grad_hidden: float32 [2, 2048, 1280], P('fsdp', 'ctx')
- grad_query_weight: float32 [2, 1280, 1280], P(None, 'fsdp', 'tp')
- grad_key_weight: float32 [2, 1280, 1280], P(None, 'fsdp', 'tp')
- grad_value_weight: float32 [2, 1280, 1280], P(None, 'fsdp', 'tp')
- grad_output_weight: float32 [2, 1280, 1280], P(None, 'tp', 'fsdp')
- grad_inner_weight: float32 [2, 1280, 5120], P(None, 'fsdp', 'tp')
- grad_outer_weight: float32 [2, 5120, 1280], P(None, 'tp', 'fsdp')
- grad_query_bias: float32 [2, 1280], P(None, 'tp')
- grad_value_bias: float32 [2, 1280], P(None, 'tp')
- grad_inner_bias: float32 [2, 5120], P(None, 'tp')
- grad_output_bias: float32 [2, 1280], P(None, 'fsdp')
- grad_outer_bias: float32 [2, 1280], P(None, 'fsdp')
- grad_first_gain: float32 [2, 1280], P(None, 'fsdp')
- grad_first_shift: float32 [2, 1280], P(None, 'fsdp')
- grad_second_gain: float32 [2, 1280], P(None, 'fsdp')
- grad_second_shift: float32 [2, 1280], P(None, 'fsdp')
Inputs may be any that keep to these rules, and one draw needn't show every extreme that they name: `lengths`: every clip has 1024 to 2048 valid frames, and some clip is full.
All inputs are finite; a program needn't handle non-finite values.
Results may differ from a plain program's by a relative error of at most 0.017.
The roundings to bfloat16 on the way count: a program that leaves them out, or rounds other values in their place, can miss the bound.
Values may be sent and summed in bfloat16 or wider, within the bound.
A program may use at most 256 MiB of HBM per device.

v0:
```python
import math

import jax
import jax.numpy as jnp
from jax import lax
from jax.sharding import PartitionSpec as P

HD = 80
LAYERS = 2


EPSILON = 1e-05
NEGATIVE = -1e30
ROOT_HALF = 1.0 / math.sqrt(2.0)
DENSITY = 1.0 / math.sqrt(2.0 * math.pi)


def norm_parts(values):
    average = jnp.mean(values, axis=-1, keepdims=True)
    centered = values - average
    spread = jnp.mean(centered * centered, axis=-1, keepdims=True)
    inverse = lax.rsqrt(spread + EPSILON)
    return (centered * inverse, inverse)


def norm_back(upstream, normal_hat, inverse, gain_full):
    scaled = upstream * gain_full
    first_mean = jnp.mean(scaled, axis=-1, keepdims=True)
    second_mean = jnp.mean(scaled * normal_hat, axis=-1, keepdims=True)
    return inverse * (scaled - first_mean - normal_hat * second_mean)


def gelu_value(values):
    return 0.5 * values * (1.0 + lax.erf(values * ROOT_HALF))


def gelu_slope(values):
    return 0.5 * (1.0 + lax.erf(values * ROOT_HALF)) + values * DENSITY * jnp.exp(
        -0.5 * values * values
    )


def matmul(left_side, right_side):
    return jnp.dot(left_side, right_side, preferred_element_type=jnp.float32)


def contract_rows(left_side, right_side):
    return lax.dot_general(
        left_side, right_side, (((0,), (0,)), ((), ())), preferred_element_type=jnp.float32
    )


def contract_cols(left_side, right_side):
    return lax.dot_general(
        left_side, right_side, (((1,), (1,)), ((), ())), preferred_element_type=jnp.float32
    )


def head_sums(partial_out):
    return lax.psum(partial_out, "tp")


def input_sums(partial_in):
    return lax.psum(partial_in, "tp")


def per_device(
    hidden,
    cotangent,
    lengths,
    query_weight,
    key_weight,
    value_weight,
    output_weight,
    inner_weight,
    outer_weight,
    query_bias,
    value_bias,
    inner_bias,
    output_bias,
    outer_bias,
    first_gain,
    first_shift,
    second_gain,
    second_shift,
):
    clip_count, frames_local, width = hidden.shape
    row_count = clip_count * frames_local
    frames_all = frames_local * lax.axis_size("ctx")
    columns = query_weight.shape[2]
    heads_local = columns // HD
    scale = 1.0 / math.sqrt(HD)
    valid_keys = jnp.arange(frames_all)[None, :] < lengths[:, None]

    def fetch_layer(layer_index):
        return (
            lax.all_gather(
                query_weight[layer_index].astype(jnp.bfloat16), "fsdp", axis=0, tiled=True
            ),
            lax.all_gather(
                key_weight[layer_index].astype(jnp.bfloat16), "fsdp", axis=0, tiled=True
            ),
            lax.all_gather(
                value_weight[layer_index].astype(jnp.bfloat16), "fsdp", axis=0, tiled=True
            ),
            lax.all_gather(
                inner_weight[layer_index].astype(jnp.bfloat16), "fsdp", axis=0, tiled=True
            ),
            lax.all_gather(
                output_weight[layer_index].astype(jnp.bfloat16), "fsdp", axis=1, tiled=True
            ),
            lax.all_gather(
                outer_weight[layer_index].astype(jnp.bfloat16), "fsdp", axis=1, tiled=True
            ),
            lax.all_gather(
                output_bias[layer_index].astype(jnp.bfloat16), "fsdp", axis=0, tiled=True
            ),
            lax.all_gather(
                outer_bias[layer_index].astype(jnp.bfloat16), "fsdp", axis=0, tiled=True
            ),
            lax.all_gather(
                first_gain[layer_index].astype(jnp.bfloat16), "fsdp", axis=0, tiled=True
            ),
            lax.all_gather(
                first_shift[layer_index].astype(jnp.bfloat16), "fsdp", axis=0, tiled=True
            ),
            lax.all_gather(
                second_gain[layer_index].astype(jnp.bfloat16), "fsdp", axis=0, tiled=True
            ),
            lax.all_gather(
                second_shift[layer_index].astype(jnp.bfloat16), "fsdp", axis=0, tiled=True
            ),
        )

    def scores_of(query_block, key_block, mask_row):
        scores = (
            jnp.einsum(
                "qhd,khd->hqk",
                query_block.reshape(frames_local, heads_local, HD),
                key_block.reshape(frames_all, heads_local, HD),
                preferred_element_type=jnp.float32,
            )
            * scale
        )
        return jnp.where(mask_row[None, None, :], scores, NEGATIVE)

    def attend(packed):
        query_block, key_block, value_block, mask_row = packed
        scores = scores_of(query_block, key_block, mask_row)
        highest = jnp.max(scores, axis=-1, keepdims=True)
        raised = jnp.exp(scores - highest)
        total = jnp.sum(raised, axis=-1, keepdims=True)
        weights_soft = (raised / total).astype(jnp.bfloat16)
        attended = jnp.einsum(
            "hqk,khd->qhd",
            weights_soft,
            value_block.reshape(frames_all, heads_local, HD),
            preferred_element_type=jnp.float32,
        )
        return (attended.reshape(frames_local, columns), (highest + jnp.log(total))[:, :, 0])

    def attend_back(packed):
        query_block, key_block, value_block, grad_block, log_total, mask_row = packed
        scores = scores_of(query_block, key_block, mask_row)
        weights_full = jnp.exp(scores - log_total[:, :, None])
        grad_heads = grad_block.reshape(frames_local, heads_local, HD)
        grad_weights = jnp.einsum(
            "qhd,khd->hqk",
            grad_heads,
            value_block.reshape(frames_all, heads_local, HD),
            preferred_element_type=jnp.float32,
        )
        row_terms = jnp.sum(weights_full * grad_weights, axis=-1, keepdims=True)
        grad_scores = (weights_full * (grad_weights - row_terms)).astype(jnp.bfloat16)
        grad_query = (
            jnp.einsum(
                "hqk,khd->qhd",
                grad_scores,
                key_block.reshape(frames_all, heads_local, HD),
                preferred_element_type=jnp.float32,
            )
            * scale
        )
        grad_key = (
            jnp.einsum(
                "hqk,qhd->khd",
                grad_scores,
                query_block.reshape(frames_local, heads_local, HD),
                preferred_element_type=jnp.float32,
            )
            * scale
        )
        grad_value = jnp.einsum(
            "hqk,qhd->khd",
            weights_full.astype(jnp.bfloat16),
            grad_heads,
            preferred_element_type=jnp.float32,
        )
        return (
            grad_query.reshape(frames_local, columns),
            grad_key.reshape(frames_all, columns),
            grad_value.reshape(frames_all, columns),
        )

    def forward_layer(layer_in, layer_index, gathered):
        (
            w_query,
            w_key,
            w_value,
            w_inner,
            w_output,
            w_outer,
            bias_output,
            bias_outer,
            gain_first,
            shift_first,
            gain_second,
            shift_second,
        ) = gathered
        hat_first, inverse_first = norm_parts(layer_in)
        normed = (
            hat_first * gain_first.astype(jnp.float32) + shift_first.astype(jnp.float32)
        ).astype(jnp.bfloat16)
        queries = (matmul(normed, w_query) + query_bias[layer_index]).astype(jnp.bfloat16)
        key_rows = matmul(normed, w_key).astype(jnp.bfloat16)
        value_rows = (matmul(normed, w_value) + value_bias[layer_index]).astype(jnp.bfloat16)
        key_all, value_all = (
            lax.all_gather(
                key_rows.reshape(clip_count, frames_local, columns), "ctx", axis=1, tiled=True
            ),
            lax.all_gather(
                value_rows.reshape(clip_count, frames_local, columns), "ctx", axis=1, tiled=True
            ),
        )
        attended, log_total = lax.map(
            attend,
            (queries.reshape(clip_count, frames_local, columns), key_all, value_all, valid_keys),
        )
        attended = attended.reshape(row_count, columns).astype(jnp.bfloat16)
        middle = layer_in + head_sums(matmul(attended, w_output)) + bias_output.astype(jnp.float32)
        hat_second, inverse_second = norm_parts(middle)
        normed_two = (
            hat_second * gain_second.astype(jnp.float32) + shift_second.astype(jnp.float32)
        ).astype(jnp.bfloat16)
        inner_pre = matmul(normed_two, w_inner) + inner_bias[layer_index]
        active = gelu_value(inner_pre).astype(jnp.bfloat16)
        layer_out = middle + head_sums(matmul(active, w_outer)) + bias_outer.astype(jnp.float32)
        kept = (
            hat_first,
            inverse_first,
            normed,
            queries,
            key_all,
            value_all,
            log_total,
            attended,
            hat_second,
            inverse_second,
            normed_two,
            inner_pre,
            active,
        )
        return (layer_out, kept)

    residual = hidden.reshape(row_count, width)
    layer_inputs = []
    for layer_index in range(LAYERS):
        gathered = fetch_layer(layer_index)
        layer_inputs.append(residual)
        residual, kept = forward_layer(residual, layer_index, gathered)
    output = residual.reshape(hidden.shape)
    gradient = cotangent.reshape(row_count, width)
    shares_all = [None] * LAYERS
    biases_all = [None] * LAYERS
    for layer_index in reversed(range(LAYERS)):
        gathered = fetch_layer(layer_index)
        kept = forward_layer(layer_inputs[layer_index], layer_index, gathered)[1]
        (
            backward_w_query,
            backward_w_key,
            backward_w_value,
            backward_w_inner,
            backward_w_output,
            backward_w_outer,
            backward_bias_output,
            backward_bias_outer,
            backward_gain_first,
            backward_shift_first,
            backward_gain_second,
            backward_shift_second,
        ) = gathered
        (
            backward_hat_first,
            backward_inverse_first,
            backward_normed,
            backward_queries,
            backward_key_all,
            backward_value_all,
            backward_log_total,
            backward_attended,
            backward_hat_second,
            backward_inverse_second,
            backward_normed_two,
            backward_inner_pre,
            backward_active,
        ) = kept
        grad_low = gradient.astype(jnp.bfloat16)
        grad_outer_w = contract_rows(backward_active, grad_low)
        grad_active = contract_cols(grad_low, backward_w_outer)
        grad_inner = (grad_active * gelu_slope(backward_inner_pre)).astype(jnp.bfloat16)
        grad_inner_w = contract_rows(backward_normed_two, grad_inner)
        grad_normed_two = input_sums(contract_cols(grad_inner, backward_w_inner))
        grad_middle = gradient + norm_back(
            grad_normed_two,
            backward_hat_second,
            backward_inverse_second,
            backward_gain_second.astype(jnp.float32),
        )
        grad_mid_low = grad_middle.astype(jnp.bfloat16)
        grad_output_w = contract_rows(backward_attended, grad_mid_low)
        grad_attended = contract_cols(grad_mid_low, backward_w_output).astype(jnp.bfloat16)
        backward_grad_query, grad_key_part, grad_value_part = lax.map(
            attend_back,
            (
                backward_queries.reshape(clip_count, frames_local, columns),
                backward_key_all,
                backward_value_all,
                grad_attended.reshape(clip_count, frames_local, columns),
                backward_log_total,
                valid_keys,
            ),
        )
        backward_grad_key = lax.psum_scatter(grad_key_part, "ctx", scatter_dimension=1, tiled=True)
        backward_grad_value = lax.psum_scatter(
            grad_value_part, "ctx", scatter_dimension=1, tiled=True
        )
        backward_grad_query = backward_grad_query.reshape(row_count, columns).astype(jnp.bfloat16)
        backward_grad_key = backward_grad_key.reshape(row_count, columns).astype(jnp.bfloat16)
        backward_grad_value = backward_grad_value.reshape(row_count, columns).astype(jnp.bfloat16)
        grad_normed = input_sums(
            contract_cols(backward_grad_query, backward_w_query)
            + contract_cols(backward_grad_key, backward_w_key)
            + contract_cols(backward_grad_value, backward_w_value)
        )
        grad_in = grad_middle + norm_back(
            grad_normed,
            backward_hat_first,
            backward_inverse_first,
            backward_gain_first.astype(jnp.float32),
        )
        backward_large_terms = (
            contract_rows(backward_normed, backward_grad_query),
            contract_rows(backward_normed, backward_grad_key),
            contract_rows(backward_normed, backward_grad_value),
            grad_inner_w,
            grad_output_w,
            grad_outer_w,
            jnp.sum(grad_middle, axis=0),
            jnp.sum(gradient, axis=0),
            jnp.sum(grad_normed * backward_hat_first, axis=0),
            jnp.sum(grad_normed, axis=0),
            jnp.sum(grad_normed_two * backward_hat_second, axis=0),
            jnp.sum(grad_normed_two, axis=0),
        )
        gradient = grad_in
        shares = (
            lax.psum_scatter(
                backward_large_terms[0], ("fsdp", "ctx"), scatter_dimension=0, tiled=True
            ),
            lax.psum_scatter(
                backward_large_terms[1], ("fsdp", "ctx"), scatter_dimension=0, tiled=True
            ),
            lax.psum_scatter(
                backward_large_terms[2], ("fsdp", "ctx"), scatter_dimension=0, tiled=True
            ),
            lax.psum_scatter(
                backward_large_terms[3], ("fsdp", "ctx"), scatter_dimension=0, tiled=True
            ),
            lax.psum_scatter(
                backward_large_terms[4], ("fsdp", "ctx"), scatter_dimension=1, tiled=True
            ),
            lax.psum_scatter(
                backward_large_terms[5], ("fsdp", "ctx"), scatter_dimension=1, tiled=True
            ),
            lax.psum_scatter(
                backward_large_terms[6], ("fsdp", "ctx"), scatter_dimension=0, tiled=True
            ),
            lax.psum_scatter(
                backward_large_terms[7], ("fsdp", "ctx"), scatter_dimension=0, tiled=True
            ),
            lax.psum_scatter(
                backward_large_terms[8], ("fsdp", "ctx"), scatter_dimension=0, tiled=True
            ),
            lax.psum_scatter(
                backward_large_terms[9], ("fsdp", "ctx"), scatter_dimension=0, tiled=True
            ),
            lax.psum_scatter(
                backward_large_terms[10], ("fsdp", "ctx"), scatter_dimension=0, tiled=True
            ),
            lax.psum_scatter(
                backward_large_terms[11], ("fsdp", "ctx"), scatter_dimension=0, tiled=True
            ),
        )
        shares = (
            lax.all_gather(shares[0], "ctx", axis=0, tiled=True),
            lax.all_gather(shares[1], "ctx", axis=0, tiled=True),
            lax.all_gather(shares[2], "ctx", axis=0, tiled=True),
            lax.all_gather(shares[3], "ctx", axis=0, tiled=True),
            lax.all_gather(shares[4], "ctx", axis=1, tiled=True),
            lax.all_gather(shares[5], "ctx", axis=1, tiled=True),
            lax.all_gather(shares[6], "ctx", axis=0, tiled=True),
            lax.all_gather(shares[7], "ctx", axis=0, tiled=True),
            lax.all_gather(shares[8], "ctx", axis=0, tiled=True),
            lax.all_gather(shares[9], "ctx", axis=0, tiled=True),
            lax.all_gather(shares[10], "ctx", axis=0, tiled=True),
            lax.all_gather(shares[11], "ctx", axis=0, tiled=True),
        )
        biases = lax.psum(
            (
                jnp.sum(backward_grad_query.astype(jnp.float32), axis=0),
                jnp.sum(backward_grad_value.astype(jnp.float32), axis=0),
                jnp.sum(grad_inner.astype(jnp.float32), axis=0),
            ),
            ("fsdp", "ctx"),
        )
        shares_all[layer_index], biases_all[layer_index] = (shares, biases)

    def stacked(position, source):
        return jnp.stack([entry[position] for entry in source])

    return (
        output,
        gradient.reshape(hidden.shape),
        stacked(0, shares_all),
        stacked(1, shares_all),
        stacked(2, shares_all),
        stacked(4, shares_all),
        stacked(3, shares_all),
        stacked(5, shares_all),
        stacked(0, biases_all),
        stacked(1, biases_all),
        stacked(2, biases_all),
        stacked(6, shares_all),
        stacked(7, shares_all),
        stacked(8, shares_all),
        stacked(9, shares_all),
        stacked(10, shares_all),
        stacked(11, shares_all),
    )


def solution(mesh):
    in_specs = (
        P("fsdp", "ctx", None),
        P("fsdp", "ctx", None),
        P("fsdp"),
        P(None, "fsdp", "tp"),
        P(None, "fsdp", "tp"),
        P(None, "fsdp", "tp"),
        P(None, "tp", "fsdp"),
        P(None, "fsdp", "tp"),
        P(None, "tp", "fsdp"),
        P(None, "tp"),
        P(None, "tp"),
        P(None, "tp"),
        P(None, "fsdp"),
        P(None, "fsdp"),
        P(None, "fsdp"),
        P(None, "fsdp"),
        P(None, "fsdp"),
        P(None, "fsdp"),
    )
    out_specs = (
        P("fsdp", "ctx", None),
        P("fsdp", "ctx", None),
        P(None, "fsdp", "tp"),
        P(None, "fsdp", "tp"),
        P(None, "fsdp", "tp"),
        P(None, "tp", "fsdp"),
        P(None, "fsdp", "tp"),
        P(None, "tp", "fsdp"),
        P(None, "tp"),
        P(None, "tp"),
        P(None, "tp"),
        P(None, "fsdp"),
        P(None, "fsdp"),
        P(None, "fsdp"),
        P(None, "fsdp"),
        P(None, "fsdp"),
        P(None, "fsdp"),
    )
    return jax.shard_map(
        per_device, mesh=mesh, in_specs=in_specs, out_specs=out_specs, check_vma=False
    )
```

profile of v0, /device:TPU:0, one launch (start us, length us, event | category | flops | bytes accessed | tf_op | source)
XLA Modules:
  0.0 1822.9 jit_solution(16535619409640345157)
XLA Ops:
  127.2 78.2 %all-reduce.36.cloned.1.call-done = f32[512,1280]{1,0:T(8,128)} async-done(((f32[512,1280]{1,0:T(8,128)}), f32[512,1280]{1,0:T(8,128)}) %all-reduce.36.cloned.1.call-update) | async-done | bytes 2621456 | tf_op jit(solution)/shard_map/psum | solution.py:60
  243.6 80.0 %all-reduce.38.cloned.1.call-done = f32[512,1280]{1,0:T(8,128)} async-done(((f32[512,1280]{1,0:T(8,128)}), f32[512,1280]{1,0:T(8,128)}) %all-reduce.38.cloned.1.call-update) | async-done | bytes 2621456 | tf_op jit(solution)/shard_map/psum | solution.py:60
  329.9 12.0 all-gather.16
  342.0 12.7 all-gather.18
  354.7 10.7 all-gather.21
  410.5 89.2 %all-reduce.40.cloned.1.call-done = f32[512,1280]{1,0:T(8,128)} async-done(((f32[512,1280]{1,0:T(8,128)}), f32[512,1280]{1,0:T(8,128)}) %all-reduce.40.cloned.1.call-update) | async-done | bytes 2621456 | tf_op jit(solution)/shard_map/psum | solution.py:60
  521.5 103.0 %all-reduce.42.cloned.1.call-done = f32[512,1280]{1,0:T(8,128)} async-done(((f32[512,1280]{1,0:T(8,128)}), f32[512,1280]{1,0:T(8,128)}) %all-reduce.42.cloned.1.call-update) | async-done | bytes 2621456 | tf_op jit(solution)/shard_map/psum | solution.py:64
  635.0 15.3 multiply_reduce_fusion.1
  686.1 11.9 reduce-scatter.17.cloned.1.call-done
  702.2 32.5 %reduce-scatter.19.cloned.1.call-done = f32[1,512,320]{1,2,0:T(8,128)} async-done(((f32[1,2048,320]{1,2,0:T(8,128)}), f32[1,512,320]{1,2,0:T(8,128)}) %reduce-scatter.19.cloned.1.call-update) | async-done | bytes 655376 | tf_op jit(solution)/shard_map/reduce_scatter | solution.py:334
  739.4 104.2 %all-reduce.44.cloned.1.call-done = f32[512,1280]{1,0:T(8,128)} async-done(((f32[512,1280]{1,0:T(8,128)}), f32[512,1280]{1,0:T(8,128)}) %all-reduce.44.cloned.1.call-update) | async-done | bytes 2621456 | tf_op jit(solution)/shard_map/psum | solution.py:64
  858.2 102.8 %all-reduce.46.cloned.1.call-done = f32[512,1280]{1,0:T(8,128)} async-done(((f32[512,1280]{1,0:T(8,128)}), f32[512,1280]{1,0:T(8,128)}) %all-reduce.46.cloned.1.call-update) | async-done | bytes 2621456 | tf_op jit(solution)/shard_map/psum | solution.py:64
  968.4 15.1 multiply_reduce_fusion
  1017.7 11.9 reduce-scatter.21.cloned.1.call-done
  1032.4 34.0 %reduce-scatter.23.cloned.1.call-done = f32[1,512,320]{1,2,0:T(8,128)} async-done(((f32[1,2048,320]{1,2,0:T(8,128)}), f32[1,512,320]{1,2,0:T(8,128)}) %reduce-scatter.23.cloned.1.call-update) | async-done | bytes 655376 | tf_op jit(solution)/shard_map/reduce_scatter | solution.py:334
  1141.7 117.6 %all-reduce.50.cloned.1.call-done = (f32[512,1280]{1,0:T(8,128)}, f32[512,1280]{1,0:T(8,128)}) async-done(((f32[512,1280]{1,0:T(8,128)}, f32[512,1280]{1,0:T(8,128)}), (f32[512,1280]{1,0:T(8,128)}, f32[512,1280]{1,0:T(8,128)})) %all-reduce.50.cloned.1.call-update) | async-done | bytes 5242896 | tf_op jit(solution)/shard_map/psum | solution.py:60
  1263.9 11.0 reduce-scatter.43.cloned.1.call-done
  1281.8 45.4 %reduce-scatter.27.cloned.1.call-done = f32[160,320]{1,0:T(8,128)} async-done(((f32[1280,320]{1,0:T(8,128)}), f32[160,320]{1,0:T(8,128)}) %reduce-scatter.27.cloned.1.call-update) | async-done | bytes 204816 | tf_op jit(solution)/shard_map/reduce_scatter | solution.py:367
  1327.3 10.2 all_gather.211
  1337.5 34.7 %reduce-scatter.39.cloned.1.call-done = f32[320,160]{0,1:T(8,128)} async-done(((f32[320,1280]{0,1:T(8,128)}), f32[320,160]{0,1:T(8,128)}) %reduce-scatter.39.cloned.1.call-update) | async-done | bytes 204816 | tf_op jit(solution)/shard_map/reduce_scatter | solution.py:379
  1372.1 11.1 all_gather.217
  1383.2 32.5 %reduce-scatter.31.cloned.1.call-done = f32[160,320]{1,0:T(8,128)} async-done(((f32[1280,320]{1,0:T(8,128)}), f32[160,320]{1,0:T(8,128)}) %reduce-scatter.31.cloned.1.call-update) | async-done | bytes 204816 | tf_op jit(solution)/shard_map/reduce_scatter | solution.py:370
  1415.6 11.1 all_gather.213
  1426.7 32.3 %reduce-scatter.35.cloned.1.call-done = f32[160,320]{1,0:T(8,128)} async-done(((f32[1280,320]{1,0:T(8,128)}), f32[160,320]{1,0:T(8,128)}) %reduce-scatter.35.cloned.1.call-update) | async-done | bytes 204816 | tf_op jit(solution)/shard_map/reduce_scatter | solution.py:373
  1459.0 11.1 all_gather.215
  1470.1 32.5 %reduce-scatter.25.cloned.1.call-done = f32[160,320]{1,0:T(8,128)} async-done(((f32[1280,320]{1,0:T(8,128)}), f32[160,320]{1,0:T(8,128)}) %reduce-scatter.25.cloned.1.call-update) | async-done | bytes 204816 | tf_op jit(solution)/shard_map/reduce_scatter | solution.py:367
  1517.8 28.0 %reduce-scatter.37.cloned.1.call-done = f32[320,160]{0,1:T(8,128)} async-done(((f32[320,1280]{0,1:T(8,128)}), f32[320,160]{0,1:T(8,128)}) %reduce-scatter.37.cloned.1.call-update) | async-done | bytes 204816 | tf_op jit(solution)/shard_map/reduce_scatter | solution.py:379
  1561.4 51.4 %reduce-scatter.41.cloned.1.call-done = f32[160,1280]{1,0:T(8,128)} async-done(((f32[1280,1280]{1,0:T(8,128)}), f32[160,1280]{1,0:T(8,128)}) %reduce-scatter.41.cloned.1.call-update) | async-done | bytes 819216 | tf_op jit(solution)/shard_map/reduce_scatter | solution.py:376
  1612.8 45.2 %reduce-scatter.29.cloned.1.call-done = f32[160,320]{1,0:T(8,128)} async-done(((f32[1280,320]{1,0:T(8,128)}), f32[160,320]{1,0:T(8,128)}) %reduce-scatter.29.cloned.1.call-update) | async-done | bytes 204816 | tf_op jit(solution)/shard_map/reduce_scatter | solution.py:370
  1673.4 28.2 %reduce-scatter.33.cloned.1.call-done = f32[160,320]{1,0:T(8,128)} async-done(((f32[1280,320]{1,0:T(8,128)}), f32[160,320]{1,0:T(8,128)}) %reduce-scatter.33.cloned.1.call-update) | async-done | bytes 204816 | tf_op jit(solution)/shard_map/reduce_scatter | solution.py:373
  1723.6 42.3 %all-reduce.48.cloned.1.call-done = (f32[1,320]{1,0:T(1,128)}, f32[1,320]{1,0:T(1,128)}, f32[1,320]{1,0:T(1,128)}, f32[1,320]{1,0:T(1,128)}, f32[1,1280]{1,0:T(1...) async-done(((f32[1,320]{1,0:T(1,128)}, f32[1,320]{1,0:T(1,128)}, ...) | async-done | bytes 76816 | tf_op jit(solution)/shard_map/psum | solution.py:418
  1776.2 11.0 all-reduce.26
  (547 shorter events, 534.3 us)
Async XLA Ops:
  51.3 154.1 %all-reduce.36.cloned.1.call-start = ((), (), s32[]{:S(2)}) async-start(), calls=%async_computation.16 | async-start | bytes 5242880 | tf_op jit(solution)/shard_map/psum | solution.py:60
  99.9 109.5 %all-gather.53.cloned.1.call-start = ((), (), s32[]{:S(2)}) async-start(), calls=%async_computation.44 | async-start | bytes 4915200 | tf_op jit(solution)/shard_map/all_gather | solution.py:106
  105.1 109.1 %all-gather.55.cloned.1.call-start = ((), (), s32[]{:S(2)}) async-start(), calls=%async_computation.45 | async-start | bytes 4915200 | tf_op jit(solution)/shard_map/all_gather | solution.py:112
  111.2 212.4 %all-reduce.38.cloned.1.call-start = ((), (), s32[]{:S(2)}) async-start(), calls=%async_computation.17 | async-start | bytes 5242880 | tf_op jit(solution)/shard_map/psum | solution.py:60
  220.3 149.7 %all-gather.59.cloned.1.call-start = ((), (), s32[]{:S(2)}) async-start(), calls=%async_computation.47 | async-start | bytes 1638400 | tf_op jit(solution)/shard_map/all_gather | solution.py:228
  366.8 133.0 %all-reduce.40.cloned.1.call-start = ((), (), s32[]{:S(2)}) async-start(), calls=%async_computation.18 | async-start | bytes 5242880 | tf_op jit(solution)/shard_map/psum | solution.py:60
  395.5 108.4 %all-gather.61.cloned.1.call-start = ((), (), s32[]{:S(2)}) async-start(), calls=%async_computation.48 | async-start | bytes 4915200 | tf_op jit(solution)/shard_map/all_gather | solution.py:106
  396.0 114.1 %all-gather.63.cloned.1.call-start = ((), (), s32[]{:S(2)}) async-start(), calls=%async_computation.49 | async-start | bytes 4915200 | tf_op jit(solution)/shard_map/all_gather | solution.py:112
  396.8 227.7 %all-reduce.42.cloned.1.call-start = ((), (), s32[]{:S(2)}) async-start(), calls=%async_computation.19 | async-start | bytes 5242880 | tf_op jit(solution)/shard_map/psum | solution.py:64
  521.3 176.7 %reduce-scatter.17.cloned.1.call-start = ((), (), s32[]{:S(2)}) async-start(), calls=%async_computation.20 | async-start | bytes 3276800 | tf_op jit(solution)/shard_map/reduce_scatter | solution.py:333
  675.5 168.0 %all-reduce.44.cloned.1.call-start = ((), (), s32[]{:S(2)}) async-start(), calls=%async_computation.22 | async-start | bytes 5242880 | tf_op jit(solution)/shard_map/psum | solution.py:64
  739.3 221.7 %all-reduce.46.cloned.1.call-start = ((), (), s32[]{:S(2)}) async-start(), calls=%async_computation.23 | async-start | bytes 5242880 | tf_op jit(solution)/shard_map/psum | solution.py:64
  857.7 171.8 %reduce-scatter.21.cloned.1.call-start = ((), (), s32[]{:S(2)}) async-start(), calls=%async_computation.24 | async-start | bytes 3276800 | tf_op jit(solution)/shard_map/reduce_scatter | solution.py:333
  996.0 70.4 %reduce-scatter.23.cloned.1.call-start = ((), (), s32[]{:S(2)}) async-start(), calls=%async_computation.25 | async-start | bytes 3276800 | tf_op jit(solution)/shard_map/reduce_scatter | solution.py:334
  1005.9 253.4 %all-reduce.50.cloned.1.call-start = ((), (), s32[]{:S(2)}) async-start(), calls=%async_computation.51 | async-start | bytes 10485760 | tf_op jit(solution)/shard_map/psum | solution.py:60
  1070.2 192.6 %reduce-scatter.47.cloned.1.call-start = ((), (), s32[]{:S(2)}) async-start(), calls=%async_computation.40 | async-start | bytes 7372800 | tf_op jit(solution)/shard_map/reduce_scatter | solution.py:382
  1078.4 184.9 %reduce-scatter.45.cloned.1.call-start = ((), (), s32[]{:S(2)}) async-start(), calls=%async_computation.38 | async-start | bytes 7372800 | tf_op jit(solution)/shard_map/reduce_scatter | solution.py:382
  1086.6 188.3 %reduce-scatter.43.cloned.1.call-start = ((), (), s32[]{:S(2)}) async-start(), calls=%async_computation.36 | async-start | bytes 7372800 | tf_op jit(solution)/shard_map/reduce_scatter | solution.py:376
  1095.3 231.9 %reduce-scatter.27.cloned.1.call-start = ((), (), s32[]{:S(2)}) async-start(), calls=%async_computation.27 | async-start | bytes 2211840 | tf_op jit(solution)/shard_map/reduce_scatter | solution.py:367
  1099.8 272.3 %reduce-scatter.39.cloned.1.call-start = ((), (), s32[]{:S(2)}) async-start(), calls=%async_computation.33 | async-start | bytes 2211840 | tf_op jit(solution)/shard_map/reduce_scatter | solution.py:379
  1102.2 313.4 %reduce-scatter.31.cloned.1.call-start = ((), (), s32[]{:S(2)}) async-start(), calls=%async_computation.29 | async-start | bytes 2211840 | tf_op jit(solution)/shard_map/reduce_scatter | solution.py:370
  1107.2 351.8 %reduce-scatter.35.cloned.1.call-start = ((), (), s32[]{:S(2)}) async-start(), calls=%async_computation.31 | async-start | bytes 2211840 | tf_op jit(solution)/shard_map/reduce_scatter | solution.py:373
  1110.9 391.6 %reduce-scatter.25.cloned.1.call-start = ((), (), s32[]{:S(2)}) async-start(), calls=%async_computation.26 | async-start | bytes 2211840 | tf_op jit(solution)/shard_map/reduce_scatter | solution.py:367
  1114.9 430.9 %reduce-scatter.37.cloned.1.call-start = ((), (), s32[]{:S(2)}) async-start(), calls=%async_computation.32 | async-start | bytes 2211840 | tf_op jit(solution)/shard_map/reduce_scatter | solution.py:379
  1119.2 493.7 %reduce-scatter.41.cloned.1.call-start = ((), (), s32[]{:S(2)}) async-start(), calls=%async_computation.34 | async-start | bytes 7372800 | tf_op jit(solution)/shard_map/reduce_scatter | solution.py:376
  1126.3 531.7 %reduce-scatter.29.cloned.1.call-start = ((), (), s32[]{:S(2)}) async-start(), calls=%async_computation.28 | async-start | bytes 2211840 | tf_op jit(solution)/shard_map/reduce_scatter | solution.py:370
  1130.0 571.5 %reduce-scatter.33.cloned.1.call-start = ((), (), s32[]{:S(2)}) async-start(), calls=%async_computation.30 | async-start | bytes 2211840 | tf_op jit(solution)/shard_map/reduce_scatter | solution.py:373
  1133.8 632.1 %all-reduce.48.cloned.1.call-start = ((), (), s32[]{:S(2)}) async-start(), calls=%async_computation.50 | async-start | bytes 229376 | tf_op jit(solution)/shard_map/psum | solution.py:418
  1262.7 532.1 %all-gather.47.cloned.1.call-start = ((), (), s32[]{:S(2)}) async-start(), calls=%async_computation.41 | async-start | bytes 4096000 | tf_op jit(solution)/shard_map/all_gather | solution.py:410
  1263.2 531.5 %all-gather.45.cloned.1.call-start = ((), (), s32[]{:S(2)}) async-start(), calls=%async_computation.39 | async-start | bytes 4096000 | tf_op jit(solution)/shard_map/all_gather | solution.py:410
  1263.8 545.1 %all-gather.43.cloned.1.call-start = ((), (), s32[]{:S(2)}) async-start(), calls=%async_computation.37 | async-start | bytes 4096000 | tf_op jit(solution)/shard_map/all_gather | solution.py:408
  1274.9 534.1 %all-gather.41.cloned.1.call-start = ((), (), s32[]{:S(2)}) async-start(), calls=%async_computation.35 | async-start | bytes 4096000 | tf_op jit(solution)/shard_map/all_gather | solution.py:408
  (126 other events, 2325.6 us)
Sparse Core Ops, SparseCore 0:
  37.0 19.6 all-gather.50
  58.8 18.1 all-gather.48
  100.1 105.2 all-reduce.35
  220.4 103.0 all-reduce.37
  330.0 17.1 all-gather.58
  366.9 17.1 all-gather.56
  395.6 104.0 all-reduce.39
  521.4 103.0 all-reduce.41
  664.5 33.3 reduce-scatter.16
  700.3 34.3 reduce-scatter.18
  739.4 104.0 all-reduce.43
  857.9 103.0 all-reduce.45
  996.2 33.3 reduce-scatter.20
  1032.0 34.3 reduce-scatter.22
  1070.3 188.9 all-reduce.49
  1264.7 28.1 all-gather.46
  1294.4 31.1 all-gather.44
  1327.0 29.5 all-gather.42
  1613.0 29.5 all-gather.40
Sparse Core Ops, SparseCore 1:
  105.2 47.5 all-gather.52
  154.7 46.2 all-gather.54
  398.1 46.2 all-gather.60
  446.5 46.2 all-gather.62
  1078.5 63.2 reduce-scatter.46
  1145.2 62.8 reduce-scatter.44
  1212.0 62.8 reduce-scatter.42
  1278.1 49.1 reduce-scatter.26
  1330.6 41.5 reduce-scatter.38
  1375.5 40.0 reduce-scatter.30
  1418.9 40.0 reduce-scatter.34
  1462.4 40.1 reduce-scatter.24
  1505.8 40.0 reduce-scatter.36
  1549.9 62.8 reduce-scatter.40
  1616.2 41.8 reduce-scatter.28
  1661.5 40.0 reduce-scatter.32
  1707.9 57.9 all-reduce.47
where the time goes:
time: 1830 us; the launch traced here: 1820 us
  waiting for transfers between devices  1150 us (63%)
  blocking collectives  228 us (12%)
  matrix products  222 us (12%)
  other arithmetic  111 us (6%)
  local copies, waits for them, and re-layouts  86.9 us (5%)
  between operations  19.8 us (1%)
    psum x4, waiting for transfers between devices, head_sums(): return lax.psum(partial_out, 'tp')  365 us
    psum x3, waiting for transfers between devices, input_sums(): return lax.psum(partial_in, 'tp')  310 us
    reduce_scatter x2, waiting for transfers between devices, per_device(): lax.psum_scatter(backward_large_terms[0], ('fsdp', 'ctx'), scatter_dimens...  77.9 us
    reduce_scatter x2, waiting for transfers between devices, per_device(): lax.psum_scatter(backward_large_terms[1], ('fsdp', 'ctx'), scatter_dimens...  77.7 us
    unnamed x275, local copies, waits for them, and re-layouts  71.8 us
    reduce_scatter x2, waiting for transfers between devices, per_device(): lax.psum_scatter(grad_value_part, 'ctx', scatter_dimension=1, tiled=True)  66.5 us
    reduce_scatter x2, waiting for transfers between devices, per_device(): lax.psum_scatter(backward_large_terms[4], ('fsdp', 'ctx'), scatter_dimens...  62.7 us
    reduce_scatter x2, waiting for transfers between devices, per_device(): lax.psum_scatter(backward_large_terms[3], ('fsdp', 'ctx'), scatter_dimens...  62.4 us
  transfers between devices with their start and end apart: 36, of which 23 were waited for; matrix products, arithmetic and copies ran while one was open for 13% of the time, Pallas kernels for 0%

commit v1 on v0

v1 whole, which is shorter than its diff:
```python
import math

import jax
import jax.numpy as jnp
from jax import lax
from jax.sharding import PartitionSpec as P

HD = 80
LAYERS = 2


EPSILON = 1e-05
NEGATIVE = -1e30
ROOT_HALF = 1.0 / math.sqrt(2.0)
DENSITY = 1.0 / math.sqrt(2.0 * math.pi)
LOW = jnp.bfloat16
WIDE = jnp.float32


def norm_parts(values):
    average = jnp.mean(values, axis=-1, keepdims=True)
    centered = values - average
    spread = jnp.mean(centered * centered, axis=-1, keepdims=True)
    inverse = lax.rsqrt(spread + EPSILON)
    return (centered * inverse, inverse)


def norm_back(upstream, normal_hat, inverse, gain_full):
    scaled = upstream * gain_full
    first_mean = jnp.mean(scaled, axis=-1, keepdims=True)
    second_mean = jnp.mean(scaled * normal_hat, axis=-1, keepdims=True)
    return inverse * (scaled - first_mean - normal_hat * second_mean)


def gelu_value(values):
    return 0.5 * values * (1.0 + lax.erf(values * ROOT_HALF))


def gelu_slope(values):
    return 0.5 * (1.0 + lax.erf(values * ROOT_HALF)) + values * DENSITY * jnp.exp(
        -0.5 * values * values
    )


def matmul(left_side, right_side):
    return jnp.dot(left_side, right_side, preferred_element_type=WIDE)


def contract_rows(left_side, right_side):
    return lax.dot_general(
        left_side, right_side, (((0,), (0,)), ((), ())), preferred_element_type=WIDE
    )


def contract_cols(left_side, right_side):
    return lax.dot_general(
        left_side, right_side, (((1,), (1,)), ((), ())), preferred_element_type=WIDE
    )


def scatter_rows(partial):
    return lax.psum_scatter(partial.astype(LOW), "tp", scatter_dimension=0, tiled=True).astype(WIDE)


def gather_rows(own):
    return lax.all_gather(own, "tp", axis=0, tiled=True)


def per_device(
    hidden,
    cotangent,
    lengths,
    query_weight,
    key_weight,
    value_weight,
    output_weight,
    inner_weight,
    outer_weight,
    query_bias,
    value_bias,
    inner_bias,
    output_bias,
    outer_bias,
    first_gain,
    first_shift,
    second_gain,
    second_shift,
):
    clip_count, frames_local, width = hidden.shape
    rows = clip_count * frames_local
    frames_all = frames_local * lax.axis_size("ctx")
    tp_size = lax.axis_size("tp")
    own_rows = rows // tp_size
    columns = query_weight.shape[2]
    heads_local = columns // HD
    scale = 1.0 / math.sqrt(HD)
    valid_keys = jnp.arange(frames_all)[None, :] < lengths[:, None]
    own_start = lax.axis_index("tp") * own_rows

    def own_slice(full):
        return lax.dynamic_slice_in_dim(full, own_start, own_rows, axis=0)

    small = jnp.concatenate(
        [output_bias, outer_bias, first_gain, first_shift, second_gain, second_shift], axis=0
    ).astype(LOW)
    small = lax.all_gather(small, "fsdp", axis=1, tiled=True).astype(WIDE)

    def vector(kind, layer):
        return small[kind * LAYERS + layer]

    def fetch(layer):
        qkv = jnp.concatenate(
            [query_weight[layer], key_weight[layer], value_weight[layer]], axis=1
        ).astype(LOW)
        qkv = lax.all_gather(qkv, "fsdp", axis=0, tiled=True)
        out = lax.all_gather(output_weight[layer].astype(LOW), "fsdp", axis=1, tiled=True)
        inner = lax.all_gather(inner_weight[layer].astype(LOW), "fsdp", axis=0, tiled=True)
        outer = lax.all_gather(outer_weight[layer].astype(LOW), "fsdp", axis=1, tiled=True)
        return (qkv, out, inner, outer)

    def scores_of(query_block, key_block, mask_row):
        scores = (
            jnp.einsum(
                "qhd,khd->hqk",
                query_block.reshape(frames_local, heads_local, HD),
                key_block.reshape(frames_all, heads_local, HD),
                preferred_element_type=WIDE,
            )
            * scale
        )
        return jnp.where(mask_row[None, None, :], scores, NEGATIVE)

    def attend(packed):
        query_block, key_block, value_block, mask_row = packed
        scores = scores_of(query_block, key_block, mask_row)
        highest = jnp.max(scores, axis=-1, keepdims=True)
        raised = jnp.exp(scores - highest)
        total = jnp.sum(raised, axis=-1, keepdims=True)
        weights_soft = (raised / total).astype(LOW)
        attended = jnp.einsum(
            "hqk,khd->qhd",
            weights_soft,
            value_block.reshape(frames_all, heads_local, HD),
            preferred_element_type=WIDE,
        )
        return (attended.reshape(frames_local, columns), (highest + jnp.log(total))[:, :, 0])

    def attend_back(packed):
        query_block, key_block, value_block, grad_block, log_total, mask_row = packed
        scores = scores_of(query_block, key_block, mask_row)
        weights_full = jnp.exp(scores - log_total[:, :, None])
        grad_heads = grad_block.reshape(frames_local, heads_local, HD)
        grad_weights = jnp.einsum(
            "qhd,khd->hqk",
            grad_heads,
            value_block.reshape(frames_all, heads_local, HD),
            preferred_element_type=WIDE,
        )
        row_terms = jnp.sum(weights_full * grad_weights, axis=-1, keepdims=True)
        grad_scores = (weights_full * (grad_weights - row_terms)).astype(LOW)
        grad_query = (
            jnp.einsum(
                "hqk,khd->qhd",
                grad_scores,
                key_block.reshape(frames_all, heads_local, HD),
                preferred_element_type=WIDE,
            )
            * scale
        )
        grad_key = (
            jnp.einsum(
                "hqk,qhd->khd",
                grad_scores,
                query_block.reshape(frames_local, heads_local, HD),
                preferred_element_type=WIDE,
            )
            * scale
        )
        grad_value = jnp.einsum(
            "hqk,qhd->khd",
            weights_full.astype(LOW),
            grad_heads,
            preferred_element_type=WIDE,
        )
        return (
            grad_query.reshape(frames_local, columns),
            grad_key.reshape(frames_all, columns),
            grad_value.reshape(frames_all, columns),
        )

    def clips(values):
        return values.reshape(clip_count, -1, values.shape[-1])

    weights = [fetch(layer) for layer in range(LAYERS)]

    residual = own_slice(hidden.reshape(rows, width))
    kept = []
    for layer in range(LAYERS):
        w_qkv, w_out, w_inner, w_outer = weights[layer]
        if layer == 0:
            hat_full, _ = norm_parts(hidden.reshape(rows, width))
            normed = (hat_full * vector(2, layer) + vector(3, layer)).astype(LOW)
            hat_first, inverse_first = norm_parts(residual)
        else:
            hat_first, inverse_first = norm_parts(residual)
            normed = gather_rows((hat_first * vector(2, layer) + vector(3, layer)).astype(LOW))
        bias_qkv = jnp.concatenate(
            [query_bias[layer], jnp.zeros_like(query_bias[layer]), value_bias[layer]]
        )
        qkv = (matmul(normed, w_qkv) + bias_qkv).astype(LOW)
        queries = qkv[:, :columns]
        key_value = lax.all_gather(clips(qkv[:, columns:]), "ctx", axis=1, tiled=True)
        key_all = key_value[:, :, :columns]
        value_all = key_value[:, :, columns:]
        attended, log_total = lax.map(attend, (clips(queries), key_all, value_all, valid_keys))
        attended = attended.reshape(rows, columns).astype(LOW)
        middle = residual + scatter_rows(matmul(attended, w_out)) + vector(0, layer)
        hat_second, inverse_second = norm_parts(middle)
        normed_two = gather_rows((hat_second * vector(4, layer) + vector(5, layer)).astype(LOW))
        inner_pre = matmul(normed_two, w_inner) + inner_bias[layer]
        active = gelu_value(inner_pre).astype(LOW)
        residual = middle + scatter_rows(matmul(active, w_outer)) + vector(1, layer)
        kept.append(
            (
                hat_first,
                inverse_first,
                normed,
                queries,
                key_all,
                value_all,
                log_total,
                attended,
                hat_second,
                inverse_second,
                normed_two,
                inner_pre,
                active,
            )
        )
    output = gather_rows(residual)

    grad_own = own_slice(cotangent.reshape(rows, width))
    grad_low = cotangent.reshape(rows, width).astype(LOW)
    grads = [None] * LAYERS
    vectors = [None] * LAYERS
    biases = [None] * LAYERS
    for layer in reversed(range(LAYERS)):
        w_qkv, w_out, w_inner, w_outer = weights[layer]
        (
            hat_first,
            inverse_first,
            normed,
            queries,
            key_all,
            value_all,
            log_total,
            attended,
            hat_second,
            inverse_second,
            normed_two,
            inner_pre,
            active,
        ) = kept[layer]
        if layer != LAYERS - 1:
            grad_low = gather_rows(grad_own.astype(LOW))
        grad_active = contract_cols(grad_low, w_outer)
        grad_inner = (grad_active * gelu_slope(inner_pre)).astype(LOW)
        grad_normed_two = scatter_rows(contract_cols(grad_inner, w_inner))
        grad_outer_w = contract_rows(active, grad_low)
        grad_inner_w = contract_rows(normed_two, grad_inner)
        grad_middle = grad_own + norm_back(
            grad_normed_two, hat_second, inverse_second, vector(4, layer)
        )
        grad_mid_low = gather_rows(grad_middle.astype(LOW))
        grad_attended = contract_cols(grad_mid_low, w_out).astype(LOW)
        grad_output_w = contract_rows(attended, grad_mid_low)
        grad_query, grad_key_part, grad_value_part = lax.map(
            attend_back,
            (clips(queries), key_all, value_all, clips(grad_attended), log_total, valid_keys),
        )
        grad_kv_part = jnp.concatenate([grad_key_part, grad_value_part], axis=-1).astype(LOW)
        grad_kv = lax.psum_scatter(grad_kv_part, "ctx", scatter_dimension=1, tiled=True)
        grad_qkv = jnp.concatenate(
            [grad_query.reshape(rows, columns).astype(LOW), grad_kv.reshape(rows, 2 * columns)],
            axis=1,
        )
        grad_normed = scatter_rows(contract_cols(grad_qkv, w_qkv))
        grad_in = grad_middle + norm_back(grad_normed, hat_first, inverse_first, vector(2, layer))
        by_rows = jnp.concatenate([contract_rows(normed, grad_qkv), grad_inner_w], axis=1)
        by_cols = jnp.concatenate([grad_output_w, grad_outer_w], axis=0)
        by_rows = lax.psum_scatter(
            by_rows.astype(LOW), ("fsdp", "ctx"), scatter_dimension=0, tiled=True
        )
        by_rows = lax.all_gather(by_rows, "ctx", axis=0, tiled=True).astype(WIDE)
        by_cols = lax.psum_scatter(
            by_cols.astype(LOW), ("fsdp", "ctx"), scatter_dimension=1, tiled=True
        )
        by_cols = lax.all_gather(by_cols, "ctx", axis=1, tiled=True).astype(WIDE)
        grads[layer] = (by_rows, by_cols)
        vectors[layer] = jnp.stack(
            [
                jnp.sum(grad_middle, axis=0),
                jnp.sum(grad_own, axis=0),
                jnp.sum(grad_normed * hat_first, axis=0),
                jnp.sum(grad_normed, axis=0),
                jnp.sum(grad_normed_two * hat_second, axis=0),
                jnp.sum(grad_normed_two, axis=0),
            ]
        )
        biases[layer] = jnp.concatenate(
            [
                jnp.sum(grad_qkv.astype(WIDE), axis=0),
                jnp.sum(grad_inner.astype(WIDE), axis=0),
            ]
        )
        grad_own = grad_in
    grad_hidden = gather_rows(grad_own)

    vector_sums = lax.psum(jnp.stack(vectors, axis=1), ("fsdp", "ctx", "tp"))
    bias_sums = lax.psum(jnp.stack(biases), ("fsdp", "ctx"))
    shard = output_bias.shape[1]
    vector_sums = lax.dynamic_slice_in_dim(
        vector_sums, lax.axis_index("fsdp") * shard, shard, axis=2
    )

    def stacked_rows(start, size):
        return jnp.stack([grads[layer][0][:, start : start + size] for layer in range(LAYERS)])

    def stacked_cols(start, size):
        return jnp.stack([grads[layer][1][start : start + size] for layer in range(LAYERS)])

    hidden_local = inner_weight.shape[2]
    return (
        output.reshape(hidden.shape),
        grad_hidden.reshape(hidden.shape),
        stacked_rows(0, columns),
        stacked_rows(columns, columns),
        stacked_rows(2 * columns, columns),
        stacked_cols(0, columns),
        stacked_rows(3 * columns, hidden_local),
        stacked_cols(columns, hidden_local),
        bias_sums[:, :columns],
        bias_sums[:, 2 * columns : 3 * columns],
        bias_sums[:, 3 * columns :],
        vector_sums[0],
        vector_sums[1],
        vector_sums[2],
        vector_sums[3],
        vector_sums[4],
        vector_sums[5],
    )


def solution(mesh):
    in_specs = (
        P("fsdp", "ctx", None),
        P("fsdp", "ctx", None),
        P("fsdp"),
        P(None, "fsdp", "tp"),
        P(None, "fsdp", "tp"),
        P(None, "fsdp", "tp"),
        P(None, "tp", "fsdp"),
        P(None, "fsdp", "tp"),
        P(None, "tp", "fsdp"),
        P(None, "tp"),
        P(None, "tp"),
        P(None, "tp"),
        P(None, "fsdp"),
        P(None, "fsdp"),
        P(None, "fsdp"),
        P(None, "fsdp"),
        P(None, "fsdp"),
        P(None, "fsdp"),
    )
    out_specs = (
        P("fsdp", "ctx", None),
        P("fsdp", "ctx", None),
        P(None, "fsdp", "tp"),
        P(None, "fsdp", "tp"),
        P(None, "fsdp", "tp"),
        P(None, "tp", "fsdp"),
        P(None, "fsdp", "tp"),
        P(None, "tp", "fsdp"),
        P(None, "tp"),
        P(None, "tp"),
        P(None, "tp"),
        P(None, "fsdp"),
        P(None, "fsdp"),
        P(None, "fsdp"),
        P(None, "fsdp"),
        P(None, "fsdp"),
        P(None, "fsdp"),
    )
    return jax.shard_map(
        per_device, mesh=mesh, in_specs=in_specs, out_specs=out_specs, check_vma=False
    )
```

time: 1830 us -> 1520 us (0.83)
  blocking collectives: 228 us -> 96.3 us
  waiting for transfers between devices: 1150 us -> 1020 us
  matrix products: 222 us -> 161 us
    psum x8 -> x0, waiting for transfers between devices: 717 us -> none  [the longest x4 365 us: head_sums(): return lax.psum(partial_out, 'tp')]
    all_gather x12 -> x20, waiting for transfers between devices: 0.54 us -> 561 us  [the longest x8 248 us: gather_rows(): return lax.all_gather(own, 'tp', axis=0, tiled=True)]
    all_gather x28 -> x3, blocking collectives: 217 us -> 28.4 us  [the longest x2 23.1 us: fetch(): lax.all_gather(output_weight[layer].astype(LOW), 'fsdp', axis=1, tiled=True)]
    unnamed x36, waiting for transfers between devices: 2.72 us -> 86.6 us
    psum x0 -> x2, blocking collectives: none -> 67.9 us  [the longest x1 44 us: per_device(): vector_sums = lax.psum(jnp.stack(vectors, axis=1), ('fsdp', 'ctx', 'tp'))]
    reduce_scatter x16 -> x12, waiting for transfers between devices: 432 us -> 372 us  [the longest x8 240 us: scatter_rows(): lax.psum_scatter(partial.astype(LOW), 'tp', scatter_dimension=0, tiled=True)]
    dot_general x12 -> x8, matrix products: 52.9 us -> 19.2 us  [contract_rows(): lax.dot_general(left_side, right_side, (((0,), (0,)), ((), ())), preferre...]
    another operation x27 -> x20, other arithmetic: 42.2 us -> 26.9 us  [the longest x4 12.5 us: stacked_rows(): jnp.stack([grads[layer][0][:, start:start + size] for layer in range(LAYE...]
  transfers between devices with their start and end apart: 36 -> 34, of which waited for: 23 -> 31; matrix products, arithmetic and copies ran while one was open for 13% -> 11% of each run, Pallas kernels for 0% -> 0%
where the time goes in v1:
time: 1520 us; the launch traced here: 1510 us
  waiting for transfers between devices  1020 us (67%)
  matrix products  161 us (11%)
  local copies, waits for them, and re-layouts  105 us (7%)
  other arithmetic  105 us (7%)
  blocking collectives  96.3 us (6%)
  between operations  17 us (1%)
    all_gather x8, waiting for transfers between devices, gather_rows(): return lax.all_gather(own, 'tp', axis=0, tiled=True)  248 us
    reduce_scatter x8, waiting for transfers between devices, scatter_rows(): lax.psum_scatter(partial.astype(LOW), 'tp', scatter_dimension=0, tiled=True)  240 us
    reduce_scatter x2, waiting for transfers between devices, per_device(): lax.psum_scatter(by_rows.astype(LOW), ('fsdp', 'ctx'), scatter_dimension=...  104 us
    unnamed x36, waiting for transfers between devices  86.6 us
    all_gather x2, waiting for transfers between devices, fetch(): lax.all_gather(outer_weight[layer].astype(LOW), 'fsdp', axis=1, tiled=True)  83 us
    all_gather x2, waiting for transfers between devices, fetch(): lax.all_gather(inner_weight[layer].astype(LOW), 'fsdp', axis=0, tiled=True)  82.3 us
    unnamed x177, local copies, waits for them, and re-layouts  73.5 us
    all_gather x2, waiting for transfers between devices, fetch(): qkv = lax.all_gather(qkv, 'fsdp', axis=0, tiled=True)  69 us
  transfers between devices with their start and end apart: 34, of which 31 were waited for; matrix products, arithmetic and copies ran while one was open for 11% of the time, Pallas kernels for 0%

profile of v1, /device:TPU:0, one launch (start us, length us, event | category | flops | bytes accessed | tf_op | source)
XLA Modules:
  0.0 1507.3 jit_solution(7102906882543084944)
XLA Ops:
  19.4 33.4 %all-gather.29.cloned.1.call-done = bf16[1280,960]{0,1:T(8,128)(2,1)} async-done(((bf16[640,960]{0,1:T(8,128)(2,1)}), bf16[1280,960]{0,1:T(8,128)(2,1)}) %all-gather.29.cloned.1.call-update) | async-done | bytes 2457616 | tf_op jit(solution)/shard_map/all_gather | solution.py:115
  107.0 26.1 %reduce-scatter.23.cloned.1.call-done = bf16[128,1280]{1,0:T(8,128)(2,1)} async-done(((bf16[512,1280]{1,0:T(8,128)(2,1)}), bf16[128,1280]{1,0:T(8,128)(2,1)}) %reduce-scatter.23.cloned.1.call-update) | async-done | bytes 327696 | tf_op jit(solution)/shard_map/reduce_scatter | solution.py:62
  141.6 38.6 %all-gather.59.cloned.1.call-done = bf16[1,1280,1280]{2,1,0:T(8,128)(2,1)} async-done(((bf16[1,640,1280]{2,1,0:T(8,128)(2,1)}), bf16[1,1280,1280]{2,1,0:T(8,128)(2,1)}) %all-gather.59.cloned.1.call-update) | async-done | bytes 3276816 | tf_op jit(solution)/shard_map/all_gather | solution.py:117
  180.2 34.5 %all-gather.31.cloned.1.call-done = bf16[512,1280]{1,0:T(8,128)(2,1)} async-done(((bf16[128,1280]{1,0:T(8,128)(2,1)}), bf16[512,1280]{1,0:T(8,128)(2,1)}) %all-gather.31.cloned.1.call-update) | async-done | bytes 1310736 | tf_op jit(solution)/shard_map/all_gather | solution.py:66
  220.5 41.7 %all-gather.61.cloned.1.call-done = bf16[1,1280,1280]{2,1,0:T(8,128)(2,1)} async-done(((bf16[1,1280,640]{2,1,0:T(8,128)(2,1)}), bf16[1,1280,1280]{2,1,0:T(8,128)(2,1)}) %all-gather.61.cloned.1.call-update) | async-done | bytes 3276816 | tf_op jit(solution)/shard_map/all_gather | solution.py:118
  268.5 30.2 %reduce-scatter.25.cloned.1.call-done = bf16[128,1280]{1,0:T(8,128)(2,1)} async-done(((bf16[512,1280]{1,0:T(8,128)(2,1)}), bf16[128,1280]{1,0:T(8,128)(2,1)}) %reduce-scatter.25.cloned.1.call-update) | async-done | bytes 327696 | tf_op jit(solution)/shard_map/reduce_scatter | solution.py:62
  301.1 35.6 %all-gather.35.cloned.1.call-done = bf16[1280,960]{0,1:T(8,128)(2,1)} async-done(((bf16[640,960]{0,1:T(8,128)(2,1)}), bf16[1280,960]{0,1:T(8,128)(2,1)}) %all-gather.35.cloned.1.call-update) | async-done | bytes 2457616 | tf_op jit(solution)/shard_map/all_gather | solution.py:115
  336.7 34.7 %all-gather.33.cloned.1.call-done = bf16[512,1280]{1,0:T(8,128)(2,1)} async-done(((bf16[128,1280]{1,0:T(8,128)(2,1)}), bf16[512,1280]{1,0:T(8,128)(2,1)}) %all-gather.33.cloned.1.call-update) | async-done | bytes 1310736 | tf_op jit(solution)/shard_map/all_gather | solution.py:66
  418.6 30.9 %reduce-scatter.27.cloned.1.call-done = bf16[128,1280]{1,0:T(8,128)(2,1)} async-done(((bf16[512,1280]{1,0:T(8,128)(2,1)}), bf16[128,1280]{1,0:T(8,128)(2,1)}) %reduce-scatter.27.cloned.1.call-update) | async-done | bytes 327696 | tf_op jit(solution)/shard_map/reduce_scatter | solution.py:62
  452.8 43.7 %all-gather.65.cloned.1.call-done = bf16[1,1280,1280]{2,1,0:T(8,128)(2,1)} async-done(((bf16[1,640,1280]{2,1,0:T(8,128)(2,1)}), bf16[1,1280,1280]{2,1,0:T(8,128)(2,1)}) %all-gather.65.cloned.1.call-update) | async-done | bytes 3276816 | tf_op jit(solution)/shard_map/all_gather | solution.py:117
  496.5 34.7 %all-gather.37.cloned.1.call-done = bf16[512,1280]{1,0:T(8,128)(2,1)} async-done(((bf16[128,1280]{1,0:T(8,128)(2,1)}), bf16[512,1280]{1,0:T(8,128)(2,1)}) %all-gather.37.cloned.1.call-update) | async-done | bytes 1310736 | tf_op jit(solution)/shard_map/all_gather | solution.py:66
  537.5 41.3 %all-gather.67.cloned.1.call-done = bf16[1,1280,1280]{2,1,0:T(8,128)(2,1)} async-done(((bf16[1,1280,640]{2,1,0:T(8,128)(2,1)}), bf16[1,1280,1280]{2,1,0:T(8,128)(2,1)}) %all-gather.67.cloned.1.call-update) | async-done | bytes 3276816 | tf_op jit(solution)/shard_map/all_gather | solution.py:118
  594.8 26.2 %reduce-scatter.31.cloned.1.call-done = bf16[128,1280]{1,0:T(8,128)(2,1)} async-done(((bf16[512,1280]{1,0:T(8,128)(2,1)}), bf16[128,1280]{1,0:T(8,128)(2,1)}) %reduce-scatter.31.cloned.1.call-update) | async-done | bytes 327696 | tf_op jit(solution)/shard_map/reduce_scatter | solution.py:62
  622.9 30.9 %reduce-scatter.29.cloned.1.call-done = bf16[128,1280]{1,0:T(8,128)(2,1)} async-done(((bf16[512,1280]{1,0:T(8,128)(2,1)}), bf16[128,1280]{1,0:T(8,128)(2,1)}) %reduce-scatter.29.cloned.1.call-update) | async-done | bytes 327696 | tf_op jit(solution)/shard_map/reduce_scatter | solution.py:62
  657.8 31.1 %all-gather.41.cloned.1.call-done = bf16[512,1280]{1,0:T(8,128)(2,1)} async-done(((bf16[128,1280]{1,0:T(8,128)(2,1)}), bf16[512,1280]{1,0:T(8,128)(2,1)}) %all-gather.41.cloned.1.call-update) | async-done | bytes 1310736 | tf_op jit(solution)/shard_map/all_gather | solution.py:66
  692.0 14.7 multiply_reduce_fusion.1
  732.5 26.9 %reduce-scatter.33.cloned.1.call-done = bf16[1,512,640]{1,2,0:T(8,128)(2,1)} async-done(((bf16[1,2048,640]{1,2,0:T(8,128)(2,1)}), bf16[1,512,640]{1,2,0:T(8,128)(2,1)}) %reduce-scatter.33.cloned.1.call-update) | async-done | bytes 655376 | tf_op jit(solution)/shard_map/reduce_scatter | solution.py:282
  764.0 31.5 %reduce-scatter.35.cloned.1.call-done = bf16[128,1280]{1,0:T(8,128)(2,1)} async-done(((bf16[512,1280]{1,0:T(8,128)(2,1)}), bf16[128,1280]{1,0:T(8,128)(2,1)}) %reduce-scatter.35.cloned.1.call-update) | async-done | bytes 327696 | tf_op jit(solution)/shard_map/reduce_scatter | solution.py:62
  798.9 31.3 %all-gather.43.cloned.1.call-done = bf16[512,1280]{1,0:T(8,128)(2,1)} async-done(((bf16[128,1280]{1,0:T(8,128)(2,1)}), bf16[512,1280]{1,0:T(8,128)(2,1)}) %all-gather.43.cloned.1.call-update) | async-done | bytes 1310736 | tf_op jit(solution)/shard_map/all_gather | solution.py:66
  838.9 30.6 %reduce-scatter.37.cloned.1.call-done = bf16[128,1280]{1,0:T(8,128)(2,1)} async-done(((bf16[512,1280]{1,0:T(8,128)(2,1)}), bf16[128,1280]{1,0:T(8,128)(2,1)}) %reduce-scatter.37.cloned.1.call-update) | async-done | bytes 327696 | tf_op jit(solution)/shard_map/reduce_scatter | solution.py:62
  873.3 30.9 %all-gather.45.cloned.1.call-done = bf16[512,1280]{1,0:T(8,128)(2,1)} async-done(((bf16[128,1280]{1,0:T(8,128)(2,1)}), bf16[512,1280]{1,0:T(8,128)(2,1)}) %all-gather.45.cloned.1.call-update) | async-done | bytes 1310736 | tf_op jit(solution)/shard_map/all_gather | solution.py:66
  906.4 14.1 multiply_reduce_fusion
  1005.5 29.5 %reduce-scatter.49.cloned.1.call-done = bf16[160,1600]{1,0:T(8,128)(2,1)} async-done(((bf16[1280,1600]{1,0:T(8,128)(2,1)}), bf16[160,1600]{1,0:T(8,128)(2,1)}) %reduce-scatter.49.cloned.1.call-update) | async-done | bytes 512016
  1053.1 45.6 %reduce-scatter.45.cloned.1.call-done = bf16[160,2240]{1,0:T(8,128)(2,1)} async-done(((bf16[1280,2240]{1,0:T(8,128)(2,1)}), bf16[160,2240]{1,0:T(8,128)(2,1)}) %reduce-scatter.45.cloned.1.call-update) | async-done | bytes 716816 | tf_op jit(solution)/shard_map/reduce_scatter | solution.py:291
  1098.7 54.9 %reduce-scatter.47.cloned.1.call-done = bf16[160,1600]{1,0:T(8,128)(2,1)} async-done(((bf16[1280,1600]{1,0:T(8,128)(2,1)}), bf16[160,1600]{1,0:T(8,128)(2,1)}) %reduce-scatter.47.cloned.1.call-update) | async-done | bytes 512016
  1153.7 34.0 %reduce-scatter.41.cloned.1.call-done = bf16[128,1280]{1,0:T(8,128)(2,1)} async-done(((bf16[512,1280]{1,0:T(8,128)(2,1)}), bf16[128,1280]{1,0:T(8,128)(2,1)}) %reduce-scatter.41.cloned.1.call-update) | async-done | bytes 327696 | tf_op jit(solution)/shard_map/reduce_scatter | solution.py:62
  1192.4 50.3 %all-gather.39.cloned.1.call-done = f32[512,1280]{1,0:T(8,128)} async-done(((f32[128,1280]{1,0:T(8,128)}), f32[512,1280]{1,0:T(8,128)}) %all-gather.39.cloned.1.call-update) | async-done | bytes 2621456 | tf_op jit(solution)/shard_map/all_gather | solution.py:66
  1244.4 21.5 %all-gather.55.cloned.1.call-done = bf16[1600,640]{0,1:T(8,128)(2,1)} async-done(((bf16[1600,160]{0,1:T(8,128)(2,1)}), bf16[1600,640]{0,1:T(8,128)(2,1)}) %all-gather.55.cloned.1.call-update) | async-done | bytes 2048016 | tf_op jit(solution)/shard_map/all_gather | solution.py:298
  1270.8 58.6 %reduce-scatter.43.cloned.1.call-done = bf16[160,2240]{1,0:T(8,128)(2,1)} async-done(((bf16[1280,2240]{1,0:T(8,128)(2,1)}), bf16[160,2240]{1,0:T(8,128)(2,1)}) %reduce-scatter.43.cloned.1.call-update) | async-done | bytes 716816 | tf_op jit(solution)/shard_map/reduce_scatter | solution.py:291
  1334.1 24.3 %all-gather.51.cloned.1.call-done = bf16[640,2240]{1,0:T(8,128)(2,1)} async-done(((bf16[160,2240]{1,0:T(8,128)(2,1)}), bf16[640,2240]{1,0:T(8,128)(2,1)}) %all-gather.51.cloned.1.call-update) | async-done | bytes 2867216 | tf_op jit(solution)/shard_map/all_gather | solution.py:294
  1364.2 23.9 %psum.14 = f32[2,2240]{1,0:T(2,128)S(1)} all-reduce(f32[2,2240]{1,0:T(2,128)S(1)} %pad_maximum_fusion.21), channel_id=1, replica_groups=mesh['fsdp'=2,'ctx'=4,'tp'=4] {'fsdp','ctx'}, use_global_device_ids=true, to_apply=%region_42.43 | all-reduce | flops 4480 | bytes 35840 | tf_op jit(solution)/shard_map/psum | solution.py:320
  1389.5 44.0 %psum.15 = f32[6,2,1280]{2,1,0:T(2,128)S(1)} all-reduce(f32[6,2,1280]{2,1,0:T(2,128)S(1)} %pad_maximum_fusion.20), channel_id=1, replica_groups=mesh['fsdp'=2,'ctx'=4,'tp'=4] {'fsdp','ctx','tp'}, use_global_device_ids=true, to_apply=%region_55.56 | all-reduce | flops 15360 | bytes 122880 | tf_op jit(solution)/shard_map/psum | solution.py:319
  (422 shorter events, 409.9 us)
Async XLA Ops:
  12.8 70.9 %all-gather.57.cloned.1.call-start = ((), (), s32[]{:S(2)}) async-start(), calls=%async_computation.38 | async-start | bytes 3276800 | tf_op jit(solution)/shard_map/all_gather | solution.py:212
  58.0 75.1 %reduce-scatter.23.cloned.1.call-start = ((), (), s32[]{:S(2)}) async-start(), calls=%async_computation.15 | async-start | bytes 1638400 | tf_op jit(solution)/shard_map/reduce_scatter | solution.py:62
  101.6 78.6 %all-gather.59.cloned.1.call-start = ((), (), s32[]{:S(2)}) async-start(), calls=%async_computation.39 | async-start | bytes 4915200 | tf_op jit(solution)/shard_map/all_gather | solution.py:117
  106.8 107.9 %all-gather.31.cloned.1.call-start = ((), (), s32[]{:S(2)}) async-start(), calls=%async_computation.16 | async-start | bytes 1638400 | tf_op jit(solution)/shard_map/all_gather | solution.py:66
  136.0 126.2 %all-gather.61.cloned.1.call-start = ((), (), s32[]{:S(2)}) async-start(), calls=%async_computation.40 | async-start | bytes 4915200 | tf_op jit(solution)/shard_map/all_gather | solution.py:118
  141.3 157.4 %reduce-scatter.25.cloned.1.call-start = ((), (), s32[]{:S(2)}) async-start(), calls=%async_computation.17 | async-start | bytes 1638400 | tf_op jit(solution)/shard_map/reduce_scatter | solution.py:62
  267.2 69.5 %all-gather.35.cloned.1.call-start = ((), (), s32[]{:S(2)}) async-start(), calls=%async_computation.19 | async-start | bytes 3686400 | tf_op jit(solution)/shard_map/all_gather | solution.py:115
  268.4 103.0 %all-gather.33.cloned.1.call-start = ((), (), s32[]{:S(2)}) async-start(), calls=%async_computation.18 | async-start | bytes 1638400 | tf_op jit(solution)/shard_map/all_gather | solution.py:66
  301.0 99.7 %all-gather.63.cloned.1.call-start = ((), (), s32[]{:S(2)}) async-start(), calls=%async_computation.41 | async-start | bytes 3276800 | tf_op jit(solution)/shard_map/all_gather | solution.py:212
  376.0 73.5 %reduce-scatter.27.cloned.1.call-start = ((), (), s32[]{:S(2)}) async-start(), calls=%async_computation.20 | async-start | bytes 1638400 | tf_op jit(solution)/shard_map/reduce_scatter | solution.py:62
  418.0 78.6 %all-gather.65.cloned.1.call-start = ((), (), s32[]{:S(2)}) async-start(), calls=%async_computation.42 | async-start | bytes 4915200 | tf_op jit(solution)/shard_map/all_gather | solution.py:117
  418.6 112.7 %all-gather.37.cloned.1.call-start = ((), (), s32[]{:S(2)}) async-start(), calls=%async_computation.21 | async-start | bytes 1638400 | tf_op jit(solution)/shard_map/all_gather | solution.py:66
  451.8 126.9 %all-gather.67.cloned.1.call-start = ((), (), s32[]{:S(2)}) async-start(), calls=%async_computation.43 | async-start | bytes 4915200 | tf_op jit(solution)/shard_map/all_gather | solution.py:118
  452.4 168.6 %reduce-scatter.31.cloned.1.call-start = ((), (), s32[]{:S(2)}) async-start(), calls=%async_computation.24 | async-start | bytes 1638400 | tf_op jit(solution)/shard_map/reduce_scatter | solution.py:62
  594.8 94.1 %all-gather.41.cloned.1.call-start = ((), (), s32[]{:S(2)}) async-start(), calls=%async_computation.25 | async-start | bytes 1638400 | tf_op jit(solution)/shard_map/all_gather | solution.py:66
  657.5 101.8 %reduce-scatter.33.cloned.1.call-start = ((), (), s32[]{:S(2)}) async-start(), calls=%async_computation.26 | async-start | bytes 3276800 | tf_op jit(solution)/shard_map/reduce_scatter | solution.py:282
  725.7 69.7 %reduce-scatter.35.cloned.1.call-start = ((), (), s32[]{:S(2)}) async-start(), calls=%async_computation.27 | async-start | bytes 1638400 | tf_op jit(solution)/shard_map/reduce_scatter | solution.py:62
  763.9 66.3 %all-gather.43.cloned.1.call-start = ((), (), s32[]{:S(2)}) async-start(), calls=%async_computation.28 | async-start | bytes 1638400 | tf_op jit(solution)/shard_map/all_gather | solution.py:66
  798.8 70.7 %reduce-scatter.37.cloned.1.call-start = ((), (), s32[]{:S(2)}) async-start(), calls=%async_computation.29 | async-start | bytes 1638400 | tf_op jit(solution)/shard_map/reduce_scatter | solution.py:62
  838.9 65.4 %all-gather.45.cloned.1.call-start = ((), (), s32[]{:S(2)}) async-start(), calls=%async_computation.30 | async-start | bytes 1638400 | tf_op jit(solution)/shard_map/all_gather | solution.py:66
  872.9 127.1 %reduce-scatter.39.cloned.1.call-start = ((), (), s32[]{:S(2)}) async-start(), calls=%async_computation.31 | async-start | bytes 3276800 | tf_op jit(solution)/shard_map/reduce_scatter | solution.py:282
  946.4 88.6 %reduce-scatter.49.cloned.1.call-start = ((), (), s32[]{:S(2)}) async-start(), calls=%async_computation.47 | async-start | bytes 4792320
  960.4 138.3 %reduce-scatter.45.cloned.1.call-start = ((), (), s32[]{:S(2)}) async-start(), calls=%async_computation.45 | async-start | bytes 6635520 | tf_op jit(solution)/shard_map/reduce_scatter | solution.py:291
  977.6 176.1 %reduce-scatter.47.cloned.1.call-start = ((), (), s32[]{:S(2)}) async-start(), calls=%async_computation.46 | async-start | bytes 4792320
  991.9 195.9 %reduce-scatter.41.cloned.1.call-start = ((), (), s32[]{:S(2)}) async-start(), calls=%async_computation.32 | async-start | bytes 1638400 | tf_op jit(solution)/shard_map/reduce_scatter | solution.py:62
  1004.7 238.1 %all-gather.39.cloned.1.call-start = ((), (), s32[]{:S(2)}) async-start(), calls=%async_computation.23 | async-start | bytes 3276800 | tf_op jit(solution)/shard_map/all_gather | solution.py:66
  1005.4 260.5 %all-gather.55.cloned.1.call-start = ((), (), s32[]{:S(2)}) async-start(), calls=%async_computation.37 | async-start | bytes 2662400 | tf_op jit(solution)/shard_map/all_gather | solution.py:298
  1035.0 294.4 %reduce-scatter.43.cloned.1.call-start = ((), (), s32[]{:S(2)}) async-start(), calls=%async_computation.44 | async-start | bytes 6635520 | tf_op jit(solution)/shard_map/reduce_scatter | solution.py:291
  1053.0 305.4 %all-gather.51.cloned.1.call-start = ((), (), s32[]{:S(2)}) async-start(), calls=%async_computation.35 | async-start | bytes 3686400 | tf_op jit(solution)/shard_map/all_gather | solution.py:294
  1098.7 335.5 %all-gather.53.cloned.1.call-start = ((), (), s32[]{:S(2)}) async-start(), calls=%async_computation.36 | async-start | bytes 2662400 | tf_op jit(solution)/shard_map/all_gather | solution.py:298
  1153.7 303.4 %all-gather.47.cloned.1.call-start = ((), (), s32[]{:S(2)}) async-start(), calls=%async_computation.33 | async-start | bytes 3276800 | tf_op jit(solution)/shard_map/all_gather | solution.py:66
  1191.2 277.5 %all-gather.49.cloned.1.call-start = ((), (), s32[]{:S(2)}) async-start(), calls=%async_computation.34 | async-start | bytes 3686400 | tf_op jit(solution)/shard_map/all_gather | solution.py:294
  (85 other events, 1678.8 us)
Sparse Core Ops, SparseCore 0:
  12.9 39.8 all-gather.28
  58.1 25.5 all-gather.56
  101.7 31.3 reduce-scatter.22
  135.1 45.0 all-gather.58
  182.2 32.5 all-gather.30
  216.7 45.4 all-gather.60
  267.3 31.3 reduce-scatter.24
  300.8 35.8 all-gather.34
  338.8 32.5 all-gather.32
  376.1 24.6 all-gather.62
  418.1 31.3 reduce-scatter.26
  451.5 45.0 all-gather.64
  498.7 32.5 all-gather.36
  533.2 45.4 all-gather.66
  589.6 31.3 reduce-scatter.30
  623.7 30.0 reduce-scatter.28
  657.7 31.1 all-gather.40
  725.8 33.5 reduce-scatter.32
  764.1 31.3 reduce-scatter.34
  799.0 31.1 all-gather.42
  839.0 30.4 reduce-scatter.36
  873.0 31.1 all-gather.44
  946.5 33.5 reduce-scatter.38
  983.3 51.6 reduce-scatter.48
  1039.0 59.6 reduce-scatter.44
  1101.9 51.6 reduce-scatter.46
  1156.3 31.3 reduce-scatter.40
  1189.3 53.3 all-gather.38
  1269.8 59.6 reduce-scatter.42
  1331.0 27.3 all-gather.50
  1385.1 55.6 all-gather.46
  1442.4 26.2 all-gather.48
  (2 shorter events, 44.5 us)

commit v2 on v1

v2 whole, which is shorter than its diff:
```python
import functools
import math
import jax
import jax.numpy as jnp
from jax import lax
from jax.experimental import pallas as pl
from jax.experimental.pallas import tpu as pltpu
from jax.sharding import PartitionSpec as P

MESH = pl.DeviceIdType.MESH
LOW = jnp.bfloat16
WIDE = jnp.float32
EPSILON = 1e-05
NEGATIVE = -1e30
HD = 80
PIECES = 4
LAYERS = 2
ROOT_HALF = 1.0 / math.sqrt(2.0)
DENSITY = 1.0 / math.sqrt(2.0 * math.pi)


def norm_parts(values):
    average = jnp.mean(values, axis=-1, keepdims=True)
    centered = values - average
    spread = jnp.mean(centered * centered, axis=-1, keepdims=True)
    inverse = lax.rsqrt(spread + EPSILON)
    return (centered * inverse, inverse)


def norm_back(upstream, normal_hat, inverse, gain_full):
    scaled = upstream * gain_full
    first_mean = jnp.mean(scaled, axis=-1, keepdims=True)
    second_mean = jnp.mean(scaled * normal_hat, axis=-1, keepdims=True)
    return inverse * (scaled - first_mean - normal_hat * second_mean)


def line_exchange(n, own, pieces, partial, gathered, from_left, from_right, total, sems, finish):
    rs_send, rs_recv, ag_send, ag_recv = sems
    me = lax.axis_index("tp")
    piece = own // pieces
    to_right, to_left = {"tp": lax.rem(me + 1, n)}, {"tp": lax.rem(me + n - 1, n)}
    has_left, has_right = me > 0, me < n - 1

    barrier = pltpu.get_barrier_semaphore()

    @pl.when(has_left)
    def _():
        pl.semaphore_signal(barrier, inc=1, device_id=to_left, device_id_type=MESH)

    @pl.when(has_right)
    def _():
        pl.semaphore_signal(barrier, inc=1, device_id=to_right, device_id_type=MESH)

    pl.semaphore_wait(barrier, has_left.astype(jnp.int32) + has_right.astype(jnp.int32))

    def rows_of(shard, step):
        return pl.ds(pl.multiple_of(shard * own + step * piece, piece), piece)

    def reduce_copy(way, src, shard, step):
        rows = rows_of(shard, step)
        landing = from_left if way == 0 else from_right
        return pltpu.make_async_remote_copy(
            src_ref=src.at[rows],
            dst_ref=landing.at[rows],
            send_sem=rs_send.at[way, shard, step],
            recv_sem=rs_recv.at[way, shard, step],
            device_id=to_right if way == 0 else to_left,
            device_id_type=MESH,
        )

    def gather_copy(way, shard, step):
        rows = rows_of(shard, step)
        return pltpu.make_async_remote_copy(
            src_ref=gathered.at[rows],
            dst_ref=gathered.at[rows],
            send_sem=ag_send.at[way, shard, step],
            recv_sem=ag_recv.at[way, shard, step],
            device_id=to_right if way == 0 else to_left,
            device_id_type=MESH,
        )

    def reduce_step(step):
        for k in range(n - 1):
            for way in range(2):
                shard = n - 1 - k if way == 0 else k
                landing = from_left if way == 0 else from_right
                first = me == 0 if way == 0 else me == n - 1
                inside = (me > 0) & (me < shard) if way == 0 else (me < n - 1) & (me > shard)

                @pl.when(first)
                def _():
                    reduce_copy(way, partial, shard, step).start()

                @pl.when(inside)
                def _():
                    rows = rows_of(shard, step)
                    reduce_copy(way, partial, shard, step).wait_recv()
                    landing[rows, :] = (
                        partial[rows, :].astype(WIDE) + landing[rows, :].astype(WIDE)
                    ).astype(LOW)
                    reduce_copy(way, landing, shard, step).start()

    def finish_step(step):
        rows = rows_of(me, step)
        total[...] = partial[rows, :].astype(WIDE)

        @pl.when(has_left)
        def _():
            reduce_copy(0, partial, me, step).wait_recv()
            total[...] += from_left[rows, :].astype(WIDE)

        @pl.when(has_right)
        def _():
            reduce_copy(1, partial, me, step).wait_recv()
            total[...] += from_right[rows, :].astype(WIDE)

        own_rows = pl.ds(pl.multiple_of(step * piece, piece), piece)
        gathered[rows, :] = finish(own_rows, total[...])

        @pl.when(has_right)
        def _():
            gather_copy(0, me, step).start()

        @pl.when(has_left)
        def _():
            gather_copy(1, me, step).start()

    def forward_step(step):
        for k in range(1, n):
            for way in range(2):
                shard = me - k if way == 0 else me + k
                there = shard >= 0 if way == 0 else shard <= n - 1
                further = has_right if way == 0 else has_left

                @pl.when(there)
                def _():
                    gather_copy(way, shard, step).wait_recv()

                @pl.when(there & further)
                def _():
                    gather_copy(way, shard, step).start()

    def body(step, carry):
        @pl.when(step < pieces)
        def _():
            reduce_step(step)

        @pl.when((step >= 1) & (step <= pieces))
        def _():
            finish_step(step - 1)

        @pl.when(step >= 2)
        def _():
            forward_step(step - 2)

        return carry

    lax.fori_loop(0, pieces + 2, body, 0)

    def drain(step, carry):
        for k in range(n - 1):
            for way in range(2):
                shard = n - 1 - k if way == 0 else k
                sends = me < shard if way == 0 else me > shard

                @pl.when(sends)
                def _():
                    reduce_copy(way, partial, shard, step).wait_send()

        for k in range(n):
            for way in range(2):
                shard = me - k if way == 0 else me + k
                there = shard >= 0 if way == 0 else shard <= n - 1
                further = has_right if way == 0 else has_left

                @pl.when(there & further)
                def _():
                    gather_copy(way, shard, step).wait_send()

        return carry

    lax.fori_loop(0, pieces, drain, 0)


def exchange_scratch(n, rows, width, pieces):
    return [
        pltpu.VMEM((rows, width), LOW),
        pltpu.VMEM((rows, width), LOW),
        pltpu.VMEM((rows // n // pieces, width), WIDE),
        pltpu.SemaphoreType.DMA((2, n, pieces)),
        pltpu.SemaphoreType.DMA((2, n, pieces)),
        pltpu.SemaphoreType.DMA((2, n, pieces)),
        pltpu.SemaphoreType.DMA((2, n, pieces)),
    ]


def forward_exchange_kernel(
    n, pieces, partial, residual, bias, gain, shift, gathered, middle, from_left, from_right, total, *sems
):
    def finish(rows, value):
        mid = value + residual[rows, :] + bias[...]
        middle[rows, :] = mid
        hat, _ = norm_parts(mid)
        return (hat * gain[...] + shift[...]).astype(LOW)

    line_exchange(
        n, residual.shape[0], pieces, partial, gathered, from_left, from_right, total, sems, finish
    )


def backward_exchange_kernel(
    n, pieces, partial, grad_out, normal_in, gain, gathered, grad_in, sums, from_left, from_right, total, *sems
):
    sums[...] = jnp.zeros_like(sums)

    def finish(rows, upstream):
        hat, inverse = norm_parts(normal_in[rows, :])
        grad = grad_out[rows, :] + norm_back(upstream, hat, inverse, gain[...])
        grad_in[rows, :] = grad
        sums[0:1, :] += jnp.sum(upstream * hat, axis=0, keepdims=True)
        sums[1:2, :] += jnp.sum(upstream, axis=0, keepdims=True)
        sums[2:3, :] += jnp.sum(grad, axis=0, keepdims=True)
        return grad.astype(LOW)

    line_exchange(
        n, grad_out.shape[0], pieces, partial, gathered, from_left, from_right, total, sems, finish
    )


def in_vmem(count):
    return [pl.BlockSpec(memory_space=pltpu.VMEM)] * count


def forward_exchange(partial, residual, bias, gain, shift, n, collective_id):
    rows, width = partial.shape
    return pl.pallas_call(
        functools.partial(forward_exchange_kernel, n, PIECES),
        out_shape=(
            jax.ShapeDtypeStruct((rows, width), LOW),
            jax.ShapeDtypeStruct(residual.shape, WIDE),
        ),
        in_specs=in_vmem(5),
        out_specs=tuple(in_vmem(2)),
        scratch_shapes=exchange_scratch(n, rows, width, PIECES),
        compiler_params=pltpu.CompilerParams(
            collective_id=collective_id, has_side_effects=True, vmem_limit_bytes=40 << 20
        ),
        name="forward_exchange",
    )(partial, residual, bias[None, :], gain[None, :], shift[None, :])


def backward_exchange(partial, grad_out, normal_in, gain, n, collective_id):
    rows, width = partial.shape
    return pl.pallas_call(
        functools.partial(backward_exchange_kernel, n, PIECES),
        out_shape=(
            jax.ShapeDtypeStruct((rows, width), LOW),
            jax.ShapeDtypeStruct(grad_out.shape, WIDE),
            jax.ShapeDtypeStruct((8, width), WIDE),
        ),
        in_specs=in_vmem(4),
        out_specs=tuple(in_vmem(3)),
        scratch_shapes=exchange_scratch(n, rows, width, PIECES),
        compiler_params=pltpu.CompilerParams(
            collective_id=collective_id, has_side_effects=True, vmem_limit_bytes=40 << 20
        ),
        name="backward_exchange",
    )(partial, grad_out, normal_in, gain[None, :])


def attend_kernel(scale, length, qkv, out, out_wide, log_total, held, high, low_sum, sems_send, sems_recv):
    columns = qkv.shape[0] // 3
    frames = qkv.shape[1]
    heads = columns // HD
    me = lax.axis_index("ctx")

    def partner(r):
        return {"ctx": jnp.bitwise_xor(me, r)}

    barrier = pltpu.get_barrier_semaphore()
    for r in (1, 2):
        pl.semaphore_signal(barrier, inc=1, device_id=partner(r), device_id_type=MESH)
    pl.semaphore_wait(barrier, 2)

    def send(slot, part, to):
        rows = pl.ds(part * columns, columns)
        src = qkv.at[pl.ds((1 + part) * columns, columns)] if slot != 3 else held.at[1, rows]
        return pltpu.make_async_remote_copy(
            src_ref=src,
            dst_ref=held.at[slot - 1, rows],
            send_sem=sems_send.at[slot - 1, part],
            recv_sem=sems_recv.at[slot - 1, part],
            device_id=partner(to),
            device_id_type=MESH,
        )

    for part in range(2):
        send(2, part, 2).start()
    for part in range(2):
        send(1, part, 1).start()

    high[...] = jnp.full_like(high, NEGATIVE)
    low_sum[...] = jnp.zeros_like(low_sum)
    out_wide[...] = jnp.zeros_like(out_wide)
    limit = length[0]

    def block(keys_ref, key_row, value_row, slot):
        owner = jnp.bitwise_xor(me, slot)
        left = limit - owner * frames
        valid = lax.broadcasted_iota(jnp.int32, (frames, frames), 0) < left
        for h in range(heads):
            rows = pl.ds(h * HD, HD)
            keys = keys_ref[pl.ds(key_row + h * HD, HD), :]
            values = keys_ref[pl.ds(value_row + h * HD, HD), :]
            scores = lax.dot_general(
                keys, qkv[rows, :], (((0,), (0,)), ((), ())), preferred_element_type=WIDE
            )
            scores = jnp.where(valid, scores * scale, NEGATIVE)
            before = high[h : h + 1, :]
            now = jnp.maximum(before, jnp.max(scores, axis=0, keepdims=True))
            shrink = jnp.exp(before - now)
            raised = jnp.exp(scores - now)
            low_sum[h : h + 1, :] = low_sum[h : h + 1, :] * shrink + jnp.sum(
                raised, axis=0, keepdims=True
            )
            high[h : h + 1, :] = now
            out_wide[rows, :] = out_wide[rows, :] * shrink + jnp.dot(
                values, raised.astype(LOW), preferred_element_type=WIDE
            )

    block(qkv, columns, 2 * columns, 0)
    for part in range(2):
        send(1, part, 1).wait_recv()
    block(held.at[0], 0, columns, 1)
    for part in range(2):
        send(2, part, 2).wait_recv()
        send(3, part, 1).start()
    block(held.at[1], 0, columns, 2)
    for part in range(2):
        send(3, part, 1).wait_recv()
    block(held.at[2], 0, columns, 3)
    for h in range(heads):
        rows = pl.ds(h * HD, HD)
        total = low_sum[h : h + 1, :]
        done = out_wide[rows, :] / total
        out_wide[rows, :] = done
        out[rows, :] = done.astype(LOW)
        log_total[h : h + 1, :] = high[h : h + 1, :] + jnp.log(total)
    for slot in (1, 2, 3):
        for part in range(2):
            send(slot, part, 2 if slot == 2 else 1).wait_send()


def attend(qkv, length, scale, collective_id):
    columns, frames = qkv.shape[0] // 3, qkv.shape[1]
    return pl.pallas_call(
        functools.partial(attend_kernel, scale),
        out_shape=(
            jax.ShapeDtypeStruct((columns, frames), LOW),
            jax.ShapeDtypeStruct((columns, frames), WIDE),
            jax.ShapeDtypeStruct((8, frames), WIDE),
            jax.ShapeDtypeStruct((3, 2 * columns, frames), LOW),
        ),
        in_specs=[pl.BlockSpec(memory_space=pltpu.SMEM)] + in_vmem(1),
        out_specs=tuple(in_vmem(4)),
        scratch_shapes=[
            pltpu.VMEM((8, frames), WIDE),
            pltpu.VMEM((8, frames), WIDE),
            pltpu.SemaphoreType.DMA((3, 2)),
            pltpu.SemaphoreType.DMA((3, 2)),
        ],
        compiler_params=pltpu.CompilerParams(
            collective_id=collective_id, has_side_effects=True, vmem_limit_bytes=56 << 20
        ),
        name="attend",
    )(length, qkv)


def attend_back_kernel(
    scale, length, qkv, held, grad, out_wide, log_total, grad_qkv, mine, parts, landed, acc, sems_send, sems_recv
):
    columns = qkv.shape[0] // 3
    frames = qkv.shape[1]
    heads = columns // HD
    me = lax.axis_index("ctx")

    def partner(r):
        return {"ctx": jnp.bitwise_xor(me, r)}

    barrier = pltpu.get_barrier_semaphore()
    for r in (1, 2):
        pl.semaphore_signal(barrier, inc=1, device_id=partner(r), device_id_type=MESH)
    pl.semaphore_wait(barrier, 2)

    def send(at, part, to):
        rows = pl.ds(part * columns, columns)
        return pltpu.make_async_remote_copy(
            src_ref=parts.at[at, rows],
            dst_ref=landed.at[at, rows],
            send_sem=sems_send.at[at, part],
            recv_sem=sems_recv.at[at, part],
            device_id=partner(to),
            device_id_type=MESH,
        )

    acc[...] = jnp.zeros_like(acc)
    limit = length[0]

    def block(keys_ref, key_row, value_row, slot, store):
        owner = jnp.bitwise_xor(me, slot)
        left = limit - owner * frames
        valid = lax.broadcasted_iota(jnp.int32, (frames, frames), 0) < left
        for h in range(heads):
            rows = pl.ds(h * HD, HD)
            keys = keys_ref[pl.ds(key_row + h * HD, HD), :]
            values = keys_ref[pl.ds(value_row + h * HD, HD), :]
            queries = qkv[rows, :]
            upstream = grad[rows, :]
            scores = lax.dot_general(
                keys, queries, (((0,), (0,)), ((), ())), preferred_element_type=WIDE
            )
            weights = jnp.where(valid, jnp.exp(scores * scale - log_total[h : h + 1, :]), 0.0)
            grad_weights = lax.dot_general(
                values, upstream, (((0,), (0,)), ((), ())), preferred_element_type=WIDE
            )
            row_terms = jnp.sum(
                upstream.astype(WIDE) * out_wide[rows, :], axis=0, keepdims=True
            )
            grad_scores = (weights * (grad_weights - row_terms)).astype(LOW)
            acc[rows, :] += jnp.dot(keys, grad_scores, preferred_element_type=WIDE)
            grad_keys = (
                lax.dot_general(
                    queries, grad_scores, (((1,), (1,)), ((), ())), preferred_element_type=WIDE
                )
                * scale
            )
            grad_values = lax.dot_general(
                upstream, weights.astype(LOW), (((1,), (1,)), ((), ())), preferred_element_type=WIDE
            )
            store(h * HD, grad_keys, grad_values)

    def store_part(at):
        def store(row, grad_keys, grad_values):
            parts[at, pl.ds(row, HD), :] = grad_keys.astype(LOW)
            parts[at, pl.ds(columns + row, HD), :] = grad_values.astype(LOW)

        return store

    def store_mine(row, grad_keys, grad_values):
        mine[pl.ds(row, HD), :] = grad_keys
        mine[pl.ds(columns + row, HD), :] = grad_values

    def store_joined(row, grad_keys, grad_values):
        for start, value in ((row, grad_keys), (columns + row, grad_values)):
            rows = pl.ds(start, HD)
            parts[1, rows, :] = (value + landed[0, rows, :].astype(WIDE)).astype(LOW)

    block(held.at[2], 0, columns, 3, store_part(0))
    for part in range(2):
        send(0, part, 1).start()
    for part in range(2):
        send(0, part, 1).wait_recv()
    block(held.at[1], 0, columns, 2, store_joined)
    for part in range(2):
        send(1, part, 2).start()
    block(held.at[0], 0, columns, 1, store_part(2))
    for part in range(2):
        send(2, part, 1).start()
    block(qkv, columns, 2 * columns, 0, store_mine)
    grad_qkv[0:columns, :] = (acc[...] * scale).astype(LOW)
    for part in range(2):
        send(2, part, 1).wait_recv()
    for part in range(2):
        send(1, part, 2).wait_recv()
    grad_qkv[columns:, :] = (
        mine[...] + landed[1].astype(WIDE) + landed[2].astype(WIDE)
    ).astype(LOW)
    for at in range(3):
        for part in range(2):
            send(at, part, 2 if at == 1 else 1).wait_send()


def attend_back(qkv, held, grad, out_wide, log_total, length, scale, collective_id):
    columns, frames = qkv.shape[0] // 3, qkv.shape[1]
    return pl.pallas_call(
        functools.partial(attend_back_kernel, scale),
        out_shape=jax.ShapeDtypeStruct((3 * columns, frames), LOW),
        in_specs=[pl.BlockSpec(memory_space=pltpu.SMEM)] + in_vmem(5),
        out_specs=in_vmem(1)[0],
        scratch_shapes=[
            pltpu.VMEM((2 * columns, frames), WIDE),
            pltpu.VMEM((3, 2 * columns, frames), LOW),
            pltpu.VMEM((3, 2 * columns, frames), LOW),
            pltpu.VMEM((columns, frames), WIDE),
            pltpu.SemaphoreType.DMA((3, 2)),
            pltpu.SemaphoreType.DMA((3, 2)),
        ],
        compiler_params=pltpu.CompilerParams(
            collective_id=collective_id, has_side_effects=True, vmem_limit_bytes=56 << 20
        ),
        name="attend_back",
    )(length, qkv, held, grad, out_wide, log_total)


def gelu_value(values):
    return 0.5 * values * (1.0 + lax.erf(values * ROOT_HALF))


def gelu_slope(values):
    return 0.5 * (1.0 + lax.erf(values * ROOT_HALF)) + values * DENSITY * jnp.exp(
        -0.5 * values * values
    )


def product(left_side, right_side, left_axis, right_axis):
    return lax.dot_general(
        left_side,
        right_side,
        (((left_axis,), (right_axis,)), ((), ())),
        preferred_element_type=WIDE,
    )


def per_device(
    hidden,
    cotangent,
    lengths,
    query_weight,
    key_weight,
    value_weight,
    output_weight,
    inner_weight,
    outer_weight,
    query_bias,
    value_bias,
    inner_bias,
    output_bias,
    outer_bias,
    first_gain,
    first_shift,
    second_gain,
    second_shift,
):
    clip_count, rows, width = hidden.shape
    assert clip_count == 1
    assert lax.axis_size("ctx") == 4
    tp_size = lax.axis_size("tp")
    own_rows = rows // tp_size
    columns = query_weight.shape[2]
    hidden_local = inner_weight.shape[2]
    scale = 1.0 / math.sqrt(HD)
    own_start = lax.axis_index("tp") * own_rows

    def own_slice(full):
        return lax.dynamic_slice_in_dim(full, own_start, own_rows, axis=0)

    small = jnp.concatenate(
        [output_bias, outer_bias, first_gain, first_shift, second_gain, second_shift], axis=0
    ).astype(LOW)
    small = lax.all_gather(small, "fsdp", axis=1, tiled=True).astype(WIDE)

    def vector(kind, layer):
        return small[kind * LAYERS + layer]

    def fetch(layer):
        qkv = jnp.concatenate(
            [query_weight[layer], key_weight[layer], value_weight[layer]], axis=1
        ).astype(LOW)
        qkv = lax.all_gather(qkv, "fsdp", axis=0, tiled=True)
        out = lax.all_gather(output_weight[layer].astype(LOW), "fsdp", axis=1, tiled=True)
        inner = lax.all_gather(inner_weight[layer].astype(LOW), "fsdp", axis=0, tiled=True)
        outer = lax.all_gather(outer_weight[layer].astype(LOW), "fsdp", axis=1, tiled=True)
        return (qkv, out, inner, outer)

    weights = [fetch(layer) for layer in range(LAYERS)]

    hidden_rows = hidden.reshape(rows, width)
    residual = own_slice(hidden_rows)
    hat_full, _ = norm_parts(hidden_rows)
    normed = (hat_full * vector(2, 0) + vector(3, 0)).astype(LOW)
    kept = []
    for layer in range(LAYERS):
        w_qkv, w_out, w_inner, w_outer = weights[layer]
        bias_qkv = jnp.concatenate(
            [query_bias[layer], jnp.zeros_like(query_bias[layer]), value_bias[layer]]
        )
        qkv = (product(w_qkv, normed, 0, 1) + bias_qkv[:, None]).astype(LOW)
        attended, attended_wide, log_total, held = attend(qkv, lengths, scale, 2 * layer)
        branch = product(attended, w_out, 0, 0).astype(LOW)
        normed_two, middle = forward_exchange(
            branch, residual, vector(0, layer), vector(4, layer), vector(5, layer), tp_size, 2 * layer + 4
        )
        inner_pre = product(normed_two, w_inner, 1, 0) + inner_bias[layer]
        active = gelu_value(inner_pre).astype(LOW)
        kept.append(
            (residual, normed, qkv, attended, attended_wide, log_total, held, middle, normed_two, inner_pre, active)
        )
        branch = product(active, w_outer, 1, 0).astype(LOW)
        if layer + 1 < LAYERS:
            normed, residual = forward_exchange(
                branch,
                middle,
                vector(1, layer),
                vector(2, layer + 1),
                vector(3, layer + 1),
                tp_size,
                2 * layer + 5,
            )
        else:
            branch = lax.psum_scatter(branch, "tp", scatter_dimension=0, tiled=True).astype(WIDE)
            residual = middle + branch + vector(1, layer)
            output = lax.all_gather(residual.astype(LOW), "tp", axis=0, tiled=True).astype(WIDE)

    grad_rows = cotangent.reshape(rows, width)
    grad_own = own_slice(grad_rows)
    grad_low = grad_rows.astype(LOW)
    outer_bias_sum = jnp.sum(grad_own, axis=0)
    grads = [None] * LAYERS
    vectors = [None] * LAYERS
    biases = [None] * LAYERS
    for layer in reversed(range(LAYERS)):
        w_qkv, w_out, w_inner, w_outer = weights[layer]
        (
            residual,
            normed,
            qkv,
            attended,
            attended_wide,
            log_total,
            held,
            middle,
            normed_two,
            inner_pre,
            active,
        ) = kept[layer]
        grad_active = product(grad_low, w_outer, 1, 1)
        grad_inner = (grad_active * gelu_slope(inner_pre)).astype(LOW)
        branch = product(grad_inner, w_inner, 1, 1).astype(LOW)
        grad_mid_low, grad_middle, sums_two = backward_exchange(
            branch, grad_own, middle, vector(4, layer), tp_size, 2 * layer + 8
        )
        grad_outer_w = product(active, grad_low, 0, 0)
        grad_inner_w = product(normed_two, grad_inner, 0, 0)
        grad_attended = product(w_out, grad_mid_low, 1, 1).astype(LOW)
        grad_qkv = attend_back(
            qkv, held, grad_attended, attended_wide, log_total, lengths, scale, 2 * layer + 12
        )
        grad_output_w = product(attended, grad_mid_low, 1, 0)
        branch = product(grad_qkv, w_qkv, 0, 1).astype(LOW)
        grad_low, grad_own, sums_one = backward_exchange(
            branch, grad_middle, residual, vector(2, layer), tp_size, 2 * layer + 9
        )
        by_rows = jnp.concatenate([product(normed, grad_qkv, 0, 1), grad_inner_w], axis=1)
        by_cols = jnp.concatenate([grad_output_w, grad_outer_w], axis=0)
        by_rows = lax.psum_scatter(
            by_rows.astype(LOW), ("fsdp", "ctx"), scatter_dimension=0, tiled=True
        )
        by_rows = lax.all_gather(by_rows, "ctx", axis=0, tiled=True).astype(WIDE)
        by_cols = lax.psum_scatter(
            by_cols.astype(LOW), ("fsdp", "ctx"), scatter_dimension=1, tiled=True
        )
        by_cols = lax.all_gather(by_cols, "ctx", axis=1, tiled=True).astype(WIDE)
        grads[layer] = (by_rows, by_cols)
        vectors[layer] = jnp.stack(
            [sums_two[2], outer_bias_sum, sums_one[0], sums_one[1], sums_two[0], sums_two[1]]
        )
        outer_bias_sum = sums_one[2]
        biases[layer] = jnp.concatenate(
            [
                jnp.sum(grad_qkv.astype(WIDE), axis=1),
                jnp.sum(grad_inner.astype(WIDE), axis=0),
            ]
        )
    grad_hidden = grad_low.astype(WIDE)

    vector_sums = lax.psum(jnp.stack(vectors, axis=1), ("fsdp", "ctx", "tp"))
    bias_sums = lax.psum(jnp.stack(biases), ("fsdp", "ctx"))
    shard = output_bias.shape[1]
    vector_sums = lax.dynamic_slice_in_dim(
        vector_sums, lax.axis_index("fsdp") * shard, shard, axis=2
    )

    def stacked_rows(start, size):
        return jnp.stack([grads[layer][0][:, start : start + size] for layer in range(LAYERS)])

    def stacked_cols(start, size):
        return jnp.stack([grads[layer][1][start : start + size] for layer in range(LAYERS)])

    return (
        output.reshape(hidden.shape),
        grad_hidden.reshape(hidden.shape),
        stacked_rows(0, columns),
        stacked_rows(columns, columns),
        stacked_rows(2 * columns, columns),
        stacked_cols(0, columns),
        stacked_rows(3 * columns, hidden_local),
        stacked_cols(columns, hidden_local),
        bias_sums[:, :columns],
        bias_sums[:, 2 * columns : 3 * columns],
        bias_sums[:, 3 * columns :],
        vector_sums[0],
        vector_sums[1],
        vector_sums[2],
        vector_sums[3],
        vector_sums[4],
        vector_sums[5],
    )


def solution(mesh):
    in_specs = (
        P("fsdp", "ctx", None),
        P("fsdp", "ctx", None),
        P("fsdp"),
        P(None, "fsdp", "tp"),
        P(None, "fsdp", "tp"),
        P(None, "fsdp", "tp"),
        P(None, "tp", "fsdp"),
        P(None, "fsdp", "tp"),
        P(None, "tp", "fsdp"),
        P(None, "tp"),
        P(None, "tp"),
        P(None, "tp"),
        P(None, "fsdp"),
        P(None, "fsdp"),
        P(None, "fsdp"),
        P(None, "fsdp"),
        P(None, "fsdp"),
        P(None, "fsdp"),
    )
    out_specs = (
        P("fsdp", "ctx", None),
        P("fsdp", "ctx", None),
        P(None, "fsdp", "tp"),
        P(None, "fsdp", "tp"),
        P(None, "fsdp", "tp"),
        P(None, "tp", "fsdp"),
        P(None, "fsdp", "tp"),
        P(None, "tp", "fsdp"),
        P(None, "tp"),
        P(None, "tp"),
        P(None, "tp"),
        P(None, "fsdp"),
        P(None, "fsdp"),
        P(None, "fsdp"),
        P(None, "fsdp"),
        P(None, "fsdp"),
        P(None, "fsdp"),
    )
    return jax.shard_map(
        per_device, mesh=mesh, in_specs=in_specs, out_specs=out_specs, check_vma=False
    )
```

time: 1520 us -> 1010 us (0.66)
  waiting for transfers between devices: 1020 us -> 67 us
  Pallas kernels: 0 us -> 614 us
  matrix products: 161 us -> 72.8 us
  other arithmetic: 105 us -> 54.7 us
  local copies, waits for them, and re-layouts: 105 us -> 76.5 us
    pallas_call x0 -> x11, Pallas kernels: none -> 614 us  [the longest x4 283 us: backward_exchange(): pl.pallas_call(functools.partial(backward_exchange_kernel, n, PIECES), ou...]
    all_gather x10 -> x1, waiting for transfers between devices: 270 us -> 0.01 us  [per_device(): lax.all_gather(residual.astype(LOW), 'tp', axis=0, tiled=True).astype(WIDE)]
    reduce_scatter x10 -> x1, waiting for transfers between devices: 267 us -> 0.02 us  [per_device(): lax.psum_scatter(branch, 'tp', scatter_dimension=0, tiled=True).astype(WIDE)]
    dot_general x36 -> x24, matrix products: 161 us -> 72.8 us  [product(): lax.dot_general(left_side, right_side, (((left_axis,), (right_axis,)), ((...]
    unnamed x36 -> x18, waiting for transfers between devices: 86.6 us -> 2.46 us
    all_gather x2, waiting for transfers between devices: 83 us -> 0.01 us  [fetch(): lax.all_gather(outer_weight[layer].astype(LOW), 'fsdp', axis=1, tiled=True)]
    all_gather x2, waiting for transfers between devices: 82.3 us -> 0.02 us  [fetch(): lax.all_gather(inner_weight[layer].astype(LOW), 'fsdp', axis=0, tiled=True)]
    all_gather x2, waiting for transfers between devices: 69 us -> 0.01 us  [fetch(): qkv = lax.all_gather(qkv, 'fsdp', axis=0, tiled=True)]
  transfers between devices with their start and end apart: 34 -> 16, of which waited for: 31 -> 3; matrix products, arithmetic and copies ran while one was open for 11% -> 17% of each run, Pallas kernels for 0% -> 61%
where the time goes in v2:
time: 1010 us
  Pallas kernels  614 us (61%)
  blocking collectives  104 us (10%)
  local copies, waits for them, and re-layouts  76.5 us (8%)
  matrix products  72.8 us (7%)
  waiting for transfers between devices  67 us (7%)
  other arithmetic  54.7 us (5%)
  between operations  15.9 us (2%)
    pallas_call x4, Pallas kernels, backward_exchange(): pl.pallas_call(functools.partial(backward_exchange_kernel, n, PIECES), ou...  283 us
    pallas_call x3, Pallas kernels, forward_exchange(): pl.pallas_call(functools.partial(forward_exchange_kernel, n, PIECES), out...  204 us
    pallas_call x2, Pallas kernels, attend_back(): pl.pallas_call(functools.partial(attend_back_kernel, scale), out_shape=ja...  78.4 us
    dot_general x24, matrix products, product(): lax.dot_general(left_side, right_side, (((left_axis,), (right_axis,)), ((...  72.8 us
    unnamed x103, local copies, waits for them, and re-layouts  57.4 us
    pallas_call x2, Pallas kernels, attend(): pl.pallas_call(functools.partial(attend_kernel, scale), out_shape=(jax.Sh...  48.1 us
    reduce_scatter x2, waiting for transfers between devices, per_device(): lax.psum_scatter(by_rows.astype(LOW), ('fsdp', 'ctx'), scatter_dimension=...  39.2 us
    psum x1, blocking collectives, per_device(): vector_sums = lax.psum(jnp.stack(vectors, axis=1), ('fsdp', 'ctx', 'tp'))  38.2 us
  transfers between devices with their start and end apart: 16, of which 3 were waited for; matrix products, arithmetic and copies ran while one was open for 17% of the time, Pallas kernels for 61%

profile of v2, /device:TPU:0, one launch (start us, length us, event | category | flops | bytes accessed | tf_op | source)
XLA Modules:
  0.0 1005.5 jit_solution(1101207607779757416)
XLA Ops:
  24.9 6.1 all_gather.44
  34.2 21.4 %all-gather.3 = bf16[1,320,1280]{2,1,0:T(8,128)(2,1)} all-gather(bf16[1,320,640]{2,1,0:T(8,128)(2,1)S(1)} %get-tuple-element.122), channel_id=5, replica_groups=mesh['fsdp'=2,'ctx'=4,'tp'=4] {'fsdp'}, dimensions={2}, use_global_device_ids=true | all-gather | bytes 1228800 | tf_op jit(solution)/shard_map/all_gather | solution.py:570
  55.6 14.1 %all-gather = bf16[1,320,1280]{2,1,0:T(8,128)(2,1)} all-gather(bf16[1,320,640]{2,1,0:T(8,128)(2,1)S(1)} %get-tuple-element.123), channel_id=2, replica_groups=mesh['fsdp'=2,'ctx'=4,'tp'=4] {'fsdp'}, dimensions={2}, use_global_device_ids=true | all-gather | bytes 1228800 | tf_op jit(solution)/shard_map/all_gather | solution.py:570
  69.8 4.6 add_convert_fusion.2.qkv
  74.4 24.3 %attend.2 = (bf16[320,512]{1,0:T(8,128)(2,1)}, f32[320,512]{1,0:T(8,128)}, f32[8,512]{1,0:T(8,128)}, bf16[3,640,512]{2,1,0:T(8,128)(2,1)}) custom-call(s32[1]{0:T(128)S(6)} %copy.71.length, bf16[960,512]{1,0:T(8,128)(2,1)} %add_convert_fusion.2.qkv), custom_call_target="tpu_custom_call" | custom-call | tf_op jit(solution)/shard_map/attend/pallas_call | solution.py:356
  100.6 68.2 %forward_exchange.3 = (bf16[512,1280]{1,0:T(8,128)(2,1)S(1)}, f32[128,1280]{1,0:T(8,128)S(1)}) custom-call(bf16[512,1280]{1,0:T(8,128)(2,1)S(1)} %convolution_convert_fusion.9.partial, f32[128,1280]{1,0:T(8,128)S(1)} %dynamic-slice_bitcast_fusion.residual.normal_in, f32[1,1280]{1,0:T(1,128)S(1)} %get-tuple-element.145.bias, ...), custom_call_target="tpu_custom_call" | custom-call | tf_op jit(solution)/shard_map/forward_exchange/pallas_call | solution.py:236
  168.8 6.0 multiply_convert_fusion.1
  174.8 4.2 fusion.15.partial
  179.0 68.3 %forward_exchange.4 = (bf16[512,1280]{1,0:T(8,128)(2,1)S(1)}, f32[128,1280]{1,0:T(8,128)S(1)}) custom-call(bf16[512,1280]{1,0:T(8,128)(2,1)S(1)} %fusion.15.partial, f32[128,1280]{1,0:T(8,128)S(1)} %get-tuple-element.44.residual.normal_in, f32[1,1280]{1,0:T(1,128)S(1)} %get-tuple-element.142.bias, f32[1,1280]{1,0:T(1,128)S(1)} %get-tuple-element.141.gain, ...), custom_call_target="tpu_custom_call" | custom-call | tf_op jit(solution)/shard_map/forward_exchange/pallas_call | solution.py:236
  248.3 4.6 add_convert_fusion.1.qkv
  252.9 23.9 %attend.3 = (bf16[320,512]{1,0:T(8,128)(2,1)}, f32[320,512]{1,0:T(8,128)}, f32[8,512]{1,0:T(8,128)}, bf16[3,640,512]{2,1,0:T(8,128)(2,1)}) custom-call(s32[1]{0:T(128)S(6)} %copy.71.length, bf16[960,512]{1,0:T(8,128)(2,1)} %add_convert_fusion.1.qkv), custom_call_target="tpu_custom_call" | custom-call | tf_op jit(solution)/shard_map/attend/pallas_call | solution.py:356
  278.6 67.6 %forward_exchange.5 = (bf16[512,1280]{1,0:T(8,128)(2,1)S(1)}, f32[128,1280]{1,0:T(8,128)S(1)}) custom-call(bf16[512,1280]{1,0:T(8,128)(2,1)S(1)} %convolution_convert_fusion.8.partial, f32[128,1280]{1,0:T(8,128)S(1)} %get-tuple-element.47.residual.normal_in, f32[1,1280]{1,0:T(1,128)S(1)} %get-tuple-element.139.bias, f32[1,1280]{1,0:T(1,128)S(1)} %get-tuple-element.138.gain, ...), custom_call_target="tpu_custom_call" | custom-call | tf_op jit(solution)/shard_map/forward_exchange/pallas_call | solution.py:236
  347.3 6.2 multiply_convert_fusion
  353.6 5.2 fusion.21
  360.1 6.3 convert_reduce_fusion
  368.3 74.8 %backward_exchange.4 = (bf16[512,1280]{1,0:T(8,128)(2,1)S(1)}, f32[128,1280]{1,0:T(8,128)S(1)}, f32[8,1280]{1,0:T(8,128)S(1)}) custom-call(bf16[512,1280]{1,0:T(8,128)(2,1)S(1)} %fusion.18.partial, f32[128,1280]{1,0:T(8,128)S(1)} %get-tuple-element.121.grad_out, f32[128,1280]{1,0:T(8,128)S(1)} %get-tuple-element.48.normal_in, ...), custom_call_target="tpu_custom_call" | custom-call | tf_op jit(solution)/shard_map/backward_exchange/pallas_call | solution.py:254
  447.9 6.8 copy.51
  458.2 39.7 %attend_back.2 = bf16[960,512]{1,0:T(8,128)(2,1)} custom-call(s32[1]{0:T(128)S(6)} %copy.71.length, bf16[960,512]{1,0:T(8,128)(2,1)} %add_convert_fusion.1.qkv, bf16[3,640,512]{2,1,0:T(8,128)(2,1)} %get-tuple-element.51.held, bf16[320,512]{1,0:T(8,128)(2,1)} %fusion.38.grad, f32[320,512]{1,0:T(8,128)} %get-tuple-element.53.out_wide, ...), custom_call_target="tpu_custom_call" | custom-call | tf_op jit(solution)/shard_map/attend_back/pallas_call | solution.py:485
  500.8 67.9 %backward_exchange.5 = (bf16[512,1280]{1,0:T(8,128)(2,1)S(1)}, f32[128,1280]{1,0:T(8,128)S(1)}, f32[8,1280]{1,0:T(8,128)S(1)}) custom-call(bf16[512,1280]{1,0:T(8,128)(2,1)S(1)} %convolution_convert_fusion.7.partial, f32[128,1280]{1,0:T(8,128)S(1)} %get-tuple-element.55.grad_out, f32[128,1280]{1,0:T(8,128)S(1)} %get-tuple-element.47.residual.normal_in, ...), custom_call_target="tpu_custom_call" | custom-call | tf_op jit(solution)/shard_map/backward_exchange/pallas_call | solution.py:254
  573.6 70.1 %backward_exchange.6 = (bf16[512,1280]{1,0:T(8,128)(2,1)S(1)}, f32[128,1280]{1,0:T(8,128)S(1)}, f32[8,1280]{1,0:T(8,128)S(1)}) custom-call(bf16[512,1280]{1,0:T(8,128)(2,1)S(1)} %fusion.12.partial, f32[128,1280]{1,0:T(8,128)S(1)} %get-tuple-element.57.grad_out, f32[128,1280]{1,0:T(8,128)S(1)} %get-tuple-element.44.residual.normal_in, ...), custom_call_target="tpu_custom_call" | custom-call | tf_op jit(solution)/shard_map/backward_exchange/pallas_call | solution.py:254
  648.4 6.8 copy.49
  657.8 38.8 %attend_back.3 = bf16[960,512]{1,0:T(8,128)(2,1)} custom-call(s32[1]{0:T(128)S(6)} %copy.71.length, bf16[960,512]{1,0:T(8,128)(2,1)} %add_convert_fusion.2.qkv, bf16[3,640,512]{2,1,0:T(8,128)(2,1)} %get-tuple-element.50.held, bf16[320,512]{1,0:T(8,128)(2,1)} %fusion.39.grad, f32[320,512]{1,0:T(8,128)} %get-tuple-element.59.out_wide, ...), custom_call_target="tpu_custom_call" | custom-call | tf_op jit(solution)/shard_map/attend_back/pallas_call | solution.py:485
  703.6 8.9 copy.45
  721.3 9.6 copy.47
  734.3 39.2 %reduce-scatter.16.cloned.1.call-done = bf16[160,2240]{1,0:T(8,128)(2,1)} async-done(((bf16[1280,2240]{1,0:T(8,128)(2,1)}), bf16[160,2240]{1,0:T(8,128)(2,1)}) %reduce-scatter.16.cloned.1.call-update) | async-done | bytes 716816 | tf_op jit(solution)/shard_map/reduce_scatter | solution.py:655
  777.7 70.4 %backward_exchange.7 = (bf16[512,1280]{1,0:T(8,128)(2,1)S(1)}, f32[128,1280]{1,0:T(8,128)}, f32[8,1280]{1,0:T(8,128)S(1)}) custom-call(bf16[512,1280]{1,0:T(8,128)(2,1)S(1)} %convolution_convert_fusion.6.partial, f32[128,1280]{1,0:T(8,128)S(1)} %copy-done.2, f32[128,1280]{1,0:T(8,128)S(1)} %dynamic-slice_bitcast_fusion.residual.normal_in, ...), custom_call_target="tpu_custom_call" | custom-call | tf_op jit(solution)/shard_map/backward_exchange/pallas_call | solution.py:254
  848.1 23.9 %psum.14 = f32[2,2240]{1,0:T(2,128)S(1)} all-reduce(f32[2,2240]{1,0:T(2,128)S(1)} %pad_maximum_fusion.13), channel_id=1, replica_groups=mesh['fsdp'=2,'ctx'=4,'tp'=4] {'fsdp','ctx'}, use_global_device_ids=true, to_apply=%region_11.0 | all-reduce | flops 4480 | bytes 35840 | tf_op jit(solution)/shard_map/psum | solution.py:677
  872.1 38.2 %psum.15 = f32[6,2,1280]{2,0,1:T(8,128)S(1)} all-reduce(f32[6,2,1280]{2,0,1:T(8,128)S(1)} %pad_maximum_fusion.12), channel_id=1, replica_groups=mesh['fsdp'=2,'ctx'=4,'tp'=4] {'fsdp','ctx','tp'}, use_global_device_ids=true, to_apply=%region_13.0 | all-reduce | flops 15360 | bytes 122880 | tf_op jit(solution)/shard_map/psum | solution.py:676
  920.0 3.9 convert_element_type.160
  933.0 8.1 copy.44
  955.8 21.9 %all-gather.26.cloned.1.call-done = bf16[640,2240]{1,0:T(8,128)(2,1)} async-done(((bf16[160,2240]{1,0:T(8,128)(2,1)}), bf16[640,2240]{1,0:T(8,128)(2,1)}) %all-gather.26.cloned.1.call-update) | async-done | bytes 2867216 | tf_op jit(solution)/shard_map/all_gather | solution.py:658
  992.7 6.1 pad_maximum_fusion
  (238 shorter events, 123.7 us)
Async XLA Ops:
  7.2 62.6 %all-gather.20.cloned.1.call-start = ((), (), s32[]{:S(2)}) async-start(), calls=%async_computation.6 | async-start | bytes 3686400 | tf_op jit(solution)/shard_map/all_gather | solution.py:569
  11.8 157.0 %all-gather.32.cloned.1.call-start = ((), (), s32[]{:S(2)}) async-start(), calls=%async_computation.13 | async-start | bytes 4915200 | tf_op jit(solution)/shard_map/all_gather | solution.py:571
  16.9 157.9 %all-gather.34.cloned.1.call-start = ((), (), s32[]{:S(2)}) async-start(), calls=%async_computation.14 | async-start | bytes 4915200 | tf_op jit(solution)/shard_map/all_gather | solution.py:572
  22.2 226.1 %all-gather.18.cloned.1.call-start = ((), (), s32[]{:S(2)}) async-start(), calls=%async_computation.5 | async-start | bytes 3686400 | tf_op jit(solution)/shard_map/all_gather | solution.py:569
  23.5 323.9 %all-gather.36.cloned.1.call-start = ((), (), s32[]{:S(2)}) async-start(), calls=%async_computation.15 | async-start | bytes 4915200 | tf_op jit(solution)/shard_map/all_gather | solution.py:571
  24.1 329.5 %all-gather.38.cloned.1.call-start = ((), (), s32[]{:S(2)}) async-start(), calls=%async_computation.16 | async-start | bytes 4915200 | tf_op jit(solution)/shard_map/all_gather | solution.py:572
  24.6 706.4 %reduce-scatter.14.cloned.1.call-start = ((), (), s32[]{:S(2)}) async-start(), calls=%async_computation.7 | async-start | bytes 1638400 | tf_op jit(solution)/shard_map/reduce_scatter | solution.py:610
  34.1 35.5 %copy-start.31 = (f32[2,320]{1,0:T(2,128)S(1)}, f32[2,320]{1,0:T(2,128)}, u32[]{:S(2)}) copy-start(f32[2,320]{1,0:T(2,128)} %param.28) | copy-start | bytes 7684
  34.1 35.5 %copy-start.32 = (f32[2,320]{1,0:T(2,128)S(1)}, f32[2,320]{1,0:T(2,128)}, u32[]{:S(2)}) copy-start(f32[2,320]{1,0:T(2,128)} %param.27) | copy-start | bytes 7684
  69.8 28.9 %copy-start.19 = (bf16[1,320,1280]{2,1,0:T(8,128)(2,1)S(1)}, bf16[1,320,1280]{2,1,0:T(8,128)(2,1)}, u32[]{:S(2)}) copy-start(bf16[1,320,1280]{2,1,0:T(8,128)(2,1)} %all-gather) | copy-start | bytes 2457604
  248.3 28.4 %copy-start.20 = (bf16[1,320,1280]{2,1,0:T(8,128)(2,1)S(1)}, bf16[1,320,1280]{2,1,0:T(8,128)(2,1)}, u32[]{:S(2)}) copy-start(bf16[1,320,1280]{2,1,0:T(8,128)(2,1)} %all-gather.3) | copy-start | bytes 2457604
  358.8 374.2 %reduce-scatter.22.cloned.1.call-start = ((), (), s32[]{:S(2)}) async-start(), calls=%async_computation.20 | async-start | bytes 4792320
  368.3 74.8 %copy-start.22 = (bf16[320,512]{1,0:T(8,128)(2,1)S(1)}, bf16[320,512]{1,0:T(8,128)(2,1)}, u32[]{:S(2)}) copy-start(bf16[320,512]{1,0:T(8,128)(2,1)} %get-tuple-element.46) | copy-start | bytes 983044
  368.3 75.4 %copy-start.23 = (f32[1,512,1280]{2,1,0:T(8,128)S(1)}, f32[1,512,1280]{2,1,0:T(8,128)}, u32[]{:S(2)}) copy-start(f32[1,512,1280]{2,1,0:T(8,128)} %param.19) | copy-start | bytes 7864324
  368.3 75.4 %copy-start.38 = (bf16[512,1280]{1,0:T(8,128)(2,1)S(1)}, bf16[512,1280]{1,0:T(8,128)(2,1)}, u32[]{:S(2)}) copy-start(bf16[512,1280]{1,0:T(8,128)(2,1)} %get-tuple-element.152) | copy-start | bytes 3932164
  454.7 279.0 %reduce-scatter.20.cloned.1.call-start = ((), (), s32[]{:S(2)}) async-start(), calls=%async_computation.19 | async-start | bytes 4792320
  458.1 39.7 %copy-start.36 = (bf16[1280,960]{0,1:T(8,128)(2,1)S(1)}, bf16[1280,960]{0,1:T(8,128)(2,1)}, u32[]{:S(2)}) copy-start(bf16[1280,960]{0,1:T(8,128)(2,1)} %all-gather.18.cloned.1.call-done) | copy-start | bytes 7372804
  497.8 70.9 %copy-start.34 = (bf16[1,1280,1280]{2,1,0:T(8,128)(2,1)S(1)}, bf16[1,1280,1280]{2,1,0:T(8,128)(2,1)}, u32[]{:S(2)}) copy-start(bf16[1,1280,1280]{2,1,0:T(8,128)(2,1)} %all-gather.34.cloned.1.call-done) | copy-start | bytes 9830404
  497.8 70.9 %copy-start.37 = (f32[512,1280]{1,0:T(8,128)S(1)}, f32[512,1280]{1,0:T(8,128)}, u32[]{:S(2)}) copy-start(f32[512,1280]{1,0:T(8,128)} %get-tuple-element.151) | copy-start | bytes 7864324
  573.5 70.1 %copy-start.21 = (bf16[320,512]{1,0:T(8,128)(2,1)S(1)}, bf16[320,512]{1,0:T(8,128)(2,1)}, u32[]{:S(2)}) copy-start(bf16[320,512]{1,0:T(8,128)(2,1)} %get-tuple-element.42) | copy-start | bytes 983044
  573.5 70.7 %copy-start.43 = (bf16[512,1280]{1,0:T(8,128)(2,1)S(1)}, bf16[512,1280]{1,0:T(8,128)(2,1)}, u32[]{:S(2)}) copy-start(bf16[512,1280]{1,0:T(8,128)(2,1)} %get-tuple-element.150) | copy-start | bytes 3932164
  655.3 118.3 %reduce-scatter.16.cloned.1.call-start = ((), (), s32[]{:S(2)}) async-start(), calls=%async_computation.17 | async-start | bytes 6635520 | tf_op jit(solution)/shard_map/reduce_scatter | solution.py:655
  657.8 38.8 %copy-start.6 = (bf16[512,1280]{1,0:T(8,128)(2,1)S(1)}, bf16[512,1280]{1,0:T(8,128)(2,1)}, u32[]{:S(2)}) copy-start(bf16[512,1280]{1,0:T(8,128)(2,1)} %copy-done.5) | copy-start | bytes 3932164
  657.8 38.8 %copy-start.42 = (bf16[512,1280]{1,0:T(8,128)(2,1)S(1)}, bf16[512,1280]{1,0:T(8,128)(2,1)}, u32[]{:S(2)}) copy-start(bf16[512,1280]{1,0:T(8,128)(2,1)} %copy-done.41) | copy-start | bytes 3932164
  712.5 200.1 %reduce-scatter.18.cloned.1.call-start = ((), (), s32[]{:S(2)}) async-start(), calls=%async_computation.18 | async-start | bytes 6635520 | tf_op jit(solution)/shard_map/reduce_scatter | solution.py:655
  730.9 42.8 %copy-start.15 = (bf16[960,512]{1,0:T(8,128)(2,1)S(1)}, bf16[960,512]{1,0:T(8,128)(2,1)}, u32[]{:S(2)}) copy-start(bf16[960,512]{1,0:T(8,128)(2,1)} %attend_back.3) | copy-start | bytes 2949124
  730.9 43.1 %copy-start.13 = (bf16[960,512]{1,0:T(8,128)(2,1)S(1)}, bf16[960,512]{1,0:T(8,128)(2,1)}, u32[]{:S(2)}) copy-start(bf16[960,512]{1,0:T(8,128)(2,1)} %attend_back.2) | copy-start | bytes 2949124
  731.0 186.0 %all-gather.22.cloned.1.call-start = ((), (), s32[]{:S(2)}) async-start(), calls=%async_computation.8 | async-start | bytes 1638400 | tf_op jit(solution)/shard_map/all_gather | solution.py:612
  733.0 187.0 %all-gather.30.cloned.1.call-start = ((), (), s32[]{:S(2)}) async-start(), calls=%async_computation.12 | async-start | bytes 2662400 | tf_op jit(solution)/shard_map/all_gather | solution.py:662
  733.7 190.2 %all-gather.28.cloned.1.call-start = ((), (), s32[]{:S(2)}) async-start(), calls=%async_computation.11 | async-start | bytes 2662400 | tf_op jit(solution)/shard_map/all_gather | solution.py:662
  734.3 214.6 %all-gather.24.cloned.1.call-start = ((), (), s32[]{:S(2)}) async-start(), calls=%async_computation.9 | async-start | bytes 3686400 | tf_op jit(solution)/shard_map/all_gather | solution.py:658
  773.6 204.2 %all-gather.26.cloned.1.call-start = ((), (), s32[]{:S(2)}) async-start(), calls=%async_computation.10 | async-start | bytes 3686400 | tf_op jit(solution)/shard_map/all_gather | solution.py:658
  (28 other events, 68.6 us)
Sparse Core Ops, SparseCore 0:
  11.9 51.4 all-gather.19
  65.5 45.7 all-gather.31
  113.5 46.3 all-gather.33
  161.8 37.1 all-gather.17
  200.9 46.3 all-gather.35
  249.3 46.3 all-gather.37
  359.0 40.8 reduce-scatter.13
  454.9 55.3 reduce-scatter.21
  655.4 54.5 reduce-scatter.19
  713.9 59.6 reduce-scatter.15
  777.6 59.6 reduce-scatter.17
  839.2 32.5 all-gather.21
  873.4 22.0 all-gather.29
  896.8 23.1 all-gather.27
  921.5 27.3 all-gather.23
  950.3 27.3 all-gather.25

commit v3 on v2

--- a/solution.py
+++ b/solution.py
@@ -17,6 +17,8 @@
 LAYERS = 2
 ROOT_HALF = 1.0 / math.sqrt(2.0)
 DENSITY = 1.0 / math.sqrt(2.0 * math.pi)
+REDUCE_LAG = 2
+GATHER_LAG = 3
 
 
 def norm_parts(values):
@@ -79,28 +81,24 @@
             device_id_type=MESH,
         )
 
-    def reduce_step(step):
-        for k in range(n - 1):
-            for way in range(2):
-                shard = n - 1 - k if way == 0 else k
-                landing = from_left if way == 0 else from_right
-                first = me == 0 if way == 0 else me == n - 1
-                inside = (me > 0) & (me < shard) if way == 0 else (me < n - 1) & (me > shard)
-
-                @pl.when(first)
-                def _():
-                    reduce_copy(way, partial, shard, step).start()
-
-                @pl.when(inside)
-                def _():
-                    rows = rows_of(shard, step)
-                    reduce_copy(way, partial, shard, step).wait_recv()
-                    landing[rows, :] = (
-                        partial[rows, :].astype(WIDE) + landing[rows, :].astype(WIDE)
-                    ).astype(LOW)
-                    reduce_copy(way, landing, shard, step).start()
-
-    def finish_step(step):
+    def reduce_one(way, shard, step):
+        landing = from_left if way == 0 else from_right
+        first = me == 0 if way == 0 else me == n - 1
+
+        @pl.when(first)
+        def _():
+            reduce_copy(way, partial, shard, step).start()
+
+        @pl.when(jnp.logical_not(first))
+        def _():
+            rows = rows_of(shard, step)
+            reduce_copy(way, partial, shard, step).wait_recv()
+            landing[rows, :] = (
+                partial[rows, :].astype(WIDE) + landing[rows, :].astype(WIDE)
+            ).astype(LOW)
+            reduce_copy(way, landing, shard, step).start()
+
+    def finish_one(step):
         rows = rows_of(me, step)
         total[...] = partial[rows, :].astype(WIDE)
 
@@ -125,37 +123,58 @@
         def _():
             gather_copy(1, me, step).start()
 
-    def forward_step(step):
-        for k in range(1, n):
+    def forward_one(way, shard, step):
+        gather_copy(way, shard, step).wait_recv()
+
+        @pl.when(has_right if way == 0 else has_left)
+        def _():
+            gather_copy(way, shard, step).start()
+
+    period = n - 1
+
+    def finish_at(device):
+        from_start = jnp.where(device > 0, n - 1 - device + REDUCE_LAG * device, 0)
+        from_end = jnp.where(device < n - 1, device + REDUCE_LAG * (n - 1 - device), 0)
+        return jnp.maximum(from_start, from_end)
+
+    def split(tick, start, length):
+        since = tick - start
+        clipped = jnp.maximum(since, 0)
+        return (since >= 0) & (clipped < length), lax.div(clipped, period), lax.rem(clipped, period)
+
+    def body(tick, carry):
+        for way in range(2):
+            hops = me if way == 0 else n - 1 - me
+            due, step, k = split(tick, REDUCE_LAG * hops, pieces * period)
+            shard = n - 1 - k if way == 0 else k
+            mine = me < shard if way == 0 else me > shard
+
+            @pl.when(due & mine)
+            def _():
+                reduce_one(way, shard, step)
+
+        due, step, k = split(tick, finish_at(me), pieces * period)
+
+        @pl.when(due & (k == 0))
+        def _():
+            finish_one(step)
+
+        for hops in range(1, n):
             for way in range(2):
-                shard = me - k if way == 0 else me + k
+                shard = me - hops if way == 0 else me + hops
                 there = shard >= 0 if way == 0 else shard <= n - 1
-                further = has_right if way == 0 else has_left
-
-                @pl.when(there)
+                due, step, k = split(
+                    tick, finish_at(shard) + GATHER_LAG * hops, pieces * period
+                )
+
+                @pl.when(there & due & (k == 0))
                 def _():
-                    gather_copy(way, shard, step).wait_recv()
-
-                @pl.when(there & further)
-                def _():
-                    gather_copy(way, shard, step).start()
-
-    def body(step, carry):
-        @pl.when(step < pieces)
-        def _():
-            reduce_step(step)
-
-        @pl.when((step >= 1) & (step <= pieces))
-        def _():
-            finish_step(step - 1)
-
-        @pl.when(step >= 2)
-        def _():
-            forward_step(step - 2)
+                    forward_one(way, shard, step)
 
         return carry
 
-    lax.fori_loop(0, pieces + 2, body, 0)
+    ticks = period * (pieces - 1) + max(REDUCE_LAG, 1) * (n - 1) + GATHER_LAG * (n - 1) + 1
+    lax.fori_loop(0, ticks, body, 0)
 
     def drain(step, carry):
         for k in range(n - 1):
@@ -647,34 +666,47 @@
         )
         grad_output_w = product(attended, grad_mid_low, 1, 0)
         branch = product(grad_qkv, w_qkv, 0, 1).astype(LOW)
+        by_rows = jnp.concatenate(
+            [product(normed, grad_qkv, 0, 1).astype(LOW), grad_inner_w.astype(LOW)], axis=1
+        )
+        by_cols = jnp.concatenate([grad_output_w.astype(LOW), grad_outer_w.astype(LOW)], axis=0)
+        branch, by_rows, by_cols = lax.optimization_barrier((branch, by_rows, by_cols))
         grad_low, grad_own, sums_one = backward_exchange(
             branch, grad_middle, residual, vector(2, layer), tp_size, 2 * layer + 9
         )
-        by_rows = jnp.concatenate([product(normed, grad_qkv, 0, 1), grad_inner_w], axis=1)
-        by_cols = jnp.concatenate([grad_output_w, grad_outer_w], axis=0)
         by_rows = lax.psum_scatter(
-            by_rows.astype(LOW), ("fsdp", "ctx"), scatter_dimension=0, tiled=True
+            by_rows, ("fsdp", "ctx"), scatter_dimension=0, tiled=True
         )
         by_rows = lax.all_gather(by_rows, "ctx", axis=0, tiled=True).astype(WIDE)
         by_cols = lax.psum_scatter(
-            by_cols.astype(LOW), ("fsdp", "ctx"), scatter_dimension=1, tiled=True
+            by_cols, ("fsdp", "ctx"), scatter_dimension=1, tiled=True
         )
         by_cols = lax.all_gather(by_cols, "ctx", axis=1, tiled=True).astype(WIDE)
         grads[layer] = (by_rows, by_cols)
-        vectors[layer] = jnp.stack(
-            [sums_two[2], outer_bias_sum, sums_one[0], sums_one[1], sums_two[0], sums_two[1]]
-        )
-        outer_bias_sum = sums_one[2]
-        biases[layer] = jnp.concatenate(
+        own_sums = jnp.concatenate(
             [
                 jnp.sum(grad_qkv.astype(WIDE), axis=1),
                 jnp.sum(grad_inner.astype(WIDE), axis=0),
             ]
         )
+        placed = jnp.where(
+            jnp.arange(tp_size)[:, None] == lax.axis_index("tp"), own_sums[None, :], 0.0
+        )
+        vector_parts = jnp.stack(
+            [sums_two[2], outer_bias_sum, sums_one[0], sums_one[1], sums_two[0], sums_two[1]]
+        )
+        outer_bias_sum = sums_one[2]
+        summed = lax.psum(
+            jnp.concatenate([placed.reshape(-1), vector_parts.reshape(-1)]), ("fsdp", "ctx", "tp")
+        )
+        biases[layer] = lax.dynamic_slice_in_dim(
+            summed, lax.axis_index("tp") * own_sums.shape[0], own_sums.shape[0]
+        )
+        vectors[layer] = summed[placed.size :].reshape(vector_parts.shape)
     grad_hidden = grad_low.astype(WIDE)
 
-    vector_sums = lax.psum(jnp.stack(vectors, axis=1), ("fsdp", "ctx", "tp"))
-    bias_sums = lax.psum(jnp.stack(biases), ("fsdp", "ctx"))
+    vector_sums = jnp.stack(vectors, axis=1)
+    bias_sums = jnp.stack(biases)
     shard = output_bias.shape[1]
     vector_sums = lax.dynamic_slice_in_dim(
         vector_sums, lax.axis_index("fsdp") * shard, shard, axis=2

time: 1010 us -> 1090 us (1.079)
  waiting for transfers between devices: 67 us -> 393 us
  Pallas kernels: 614 us -> 416 us
  blocking collectives: 104 us -> 38.9 us
    psum x0 -> x1, waiting for transfers between devices: none -> 127 us  [per_device(): lax.psum(jnp.concatenate([placed.reshape(-1), vector_parts.reshape(-1)]),...]
    pallas_call x4, Pallas kernels: 283 us -> 177 us  [backward_exchange(): pl.pallas_call(functools.partial(backward_exchange_kernel, n, PIECES), ou...]
    reduce_scatter x2, waiting for transfers between devices: 39.2 us -> 125 us  [per_device(): lax.psum_scatter(by_rows, ('fsdp', 'ctx'), scatter_dimension=0, tiled=True)]
    pallas_call x3, Pallas kernels: 204 us -> 134 us  [forward_exchange(): pl.pallas_call(functools.partial(forward_exchange_kernel, n, PIECES), out...]
    psum x2 -> x0, blocking collectives: 62.1 us -> none  [the longest x1 38.2 us: per_device(): vector_sums = lax.psum(jnp.stack(vectors, axis=1), ('fsdp', 'ctx', 'tp'))]
    all_gather x2, waiting for transfers between devices: 0.01 us -> 40.6 us  [per_device(): by_cols = lax.all_gather(by_cols, 'ctx', axis=1, tiled=True).astype(WIDE)]
    all_gather x1, waiting for transfers between devices: 0.01 us -> 34.1 us  [per_device(): lax.all_gather(residual.astype(LOW), 'tp', axis=0, tiled=True).astype(WIDE)]
    unnamed x18 -> x19, waiting for transfers between devices: 2.46 us -> 29.8 us
  transfers between devices with their start and end apart: 16 -> 17, of which waited for: 3 -> 11; matrix products, arithmetic and copies ran while one was open for 17% -> 15% of each run, Pallas kernels for 61% -> 34%
where the time goes in v3:
time: 1090 us
  Pallas kernels  416 us (38%)
  waiting for transfers between devices  393 us (36%)
  local copies, waits for them, and re-layouts  81.3 us (7%)
  matrix products  74.1 us (7%)
  other arithmetic  65.5 us (6%)
  blocking collectives  38.9 us (4%)
  between operations  15.9 us (1%)
    pallas_call x4, Pallas kernels, backward_exchange(): pl.pallas_call(functools.partial(backward_exchange_kernel, n, PIECES), ou...  177 us
    pallas_call x3, Pallas kernels, forward_exchange(): pl.pallas_call(functools.partial(forward_exchange_kernel, n, PIECES), out...  134 us
    psum x1, waiting for transfers between devices, per_device(): lax.psum(jnp.concatenate([placed.reshape(-1), vector_parts.reshape(-1)]),...  127 us
    reduce_scatter x2, waiting for transfers between devices, per_device(): lax.psum_scatter(by_rows, ('fsdp', 'ctx'), scatter_dimension=0, tiled=True)  125 us
    dot_general x24, matrix products, product(): lax.dot_general(left_side, right_side, (((left_axis,), (right_axis,)), ((...  74.1 us
    unnamed x103, local copies, waits for them, and re-layouts  60.3 us
    pallas_call x2, Pallas kernels, attend_back(): pl.pallas_call(functools.partial(attend_back_kernel, scale), out_shape=ja...  56.7 us
    pallas_call x2, Pallas kernels, attend(): pl.pallas_call(functools.partial(attend_kernel, scale), out_shape=(jax.Sh...  48.5 us
  transfers between devices with their start and end apart: 17, of which 11 were waited for; matrix products, arithmetic and copies ran while one was open for 15% of the time, Pallas kernels for 34%

profile of v3, /device:TPU:0, one launch (start us, length us, event | category | flops | bytes accessed | tf_op | source)
XLA Modules:
  0.0 1085.7 jit_solution(155487892351523330)
XLA Ops:
  24.9 6.1 all_gather.44
  36.8 21.4 %all-gather.3 = bf16[1,320,1280]{2,1,0:T(8,128)(2,1)} all-gather(bf16[1,320,640]{2,1,0:T(8,128)(2,1)S(1)} %get-tuple-element.136), channel_id=5, replica_groups=mesh['fsdp'=2,'ctx'=4,'tp'=4] {'fsdp'}, dimensions={2}, use_global_device_ids=true | all-gather | bytes 1228800 | tf_op jit(solution)/shard_map/all_gather | solution.py:589
  58.1 11.4 %all-gather = bf16[1,320,1280]{2,1,0:T(8,128)(2,1)S(1)} all-gather(bf16[1,320,640]{2,1,0:T(8,128)(2,1)S(1)} %get-tuple-element.137), channel_id=2, replica_groups=mesh['fsdp'=2,'ctx'=4,'tp'=4] {'fsdp'}, dimensions={2}, use_global_device_ids=true | all-gather | bytes 1228800 | tf_op jit(solution)/shard_map/all_gather | solution.py:589
  71.6 5.6 add_convert_fusion.2.qkv
  77.2 24.3 %attend.2 = (bf16[320,512]{1,0:T(8,128)(2,1)}, f32[320,512]{1,0:T(8,128)}, f32[8,512]{1,0:T(8,128)}, bf16[3,640,512]{2,1,0:T(8,128)(2,1)}) custom-call(s32[1]{0:T(128)S(6)} %copy.55.length, bf16[960,512]{1,0:T(8,128)(2,1)} %add_convert_fusion.2.qkv), custom_call_target="tpu_custom_call" | custom-call | tf_op jit(solution)/shard_map/attend/pallas_call | solution.py:375
  103.3 45.7 %forward_exchange.3 = (bf16[512,1280]{1,0:T(8,128)(2,1)S(1)}, f32[128,1280]{1,0:T(8,128)S(1)}) custom-call(bf16[512,1280]{1,0:T(8,128)(2,1)S(1)} %convolution_convert_fusion.9.partial, f32[128,1280]{1,0:T(8,128)S(1)} %dynamic-slice_bitcast_fusion.residual.normal_in, f32[1,1280]{1,0:T(1,128)S(1)} %get-tuple-element.153.bias, ...), custom_call_target="tpu_custom_call" | custom-call | tf_op jit(solution)/shard_map/forward_exchange/pallas_call | solution.py:255
  150.1 6.2 multiply_convert_fusion.1
  162.3 45.2 %forward_exchange.4 = (bf16[512,1280]{1,0:T(8,128)(2,1)S(1)}, f32[128,1280]{1,0:T(8,128)S(1)}) custom-call(bf16[512,1280]{1,0:T(8,128)(2,1)S(1)} %fusion.15.partial, f32[128,1280]{1,0:T(8,128)S(1)} %get-tuple-element.50.residual.normal_in, f32[1,1280]{1,0:T(1,128)S(1)} %get-tuple-element.150.bias, f32[1,1280]{1,0:T(1,128)S(1)} %get-tuple-element.149.gain, ...), custom_call_target="tpu_custom_call" | custom-call | tf_op jit(solution)/shard_map/forward_exchange/pallas_call | solution.py:255
  213.5 24.2 %attend.3 = (bf16[320,512]{1,0:T(8,128)(2,1)}, f32[320,512]{1,0:T(8,128)}, f32[8,512]{1,0:T(8,128)}, bf16[3,640,512]{2,1,0:T(8,128)(2,1)}) custom-call(s32[1]{0:T(128)S(6)} %copy.55.length, bf16[960,512]{1,0:T(8,128)(2,1)} %add_convert_fusion.1.qkv), custom_call_target="tpu_custom_call" | custom-call | tf_op jit(solution)/shard_map/attend/pallas_call | solution.py:375
  239.6 42.7 %forward_exchange.5 = (bf16[512,1280]{1,0:T(8,128)(2,1)S(1)}, f32[128,1280]{1,0:T(8,128)S(1)}) custom-call(bf16[512,1280]{1,0:T(8,128)(2,1)S(1)} %convolution_convert_fusion.8.partial, f32[128,1280]{1,0:T(8,128)S(1)} %get-tuple-element.53.residual.normal_in, f32[1,1280]{1,0:T(1,128)S(1)} %get-tuple-element.147.bias, f32[1,1280]{1,0:T(1,128)S(1)} %get-tuple-element.146.gain, ...), custom_call_target="tpu_custom_call" | custom-call | tf_op jit(solution)/shard_map/forward_exchange/pallas_call | solution.py:255
  283.4 6.2 multiply_convert_fusion
  294.1 6.0 convert_reduce_fusion
  302.0 45.7 %backward_exchange.4 = (bf16[512,1280]{1,0:T(8,128)(2,1)S(1)}, f32[128,1280]{1,0:T(8,128)S(1)}, f32[8,1280]{1,0:T(8,128)S(1)}) custom-call(bf16[512,1280]{1,0:T(8,128)(2,1)S(1)} %fusion.18.partial, f32[128,1280]{1,0:T(8,128)S(1)} %get-tuple-element.135.grad_out, f32[128,1280]{1,0:T(8,128)S(1)} %get-tuple-element.54.normal_in, ...), custom_call_target="tpu_custom_call" | custom-call | tf_op jit(solution)/shard_map/backward_exchange/pallas_call | solution.py:273
  361.0 29.0 %attend_back.2 = bf16[960,512]{1,0:T(8,128)(2,1)} custom-call(s32[1]{0:T(128)S(6)} %copy.55.length, bf16[960,512]{1,0:T(8,128)(2,1)} %add_convert_fusion.1.qkv, bf16[3,640,512]{2,1,0:T(8,128)(2,1)} %get-tuple-element.57.held, bf16[320,512]{1,0:T(8,128)(2,1)} %fusion.38.grad, f32[320,512]{1,0:T(8,128)} %get-tuple-element.59.out_wide, ...), custom_call_target="tpu_custom_call" | custom-call | tf_op jit(solution)/shard_map/attend_back/pallas_call | solution.py:504
  402.4 42.3 %backward_exchange.5 = (bf16[512,1280]{1,0:T(8,128)(2,1)S(1)}, f32[128,1280]{1,0:T(8,128)S(1)}, f32[8,1280]{1,0:T(8,128)S(1)}) custom-call(bf16[512,1280]{1,0:T(8,128)(2,1)S(1)} %convolution_convert_fusion.7.partial, f32[128,1280]{1,0:T(8,128)S(1)} %copy-done.3, f32[128,1280]{1,0:T(8,128)S(1)} %get-tuple-element.53.residual.normal_in, ...), custom_call_target="tpu_custom_call" | custom-call | tf_op jit(solution)/shard_map/backward_exchange/pallas_call | solution.py:273
  455.1 45.5 %backward_exchange.6 = (bf16[512,1280]{1,0:T(8,128)(2,1)S(1)}, f32[128,1280]{1,0:T(8,128)S(1)}, f32[8,1280]{1,0:T(8,128)S(1)}) custom-call(bf16[512,1280]{1,0:T(8,128)(2,1)S(1)} %fusion.12.partial, f32[128,1280]{1,0:T(8,128)S(1)} %get-tuple-element.64.grad_out, f32[128,1280]{1,0:T(8,128)S(1)} %get-tuple-element.50.residual.normal_in, ...), custom_call_target="tpu_custom_call" | custom-call | tf_op jit(solution)/shard_map/backward_exchange/pallas_call | solution.py:273
  502.5 27.7 %attend_back.3 = bf16[960,512]{1,0:T(8,128)(2,1)} custom-call(s32[1]{0:T(128)S(6)} %copy.55.length, bf16[960,512]{1,0:T(8,128)(2,1)} %add_convert_fusion.2.qkv, bf16[3,640,512]{2,1,0:T(8,128)(2,1)} %get-tuple-element.56.held, bf16[320,512]{1,0:T(8,128)(2,1)} %fusion.39.grad, f32[320,512]{1,0:T(8,128)} %get-tuple-element.66.out_wide, ...), custom_call_target="tpu_custom_call" | custom-call | tf_op jit(solution)/shard_map/attend_back/pallas_call | solution.py:504
  541.2 6.8 copy.49
  548.1 7.0 copy.51
  555.2 9.2 copy.45
  567.9 43.7 %backward_exchange.7 = (bf16[512,1280]{1,0:T(8,128)(2,1)S(1)}, f32[128,1280]{1,0:T(8,128)}, f32[8,1280]{1,0:T(8,128)S(1)}) custom-call(bf16[512,1280]{1,0:T(8,128)(2,1)S(1)} %convolution_convert_fusion.6.partial, f32[128,1280]{1,0:T(8,128)S(1)} %get-tuple-element.69.grad_out, f32[128,1280]{1,0:T(8,128)S(1)} %dynamic-slice_bitcast_fusion.residual.normal_in, ...), custom_call_target="tpu_custom_call" | custom-call | tf_op jit(solution)/shard_map/backward_exchange/pallas_call | solution.py:273
  614.1 8.9 copy.47
  625.7 28.0 %reduce-scatter.22.cloned.1.call-done = bf16[160,1600]{1,0:T(8,128)(2,1)} async-done(((bf16[1280,1600]{1,0:T(8,128)(2,1)}), bf16[160,1600]{1,0:T(8,128)(2,1)}) %reduce-scatter.22.cloned.1.call-update) | async-done | bytes 512016
  653.7 63.5 %reduce-scatter.16.cloned.1.call-done = bf16[160,2240]{1,0:T(8,128)(2,1)} async-done(((bf16[1280,2240]{1,0:T(8,128)(2,1)}), bf16[160,2240]{1,0:T(8,128)(2,1)}) %reduce-scatter.16.cloned.1.call-update) | async-done | bytes 716816 | tf_op jit(solution)/shard_map/reduce_scatter | solution.py:677
  719.0 126.6 %all-reduce.3.cloned.1.call-done = (f32[16640]{0:T(1024)}, f32[16640]{0:T(1024)}) async-done(((f32[16640]{0:T(1024)}, f32[16640]{0:T(1024)}), (f32[16640]{0:T(1024)}, f32[16640]{0:T(1024)})) %all-reduce.3.cloned.1.call-update) | async-done | bytes 133136 | tf_op jit(solution)/shard_map/psum | solution.py:699
  850.2 61.9 %reduce-scatter.18.cloned.1.call-done = bf16[160,2240]{1,0:T(8,128)(2,1)} async-done(((bf16[1280,2240]{1,0:T(8,128)(2,1)}), bf16[160,2240]{1,0:T(8,128)(2,1)}) %reduce-scatter.18.cloned.1.call-update) | async-done | bytes 716816 | tf_op jit(solution)/shard_map/reduce_scatter | solution.py:677
  912.7 34.1 %all-gather.22.cloned.1.call-done = bf16[512,1280]{1,0:T(8,128)(2,1)} async-done(((bf16[128,1280]{1,0:T(8,128)(2,1)}), bf16[512,1280]{1,0:T(8,128)(2,1)}) %all-gather.22.cloned.1.call-update) | async-done | bytes 1310736 | tf_op jit(solution)/shard_map/all_gather | solution.py:631
  949.8 20.3 %all-gather.28.cloned.1.call-done = bf16[1600,640]{0,1:T(8,128)(2,1)} async-done(((bf16[1600,160]{0,1:T(8,128)(2,1)}), bf16[1600,640]{0,1:T(8,128)(2,1)}) %all-gather.28.cloned.1.call-update) | async-done | bytes 2048016 | tf_op jit(solution)/shard_map/all_gather | solution.py:684
  974.0 20.3 %all-gather.30.cloned.1.call-done = bf16[1600,640]{0,1:T(8,128)(2,1)} async-done(((bf16[1600,160]{0,1:T(8,128)(2,1)}), bf16[1600,640]{0,1:T(8,128)(2,1)}) %all-gather.30.cloned.1.call-update) | async-done | bytes 2048016 | tf_op jit(solution)/shard_map/all_gather | solution.py:684
  1003.3 8.6 copy.44
  1016.2 6.9 all-gather.24.cloned.1.call-done
  1028.3 23.6 %all-gather.26.cloned.1.call-done = bf16[640,2240]{1,0:T(8,128)(2,1)} async-done(((bf16[160,2240]{1,0:T(8,128)(2,1)}), bf16[640,2240]{1,0:T(8,128)(2,1)}) %all-gather.26.cloned.1.call-update) | async-done | bytes 2867216 | tf_op jit(solution)/shard_map/all_gather | solution.py:680
  (252 shorter events, 165.2 us)
Async XLA Ops:
  7.2 64.4 %all-gather.20.cloned.1.call-start = ((), (), s32[]{:S(2)}) async-start(), calls=%async_computation.6 | async-start | bytes 3686400 | tf_op jit(solution)/shard_map/all_gather | solution.py:588
  11.8 138.3 %all-gather.32.cloned.1.call-start = ((), (), s32[]{:S(2)}) async-start(), calls=%async_computation.13 | async-start | bytes 4915200 | tf_op jit(solution)/shard_map/all_gather | solution.py:590
  16.9 141.2 %all-gather.34.cloned.1.call-start = ((), (), s32[]{:S(2)}) async-start(), calls=%async_computation.14 | async-start | bytes 4915200 | tf_op jit(solution)/shard_map/all_gather | solution.py:591
  22.2 186.4 %all-gather.18.cloned.1.call-start = ((), (), s32[]{:S(2)}) async-start(), calls=%async_computation.5 | async-start | bytes 3686400 | tf_op jit(solution)/shard_map/all_gather | solution.py:588
  23.5 259.9 %all-gather.36.cloned.1.call-start = ((), (), s32[]{:S(2)}) async-start(), calls=%async_computation.15 | async-start | bytes 4915200 | tf_op jit(solution)/shard_map/all_gather | solution.py:590
  24.1 270.0 %all-gather.38.cloned.1.call-start = ((), (), s32[]{:S(2)}) async-start(), calls=%async_computation.16 | async-start | bytes 4915200 | tf_op jit(solution)/shard_map/all_gather | solution.py:591
  24.6 598.5 %reduce-scatter.14.cloned.1.call-start = ((), (), s32[]{:S(2)}) async-start(), calls=%async_computation.7 | async-start | bytes 1638400 | tf_op jit(solution)/shard_map/reduce_scatter | solution.py:629
  31.1 4.2 copy-start.30
  36.7 32.9 %copy-start.37 = (f32[2,320]{1,0:T(2,128)S(1)}, f32[2,320]{1,0:T(2,128)}, u32[]{:S(2)}) copy-start(f32[2,320]{1,0:T(2,128)} %param.28) | copy-start | bytes 7684
  36.7 32.9 %copy-start.38 = (f32[2,320]{1,0:T(2,128)S(1)}, f32[2,320]{1,0:T(2,128)}, u32[]{:S(2)}) copy-start(f32[2,320]{1,0:T(2,128)} %param.27) | copy-start | bytes 7684
  69.6 31.9 %copy-start.23 = (bf16[1,320,1280]{2,1,0:T(8,128)(2,1)}, bf16[1,320,1280]{2,1,0:T(8,128)(2,1)S(1)}, u32[]{:S(2)}) copy-start(bf16[1,320,1280]{2,1,0:T(8,128)(2,1)S(1)} %all-gather) | copy-start | bytes 2457604
  208.6 29.2 %copy-start.25 = (bf16[1,320,1280]{2,1,0:T(8,128)(2,1)S(1)}, bf16[1,320,1280]{2,1,0:T(8,128)(2,1)}, u32[]{:S(2)}) copy-start(bf16[1,320,1280]{2,1,0:T(8,128)(2,1)} %all-gather.3) | copy-start | bytes 2457604
  294.1 6.0 copy-start.42
  302.0 45.7 %copy-start.26 = (bf16[1,320,1280]{2,1,0:T(8,128)(2,1)S(1)}, bf16[1,320,1280]{2,1,0:T(8,128)(2,1)}, u32[]{:S(2)}) copy-start(bf16[1,320,1280]{2,1,0:T(8,128)(2,1)} %all-gather.3) | copy-start | bytes 2457604
  302.0 47.1 %copy-start.28 = (bf16[320,512]{1,0:T(8,128)(2,1)S(1)}, bf16[320,512]{1,0:T(8,128)(2,1)}, u32[]{:S(2)}) copy-start(bf16[320,512]{1,0:T(8,128)(2,1)} %get-tuple-element.52) | copy-start | bytes 983044
  360.8 264.3 %reduce-scatter.20.cloned.1.call-start = ((), (), s32[]{:S(2)}) async-start(), calls=%async_computation.19 | async-start | bytes 4792320
  361.0 29.0 %copy-start.7 = (bf16[512,1280]{1,0:T(8,128)(2,1)S(1)}, bf16[512,1280]{1,0:T(8,128)(2,1)}, u32[]{:S(2)}) copy-start(bf16[512,1280]{1,0:T(8,128)(2,1)} %copy-done.6) | copy-start | bytes 3932164
  392.9 4.2 copy-start.19
  400.6 44.2 %copy-start.46 = (bf16[512,1280]{1,0:T(8,128)(2,1)S(1)}, bf16[512,1280]{1,0:T(8,128)(2,1)}, u32[]{:S(2)}) copy-start(bf16[512,1280]{1,0:T(8,128)(2,1)} %get-tuple-element.166) | copy-start | bytes 3932164
  455.1 45.5 %copy-start.24 = (bf16[1,320,1280]{2,1,0:T(8,128)(2,1)S(1)}, bf16[1,320,1280]{2,1,0:T(8,128)(2,1)}, u32[]{:S(2)}) copy-start(bf16[1,320,1280]{2,1,0:T(8,128)(2,1)} %copy-done.23) | copy-start | bytes 2457604
  455.1 46.9 %copy-start.27 = (bf16[320,512]{1,0:T(8,128)(2,1)S(1)}, bf16[320,512]{1,0:T(8,128)(2,1)}, u32[]{:S(2)}) copy-start(bf16[320,512]{1,0:T(8,128)(2,1)} %get-tuple-element.48) | copy-start | bytes 983044
  530.2 3.9 copy-start.12
  548.1 105.6 %reduce-scatter.22.cloned.1.call-start = ((), (), s32[]{:S(2)}) async-start(), calls=%async_computation.20 | async-start | bytes 4792320
  555.2 162.1 %reduce-scatter.16.cloned.1.call-start = ((), (), s32[]{:S(2)}) async-start(), calls=%async_computation.17 | async-start | bytes 6635520 | tf_op jit(solution)/shard_map/reduce_scatter | solution.py:677
  564.5 281.1 %all-reduce.3.cloned.1.call-start = ((), (), s32[]{:S(2)}) async-start(), calls=%async_computation.21 | async-start | bytes 278528 | tf_op jit(solution)/shard_map/psum | solution.py:699
  614.1 298.0 %reduce-scatter.18.cloned.1.call-start = ((), (), s32[]{:S(2)}) async-start(), calls=%async_computation.18 | async-start | bytes 6635520 | tf_op jit(solution)/shard_map/reduce_scatter | solution.py:677
  623.1 94.2 %copy-start.1 = (bf16[512,1280]{1,0:T(8,128)(2,1)S(1)}, bf16[512,1280]{1,0:T(8,128)(2,1)}, u32[]{:S(2)}) copy-start(bf16[512,1280]{1,0:T(8,128)(2,1)} %copy-done) | copy-start | bytes 3932164
  623.1 323.7 %all-gather.22.cloned.1.call-start = ((), (), s32[]{:S(2)}) async-start(), calls=%async_computation.8 | async-start | bytes 1638400 | tf_op jit(solution)/shard_map/all_gather | solution.py:631
  625.0 345.0 %all-gather.28.cloned.1.call-start = ((), (), s32[]{:S(2)}) async-start(), calls=%async_computation.11 | async-start | bytes 2662400 | tf_op jit(solution)/shard_map/all_gather | solution.py:684
  625.6 368.6 %all-gather.30.cloned.1.call-start = ((), (), s32[]{:S(2)}) async-start(), calls=%async_computation.12 | async-start | bytes 2662400 | tf_op jit(solution)/shard_map/all_gather | solution.py:684
  653.7 369.4 %all-gather.24.cloned.1.call-start = ((), (), s32[]{:S(2)}) async-start(), calls=%async_computation.9 | async-start | bytes 3686400 | tf_op jit(solution)/shard_map/all_gather | solution.py:680
  717.3 334.7 %all-gather.26.cloned.1.call-start = ((), (), s32[]{:S(2)}) async-start(), calls=%async_computation.10 | async-start | bytes 3686400 | tf_op jit(solution)/shard_map/all_gather | solution.py:680
  (32 other events, 75.0 us)
Sparse Core Ops, SparseCore 0:
  11.9 49.3 all-gather.19
  63.4 46.0 all-gather.31
  111.7 46.3 all-gather.33
  160.1 37.1 all-gather.17
  199.2 46.3 all-gather.35
  247.6 46.3 all-gather.37
  360.9 28.6 reduce-scatter.13
  548.2 50.2 reduce-scatter.19
  602.0 51.6 reduce-scatter.21
  657.6 59.6 reduce-scatter.15
  723.4 122.0 all-reduce.2
  849.5 62.5 reduce-scatter.17
  914.2 32.5 all-gather.21
  948.2 21.8 all-gather.27
  971.5 22.7 all-gather.29
  995.7 27.3 all-gather.23
  1024.5 27.3 all-gather.25

commit v4 on v3

--- a/solution.py
+++ b/solution.py
@@ -36,7 +36,7 @@
     return inverse * (scaled - first_mean - normal_hat * second_mean)
 
 
-def line_exchange(n, own, pieces, partial, gathered, from_left, from_right, total, sems, finish):
+def line_exchange(n, own, pieces, partial, gathered, from_left, from_right, total, sems, finish, side=None):
     rs_send, rs_recv, ag_send, ag_recv = sems
     me = lax.axis_index("tp")
     piece = own // pieces
@@ -53,7 +53,14 @@
     def _():
         pl.semaphore_signal(barrier, inc=1, device_id=to_right, device_id_type=MESH)
 
-    pl.semaphore_wait(barrier, has_left.astype(jnp.int32) + has_right.astype(jnp.int32))
+    peers = has_left.astype(jnp.int32) + has_right.astype(jnp.int32)
+    if side is not None:
+        for peer in side.peers:
+            pl.semaphore_signal(barrier, inc=1, device_id=peer, device_id_type=MESH)
+        peers = peers + len(side.peers)
+    pl.semaphore_wait(barrier, peers)
+    if side is not None:
+        side.start()
 
     def rows_of(shard, step):
         return pl.ds(pl.multiple_of(shard * own + step * piece, piece), piece)
@@ -171,10 +178,16 @@
                 def _():
                     forward_one(way, shard, step)
 
+        if side is not None:
+            side.at(tick)
         return carry
 
     ticks = period * (pieces - 1) + max(REDUCE_LAG, 1) * (n - 1) + GATHER_LAG * (n - 1) + 1
+    if side is not None:
+        ticks = max(ticks, side.ticks)
     lax.fori_loop(0, ticks, body, 0)
+    if side is not None:
+        side.drain()
 
     def drain(step, carry):
         for k in range(n - 1):
@@ -228,7 +241,7 @@
 
 
 def backward_exchange_kernel(
-    n, pieces, partial, grad_out, normal_in, gain, gathered, grad_in, sums, from_left, from_right, total, *sems
+    n, pieces, partial, grad_out, normal_in, gain, gathered, grad_in, sums, from_left, from_right, total, *sems, side=None
 ):
     sums[...] = jnp.zeros_like(sums)
 
@@ -242,12 +255,213 @@
         return grad.astype(LOW)
 
     line_exchange(
-        n, grad_out.shape[0], pieces, partial, gathered, from_left, from_right, total, sems, finish
+        n, grad_out.shape[0], pieces, partial, gathered, from_left, from_right, total, sems, finish, side
     )
 
 
 def in_vmem(count):
     return [pl.BlockSpec(memory_space=pltpu.VMEM)] * count
+
+
+CHUNKS = 10
+
+
+class GradientSum:
+    LAGS = (1, 5, 9, 12)
+
+    def __init__(self, arrays, outs, landings, sems):
+        self.arrays, self.outs, self.landings = arrays, outs, landings
+        self.sends, self.recvs = sems
+        self.half = lax.axis_index("fsdp")
+        self.ctx = lax.axis_index("ctx")
+        self.core = lax.rem(self.ctx, 2)
+        pair = {"ctx": jnp.bitwise_xor(self.ctx, 1)}
+        across = {"ctx": jnp.bitwise_xor(self.ctx, 2)}
+        other = {"fsdp": 1 - self.half}
+        self.peers = (pair, across, other)
+        self.ticks = 2 * (CHUNKS - 1) + self.LAGS[3] + 1
+
+    def view(self, which, half, core, chunk):
+        rows, cols = self.arrays[which].shape
+        if which == 0:
+            part = rows // 4
+            height = part // CHUNKS
+            start = half * (2 * part) + core * part + chunk * height
+            return pl.ds(pl.multiple_of(start, 16), height), slice(None)
+        part = rows // 2
+        height = part // CHUNKS
+        start = core * part + chunk * height
+        width = cols // 2
+        return (
+            pl.ds(pl.multiple_of(start, 16), height),
+            pl.ds(pl.multiple_of(half * width, 128), width),
+        )
+
+    def out_rows(self, which, core, chunk):
+        part = self.outs[which].shape[0] // 2
+        height = part // CHUNKS
+        return pl.ds(pl.multiple_of(core * part + chunk * height, 8), height)
+
+    def copy(self, which, stage, chunk, half=0):
+        pair, across, other = self.peers
+        landing = self.landings[which]
+        if stage == 0:
+            src = self.arrays[which].at[self.view(which, half, 1 - self.core, chunk)]
+            slot, peer = half, pair
+        elif stage == 1:
+            src = landing.at[1 - self.half, chunk]
+            slot, peer = 2, other
+        elif stage == 2:
+            src = landing.at[2, chunk]
+            slot, peer = 3, across
+        else:
+            src = landing.at[3, chunk]
+            slot, peer = 4, pair
+        return pltpu.make_async_remote_copy(
+            src_ref=src,
+            dst_ref=landing.at[slot, chunk],
+            send_sem=self.sends.at[which, slot, chunk],
+            recv_sem=self.recvs.at[which, slot, chunk],
+            device_id=peer,
+            device_id_type=MESH,
+        )
+
+    def start(self):
+        def body(chunk, carry):
+            for which in range(2):
+                for half in range(2):
+                    self.copy(which, 0, chunk, half).start()
+            return carry
+
+        lax.fori_loop(0, CHUNKS, body, 0)
+
+    def when_due(self, tick, lag, action):
+        since = tick - lag
+        clipped = jnp.maximum(since, 0)
+        chunk = lax.div(clipped, 2)
+
+        @pl.when((since >= 0) & (lax.rem(clipped, 2) == 0) & (chunk < CHUNKS))
+        def _():
+            for which in range(2):
+                action(which, chunk)
+
+    def at(self, tick):
+        def joined(which, chunk):
+            landing = self.landings[which]
+            for half in range(2):
+                self.copy(which, 0, chunk, half).wait_recv()
+                rows, cols = self.view(which, half, self.core, chunk)
+                landing[half, chunk] = (
+                    self.arrays[which][rows, cols].astype(WIDE) + landing[half, chunk].astype(WIDE)
+                ).astype(LOW)
+            self.copy(which, 1, chunk).start()
+
+        def crossed(which, chunk):
+            landing = self.landings[which]
+            self.copy(which, 1, chunk).wait_recv()
+            landing[2, chunk] = (
+                landing[self.half, chunk].astype(WIDE) + landing[2, chunk].astype(WIDE)
+            ).astype(LOW)
+            self.copy(which, 2, chunk).start()
+
+        def summed(which, chunk):
+            landing = self.landings[which]
+            self.copy(which, 2, chunk).wait_recv()
+            low = (landing[2, chunk].astype(WIDE) + landing[3, chunk].astype(WIDE)).astype(LOW)
+            landing[3, chunk] = low
+            self.outs[which][self.out_rows(which, self.core, chunk), :] = low.astype(WIDE)
+            self.copy(which, 3, chunk).start()
+
+        def shared(which, chunk):
+            self.copy(which, 3, chunk).wait_recv()
+            self.outs[which][self.out_rows(which, 1 - self.core, chunk), :] = self.landings[which][
+                4, chunk
+            ].astype(WIDE)
+
+        for lag, action in zip(self.LAGS, (joined, crossed, summed, shared)):
+            self.when_due(tick, lag, action)
+
+    def drain(self):
+        def body(chunk, carry):
+            for which in range(2):
+                for half in range(2):
+                    self.copy(which, 0, chunk, half).wait_send()
+                for stage in range(1, 4):
+                    self.copy(which, stage, chunk).wait_send()
+            return carry
+
+        lax.fori_loop(0, CHUNKS, body, 0)
+
+
+def gradient_shapes(by_rows, by_cols):
+    rows, cols = by_rows.shape
+    rows_two, cols_two = by_cols.shape
+    outs = (
+        jax.ShapeDtypeStruct((rows // 2, cols), WIDE),
+        jax.ShapeDtypeStruct((rows_two, cols_two // 2), WIDE),
+    )
+    landings = [
+        pltpu.VMEM((5, CHUNKS, rows // 4 // CHUNKS, cols), LOW),
+        pltpu.VMEM((5, CHUNKS, rows_two // 2 // CHUNKS, cols_two // 2), LOW),
+    ]
+    return outs, landings
+
+
+def backward_gradient_kernel(
+    n, pieces, partial, grad_out, normal_in, gain, by_rows, by_cols, gathered, grad_in, sums, out_rows, out_cols,
+    from_left, from_right, total, rs_send, rs_recv, ag_send, ag_recv, landing_rows, landing_cols, side_send, side_recv
+):
+    side = GradientSum(
+        (by_rows, by_cols), (out_rows, out_cols), (landing_rows, landing_cols), (side_send, side_recv)
+    )
+    backward_exchange_kernel(
+        n, pieces, partial, grad_out, normal_in, gain, gathered, grad_in, sums, from_left, from_right, total,
+        rs_send, rs_recv, ag_send, ag_recv, side=side
+    )
+
+
+def sum_all_kernel(axes, shared_rows, values, out, landing, sends, recvs):
+    steps = [(axis, 1 << b) for axis, size in axes for b in range(size.bit_length() - 1)]
+
+    def peer(axis, k):
+        return {axis: jnp.bitwise_xor(lax.axis_index(axis), k)}
+
+    barrier = pltpu.get_barrier_semaphore()
+    for axis, k in steps:
+        pl.semaphore_signal(barrier, inc=1, device_id=peer(axis, k), device_id_type=MESH)
+    pl.semaphore_wait(barrier, len(steps))
+    out[...] = values[...]
+    for at, (axis, k) in enumerate(steps):
+        rows = pl.ds(0, shared_rows) if axis == "tp" else pl.ds(0, values.shape[0])
+        landing[at, 0, rows] = out[rows, :]
+        copy = pltpu.make_async_remote_copy(
+            src_ref=landing.at[at, 0, rows],
+            dst_ref=landing.at[at, 1, rows],
+            send_sem=sends.at[at],
+            recv_sem=recvs.at[at],
+            device_id=peer(axis, k),
+            device_id_type=MESH,
+        )
+        copy.start()
+        copy.wait()
+        out[rows, :] = landing[at, 0, rows] + landing[at, 1, rows]
+
+
+def sum_all(values, shared_rows, axes, collective_id):
+    steps = sum(size.bit_length() - 1 for _, size in axes)
+    return pl.pallas_call(
+        functools.partial(sum_all_kernel, axes, shared_rows),
+        out_shape=jax.ShapeDtypeStruct(values.shape, WIDE),
+        in_specs=in_vmem(1),
+        out_specs=in_vmem(1)[0],
+        scratch_shapes=[
+            pltpu.VMEM((steps, 2) + values.shape, WIDE),
+            pltpu.SemaphoreType.DMA((steps,)),
+            pltpu.SemaphoreType.DMA((steps,)),
+        ],
+        compiler_params=pltpu.CompilerParams(collective_id=collective_id, has_side_effects=True),
+        name="sum_all",
+    )(values)
 
 
 def forward_exchange(partial, residual, bias, gain, shift, n, collective_id):
@@ -268,23 +482,31 @@
     )(partial, residual, bias[None, :], gain[None, :], shift[None, :])
 
 
-def backward_exchange(partial, grad_out, normal_in, gain, n, collective_id):
+def backward_exchange(partial, grad_out, normal_in, gain, n, collective_id, by_rows=None, by_cols=None):
     rows, width = partial.shape
+    out_shape = (
+        jax.ShapeDtypeStruct((rows, width), LOW),
+        jax.ShapeDtypeStruct(grad_out.shape, WIDE),
+        jax.ShapeDtypeStruct((8, width), WIDE),
+    )
+    scratch = exchange_scratch(n, rows, width, PIECES)
+    kernel, extra = backward_exchange_kernel, ()
+    if by_rows is not None:
+        outs, landings = gradient_shapes(by_rows, by_cols)
+        out_shape = out_shape + outs
+        scratch = scratch + landings + [pltpu.SemaphoreType.DMA((2, 5, CHUNKS))] * 2
+        kernel, extra = backward_gradient_kernel, (by_rows, by_cols)
     return pl.pallas_call(
-        functools.partial(backward_exchange_kernel, n, PIECES),
-        out_shape=(
-            jax.ShapeDtypeStruct((rows, width), LOW),
-            jax.ShapeDtypeStruct(grad_out.shape, WIDE),
-            jax.ShapeDtypeStruct((8, width), WIDE),
-        ),
-        in_specs=in_vmem(4),
-        out_specs=tuple(in_vmem(3)),
-        scratch_shapes=exchange_scratch(n, rows, width, PIECES),
+        functools.partial(kernel, n, PIECES),
+        out_shape=out_shape,
+        in_specs=in_vmem(4 + len(extra)),
+        out_specs=tuple(in_vmem(len(out_shape))),
+        scratch_shapes=scratch,
         compiler_params=pltpu.CompilerParams(
-            collective_id=collective_id, has_side_effects=True, vmem_limit_bytes=40 << 20
+            collective_id=collective_id, has_side_effects=True, vmem_limit_bytes=56 << 20
         ),
         name="backward_exchange",
-    )(partial, grad_out, normal_in, gain[None, :])
+    )(partial, grad_out, normal_in, gain[None, :], *extra)
 
 
 def attend_kernel(scale, length, qkv, out, out_wide, log_total, held, high, low_sum, sems_send, sems_recv):
@@ -630,6 +852,18 @@
             residual = middle + branch + vector(1, layer)
             output = lax.all_gather(residual.astype(LOW), "tp", axis=0, tiled=True).astype(WIDE)
 
+    def exchange_back(branch, grad_out, normal_in, gain, collective_id, by_rows, by_cols):
+        if lax.axis_size("fsdp") == 2:
+            return backward_exchange(
+                branch, grad_out, normal_in, gain, tp_size, collective_id, by_rows, by_cols
+            )
+        first = backward_exchange(branch, grad_out, normal_in, gain, tp_size, collective_id)
+        by_rows = lax.psum_scatter(by_rows, ("fsdp", "ctx"), scatter_dimension=0, tiled=True)
+        by_rows = lax.all_gather(by_rows, "ctx", axis=0, tiled=True).astype(WIDE)
+        by_cols = lax.psum_scatter(by_cols, ("fsdp", "ctx"), scatter_dimension=1, tiled=True)
+        by_cols = lax.all_gather(by_cols, "ctx", axis=1, tiled=True).astype(WIDE)
+        return (*first, by_rows, by_cols)
+
     grad_rows = cotangent.reshape(rows, width)
     grad_own = own_slice(grad_rows)
     grad_low = grad_rows.astype(LOW)
@@ -655,78 +889,70 @@
         grad_active = product(grad_low, w_outer, 1, 1)
         grad_inner = (grad_active * gelu_slope(inner_pre)).astype(LOW)
         branch = product(grad_inner, w_inner, 1, 1).astype(LOW)
-        grad_mid_low, grad_middle, sums_two = backward_exchange(
-            branch, grad_own, middle, vector(4, layer), tp_size, 2 * layer + 8
-        )
-        grad_outer_w = product(active, grad_low, 0, 0)
-        grad_inner_w = product(normed_two, grad_inner, 0, 0)
+        grad_outer_w = product(active, grad_low, 0, 0).astype(LOW)
+        grad_inner_w = product(normed_two, grad_inner, 0, 0).astype(LOW)
+        grad_mid_low, grad_middle, sums_two, *summed_two = exchange_back(
+            branch, grad_own, middle, vector(4, layer), 2 * layer + 8, grad_inner_w, grad_outer_w
+        )
         grad_attended = product(w_out, grad_mid_low, 1, 1).astype(LOW)
         grad_qkv = attend_back(
             qkv, held, grad_attended, attended_wide, log_total, lengths, scale, 2 * layer + 12
         )
-        grad_output_w = product(attended, grad_mid_low, 1, 0)
+        grad_output_w = product(attended, grad_mid_low, 1, 0).astype(LOW)
         branch = product(grad_qkv, w_qkv, 0, 1).astype(LOW)
-        by_rows = jnp.concatenate(
-            [product(normed, grad_qkv, 0, 1).astype(LOW), grad_inner_w.astype(LOW)], axis=1
-        )
-        by_cols = jnp.concatenate([grad_output_w.astype(LOW), grad_outer_w.astype(LOW)], axis=0)
-        branch, by_rows, by_cols = lax.optimization_barrier((branch, by_rows, by_cols))
-        grad_low, grad_own, sums_one = backward_exchange(
-            branch, grad_middle, residual, vector(2, layer), tp_size, 2 * layer + 9
-        )
-        by_rows = lax.psum_scatter(
-            by_rows, ("fsdp", "ctx"), scatter_dimension=0, tiled=True
-        )
-        by_rows = lax.all_gather(by_rows, "ctx", axis=0, tiled=True).astype(WIDE)
-        by_cols = lax.psum_scatter(
-            by_cols, ("fsdp", "ctx"), scatter_dimension=1, tiled=True
-        )
-        by_cols = lax.all_gather(by_cols, "ctx", axis=1, tiled=True).astype(WIDE)
-        grads[layer] = (by_rows, by_cols)
-        own_sums = jnp.concatenate(
+        grad_qkv_w = product(normed, grad_qkv, 0, 1).astype(LOW)
+        grad_low, grad_own, sums_one, *summed_one = exchange_back(
+            branch, grad_middle, residual, vector(2, layer), 2 * layer + 9, grad_qkv_w, grad_output_w
+        )
+        grads[layer] = (*summed_one, *summed_two)
+        vectors[layer] = [
+            sums_two[2], outer_bias_sum, sums_one[0], sums_one[1], sums_two[0], sums_two[1]
+        ]
+        outer_bias_sum = sums_one[2]
+        biases[layer] = jnp.concatenate(
             [
                 jnp.sum(grad_qkv.astype(WIDE), axis=1),
                 jnp.sum(grad_inner.astype(WIDE), axis=0),
             ]
         )
-        placed = jnp.where(
-            jnp.arange(tp_size)[:, None] == lax.axis_index("tp"), own_sums[None, :], 0.0
-        )
-        vector_parts = jnp.stack(
-            [sums_two[2], outer_bias_sum, sums_one[0], sums_one[1], sums_two[0], sums_two[1]]
-        )
-        outer_bias_sum = sums_one[2]
-        summed = lax.psum(
-            jnp.concatenate([placed.reshape(-1), vector_parts.reshape(-1)]), ("fsdp", "ctx", "tp")
-        )
-        biases[layer] = lax.dynamic_slice_in_dim(
-            summed, lax.axis_index("tp") * own_sums.shape[0], own_sums.shape[0]
-        )
-        vectors[layer] = summed[placed.size :].reshape(vector_parts.shape)
     grad_hidden = grad_low.astype(WIDE)
 
-    vector_sums = jnp.stack(vectors, axis=1)
-    bias_sums = jnp.stack(biases)
+    flat_biases = jnp.concatenate(biases)
+    bias_rows = -(-flat_biases.size // width)
+    flat_biases = jnp.pad(flat_biases, (0, bias_rows * width - flat_biases.size))
+    vector_count = 6 * LAYERS
+    shared_rows = -(-vector_count // 8) * 8
+    total_rows = shared_rows + -(-bias_rows // 8) * 8
+    small_sums = jnp.concatenate(
+        [
+            jnp.stack([row for parts in zip(*vectors) for row in parts]),
+            jnp.zeros((shared_rows - vector_count, width), WIDE),
+            flat_biases.reshape(bias_rows, width),
+            jnp.zeros((total_rows - shared_rows - bias_rows, width), WIDE),
+        ]
+    )
+    small_sums = sum_all(
+        small_sums, shared_rows, tuple((axis, lax.axis_size(axis)) for axis in ("ctx", "fsdp", "tp")), 16
+    )
     shard = output_bias.shape[1]
     vector_sums = lax.dynamic_slice_in_dim(
-        vector_sums, lax.axis_index("fsdp") * shard, shard, axis=2
-    )
-
-    def stacked_rows(start, size):
-        return jnp.stack([grads[layer][0][:, start : start + size] for layer in range(LAYERS)])
-
-    def stacked_cols(start, size):
-        return jnp.stack([grads[layer][1][start : start + size] for layer in range(LAYERS)])
+        small_sums[:vector_count].reshape(6, LAYERS, width), lax.axis_index("fsdp") * shard, shard, axis=2
+    )
+    bias_sums = small_sums[shared_rows:].reshape(-1)[: LAYERS * biases[0].size].reshape(LAYERS, -1)
+
+    def stacked(which, start=0, size=None):
+        size = grads[0][which].shape[1] if size is None else size
+        return jnp.stack([grads[layer][which][:, start : start + size] for layer in range(LAYERS)])
 
     return (
         output.reshape(hidden.shape),
         grad_hidden.reshape(hidden.shape),
-        stacked_rows(0, columns),
-        stacked_rows(columns, columns),
-        stacked_rows(2 * columns, columns),
-        stacked_cols(0, columns),
-        stacked_rows(3 * columns, hidden_local),
-        stacked_cols(columns, hidden_local),
+        stacked(0, 0, columns),
+        stacked(0, columns, columns),
+        stacked(0, 2 * columns, columns),
+        stacked(1),
+        stacked(2),
+        stacked(3),
         bias_sums[:, :columns],
         bias_sums[:, 2 * columns : 3 * columns],
         bias_sums[:, 3 * columns :],

time: 1090 us -> 755 us (0.69)
  waiting for transfers between devices: 393 us -> 18.3 us
  Pallas kernels: 416 us -> 514 us
  local copies, waits for them, and re-layouts: 81.3 us -> 36.4 us
  other arithmetic: 65.5 us -> 38.4 us
  matrix products: 74.1 us -> 88.7 us
    psum x1 -> x0, waiting for transfers between devices: 127 us -> none  [per_device(): lax.psum(jnp.concatenate([placed.reshape(-1), vector_parts.reshape(-1)]),...]
    reduce_scatter x2 -> x0, waiting for transfers between devices: 125 us -> none  [per_device(): lax.psum_scatter(by_rows, ('fsdp', 'ctx'), scatter_dimension=0, tiled=True)]
    pallas_call x4 -> x5, Pallas kernels: 177 us -> 274 us  [the longest x4 253 us: backward_exchange(): pl.pallas_call(functools.partial(kernel, n, PIECES), out_shape=out_shape,...]
    all_gather x4 -> x0, waiting for transfers between devices: 71.1 us -> none  [the longest x2 40.6 us: per_device(): by_cols = lax.all_gather(by_cols, 'ctx', axis=1, tiled=True).astype(WIDE)]
    unnamed x103 -> x107, local copies, waits for them, and re-layouts: 60.3 us -> 9.24 us
    unnamed x19 -> x8, waiting for transfers between devices: 29.8 us -> 1.15 us
    all_gather x1, waiting for transfers between devices: 34.1 us -> 9.85 us  [per_device(): lax.all_gather(residual.astype(LOW), 'tp', axis=0, tiled=True).astype(WIDE)]
    dot_general x24, matrix products: 74.1 us -> 88.7 us  [product(): lax.dot_general(left_side, right_side, (((left_axis,), (right_axis,)), ((...]
  transfers between devices with their start and end apart: 17 -> 8, of which waited for: 11 -> 3; matrix products, arithmetic and copies ran while one was open for 15% -> 12% of each run, Pallas kernels for 34% -> 37%
where the time goes in v4:
time: 755 us; the launch traced here: 750 us
  Pallas kernels  514 us (68%)
  matrix products  88.7 us (12%)
  other arithmetic  38.4 us (5%)
  blocking collectives  38.3 us (5%)
  local copies, waits for them, and re-layouts  36.4 us (5%)
  waiting for transfers between devices  18.3 us (2%)
  between operations  15.8 us (2%)
    pallas_call x4, Pallas kernels, backward_exchange(): pl.pallas_call(functools.partial(kernel, n, PIECES), out_shape=out_shape,...  253 us
    pallas_call x3, Pallas kernels, forward_exchange(): pl.pallas_call(functools.partial(forward_exchange_kernel, n, PIECES), out...  133 us
    dot_general x24, matrix products, product(): lax.dot_general(left_side, right_side, (((left_axis,), (right_axis,)), ((...  88.7 us
    pallas_call x2, Pallas kernels, attend_back(): pl.pallas_call(functools.partial(attend_back_kernel, scale), out_shape=ja...  58.1 us
    pallas_call x2, Pallas kernels, attend(): pl.pallas_call(functools.partial(attend_kernel, scale), out_shape=(jax.Sh...  48.8 us
    all_gather x2, blocking collectives, fetch(): lax.all_gather(output_weight[layer].astype(LOW), 'fsdp', axis=1, tiled=True)  32.2 us
    pallas_call x1, Pallas kernels, sum_all(): pl.pallas_call(functools.partial(sum_all_kernel, axes, shared_rows), out_...  21.1 us
  transfers between devices with their start and end apart: 8, of which 3 were waited for; matrix products, arithmetic and copies ran while one was open for 12% of the time, Pallas kernels for 37%

profile of v4, /device:TPU:0, one launch (start us, length us, event | category | flops | bytes accessed | tf_op | source)
XLA Modules:
  0.0 750.0 jit_solution(11272069131066039781)
XLA Ops:
  24.2 6.1 all_gather.32
  36.8 21.3 %all-gather = bf16[1,320,1280]{2,1,0:T(8,128)(2,1)S(1)} all-gather(bf16[1,320,640]{2,1,0:T(8,128)(2,1)S(1)} %get-tuple-element.139), channel_id=2, replica_groups=mesh['fsdp'=2,'ctx'=4,'tp'=4] {'fsdp'}, dimensions={2}, use_global_device_ids=true | all-gather | bytes 1228800 | tf_op jit(solution)/shard_map/all_gather | solution.py:811
  59.5 10.9 %all-gather.3 = bf16[1,320,1280]{2,1,0:T(8,128)(2,1)S(1)} all-gather(bf16[1,320,640]{2,1,0:T(8,128)(2,1)S(1)} %get-tuple-element.138), channel_id=5, replica_groups=mesh['fsdp'=2,'ctx'=4,'tp'=4] {'fsdp'}, dimensions={2}, use_global_device_ids=true | all-gather | bytes 1228800 | tf_op jit(solution)/shard_map/all_gather | solution.py:811
  72.8 5.3 add_convert_fusion.2.qkv
  78.1 24.5 %attend.2 = (bf16[320,512]{1,0:T(8,128)(2,1)}, f32[320,512]{1,0:T(8,128)}, f32[8,512]{1,0:T(8,128)}, bf16[3,640,512]{2,1,0:T(8,128)(2,1)}) custom-call(s32[1]{0:T(128)S(6)} %copy.45.length, bf16[960,512]{1,0:T(8,128)(2,1)} %add_convert_fusion.2.qkv), custom_call_target="tpu_custom_call" | custom-call | tf_op jit(solution)/shard_map/attend/pallas_call | solution.py:597
  104.5 45.4 %forward_exchange.3 = (bf16[512,1280]{1,0:T(8,128)(2,1)S(1)}, f32[128,1280]{1,0:T(8,128)S(1)}) custom-call(bf16[512,1280]{1,0:T(8,128)(2,1)S(1)} %convolution_convert_fusion.9.partial, f32[128,1280]{1,0:T(8,128)S(1)} %dynamic-slice_bitcast_fusion.residual.normal_in, f32[1,1280]{1,0:T(1,128)S(1)} %get-tuple-element.172.bias, ...), custom_call_target="tpu_custom_call" | custom-call | tf_op jit(solution)/shard_map/forward_exchange/pallas_call | solution.py:469
  150.0 5.6 multiply_convert_fusion.1
  157.4 4.2 fusion.15.partial
  161.6 45.2 %forward_exchange.4 = (bf16[512,1280]{1,0:T(8,128)(2,1)S(1)}, f32[128,1280]{1,0:T(8,128)S(1)}) custom-call(bf16[512,1280]{1,0:T(8,128)(2,1)S(1)} %fusion.15.partial, f32[128,1280]{1,0:T(8,128)S(1)} %get-tuple-element.52.residual.normal_in, f32[1,1280]{1,0:T(1,128)S(1)} %get-tuple-element.169.bias, f32[1,1280]{1,0:T(1,128)S(1)} %get-tuple-element.168.gain, ...), custom_call_target="tpu_custom_call" | custom-call | tf_op jit(solution)/shard_map/forward_exchange/pallas_call | solution.py:469
  207.9 5.1 add_convert_fusion.1.qkv
  213.0 24.3 %attend.3 = (bf16[320,512]{1,0:T(8,128)(2,1)}, f32[320,512]{1,0:T(8,128)}, f32[8,512]{1,0:T(8,128)}, bf16[3,640,512]{2,1,0:T(8,128)(2,1)}) custom-call(s32[1]{0:T(128)S(6)} %copy.45.length, bf16[960,512]{1,0:T(8,128)(2,1)} %add_convert_fusion.1.qkv), custom_call_target="tpu_custom_call" | custom-call | tf_op jit(solution)/shard_map/attend/pallas_call | solution.py:597
  239.2 42.5 %forward_exchange.5 = (bf16[512,1280]{1,0:T(8,128)(2,1)S(1)}, f32[128,1280]{1,0:T(8,128)S(1)}) custom-call(bf16[512,1280]{1,0:T(8,128)(2,1)S(1)} %convolution_convert_fusion.8.partial, f32[128,1280]{1,0:T(8,128)S(1)} %get-tuple-element.55.residual.normal_in, f32[1,1280]{1,0:T(1,128)S(1)} %get-tuple-element.166.bias, f32[1,1280]{1,0:T(1,128)S(1)} %get-tuple-element.165.gain, ...), custom_call_target="tpu_custom_call" | custom-call | tf_op jit(solution)/shard_map/forward_exchange/pallas_call | solution.py:469
  282.5 5.4 multiply_convert_fusion
  287.9 5.5 all-gather.26.cloned.1.call-done
  293.4 5.9 convert_reduce_fusion
  299.3 3.6 convolution_convert_fusion.3.by_rows
  309.5 63.0 %backward_exchange.4 = (bf16[512,1280]{1,0:T(8,128)(2,1)}, f32[128,1280]{1,0:T(8,128)}, f32[8,1280]{1,0:T(8,128)}, f32[640,1280]{1,0:T(8,128)}, f32[1280,640]{1,0:T(8,128)}) custom-call(bf16[512,1280]{1,0:T(8,128)(2,1)} %fusion.18.partial, f32[128,1280]{1,0:T(8,128)} %get-tuple-element.131.grad_out, f32[128,1280]{1,0:T(8,128)} %copy-done.1, ...), custom_call_target="tpu_custom_call" | custom-call | tf_op jit(solution)/shard_map/backward_exchange/pallas_call | solution.py:499
  376.8 29.0 %attend_back.2 = bf16[960,512]{1,0:T(8,128)(2,1)} custom-call(s32[1]{0:T(128)S(6)} %copy.45.length, bf16[960,512]{1,0:T(8,128)(2,1)} %add_convert_fusion.1.qkv, bf16[3,640,512]{2,1,0:T(8,128)(2,1)} %get-tuple-element.59.held, bf16[320,512]{1,0:T(8,128)(2,1)} %fusion.38.grad, f32[320,512]{1,0:T(8,128)} %get-tuple-element.61.out_wide, ...), custom_call_target="tpu_custom_call" | custom-call | tf_op jit(solution)/shard_map/attend_back/pallas_call | solution.py:726
  405.8 4.3 convolution_convert_fusion.5
  410.2 4.4 copy.40.by_rows
  414.6 4.3 convolution_convert_fusion.7.partial
  418.9 55.4 %backward_exchange.5 = (bf16[512,1280]{1,0:T(8,128)(2,1)}, f32[128,1280]{1,0:T(8,128)}, f32[8,1280]{1,0:T(8,128)}, f32[640,960]{1,0:T(8,128)}, f32[320,640]{1,0:T(8,128)}) custom-call(bf16[512,1280]{1,0:T(8,128)(2,1)} %convolution_convert_fusion.7.partial, f32[128,1280]{1,0:T(8,128)} %get-tuple-element.63.grad_out, f32[128,1280]{1,0:T(8,128)} %copy-done.4, ...), custom_call_target="tpu_custom_call" | custom-call | tf_op jit(solution)/shard_map/backward_exchange/pallas_call | solution.py:499
  474.4 5.1 convolution_convert_fusion.by_cols
  488.9 62.7 %backward_exchange.6 = (bf16[512,1280]{1,0:T(8,128)(2,1)}, f32[128,1280]{1,0:T(8,128)}, f32[8,1280]{1,0:T(8,128)}, f32[640,1280]{1,0:T(8,128)}, f32[1280,640]{1,0:T(8,128)}) custom-call(bf16[512,1280]{1,0:T(8,128)(2,1)} %fusion.12.partial, f32[128,1280]{1,0:T(8,128)} %get-tuple-element.65.grad_out, f32[128,1280]{1,0:T(8,128)} %copy-done.3, ...), custom_call_target="tpu_custom_call" | custom-call | tf_op jit(solution)/shard_map/backward_exchange/pallas_call | solution.py:499
  555.9 29.1 %attend_back.3 = bf16[960,512]{1,0:T(8,128)(2,1)} custom-call(s32[1]{0:T(128)S(6)} %copy.45.length, bf16[960,512]{1,0:T(8,128)(2,1)} %add_convert_fusion.2.qkv, bf16[3,640,512]{2,1,0:T(8,128)(2,1)} %get-tuple-element.58.held, bf16[320,512]{1,0:T(8,128)(2,1)} %fusion.39.grad, f32[320,512]{1,0:T(8,128)} %get-tuple-element.67.out_wide, ...), custom_call_target="tpu_custom_call" | custom-call | tf_op jit(solution)/shard_map/attend_back/pallas_call | solution.py:726
  585.0 4.6 convolution_convert_fusion.4
  592.9 4.4 copy.41.by_rows
  597.2 4.3 convolution_convert_fusion.6.partial
  601.6 71.4 %backward_exchange.7 = (bf16[512,1280]{1,0:T(8,128)(2,1)}, f32[128,1280]{1,0:T(8,128)}, f32[8,1280]{1,0:T(8,128)}, f32[640,960]{1,0:T(8,128)}, f32[320,640]{1,0:T(8,128)}) custom-call(bf16[512,1280]{1,0:T(8,128)(2,1)} %convolution_convert_fusion.6.partial, f32[128,1280]{1,0:T(8,128)} %get-tuple-element.69.grad_out, f32[128,1280]{1,0:T(8,128)} %copy-done, ...), custom_call_target="tpu_custom_call" | custom-call | tf_op jit(solution)/shard_map/backward_exchange/pallas_call | solution.py:499
  678.9 21.1 %sum_all.1 = f32[24,1280]{1,0:T(8,128)} custom-call(f32[24,1280]{1,0:T(8,128)} %concatenate.30.values), custom_call_target="tpu_custom_call" | custom-call | tf_op jit(solution)/shard_map/sum_all/pallas_call | solution.py:452
  719.9 5.3 pad_maximum_fusion
  730.1 9.8 %all-gather.18.cloned.1.call-done = bf16[512,1280]{1,0:T(8,128)(2,1)} async-done(((bf16[128,1280]{1,0:T(8,128)(2,1)}), bf16[512,1280]{1,0:T(8,128)(2,1)}) %all-gather.18.cloned.1.call-update) | async-done | bytes 1310736 | tf_op jit(solution)/shard_map/all_gather | solution.py:853
  (206 shorter events, 95.2 us)
Async XLA Ops:
  7.2 65.6 %all-gather.16.cloned.1.call-start = ((), (), s32[]{:S(2)}) async-start(), calls=%async_computation.2 | async-start | bytes 3686400 | tf_op jit(solution)/shard_map/all_gather | solution.py:810
  11.1 138.9 %all-gather.20.cloned.1.call-start = ((), (), s32[]{:S(2)}) async-start(), calls=%async_computation.5 | async-start | bytes 4915200 | tf_op jit(solution)/shard_map/all_gather | solution.py:812
  16.3 141.2 %all-gather.22.cloned.1.call-start = ((), (), s32[]{:S(2)}) async-start(), calls=%async_computation.6 | async-start | bytes 4915200 | tf_op jit(solution)/shard_map/all_gather | solution.py:813
  21.5 186.4 %all-gather.14.cloned.1.call-start = ((), (), s32[]{:S(2)}) async-start(), calls=%async_computation.1 | async-start | bytes 3686400 | tf_op jit(solution)/shard_map/all_gather | solution.py:810
  22.8 8.9 %copy-start.31 = (f32[2,1280]{1,0:T(2,128)S(1)}, f32[2,1280]{1,0:T(2,128)}, u32[]{:S(2)}) copy-start(f32[2,1280]{1,0:T(2,128)} %param.29) | copy-start | bytes 30724
  22.8 259.8 %all-gather.24.cloned.1.call-start = ((), (), s32[]{:S(2)}) async-start(), calls=%async_computation.7 | async-start | bytes 4915200 | tf_op jit(solution)/shard_map/all_gather | solution.py:812
  23.4 270.0 %all-gather.26.cloned.1.call-start = ((), (), s32[]{:S(2)}) async-start(), calls=%async_computation.8 | async-start | bytes 4915200 | tf_op jit(solution)/shard_map/all_gather | solution.py:813
  24.0 683.0 %reduce-scatter.2.cloned.1.call-start = ((), (), s32[]{:S(2)}) async-start(), calls=%async_computation.3 | async-start | bytes 1638400 | tf_op jit(solution)/shard_map/reduce_scatter | solution.py:851
  31.0 73.5 %copy-start.5 = (f32[1,1280]{1,0:T(1,128)}, f32[1,1280]{1,0:T(1,128)S(1)}, u32[]{:S(2)}) copy-start(f32[1,1280]{1,0:T(1,128)S(1)} %get-tuple-element.171.gain) | copy-start | bytes 15364
  31.0 130.6 %copy-start.6 = (f32[1,1280]{1,0:T(1,128)}, f32[1,1280]{1,0:T(1,128)S(1)}, u32[]{:S(2)}) copy-start(f32[1,1280]{1,0:T(1,128)S(1)} %get-tuple-element.168.gain) | copy-start | bytes 15364
  31.0 208.2 %copy-start.7 = (f32[1,1280]{1,0:T(1,128)}, f32[1,1280]{1,0:T(1,128)S(1)}, u32[]{:S(2)}) copy-start(f32[1,1280]{1,0:T(1,128)S(1)} %get-tuple-element.165.gain) | copy-start | bytes 15364
  36.6 36.3 %copy-start.41 = (f32[512]{0:T(512)}, f32[512]{0:T(512)S(1)}, u32[]{:S(2)}) copy-start(f32[512]{0:T(512)S(1)} %add_rsqrt_fusion) | copy-start | bytes 6148
  36.8 35.9 %copy-start.39 = (f32[2,320]{1,0:T(2,128)S(1)}, f32[2,320]{1,0:T(2,128)}, u32[]{:S(2)}) copy-start(f32[2,320]{1,0:T(2,128)} %param.28) | copy-start | bytes 7684
  36.8 35.9 %copy-start.40 = (f32[2,320]{1,0:T(2,128)S(1)}, f32[2,320]{1,0:T(2,128)}, u32[]{:S(2)}) copy-start(f32[2,320]{1,0:T(2,128)} %param.27) | copy-start | bytes 7684
  58.1 44.6 %copy-start.24 = (bf16[1,320,1280]{2,1,0:T(8,128)(2,1)}, bf16[1,320,1280]{2,1,0:T(8,128)(2,1)S(1)}, u32[]{:S(2)}) copy-start(bf16[1,320,1280]{2,1,0:T(8,128)(2,1)S(1)} %all-gather) | copy-start | bytes 2457604
  59.5 45.0 %copy-start = (f32[128,1280]{1,0:T(8,128)}, f32[128,1280]{1,0:T(8,128)S(1)}, u32[]{:S(2)}) copy-start(f32[128,1280]{1,0:T(8,128)S(1)} %dynamic-slice_bitcast_fusion.residual.normal_in) | copy-start | bytes 1966084
  70.4 166.9 %copy-start.26 = (bf16[1,320,1280]{2,1,0:T(8,128)(2,1)}, bf16[1,320,1280]{2,1,0:T(8,128)(2,1)S(1)}, u32[]{:S(2)}) copy-start(bf16[1,320,1280]{2,1,0:T(8,128)(2,1)S(1)} %all-gather.3) | copy-start | bytes 2457604
  150.0 11.7 %copy-start.3 = (f32[128,1280]{1,0:T(8,128)}, f32[128,1280]{1,0:T(8,128)S(1)}, u32[]{:S(2)}) copy-start(f32[128,1280]{1,0:T(8,128)S(1)} %get-tuple-element.52.residual.normal_in) | copy-start | bytes 1966084
  207.9 31.3 %copy-start.4 = (f32[128,1280]{1,0:T(8,128)}, f32[128,1280]{1,0:T(8,128)S(1)}, u32[]{:S(2)}) copy-start(f32[128,1280]{1,0:T(8,128)S(1)} %get-tuple-element.55.residual.normal_in) | copy-start | bytes 1966084
  237.3 45.2 %copy-start.32 = (f32[1280]{0:T(1024)S(1)}, f32[1280]{0:T(1024)}, u32[]{:S(2)}) copy-start(f32[1280]{0:T(1024)} %get-tuple-element.120) | copy-start | bytes 15364
  309.5 63.1 %copy-start.27 = (bf16[1,320,1280]{2,1,0:T(8,128)(2,1)S(1)}, bf16[1,320,1280]{2,1,0:T(8,128)(2,1)}, u32[]{:S(2)}) copy-start(bf16[1,320,1280]{2,1,0:T(8,128)(2,1)} %copy-done.26) | copy-start | bytes 2457604
  376.8 29.0 %copy-start.9 = (bf16[512,1280]{1,0:T(8,128)(2,1)S(1)}, bf16[512,1280]{1,0:T(8,128)(2,1)}, u32[]{:S(2)}) copy-start(bf16[512,1280]{1,0:T(8,128)(2,1)} %copy-done.8) | copy-start | bytes 3932164
  418.9 55.4 %copy-start.51 = (bf16[512,1280]{1,0:T(8,128)(2,1)S(1)}, bf16[512,1280]{1,0:T(8,128)(2,1)}, u32[]{:S(2)}) copy-start(bf16[512,1280]{1,0:T(8,128)(2,1)} %get-tuple-element.177) | copy-start | bytes 3932164
  474.3 5.1 copy-start.45
  474.3 5.1 copy-start.47
  474.3 5.1 copy-start.48
  488.9 62.7 %copy-start.25 = (bf16[1,320,1280]{2,1,0:T(8,128)(2,1)S(1)}, bf16[1,320,1280]{2,1,0:T(8,128)(2,1)}, u32[]{:S(2)}) copy-start(bf16[1,320,1280]{2,1,0:T(8,128)(2,1)} %copy-done.24) | copy-start | bytes 2457604
  555.8 29.1 %copy-start.10 = (f32[1,512,1280]{2,1,0:T(8,128)S(1)}, f32[1,512,1280]{2,1,0:T(8,128)}, u32[]{:S(2)}) copy-start(f32[1,512,1280]{2,1,0:T(8,128)} %param.18) | copy-start | bytes 7864324
  555.9 29.1 %copy-start.42 = (f32[512]{0:T(512)S(1)}, f32[512]{0:T(512)}, u32[]{:S(2)}) copy-start(f32[512]{0:T(512)} %copy-done.41) | copy-start | bytes 6148
  592.8 147.1 %all-gather.18.cloned.1.call-start = ((), (), s32[]{:S(2)}) async-start(), calls=%async_computation.4 | async-start | bytes 1638400 | tf_op jit(solution)/shard_map/all_gather | solution.py:853
  719.9 5.3 copy-start.15
  719.9 5.3 copy-start.17
  (29 other events, 79.3 us)
Sparse Core Ops, SparseCore 0:
  11.2 49.0 all-gather.15
  62.5 46.3 all-gather.19
  111.0 46.3 all-gather.21
  159.4 37.1 all-gather.13
  198.6 46.3 all-gather.23
  246.9 46.3 all-gather.25
  592.9 45.4 reduce-scatter.1
  708.9 31.0 all-gather.17

commit v5 on v4

--- a/solution.py
+++ b/solution.py
@@ -263,13 +263,11 @@
     return [pl.BlockSpec(memory_space=pltpu.VMEM)] * count
 
 
-CHUNKS = 10
-
-
 class GradientSum:
-    LAGS = (1, 5, 9, 12)
+    LAGS = (0, 3, 6, 9)
 
     def __init__(self, arrays, outs, landings, sems):
+        self.chunks = landings[0].shape[1]
         self.arrays, self.outs, self.landings = arrays, outs, landings
         self.sends, self.recvs = sems
         self.half = lax.axis_index("fsdp")
@@ -279,17 +277,17 @@
         across = {"ctx": jnp.bitwise_xor(self.ctx, 2)}
         other = {"fsdp": 1 - self.half}
         self.peers = (pair, across, other)
-        self.ticks = 2 * (CHUNKS - 1) + self.LAGS[3] + 1
+        self.ticks = 2 * (self.chunks - 1) + self.LAGS[3] + 1
 
     def view(self, which, half, core, chunk):
         rows, cols = self.arrays[which].shape
         if which == 0:
             part = rows // 4
-            height = part // CHUNKS
+            height = part // self.chunks
             start = half * (2 * part) + core * part + chunk * height
             return pl.ds(pl.multiple_of(start, 16), height), slice(None)
         part = rows // 2
-        height = part // CHUNKS
+        height = part // self.chunks
         start = core * part + chunk * height
         width = cols // 2
         return (
@@ -299,7 +297,7 @@
 
     def out_rows(self, which, core, chunk):
         part = self.outs[which].shape[0] // 2
-        height = part // CHUNKS
+        height = part // self.chunks
         return pl.ds(pl.multiple_of(core * part + chunk * height, 8), height)
 
     def copy(self, which, stage, chunk, half=0):
@@ -333,14 +331,14 @@
                     self.copy(which, 0, chunk, half).start()
             return carry
 
-        lax.fori_loop(0, CHUNKS, body, 0)
+        lax.fori_loop(0, self.chunks, body, 0)
 
     def when_due(self, tick, lag, action):
         since = tick - lag
         clipped = jnp.maximum(since, 0)
         chunk = lax.div(clipped, 2)
 
-        @pl.when((since >= 0) & (lax.rem(clipped, 2) == 0) & (chunk < CHUNKS))
+        @pl.when((since >= 0) & (lax.rem(clipped, 2) == 0) & (chunk < self.chunks))
         def _():
             for which in range(2):
                 action(which, chunk)
@@ -390,21 +388,22 @@
                     self.copy(which, stage, chunk).wait_send()
             return carry
 
-        lax.fori_loop(0, CHUNKS, body, 0)
+        lax.fori_loop(0, self.chunks, body, 0)
 
 
 def gradient_shapes(by_rows, by_cols):
     rows, cols = by_rows.shape
     rows_two, cols_two = by_cols.shape
+    chunks = 10 if rows_two >= rows else 5
     outs = (
         jax.ShapeDtypeStruct((rows // 2, cols), WIDE),
         jax.ShapeDtypeStruct((rows_two, cols_two // 2), WIDE),
     )
     landings = [
-        pltpu.VMEM((5, CHUNKS, rows // 4 // CHUNKS, cols), LOW),
-        pltpu.VMEM((5, CHUNKS, rows_two // 2 // CHUNKS, cols_two // 2), LOW),
+        pltpu.VMEM((5, chunks, rows // 4 // chunks, cols), LOW),
+        pltpu.VMEM((5, chunks, rows_two // 2 // chunks, cols_two // 2), LOW),
     ]
-    return outs, landings
+    return outs, landings, pltpu.SemaphoreType.DMA((2, 5, chunks))
 
 
 def backward_gradient_kernel(
@@ -462,6 +461,110 @@
         compiler_params=pltpu.CompilerParams(collective_id=collective_id, has_side_effects=True),
         name="sum_all",
     )(values)
+
+
+FETCH_PARTS = 2
+
+
+def fetch_kernel(by_column, *refs):
+    count = len(by_column)
+    shards, small, outs, out_small = refs[:count], refs[count], refs[count + 1 : -5], refs[-5]
+    sends, recvs, small_send, small_recv = refs[-4:]
+    half = lax.axis_index("fsdp")
+    ctx = lax.axis_index("ctx")
+    pair, across = jnp.bitwise_xor(ctx, 1), jnp.bitwise_xor(ctx, 2)
+    peers = ({"fsdp": 1 - half}, {"ctx": across}, {"ctx": pair}, {"ctx": pair})
+
+    barrier = pltpu.get_barrier_semaphore()
+    for peer in peers[:3]:
+        pl.semaphore_signal(barrier, inc=1, device_id=peer, device_id_type=MESH)
+    pl.semaphore_wait(barrier, 3)
+
+    def rows_of(which, quarter, part, base=0):
+        height = shards[which].shape[0] // 4 // FETCH_PARTS
+        return pl.ds(pl.multiple_of(base + (quarter * FETCH_PARTS + part) * height, 16), height)
+
+    def place(which, side, quarter, part):
+        rows, cols = shards[which].shape
+        if by_column[which]:
+            return outs[which].at[rows_of(which, quarter, part), pl.ds(pl.multiple_of(side * cols, 128), cols)]
+        return outs[which].at[rows_of(which, quarter, part, side * rows)]
+
+    def copy(which, stage, part, arriving=False):
+        quarter = (ctx, ctx, ctx, across)[stage]
+        src = shards[which].at[rows_of(which, quarter, part)]
+        dst = place(which, half, quarter, part)
+        if stage > 0:
+            src = dst = place(which, 1 - half, quarter, part)
+        if arriving:
+            quarter = (ctx, across, pair, jnp.bitwise_xor(ctx, 3))[stage]
+            dst = place(which, 1 - half, quarter, part)
+        return pltpu.make_async_remote_copy(
+            src_ref=src,
+            dst_ref=dst,
+            send_sem=sends.at[which, stage, part],
+            recv_sem=recvs.at[which, stage, part],
+            device_id=peers[stage],
+            device_id_type=MESH,
+        )
+
+    def small_copy(side):
+        cols = small.shape[1]
+        return pltpu.make_async_remote_copy(
+            src_ref=small,
+            dst_ref=out_small.at[:, pl.ds(pl.multiple_of(side * cols, 128), cols)],
+            send_sem=small_send,
+            recv_sem=small_recv,
+            device_id=peers[0],
+            device_id_type=MESH,
+        )
+
+    each = [(which, part) for which in range(count) for part in range(FETCH_PARTS)]
+    for which, part in each:
+        copy(which, 0, part).start()
+    small_copy(half).start()
+    for shard, out, column in zip((*shards, small), (*outs, out_small), (*by_column, True)):
+        rows, cols = shard.shape
+        if column:
+            out[:, pl.ds(pl.multiple_of(half * cols, 128), cols)] = shard[...]
+        else:
+            out[pl.ds(pl.multiple_of(half * rows, 16), rows), :] = shard[...]
+    for at in range(len(each) + 1):
+        if at < len(each):
+            copy(each[at][0], 0, each[at][1], True).wait_recv()
+            copy(each[at][0], 1, each[at][1]).start()
+            copy(each[at][0], 2, each[at][1]).start()
+        if at > 0:
+            copy(each[at - 1][0], 1, each[at - 1][1], True).wait_recv()
+            copy(each[at - 1][0], 3, each[at - 1][1]).start()
+    small_copy(1 - half).wait_recv()
+    for stage in (2, 3):
+        for which, part in each:
+            copy(which, stage, part, True).wait_recv()
+    for stage in range(4):
+        for which, part in each:
+            copy(which, stage, part).wait_send()
+    small_copy(half).wait_send()
+
+
+def fetch_first(shards, by_column, small, collective_id):
+    def whole(shape, column):
+        return (shape[0], 2 * shape[1]) if column else (2 * shape[0], shape[1])
+
+    shapes = [whole(shard.shape, column) for shard, column in zip(shards, by_column)]
+    shapes.append(whole(small.shape, True))
+    sems = pltpu.SemaphoreType.DMA((len(shards), 4, FETCH_PARTS))
+    return pl.pallas_call(
+        functools.partial(fetch_kernel, by_column),
+        out_shape=tuple(jax.ShapeDtypeStruct(shape, LOW) for shape in shapes),
+        in_specs=in_vmem(len(shapes)),
+        out_specs=tuple(in_vmem(len(shapes))),
+        scratch_shapes=[sems, sems, pltpu.SemaphoreType.DMA, pltpu.SemaphoreType.DMA],
+        compiler_params=pltpu.CompilerParams(
+            collective_id=collective_id, has_side_effects=True, vmem_limit_bytes=40 << 20
+        ),
+        name="fetch_first",
+    )(*shards, small)
 
 
 def forward_exchange(partial, residual, bias, gain, shift, n, collective_id):
@@ -492,9 +595,9 @@
     scratch = exchange_scratch(n, rows, width, PIECES)
     kernel, extra = backward_exchange_kernel, ()
     if by_rows is not None:
-        outs, landings = gradient_shapes(by_rows, by_cols)
+        outs, landings, sems = gradient_shapes(by_rows, by_cols)
         out_shape = out_shape + outs
-        scratch = scratch + landings + [pltpu.SemaphoreType.DMA((2, 5, CHUNKS))] * 2
+        scratch = scratch + landings + [sems] * 2
         kernel, extra = backward_gradient_kernel, (by_rows, by_cols)
     return pl.pallas_call(
         functools.partial(kernel, n, PIECES),
@@ -509,6 +612,25 @@
     )(partial, grad_out, normal_in, gain[None, :], *extra)
 
 
+GROUPS = 2
+PARTS = 2 * GROUPS
+
+
+def part_rows(columns, part, base=0):
+    size = columns // GROUPS
+    return pl.ds(base + (part % 2) * columns + (part // 2) * size, size)
+
+
+def group_parts(group):
+    return (2 * group, 2 * group + 1)
+
+
+def group_heads(heads, group):
+    assert heads % GROUPS == 0
+    size = heads // GROUPS
+    return range(heads) if group is None else range(group * size, (group + 1) * size)
+
+
 def attend_kernel(scale, length, qkv, out, out_wide, log_total, held, high, low_sum, sems_send, sems_recv):
     columns = qkv.shape[0] // 3
     frames = qkv.shape[1]
@@ -524,8 +646,8 @@
     pl.semaphore_wait(barrier, 2)
 
     def send(slot, part, to):
-        rows = pl.ds(part * columns, columns)
-        src = qkv.at[pl.ds((1 + part) * columns, columns)] if slot != 3 else held.at[1, rows]
+        rows, own_rows = part_rows(columns, part), part_rows(columns, part, columns)
+        src = qkv.at[own_rows] if slot != 3 else held.at[1, rows]
         return pltpu.make_async_remote_copy(
             src_ref=src,
             dst_ref=held.at[slot - 1, rows],
@@ -535,9 +657,9 @@
             device_id_type=MESH,
         )
 
-    for part in range(2):
+    for part in range(PARTS):
         send(2, part, 2).start()
-    for part in range(2):
+    for part in range(PARTS):
         send(1, part, 1).start()
 
     high[...] = jnp.full_like(high, NEGATIVE)
@@ -545,11 +667,11 @@
     out_wide[...] = jnp.zeros_like(out_wide)
     limit = length[0]
 
-    def block(keys_ref, key_row, value_row, slot):
+    def block(keys_ref, key_row, value_row, slot, group=None):
         owner = jnp.bitwise_xor(me, slot)
         left = limit - owner * frames
         valid = lax.broadcasted_iota(jnp.int32, (frames, frames), 0) < left
-        for h in range(heads):
+        for h in group_heads(heads, group):
             rows = pl.ds(h * HD, HD)
             keys = keys_ref[pl.ds(key_row + h * HD, HD), :]
             values = keys_ref[pl.ds(value_row + h * HD, HD), :]
@@ -570,16 +692,18 @@
             )
 
     block(qkv, columns, 2 * columns, 0)
-    for part in range(2):
+    for part in range(PARTS):
         send(1, part, 1).wait_recv()
     block(held.at[0], 0, columns, 1)
-    for part in range(2):
-        send(2, part, 2).wait_recv()
-        send(3, part, 1).start()
-    block(held.at[1], 0, columns, 2)
-    for part in range(2):
-        send(3, part, 1).wait_recv()
-    block(held.at[2], 0, columns, 3)
+    for group in range(GROUPS):
+        for part in group_parts(group):
+            send(2, part, 2).wait_recv()
+            send(3, part, 1).start()
+        block(held.at[1], 0, columns, 2, group)
+    for group in range(GROUPS):
+        for part in group_parts(group):
+            send(3, part, 1).wait_recv()
+        block(held.at[2], 0, columns, 3, group)
     for h in range(heads):
         rows = pl.ds(h * HD, HD)
         total = low_sum[h : h + 1, :]
@@ -588,7 +712,7 @@
         out[rows, :] = done.astype(LOW)
         log_total[h : h + 1, :] = high[h : h + 1, :] + jnp.log(total)
     for slot in (1, 2, 3):
-        for part in range(2):
+        for part in range(PARTS):
             send(slot, part, 2 if slot == 2 else 1).wait_send()
 
 
@@ -607,8 +731,8 @@
         scratch_shapes=[
             pltpu.VMEM((8, frames), WIDE),
             pltpu.VMEM((8, frames), WIDE),
-            pltpu.SemaphoreType.DMA((3, 2)),
-            pltpu.SemaphoreType.DMA((3, 2)),
+            pltpu.SemaphoreType.DMA((3, PARTS)),
+            pltpu.SemaphoreType.DMA((3, PARTS)),
         ],
         compiler_params=pltpu.CompilerParams(
             collective_id=collective_id, has_side_effects=True, vmem_limit_bytes=56 << 20
@@ -617,9 +741,83 @@
     )(length, qkv)
 
 
-def attend_back_kernel(
-    scale, length, qkv, held, grad, out_wide, log_total, grad_qkv, mine, parts, landed, acc, sems_send, sems_recv
-):
+class LineGather:
+    def __init__(self, own, gathered, sends, recvs):
+        self.own, self.gathered, self.sends, self.recvs = own, gathered, sends, recvs
+        self.n = gathered.shape[0] // own.shape[0]
+        self.me = lax.axis_index("tp")
+        self.further = (self.me < self.n - 1, self.me > 0)
+        self.peers = ({"tp": lax.rem(self.me + 1, self.n)}, {"tp": lax.rem(self.me + self.n - 1, self.n)})
+
+    def greet(self, barrier):
+        for way in range(2):
+
+            @pl.when(self.further[way])
+            def _():
+                pl.semaphore_signal(barrier, inc=1, device_id=self.peers[way], device_id_type=MESH)
+
+        return self.further[0].astype(jnp.int32) + self.further[1].astype(jnp.int32)
+
+    def rows(self, shard):
+        size = self.own.shape[0]
+        return pl.ds(pl.multiple_of(shard * size, size), size)
+
+    def there(self, way, hops):
+        return self.me - hops >= 0 if way == 0 else self.me + hops <= self.n - 1
+
+    def send(self, way, hops):
+        shard = self.me - hops if way == 0 else self.me + hops
+        rows = self.rows(shard)
+        return pltpu.make_async_remote_copy(
+            src_ref=self.own if hops == 0 else self.gathered.at[rows],
+            dst_ref=self.gathered.at[rows],
+            send_sem=self.sends.at[way, hops],
+            recv_sem=self.recvs.at[way, hops],
+            device_id=self.peers[way],
+            device_id_type=MESH,
+        )
+
+    def arrival(self, way, hops):
+        rows = self.rows(self.me - hops if way == 0 else self.me + hops)
+        return pltpu.make_async_remote_copy(
+            src_ref=self.gathered.at[rows],
+            dst_ref=self.gathered.at[rows],
+            send_sem=self.sends.at[way, hops],
+            recv_sem=self.recvs.at[way, hops - 1],
+            device_id=self.peers[way],
+            device_id_type=MESH,
+        )
+
+    def hop(self, hops):
+        for way in range(2):
+            if hops > 0:
+
+                @pl.when(self.there(way, hops))
+                def _():
+                    self.arrival(way, hops).wait_recv()
+
+            if hops < self.n - 1:
+
+                @pl.when(self.there(way, hops) & self.further[way])
+                def _():
+                    self.send(way, hops).start()
+
+    def drain(self):
+        for hops in range(self.n - 1):
+            for way in range(2):
+
+                @pl.when(self.there(way, hops) & self.further[way])
+                def _():
+                    self.send(way, hops).wait_send()
+
+
+def attend_back_kernel(scale, sharing, length, qkv, held, grad, out_wide, log_total, *refs):
+    if sharing:
+        own, grad_qkv, gathered, mine, parts, landed, acc, sems_send, sems_recv, sends, recvs = refs
+        share = LineGather(own, gathered, sends, recvs)
+    else:
+        grad_qkv, mine, parts, landed, acc, sems_send, sems_recv = refs
+        share = None
     columns = qkv.shape[0] // 3
     frames = qkv.shape[1]
     heads = columns // HD
@@ -631,10 +829,16 @@
     barrier = pltpu.get_barrier_semaphore()
     for r in (1, 2):
         pl.semaphore_signal(barrier, inc=1, device_id=partner(r), device_id_type=MESH)
-    pl.semaphore_wait(barrier, 2)
+    waiting = 2
+    if share is not None:
+        waiting = waiting + share.greet(barrier)
+    pl.semaphore_wait(barrier, waiting)
+    if share is not None:
+        share.hop(0)
+        gathered[share.rows(share.me), :] = own[...]
 
     def send(at, part, to):
-        rows = pl.ds(part * columns, columns)
+        rows = part_rows(columns, part)
         return pltpu.make_async_remote_copy(
             src_ref=parts.at[at, rows],
             dst_ref=landed.at[at, rows],
@@ -647,11 +851,11 @@
     acc[...] = jnp.zeros_like(acc)
     limit = length[0]
 
-    def block(keys_ref, key_row, value_row, slot, store):
+    def block(keys_ref, key_row, value_row, slot, store, group=None):
         owner = jnp.bitwise_xor(me, slot)
         left = limit - owner * frames
         valid = lax.broadcasted_iota(jnp.int32, (frames, frames), 0) < left
-        for h in range(heads):
+        for h in group_heads(heads, group):
             rows = pl.ds(h * HD, HD)
             keys = keys_ref[pl.ds(key_row + h * HD, HD), :]
             values = keys_ref[pl.ds(value_row + h * HD, HD), :]
@@ -696,51 +900,70 @@
             rows = pl.ds(start, HD)
             parts[1, rows, :] = (value + landed[0, rows, :].astype(WIDE)).astype(LOW)
 
-    block(held.at[2], 0, columns, 3, store_part(0))
-    for part in range(2):
-        send(0, part, 1).start()
-    for part in range(2):
-        send(0, part, 1).wait_recv()
-    block(held.at[1], 0, columns, 2, store_joined)
-    for part in range(2):
-        send(1, part, 2).start()
-    block(held.at[0], 0, columns, 1, store_part(2))
-    for part in range(2):
-        send(2, part, 1).start()
+    for group in range(GROUPS):
+        block(held.at[2], 0, columns, 3, store_part(0), group)
+        for part in group_parts(group):
+            send(0, part, 1).start()
+    for group in range(GROUPS):
+        for part in group_parts(group):
+            send(0, part, 1).wait_recv()
+        block(held.at[1], 0, columns, 2, store_joined, group)
+        for part in group_parts(group):
+            send(1, part, 2).start()
+        if share is not None and group == 0:
+            share.hop(1)
+    for group in range(GROUPS):
+        block(held.at[0], 0, columns, 1, store_part(2), group)
+        for part in group_parts(group):
+            send(2, part, 1).start()
+        if share is not None and group == 0:
+            share.hop(2)
     block(qkv, columns, 2 * columns, 0, store_mine)
     grad_qkv[0:columns, :] = (acc[...] * scale).astype(LOW)
-    for part in range(2):
+    for part in range(PARTS):
         send(2, part, 1).wait_recv()
-    for part in range(2):
+    for part in range(PARTS):
         send(1, part, 2).wait_recv()
     grad_qkv[columns:, :] = (
         mine[...] + landed[1].astype(WIDE) + landed[2].astype(WIDE)
     ).astype(LOW)
     for at in range(3):
-        for part in range(2):
+        for part in range(PARTS):
             send(at, part, 2 if at == 1 else 1).wait_send()
-
-
-def attend_back(qkv, held, grad, out_wide, log_total, length, scale, collective_id):
+    if share is not None:
+        for hops in range(3, share.n):
+            share.hop(hops)
+        share.drain()
+
+
+def attend_back(qkv, held, grad, out_wide, log_total, length, scale, collective_id, own=None):
     columns, frames = qkv.shape[0] // 3, qkv.shape[1]
+    out_shape = (jax.ShapeDtypeStruct((3 * columns, frames), LOW),)
+    extra, sems = (), []
+    if own is not None:
+        n = lax.axis_size("tp")
+        assert n >= 3
+        out_shape += (jax.ShapeDtypeStruct((n * own.shape[0], own.shape[1]), LOW),)
+        extra, sems = (own,), [pltpu.SemaphoreType.DMA((2, n))] * 2
     return pl.pallas_call(
-        functools.partial(attend_back_kernel, scale),
-        out_shape=jax.ShapeDtypeStruct((3 * columns, frames), LOW),
-        in_specs=[pl.BlockSpec(memory_space=pltpu.SMEM)] + in_vmem(5),
-        out_specs=in_vmem(1)[0],
+        functools.partial(attend_back_kernel, scale, own is not None),
+        out_shape=out_shape,
+        in_specs=[pl.BlockSpec(memory_space=pltpu.SMEM)] + in_vmem(5 + len(extra)),
+        out_specs=tuple(in_vmem(len(out_shape))),
         scratch_shapes=[
             pltpu.VMEM((2 * columns, frames), WIDE),
             pltpu.VMEM((3, 2 * columns, frames), LOW),
             pltpu.VMEM((3, 2 * columns, frames), LOW),
             pltpu.VMEM((columns, frames), WIDE),
-            pltpu.SemaphoreType.DMA((3, 2)),
-            pltpu.SemaphoreType.DMA((3, 2)),
+            pltpu.SemaphoreType.DMA((3, PARTS)),
+            pltpu.SemaphoreType.DMA((3, PARTS)),
+            *sems,
         ],
         compiler_params=pltpu.CompilerParams(
             collective_id=collective_id, has_side_effects=True, vmem_limit_bytes=56 << 20
         ),
         name="attend_back",
-    )(length, qkv, held, grad, out_wide, log_total)
+    )(length, qkv, held, grad, out_wide, log_total, *extra)
 
 
 def gelu_value(values):
@@ -798,18 +1021,38 @@
     small = jnp.concatenate(
         [output_bias, outer_bias, first_gain, first_shift, second_gain, second_shift], axis=0
     ).astype(LOW)
-    small = lax.all_gather(small, "fsdp", axis=1, tiled=True).astype(WIDE)
+    small = jnp.pad(small, ((0, -small.shape[0] % 16), (0, 0)))
+
+    def qkv_shard(layer):
+        return jnp.concatenate(
+            [query_weight[layer], key_weight[layer], value_weight[layer]], axis=1
+        ).astype(LOW)
+
+    projections = output_weight.astype(LOW).reshape(-1, output_weight.shape[2])
+    if lax.axis_size("fsdp") == 2:
+        qkv_first, projections, inner_first, small = fetch_first(
+            (qkv_shard(0), projections, inner_weight[0].astype(LOW)), (False, True, False), small, 17
+        )
+        small, outer_weight, inner_weight, query_weight, key_weight, value_weight = lax.optimization_barrier(
+            (small, outer_weight, inner_weight, query_weight, key_weight, value_weight)
+        )
+    else:
+        qkv_first = lax.all_gather(qkv_shard(0), "fsdp", axis=0, tiled=True)
+        inner_first = lax.all_gather(inner_weight[0].astype(LOW), "fsdp", axis=0, tiled=True)
+        projections = lax.all_gather(projections, "fsdp", axis=1, tiled=True)
+        small = lax.all_gather(small, "fsdp", axis=1, tiled=True)
+    small = small.astype(WIDE)
+    projections = projections.reshape(LAYERS, columns, width)
 
     def vector(kind, layer):
         return small[kind * LAYERS + layer]
 
     def fetch(layer):
-        qkv = jnp.concatenate(
-            [query_weight[layer], key_weight[layer], value_weight[layer]], axis=1
-        ).astype(LOW)
-        qkv = lax.all_gather(qkv, "fsdp", axis=0, tiled=True)
-        out = lax.all_gather(output_weight[layer].astype(LOW), "fsdp", axis=1, tiled=True)
-        inner = lax.all_gather(inner_weight[layer].astype(LOW), "fsdp", axis=0, tiled=True)
+        qkv, inner = qkv_first, inner_first
+        if layer > 0:
+            qkv = lax.all_gather(qkv_shard(layer), "fsdp", axis=0, tiled=True)
+            inner = lax.all_gather(inner_weight[layer].astype(LOW), "fsdp", axis=0, tiled=True)
+        out = projections[layer]
         outer = lax.all_gather(outer_weight[layer].astype(LOW), "fsdp", axis=1, tiled=True)
         return (qkv, out, inner, outer)
 
@@ -848,9 +1091,7 @@
                 2 * layer + 5,
             )
         else:
-            branch = lax.psum_scatter(branch, "tp", scatter_dimension=0, tiled=True).astype(WIDE)
-            residual = middle + branch + vector(1, layer)
-            output = lax.all_gather(residual.astype(LOW), "tp", axis=0, tiled=True).astype(WIDE)
+            last_branch, last_middle = branch, middle
 
     def exchange_back(branch, grad_out, normal_in, gain, collective_id, by_rows, by_cols):
         if lax.axis_size("fsdp") == 2:
@@ -894,13 +1135,29 @@
         grad_mid_low, grad_middle, sums_two, *summed_two = exchange_back(
             branch, grad_own, middle, vector(4, layer), 2 * layer + 8, grad_inner_w, grad_outer_w
         )
+        if layer == LAYERS - 1:
+            last_branch, grad_mid_low = lax.optimization_barrier((last_branch, grad_mid_low))
+            last_branch = lax.psum_scatter(last_branch, "tp", scatter_dimension=0, tiled=True)
         grad_attended = product(w_out, grad_mid_low, 1, 1).astype(LOW)
-        grad_qkv = attend_back(
-            qkv, held, grad_attended, attended_wide, log_total, lengths, scale, 2 * layer + 12
+        grad_qkv, *shared = attend_back(
+            qkv,
+            held,
+            grad_attended,
+            attended_wide,
+            log_total,
+            lengths,
+            scale,
+            2 * layer + 12,
+            last_rows if layer == 0 else None,
         )
         grad_output_w = product(attended, grad_mid_low, 1, 0).astype(LOW)
         branch = product(grad_qkv, w_qkv, 0, 1).astype(LOW)
         grad_qkv_w = product(normed, grad_qkv, 0, 1).astype(LOW)
+        if layer == LAYERS - 1:
+            last_branch, branch = lax.optimization_barrier((last_branch, branch))
+            last_rows = (last_middle + last_branch.astype(WIDE) + vector(1, layer)).astype(LOW)
+        if layer == 0:
+            output = shared[0].astype(WIDE)
         grad_low, grad_own, sums_one, *summed_one = exchange_back(
             branch, grad_middle, residual, vector(2, layer), 2 * layer + 9, grad_qkv_w, grad_output_w
         )

time: 755 us -> 695 us (0.921)
  blocking collectives: 38.3 us -> 0 us
  waiting for transfers between devices: 18.3 us -> 0.62 us
  local copies, waits for them, and re-layouts: 36.4 us -> 46.7 us
    all_gather x3 -> x0, blocking collectives: 38.3 us -> none  [the longest x2 32.2 us: fetch(): lax.all_gather(output_weight[layer].astype(LOW), 'fsdp', axis=1, tiled=True)]
    pallas_call x4, Pallas kernels: 253 us -> 219 us  [backward_exchange(): pl.pallas_call(functools.partial(kernel, n, PIECES), out_shape=out_shape,...]
    pallas_call x2 -> x3, Pallas kernels: 58.1 us -> 90.3 us  [the longest x2 57.2 us: attend_back(): pl.pallas_call(functools.partial(attend_back_kernel, scale, own is not No...]
    all_gather x3 -> x1, waiting for transfers between devices: 9.85 us -> 0.01 us  [fetch(): qkv = lax.all_gather(qkv_shard(layer), 'fsdp', axis=0, tiled=True)]
  transfers between devices with their start and end apart: 8 -> 5, of which waited for: 3 -> 0; matrix products, arithmetic and copies ran while one was open for 12% -> 9% of each run, Pallas kernels for 37% -> 30%
where the time goes in v5:
time: 695 us; the launch traced here: 691 us
  Pallas kernels  510 us (73%)
  matrix products  82.8 us (12%)
  local copies, waits for them, and re-layouts  46.7 us (7%)
  other arithmetic  34.6 us (5%)
  between operations  15.5 us (2%)
    pallas_call x4, Pallas kernels, backward_exchange(): pl.pallas_call(functools.partial(kernel, n, PIECES), out_shape=out_shape,...  219 us
    pallas_call x3, Pallas kernels, forward_exchange(): pl.pallas_call(functools.partial(forward_exchange_kernel, n, PIECES), out...  134 us
    dot_general x24, matrix products, product(): lax.dot_general(left_side, right_side, (((left_axis,), (right_axis,)), ((...  82.8 us
    pallas_call x2, Pallas kernels, attend_back(): pl.pallas_call(functools.partial(attend_back_kernel, scale, own is not No...  57.2 us
    pallas_call x2, Pallas kernels, attend(): pl.pallas_call(functools.partial(attend_kernel, scale), out_shape=(jax.Sh...  46.1 us
    pallas_call x1, Pallas kernels, fetch_first(): pl.pallas_call(functools.partial(fetch_kernel, by_column), out_shape=tupl...  33.1 us
    pallas_call x1, Pallas kernels, sum_all(): pl.pallas_call(functools.partial(sum_all_kernel, axes, shared_rows), out_...  21.5 us
    another operation x6, other arithmetic, stacked(): jnp.stack([grads[layer][which][:, start:start + size] for layer in range(...  14.4 us
  transfers between devices with their start and end apart: 5, of which 0 were waited for; matrix products, arithmetic and copies ran while one was open for 9% of the time, Pallas kernels for 30%

profile of v5, /device:TPU:0, one launch (start us, length us, event | category | flops | bytes accessed | tf_op | source)
XLA Modules:
  0.0 691.0 jit_solution(7597105181411787145)
XLA Ops:
  16.4 33.1 %fetch_first.1 = (bf16[1280,960]{1,0:T(8,128)(2,1)S(1)}, bf16[640,1280]{1,0:T(8,128)(2,1)S(1)}, bf16[1280,1280]{1,0:T(8,128)(2,1)S(1)}, bf16[16,1280]{1,0:T(8,128)(2,1)S(1)}) custom-call(bf16[640,960]{1,0:T(8,128)(2,1)S(1)} %pad_maximum_fusion.6.refs_0_, bf16[640,640]{1,0:T(8,128)(2,1)S(1)} %bitcast.142, bf16[640,1280]{1,0:T(8,128)(2,1)S(1)} %fusion.37.refs_2_, ...), custom_call_target="tpu_custom_call" | custom-call | tf_op jit(solution)/shard_map/fetch_first/pallas_call | solution.py:557
  49.5 5.9 convert.73
  61.4 3.4 slice.317
  70.4 4.7 add_convert_fusion.2.qkv
  76.9 23.8 %attend.2 = (bf16[320,512]{1,0:T(8,128)(2,1)}, f32[320,512]{1,0:T(8,128)}, f32[8,512]{1,0:T(8,128)}, bf16[3,640,512]{2,1,0:T(8,128)(2,1)}) custom-call(s32[1]{0:T(128)S(6)} %copy.54.length, bf16[960,512]{1,0:T(8,128)(2,1)} %add_convert_fusion.2.qkv), custom_call_target="tpu_custom_call" | custom-call | tf_op jit(solution)/shard_map/attend/pallas_call | solution.py:721
  103.3 45.4 %forward_exchange.3 = (bf16[512,1280]{1,0:T(8,128)(2,1)S(1)}, f32[128,1280]{1,0:T(8,128)S(1)}) custom-call(bf16[512,1280]{1,0:T(8,128)(2,1)S(1)} %convolution_convert_fusion.10.partial, f32[128,1280]{1,0:T(8,128)S(1)} %dynamic-slice_bitcast_fusion.residual.normal_in, f32[1,1280]{1,0:T(1,128)S(1)} %get-tuple-element.194.bias, ...), custom_call_target="tpu_custom_call" | custom-call | tf_op jit(solution)/shard_map/forward_exchange/pallas_call | solution.py:572
  151.3 3.5 multiply_convert_fusion.1
  154.8 4.6 fusion.16.partial
  159.4 44.0 %forward_exchange.4 = (bf16[512,1280]{1,0:T(8,128)(2,1)S(1)}, f32[128,1280]{1,0:T(8,128)S(1)}) custom-call(bf16[512,1280]{1,0:T(8,128)(2,1)S(1)} %fusion.16.partial, f32[128,1280]{1,0:T(8,128)S(1)} %get-tuple-element.78.residual.normal_in, f32[1,1280]{1,0:T(1,128)S(1)} %get-tuple-element.191.bias, f32[1,1280]{1,0:T(1,128)S(1)} %get-tuple-element.190.gain, ...), custom_call_target="tpu_custom_call" | custom-call | tf_op jit(solution)/shard_map/forward_exchange/pallas_call | solution.py:572
  204.5 4.8 add_convert_fusion.1.qkv
  209.3 22.4 %attend.3 = (bf16[320,512]{1,0:T(8,128)(2,1)}, f32[320,512]{1,0:T(8,128)}, f32[8,512]{1,0:T(8,128)}, bf16[3,640,512]{2,1,0:T(8,128)(2,1)}) custom-call(s32[1]{0:T(128)S(6)} %copy.54.length, bf16[960,512]{1,0:T(8,128)(2,1)} %add_convert_fusion.1.qkv), custom_call_target="tpu_custom_call" | custom-call | tf_op jit(solution)/shard_map/attend/pallas_call | solution.py:721
  233.6 44.5 %forward_exchange.5 = (bf16[512,1280]{1,0:T(8,128)(2,1)S(1)}, f32[128,1280]{1,0:T(8,128)S(1)}) custom-call(bf16[512,1280]{1,0:T(8,128)(2,1)S(1)} %convolution_convert_fusion.9.partial, f32[128,1280]{1,0:T(8,128)S(1)} %get-tuple-element.81.residual.normal_in, f32[1,1280]{1,0:T(1,128)S(1)} %get-tuple-element.188.bias, f32[1,1280]{1,0:T(1,128)S(1)} %get-tuple-element.187.gain, ...), custom_call_target="tpu_custom_call" | custom-call | tf_op jit(solution)/shard_map/forward_exchange/pallas_call | solution.py:572
  280.0 5.8 multiply_convert_fusion
  285.8 6.4 convert_reduce_fusion
  292.2 3.6 convolution_convert_fusion.3.by_rows
  295.8 3.6 convolution_convert_fusion.2.by_cols
  302.3 59.7 %backward_exchange.4 = (bf16[512,1280]{1,0:T(8,128)(2,1)}, f32[128,1280]{1,0:T(8,128)}, f32[8,1280]{1,0:T(8,128)}, f32[640,1280]{1,0:T(8,128)}, f32[1280,640]{1,0:T(8,128)}) custom-call(bf16[512,1280]{1,0:T(8,128)(2,1)} %fusion.19.partial, f32[128,1280]{1,0:T(8,128)} %get-tuple-element.161.grad_out, f32[128,1280]{1,0:T(8,128)} %copy-done.1, ...), custom_call_target="tpu_custom_call" | custom-call | tf_op jit(solution)/shard_map/backward_exchange/pallas_call | solution.py:602
  366.4 26.0 %attend_back.2 = bf16[960,512]{1,0:T(8,128)(2,1)} custom-call(s32[1]{0:T(128)S(6)} %copy.54.length, bf16[960,512]{1,0:T(8,128)(2,1)} %add_convert_fusion.1.qkv, bf16[3,640,512]{2,1,0:T(8,128)(2,1)} %get-tuple-element.87.held, bf16[320,512]{1,0:T(8,128)(2,1)} %convolution_convert_fusion.14.grad, f32[320,512]{1,0:T(8,128)} %get-tuple-element.89.out_wide, ...), custom_call_target="tpu_custom_call" | custom-call | tf_op jit(solution)/shard_map/attend_back/pallas_call | solution.py:948
  392.4 4.1 convolution_convert_fusion.5
  396.5 4.5 copy.46.by_rows
  407.7 50.1 %backward_exchange.5 = (bf16[512,1280]{1,0:T(8,128)(2,1)}, f32[128,1280]{1,0:T(8,128)}, f32[8,1280]{1,0:T(8,128)}, f32[640,960]{1,0:T(8,128)}, f32[320,640]{1,0:T(8,128)}) custom-call(bf16[512,1280]{1,0:T(8,128)(2,1)} %convolution_convert_fusion.8.partial, f32[128,1280]{1,0:T(8,128)} %get-tuple-element.92.grad_out, f32[128,1280]{1,0:T(8,128)} %copy-done.4, ...), custom_call_target="tpu_custom_call" | custom-call | tf_op jit(solution)/shard_map/backward_exchange/pallas_call | solution.py:602
  457.9 4.7 convert_reduce_fusion.1
  465.5 3.6 convolution_convert_fusion.1.by_rows
  469.2 3.6 convolution_convert_fusion.by_cols
  472.8 58.7 %backward_exchange.6 = (bf16[512,1280]{1,0:T(8,128)(2,1)}, f32[128,1280]{1,0:T(8,128)}, f32[8,1280]{1,0:T(8,128)}, f32[640,1280]{1,0:T(8,128)}, f32[1280,640]{1,0:T(8,128)}) custom-call(bf16[512,1280]{1,0:T(8,128)(2,1)} %convolution_convert_fusion.7.partial, f32[128,1280]{1,0:T(8,128)} %get-tuple-element.94.grad_out, f32[128,1280]{1,0:T(8,128)} %copy-done.3, ...), custom_call_target="tpu_custom_call" | custom-call | tf_op jit(solution)/shard_map/backward_exchange/pallas_call | solution.py:602
  535.1 31.2 %attend_back.3 = (bf16[960,512]{1,0:T(8,128)(2,1)}, bf16[512,1280]{1,0:T(8,128)(2,1)}) custom-call(s32[1]{0:T(128)S(6)} %copy.54.length, bf16[960,512]{1,0:T(8,128)(2,1)} %add_convert_fusion.2.qkv, bf16[3,640,512]{2,1,0:T(8,128)(2,1)} %get-tuple-element.69.held, bf16[320,512]{1,0:T(8,128)(2,1)} %convolution_convert_fusion.13.grad, ...), custom_call_target="tpu_custom_call" | custom-call | tf_op jit(solution)/shard_map/attend_back/pallas_call | solution.py:948
  566.4 4.0 convolution_convert_fusion.6.partial
  574.0 3.4 copy.47.by_rows
  579.3 50.0 %backward_exchange.7 = (bf16[512,1280]{1,0:T(8,128)(2,1)}, f32[128,1280]{1,0:T(8,128)}, f32[8,1280]{1,0:T(8,128)}, f32[640,960]{1,0:T(8,128)}, f32[320,640]{1,0:T(8,128)}) custom-call(bf16[512,1280]{1,0:T(8,128)(2,1)} %convolution_convert_fusion.6.partial, f32[128,1280]{1,0:T(8,128)} %get-tuple-element.101.grad_out, f32[128,1280]{1,0:T(8,128)} %copy-done, ...), custom_call_target="tpu_custom_call" | custom-call | tf_op jit(solution)/shard_map/backward_exchange/pallas_call | solution.py:602
  632.3 21.5 %sum_all.1 = f32[24,1280]{1,0:T(8,128)} custom-call(f32[24,1280]{1,0:T(8,128)} %concatenate.30.values), custom_call_target="tpu_custom_call" | custom-call | tf_op jit(solution)/shard_map/sum_all/pallas_call | solution.py:451
  675.1 5.3 pad_maximum_fusion
  680.4 3.2 pad_maximum_fusion.1
  (208 shorter events, 82.4 us)
Async XLA Ops:
  7.2 5.3 copy-start.30
  7.2 147.6 %all-gather.10.cloned.1.call-start = ((), (), s32[]{:S(2)}) async-start(), calls=%async_computation.3 | async-start | bytes 4915200 | tf_op jit(solution)/shard_map/all_gather | solution.py:1056
  49.5 5.9 copy-start.8
  49.5 5.9 copy-start.11
  49.5 5.9 copy-start.14
  57.4 147.1 %all-gather.8.cloned.1.call-start = ((), (), s32[]{:S(2)}) async-start(), calls=%async_computation.1 | async-start | bytes 3686400 | tf_op jit(solution)/shard_map/all_gather | solution.py:1053
  61.3 218.7 %all-gather.12.cloned.1.call-start = ((), (), s32[]{:S(2)}) async-start(), calls=%async_computation.4 | async-start | bytes 4915200 | tf_op jit(solution)/shard_map/all_gather | solution.py:1054
  64.7 221.0 %all-gather.14.cloned.1.call-start = ((), (), s32[]{:S(2)}) async-start(), calls=%async_computation.5 | async-start | bytes 4915200 | tf_op jit(solution)/shard_map/all_gather | solution.py:1056
  65.3 342.4 %reduce-scatter.2.cloned.1.call-start = ((), (), s32[]{:S(2)}) async-start(), calls=%async_computation.2 | async-start | bytes 1638400 | tf_op jit(solution)/shard_map/reduce_scatter | solution.py:1140
  65.7 4.7 copy-start.12
  70.4 30.3 %copy-start.15 = (bf16[640,1280]{1,0:T(8,128)(2,1)S(1)}, bf16[640,1280]{1,0:T(8,128)(2,1)}, u32[]{:S(2)}) copy-start(bf16[640,1280]{1,0:T(8,128)(2,1)} %copy-done.14) | copy-start | bytes 4915204
  76.2 72.5 %copy-start = (f32[128,1280]{1,0:T(8,128)}, f32[128,1280]{1,0:T(8,128)S(1)}, u32[]{:S(2)}) copy-start(f32[128,1280]{1,0:T(8,128)S(1)} %dynamic-slice_bitcast_fusion.residual.normal_in) | copy-start | bytes 1966084
  100.6 50.6 %copy-start.40 = (f32[2,1280]{1,0:T(2,128)S(1)}, f32[2,1280]{1,0:T(2,128)}, u32[]{:S(2)}) copy-start(f32[2,1280]{1,0:T(2,128)} %param.29) | copy-start | bytes 30724
  100.6 50.6 %copy-start.9 = (bf16[1280,1280]{1,0:T(8,128)(2,1)S(1)}, bf16[1280,1280]{1,0:T(8,128)(2,1)}, u32[]{:S(2)}) copy-start(bf16[1280,1280]{1,0:T(8,128)(2,1)} %copy-done.8) | copy-start | bytes 9830404
  103.3 51.5 %copy-start.5 = (f32[1,1280]{1,0:T(1,128)}, f32[1,1280]{1,0:T(1,128)S(1)}, u32[]{:S(2)}) copy-start(f32[1,1280]{1,0:T(1,128)S(1)} %get-tuple-element.193.gain) | copy-start | bytes 15364
  103.3 56.1 %copy-start.6 = (f32[1,1280]{1,0:T(1,128)}, f32[1,1280]{1,0:T(1,128)S(1)}, u32[]{:S(2)}) copy-start(f32[1,1280]{1,0:T(1,128)S(1)} %get-tuple-element.190.gain) | copy-start | bytes 15364
  103.3 130.3 %copy-start.7 = (f32[1,1280]{1,0:T(1,128)}, f32[1,1280]{1,0:T(1,128)S(1)}, u32[]{:S(2)}) copy-start(f32[1,1280]{1,0:T(1,128)S(1)} %get-tuple-element.187.gain) | copy-start | bytes 15364
  148.7 10.7 %copy-start.3 = (f32[128,1280]{1,0:T(8,128)}, f32[128,1280]{1,0:T(8,128)S(1)}, u32[]{:S(2)}) copy-start(f32[128,1280]{1,0:T(8,128)S(1)} %get-tuple-element.78.residual.normal_in) | copy-start | bytes 1966084
  204.5 29.1 %copy-start.4 = (f32[128,1280]{1,0:T(8,128)}, f32[128,1280]{1,0:T(8,128)S(1)}, u32[]{:S(2)}) copy-start(f32[128,1280]{1,0:T(8,128)S(1)} %get-tuple-element.81.residual.normal_in) | copy-start | bytes 1966084
  204.5 27.2 %copy-start.16 = (bf16[640,1280]{1,0:T(8,128)(2,1)S(1)}, bf16[640,1280]{1,0:T(8,128)(2,1)}, u32[]{:S(2)}) copy-start(bf16[640,1280]{1,0:T(8,128)(2,1)} %copy-done.14) | copy-start | bytes 4915204
  285.8 10.0 %copy-start.54 = (bf16[512,1280]{1,0:T(8,128)(2,1)}, bf16[512,1280]{1,0:T(8,128)(2,1)S(1)}, u32[]{:S(2)}) copy-start(bf16[512,1280]{1,0:T(8,128)(2,1)S(1)} %get-tuple-element.201) | copy-start | bytes 3932164
  285.8 6.4 copy-start.22
  302.3 59.7 %copy-start.50 = (bf16[1,1280,1280]{2,1,0:T(8,128)(2,1)S(1)}, bf16[1,1280,1280]{2,1,0:T(8,128)(2,1)}, u32[]{:S(2)}) copy-start(bf16[1,1280,1280]{2,1,0:T(8,128)(2,1)} %all-gather.14.cloned.1.call-done) | copy-start | bytes 9830404
  302.3 59.7 %copy-start.55 = (bf16[512,1280]{1,0:T(8,128)(2,1)S(1)}, bf16[512,1280]{1,0:T(8,128)(2,1)}, u32[]{:S(2)}) copy-start(bf16[512,1280]{1,0:T(8,128)(2,1)} %copy-done.54) | copy-start | bytes 3932164
  366.4 26.0 %copy-start.20 = (bf16[512,1280]{1,0:T(8,128)(2,1)S(1)}, bf16[512,1280]{1,0:T(8,128)(2,1)}, u32[]{:S(2)}) copy-start(bf16[512,1280]{1,0:T(8,128)(2,1)} %copy-done.19) | copy-start | bytes 3932164
  407.7 50.1 %copy-start.49 = (bf16[1,1280,1280]{2,1,0:T(8,128)(2,1)S(1)}, bf16[1,1280,1280]{2,1,0:T(8,128)(2,1)}, u32[]{:S(2)}) copy-start(bf16[1,1280,1280]{2,1,0:T(8,128)(2,1)} %all-gather.10.cloned.1.call-done) | copy-start | bytes 9830404
  457.9 4.7 copy-start.10
  534.3 32.0 %copy-start.13 = (bf16[1280,960]{1,0:T(8,128)(2,1)S(1)}, bf16[1280,960]{1,0:T(8,128)(2,1)}, u32[]{:S(2)}) copy-start(bf16[1280,960]{1,0:T(8,128)(2,1)} %copy-done.11) | copy-start | bytes 7372804
  579.3 76.7 %copy-start.33 = (bf16[512,1280]{1,0:T(8,128)(2,1)S(1)}, bf16[512,1280]{1,0:T(8,128)(2,1)}, u32[]{:S(2)}) copy-start(bf16[512,1280]{1,0:T(8,128)(2,1)} %get-tuple-element.99) | copy-start | bytes 3932164
  629.3 28.3 %copy-start.34 = (bf16[512,1280]{1,0:T(8,128)(2,1)S(1)}, bf16[512,1280]{1,0:T(8,128)(2,1)}, u32[]{:S(2)}) copy-start(bf16[512,1280]{1,0:T(8,128)(2,1)} %get-tuple-element.102) | copy-start | bytes 3932164
  675.1 5.3 copy-start.27
  675.1 5.3 copy-start.29
  (31 other events, 87.9 us)
Sparse Core Ops, SparseCore 0:
  57.5 46.0 all-gather.9
  105.8 37.1 all-gather.7
  145.1 46.3 all-gather.11
  193.5 46.3 all-gather.13
  365.1 29.6 reduce-scatter.1

commit v6 on v5

--- a/solution.py
+++ b/solution.py
@@ -266,7 +266,8 @@
 class GradientSum:
     LAGS = (0, 3, 6, 9)
 
-    def __init__(self, arrays, outs, landings, sems):
+    def __init__(self, by_column, arrays, outs, landings, sems):
+        self.by_column = by_column
         self.chunks = landings[0].shape[1]
         self.arrays, self.outs, self.landings = arrays, outs, landings
         self.sends, self.recvs = sems
@@ -281,7 +282,7 @@
 
     def view(self, which, half, core, chunk):
         rows, cols = self.arrays[which].shape
-        if which == 0:
+        if not self.by_column[which]:
             part = rows // 4
             height = part // self.chunks
             start = half * (2 * part) + core * part + chunk * height
@@ -298,7 +299,7 @@
     def out_rows(self, which, core, chunk):
         part = self.outs[which].shape[0] // 2
         height = part // self.chunks
-        return pl.ds(pl.multiple_of(core * part + chunk * height, 8), height)
+        return pl.ds(pl.multiple_of(core * part + chunk * height, 16), height)
 
     def copy(self, which, stage, chunk, half=0):
         pair, across, other = self.peers
@@ -367,14 +368,14 @@
             self.copy(which, 2, chunk).wait_recv()
             low = (landing[2, chunk].astype(WIDE) + landing[3, chunk].astype(WIDE)).astype(LOW)
             landing[3, chunk] = low
-            self.outs[which][self.out_rows(which, self.core, chunk), :] = low.astype(WIDE)
+            self.outs[which][self.out_rows(which, self.core, chunk), :] = low
             self.copy(which, 3, chunk).start()
 
         def shared(which, chunk):
             self.copy(which, 3, chunk).wait_recv()
             self.outs[which][self.out_rows(which, 1 - self.core, chunk), :] = self.landings[which][
                 4, chunk
-            ].astype(WIDE)
+            ]
 
         for lag, action in zip(self.LAGS, (joined, crossed, summed, shared)):
             self.when_due(tick, lag, action)
@@ -391,27 +392,24 @@
         lax.fori_loop(0, self.chunks, body, 0)
 
 
-def gradient_shapes(by_rows, by_cols):
-    rows, cols = by_rows.shape
-    rows_two, cols_two = by_cols.shape
-    chunks = 10 if rows_two >= rows else 5
-    outs = (
-        jax.ShapeDtypeStruct((rows // 2, cols), WIDE),
-        jax.ShapeDtypeStruct((rows_two, cols_two // 2), WIDE),
-    )
-    landings = [
-        pltpu.VMEM((5, chunks, rows // 4 // chunks, cols), LOW),
-        pltpu.VMEM((5, chunks, rows_two // 2 // chunks, cols_two // 2), LOW),
-    ]
+def gradient_shapes(arrays, by_column):
+    chunks = 10 if arrays[0].shape == arrays[1].shape else 5
+    outs, landings = (), []
+    for array, column in zip(arrays, by_column):
+        rows, cols = array.shape
+        rows, cols = (rows, cols // 2) if column else (rows // 2, cols)
+        outs += (jax.ShapeDtypeStruct((rows, cols), LOW),)
+        landings.append(pltpu.VMEM((5, chunks, rows // 2 // chunks, cols), LOW))
     return outs, landings, pltpu.SemaphoreType.DMA((2, 5, chunks))
 
 
 def backward_gradient_kernel(
-    n, pieces, partial, grad_out, normal_in, gain, by_rows, by_cols, gathered, grad_in, sums, out_rows, out_cols,
-    from_left, from_right, total, rs_send, rs_recv, ag_send, ag_recv, landing_rows, landing_cols, side_send, side_recv
+    by_column, n, pieces, partial, grad_out, normal_in, gain, first, second, gathered, grad_in, sums, out_first,
+    out_second, from_left, from_right, total, rs_send, rs_recv, ag_send, ag_recv, landing_first, landing_second,
+    side_send, side_recv
 ):
     side = GradientSum(
-        (by_rows, by_cols), (out_rows, out_cols), (landing_rows, landing_cols), (side_send, side_recv)
+        by_column, (first, second), (out_first, out_second), (landing_first, landing_second), (side_send, side_recv)
     )
     backward_exchange_kernel(
         n, pieces, partial, grad_out, normal_in, gain, gathered, grad_in, sums, from_left, from_right, total,
@@ -419,8 +417,10 @@
     )
 
 
-def sum_all_kernel(axes, shared_rows, values, out, landing, sends, recvs):
-    steps = [(axis, 1 << b) for axis, size in axes for b in range(size.bit_length() - 1)]
+def sum_all_kernel(axes, vectors, biases, out, staged, landing, sends, recvs):
+    half = lax.axis_index("fsdp")
+    shared, width = vectors.shape[0], out.shape[1]
+    steps = [("fsdp", 1)] + [(axis, 1 << b) for axis, size in axes for b in range(size.bit_length() - 1)]
 
     def peer(axis, k):
         return {axis: jnp.bitwise_xor(lax.axis_index(axis), k)}
@@ -428,13 +428,16 @@
     barrier = pltpu.get_barrier_semaphore()
     for axis, k in steps:
         pl.semaphore_signal(barrier, inc=1, device_id=peer(axis, k), device_id_type=MESH)
+    for side in range(2):
+        staged[side, 0:shared, :] = vectors[:, side * width : (side + 1) * width]
+        staged[side, shared:, :] = biases[...]
     pl.semaphore_wait(barrier, len(steps))
-    out[...] = values[...]
     for at, (axis, k) in enumerate(steps):
-        rows = pl.ds(0, shared_rows) if axis == "tp" else pl.ds(0, values.shape[0])
-        landing[at, 0, rows] = out[rows, :]
+        rows = pl.ds(0, shared) if axis == "tp" else pl.ds(0, out.shape[0])
+        if at > 0:
+            landing[at, 0, rows] = out[rows, :]
         copy = pltpu.make_async_remote_copy(
-            src_ref=landing.at[at, 0, rows],
+            src_ref=landing.at[at, 0, rows] if at > 0 else staged.at[1 - half],
             dst_ref=landing.at[at, 1, rows],
             send_sem=sends.at[at],
             recv_sem=recvs.at[at],
@@ -443,33 +446,42 @@
         )
         copy.start()
         copy.wait()
-        out[rows, :] = landing[at, 0, rows] + landing[at, 1, rows]
-
-
-def sum_all(values, shared_rows, axes, collective_id):
-    steps = sum(size.bit_length() - 1 for _, size in axes)
+        own = landing[at, 0, rows] if at > 0 else staged[half]
+        out[rows, :] = own + landing[at, 1, rows]
+
+
+def sum_all(vectors, biases, axes, collective_id):
+    shape = (vectors.shape[0] + biases.shape[0], biases.shape[1])
+    steps = 1 + sum(size.bit_length() - 1 for _, size in axes)
     return pl.pallas_call(
-        functools.partial(sum_all_kernel, axes, shared_rows),
-        out_shape=jax.ShapeDtypeStruct(values.shape, WIDE),
-        in_specs=in_vmem(1),
+        functools.partial(sum_all_kernel, axes),
+        out_shape=jax.ShapeDtypeStruct(shape, WIDE),
+        in_specs=in_vmem(2),
         out_specs=in_vmem(1)[0],
         scratch_shapes=[
-            pltpu.VMEM((steps, 2) + values.shape, WIDE),
+            pltpu.VMEM((2,) + shape, WIDE),
+            pltpu.VMEM((steps, 2) + shape, WIDE),
             pltpu.SemaphoreType.DMA((steps,)),
             pltpu.SemaphoreType.DMA((steps,)),
         ],
         compiler_params=pltpu.CompilerParams(collective_id=collective_id, has_side_effects=True),
         name="sum_all",
-    )(values)
-
-
-FETCH_PARTS = 2
-
-
-def fetch_kernel(by_column, *refs):
+    )(vectors, biases)
+
+
+def fetch_parts(rows):
+    return next(parts for parts in (2, 3, 1) if rows // 4 % (16 * parts) == 0)
+
+
+CAST_ROWS = 64
+
+
+def fetch_kernel(by_column, casts, *refs):
     count = len(by_column)
-    shards, small, outs, out_small = refs[:count], refs[count], refs[count + 1 : -5], refs[-5]
-    sends, recvs, small_send, small_recv = refs[-4:]
+    shards, small, wides, refs = refs[:count], refs[count], refs[count + 1 : count + 1 + casts], refs[count + 1 + casts :]
+    outs, out_small, refs = refs[:count], refs[count], refs[count + 1 :]
+    lows, refs = refs[: casts * LAYERS], refs[casts * LAYERS :]
+    buffers, (cast_sems, sends, recvs, small_send, small_recv) = refs[:casts], refs[casts:]
     half = lax.axis_index("fsdp")
     ctx = lax.axis_index("ctx")
     pair, across = jnp.bitwise_xor(ctx, 1), jnp.bitwise_xor(ctx, 2)
@@ -481,8 +493,9 @@
     pl.semaphore_wait(barrier, 3)
 
     def rows_of(which, quarter, part, base=0):
-        height = shards[which].shape[0] // 4 // FETCH_PARTS
-        return pl.ds(pl.multiple_of(base + (quarter * FETCH_PARTS + part) * height, 16), height)
+        parts = fetch_parts(shards[which].shape[0])
+        height = shards[which].shape[0] // 4 // parts
+        return pl.ds(pl.multiple_of(base + (quarter * parts + part) * height, 16), height)
 
     def place(which, side, quarter, part):
         rows, cols = shards[which].shape
@@ -519,16 +532,35 @@
             device_id_type=MESH,
         )
 
-    each = [(which, part) for which in range(count) for part in range(FETCH_PARTS)]
+    each = [(which, part) for which in range(count) for part in range(fetch_parts(shards[which].shape[0]))]
     for which, part in each:
         copy(which, 0, part).start()
     small_copy(half).start()
+    to_cast = [(layer, which) for layer in range(LAYERS) for which in range(casts)]
+
+    def load(layer, which):
+        return pltpu.make_async_copy(
+            wides[which].at[layer], buffers[which].at[layer], cast_sems.at[which, layer]
+        )
+
+    for layer, which in to_cast:
+        load(layer, which).start()
     for shard, out, column in zip((*shards, small), (*outs, out_small), (*by_column, True)):
         rows, cols = shard.shape
         if column:
             out[:, pl.ds(pl.multiple_of(half * cols, 128), cols)] = shard[...]
         else:
             out[pl.ds(pl.multiple_of(half * rows, 16), rows), :] = shard[...]
+    for layer, which in to_cast:
+        load(layer, which).wait()
+        low = lows[which * LAYERS + layer]
+
+        def cast(at, carry):
+            rows = pl.ds(pl.multiple_of(at * CAST_ROWS, CAST_ROWS), CAST_ROWS)
+            low[rows, :] = buffers[which][layer, rows, :].astype(LOW)
+            return carry
+
+        lax.fori_loop(0, low.shape[0] // CAST_ROWS, cast, 0)
     for at in range(len(each) + 1):
         if at < len(each):
             copy(each[at][0], 0, each[at][1], True).wait_recv()
@@ -547,24 +579,35 @@
     small_copy(half).wait_send()
 
 
-def fetch_first(shards, by_column, small, collective_id):
+def fetch_first(shards, by_column, small, wides, collective_id):
     def whole(shape, column):
         return (shape[0], 2 * shape[1]) if column else (2 * shape[0], shape[1])
 
     shapes = [whole(shard.shape, column) for shard, column in zip(shards, by_column)]
     shapes.append(whole(small.shape, True))
-    sems = pltpu.SemaphoreType.DMA((len(shards), 4, FETCH_PARTS))
+    gathered = len(shapes)
+    for wide in wides:
+        assert wide.shape[0] == LAYERS and wide.shape[1] % CAST_ROWS == 0
+        shapes += [wide.shape[1:]] * LAYERS
+    sems = pltpu.SemaphoreType.DMA((len(shards), 4, max(fetch_parts(shard.shape[0]) for shard in shards)))
     return pl.pallas_call(
-        functools.partial(fetch_kernel, by_column),
+        functools.partial(fetch_kernel, by_column, len(wides)),
         out_shape=tuple(jax.ShapeDtypeStruct(shape, LOW) for shape in shapes),
-        in_specs=in_vmem(len(shapes)),
+        in_specs=in_vmem(gathered) + [pl.BlockSpec(memory_space=pl.ANY)] * len(wides),
         out_specs=tuple(in_vmem(len(shapes))),
-        scratch_shapes=[sems, sems, pltpu.SemaphoreType.DMA, pltpu.SemaphoreType.DMA],
+        scratch_shapes=[pltpu.VMEM(wide.shape, WIDE) for wide in wides]
+        + [
+            pltpu.SemaphoreType.DMA((len(wides), LAYERS)),
+            sems,
+            sems,
+            pltpu.SemaphoreType.DMA,
+            pltpu.SemaphoreType.DMA,
+        ],
         compiler_params=pltpu.CompilerParams(
             collective_id=collective_id, has_side_effects=True, vmem_limit_bytes=40 << 20
         ),
         name="fetch_first",
-    )(*shards, small)
+    )(*shards, small, *wides)
 
 
 def forward_exchange(partial, residual, bias, gain, shift, n, collective_id):
@@ -585,7 +628,7 @@
     )(partial, residual, bias[None, :], gain[None, :], shift[None, :])
 
 
-def backward_exchange(partial, grad_out, normal_in, gain, n, collective_id, by_rows=None, by_cols=None):
+def backward_exchange(partial, grad_out, normal_in, gain, n, collective_id, arrays=(), by_column=()):
     rows, width = partial.shape
     out_shape = (
         jax.ShapeDtypeStruct((rows, width), LOW),
@@ -594,11 +637,11 @@
     )
     scratch = exchange_scratch(n, rows, width, PIECES)
     kernel, extra = backward_exchange_kernel, ()
-    if by_rows is not None:
-        outs, landings, sems = gradient_shapes(by_rows, by_cols)
+    if arrays:
+        outs, landings, sems = gradient_shapes(arrays, by_column)
         out_shape = out_shape + outs
         scratch = scratch + landings + [sems] * 2
-        kernel, extra = backward_gradient_kernel, (by_rows, by_cols)
+        kernel, extra = functools.partial(backward_gradient_kernel, by_column), arrays
     return pl.pallas_call(
         functools.partial(kernel, n, PIECES),
         out_shape=out_shape,
@@ -1025,22 +1068,20 @@
 
     def qkv_shard(layer):
         return jnp.concatenate(
-            [query_weight[layer], key_weight[layer], value_weight[layer]], axis=1
+            [query_weight[layer].T, key_weight[layer].T, value_weight[layer].T], axis=0
         ).astype(LOW)
 
     projections = output_weight.astype(LOW).reshape(-1, output_weight.shape[2])
     if lax.axis_size("fsdp") == 2:
-        qkv_first, projections, inner_first, small = fetch_first(
-            (qkv_shard(0), projections, inner_weight[0].astype(LOW)), (False, True, False), small, 17
-        )
-        small, outer_weight, inner_weight, query_weight, key_weight, value_weight = lax.optimization_barrier(
-            (small, outer_weight, inner_weight, query_weight, key_weight, value_weight)
-        )
+        qkv_first, projections, small, *lows = fetch_first(
+            (qkv_shard(0), projections), (True, True), small, (inner_weight, outer_weight), 17
+        )
+        inner_low, outer_low = lows[:LAYERS], lows[LAYERS:]
     else:
-        qkv_first = lax.all_gather(qkv_shard(0), "fsdp", axis=0, tiled=True)
-        inner_first = lax.all_gather(inner_weight[0].astype(LOW), "fsdp", axis=0, tiled=True)
+        qkv_first = lax.all_gather(qkv_shard(0), "fsdp", axis=1, tiled=True)
         projections = lax.all_gather(projections, "fsdp", axis=1, tiled=True)
         small = lax.all_gather(small, "fsdp", axis=1, tiled=True)
+        inner_low, outer_low = inner_weight.astype(LOW), outer_weight.astype(LOW)
     small = small.astype(WIDE)
     projections = projections.reshape(LAYERS, columns, width)
 
@@ -1048,12 +1089,12 @@
         return small[kind * LAYERS + layer]
 
     def fetch(layer):
-        qkv, inner = qkv_first, inner_first
+        qkv = qkv_first
         if layer > 0:
-            qkv = lax.all_gather(qkv_shard(layer), "fsdp", axis=0, tiled=True)
-            inner = lax.all_gather(inner_weight[layer].astype(LOW), "fsdp", axis=0, tiled=True)
+            qkv = lax.all_gather(qkv_shard(layer), "fsdp", axis=1, tiled=True)
         out = projections[layer]
-        outer = lax.all_gather(outer_weight[layer].astype(LOW), "fsdp", axis=1, tiled=True)
+        inner = lax.all_gather(inner_low[layer], "fsdp", axis=0, tiled=True)
+        outer = lax.all_gather(outer_low[layer], "fsdp", axis=1, tiled=True)
         return (qkv, out, inner, outer)
 
     weights = [fetch(layer) for layer in range(LAYERS)]
@@ -1068,7 +1109,7 @@
         bias_qkv = jnp.concatenate(
             [query_bias[layer], jnp.zeros_like(query_bias[layer]), value_bias[layer]]
         )
-        qkv = (product(w_qkv, normed, 0, 1) + bias_qkv[:, None]).astype(LOW)
+        qkv = (product(w_qkv, normed, 1, 1) + bias_qkv[:, None]).astype(LOW)
         attended, attended_wide, log_total, held = attend(qkv, lengths, scale, 2 * layer)
         branch = product(attended, w_out, 0, 0).astype(LOW)
         normed_two, middle = forward_exchange(
@@ -1093,17 +1134,17 @@
         else:
             last_branch, last_middle = branch, middle
 
-    def exchange_back(branch, grad_out, normal_in, gain, collective_id, by_rows, by_cols):
+    def exchange_back(branch, grad_out, normal_in, gain, collective_id, arrays, by_column):
         if lax.axis_size("fsdp") == 2:
             return backward_exchange(
-                branch, grad_out, normal_in, gain, tp_size, collective_id, by_rows, by_cols
+                branch, grad_out, normal_in, gain, tp_size, collective_id, arrays, by_column
             )
-        first = backward_exchange(branch, grad_out, normal_in, gain, tp_size, collective_id)
-        by_rows = lax.psum_scatter(by_rows, ("fsdp", "ctx"), scatter_dimension=0, tiled=True)
-        by_rows = lax.all_gather(by_rows, "ctx", axis=0, tiled=True).astype(WIDE)
-        by_cols = lax.psum_scatter(by_cols, ("fsdp", "ctx"), scatter_dimension=1, tiled=True)
-        by_cols = lax.all_gather(by_cols, "ctx", axis=1, tiled=True).astype(WIDE)
-        return (*first, by_rows, by_cols)
+        result = backward_exchange(branch, grad_out, normal_in, gain, tp_size, collective_id)
+        for array, column in zip(arrays, by_column):
+            axis = 1 if column else 0
+            array = lax.psum_scatter(array, ("fsdp", "ctx"), scatter_dimension=axis, tiled=True)
+            result += (lax.all_gather(array, "ctx", axis=axis, tiled=True),)
+        return result
 
     grad_rows = cotangent.reshape(rows, width)
     grad_own = own_slice(grad_rows)
@@ -1133,7 +1174,7 @@
         grad_outer_w = product(active, grad_low, 0, 0).astype(LOW)
         grad_inner_w = product(normed_two, grad_inner, 0, 0).astype(LOW)
         grad_mid_low, grad_middle, sums_two, *summed_two = exchange_back(
-            branch, grad_own, middle, vector(4, layer), 2 * layer + 8, grad_inner_w, grad_outer_w
+            branch, grad_own, middle, vector(4, layer), 2 * layer + 8, (grad_inner_w, grad_outer_w), (False, True)
         )
         if layer == LAYERS - 1:
             last_branch, grad_mid_low = lax.optimization_barrier((last_branch, grad_mid_low))
@@ -1151,15 +1192,15 @@
             last_rows if layer == 0 else None,
         )
         grad_output_w = product(attended, grad_mid_low, 1, 0).astype(LOW)
-        branch = product(grad_qkv, w_qkv, 0, 1).astype(LOW)
-        grad_qkv_w = product(normed, grad_qkv, 0, 1).astype(LOW)
+        branch = product(grad_qkv, w_qkv, 0, 0).astype(LOW)
+        grad_qkv_w = product(grad_qkv, normed, 1, 0).astype(LOW)
         if layer == LAYERS - 1:
             last_branch, branch = lax.optimization_barrier((last_branch, branch))
             last_rows = (last_middle + last_branch.astype(WIDE) + vector(1, layer)).astype(LOW)
         if layer == 0:
             output = shared[0].astype(WIDE)
         grad_low, grad_own, sums_one, *summed_one = exchange_back(
-            branch, grad_middle, residual, vector(2, layer), 2 * layer + 9, grad_qkv_w, grad_output_w
+            branch, grad_middle, residual, vector(2, layer), 2 * layer + 9, (grad_qkv_w, grad_output_w), (True, True)
         )
         grads[layer] = (*summed_one, *summed_two)
         vectors[layer] = [
@@ -1174,39 +1215,37 @@
         )
     grad_hidden = grad_low.astype(WIDE)
 
+    shard = output_bias.shape[1]
     flat_biases = jnp.concatenate(biases)
-    bias_rows = -(-flat_biases.size // width)
-    flat_biases = jnp.pad(flat_biases, (0, bias_rows * width - flat_biases.size))
+    flat_biases = jnp.pad(flat_biases, (0, -flat_biases.size % (8 * shard))).reshape(-1, shard)
     vector_count = 6 * LAYERS
-    shared_rows = -(-vector_count // 8) * 8
-    total_rows = shared_rows + -(-bias_rows // 8) * 8
-    small_sums = jnp.concatenate(
-        [
-            jnp.stack([row for parts in zip(*vectors) for row in parts]),
-            jnp.zeros((shared_rows - vector_count, width), WIDE),
-            flat_biases.reshape(bias_rows, width),
-            jnp.zeros((total_rows - shared_rows - bias_rows, width), WIDE),
-        ]
-    )
-    small_sums = sum_all(
-        small_sums, shared_rows, tuple((axis, lax.axis_size(axis)) for axis in ("ctx", "fsdp", "tp")), 16
-    )
-    shard = output_bias.shape[1]
-    vector_sums = lax.dynamic_slice_in_dim(
-        small_sums[:vector_count].reshape(6, LAYERS, width), lax.axis_index("fsdp") * shard, shard, axis=2
-    )
-    bias_sums = small_sums[shared_rows:].reshape(-1)[: LAYERS * biases[0].size].reshape(LAYERS, -1)
-
-    def stacked(which, start=0, size=None):
-        size = grads[0][which].shape[1] if size is None else size
-        return jnp.stack([grads[layer][which][:, start : start + size] for layer in range(LAYERS)])
+    small_sums = jnp.stack([row for parts in zip(*vectors) for row in parts])
+    if lax.axis_size("fsdp") == 2:
+        small_sums = jnp.pad(small_sums, ((0, -vector_count % 8), (0, 0)))
+        shared_rows = small_sums.shape[0]
+        small_sums = sum_all(
+            small_sums, flat_biases, tuple((axis, lax.axis_size(axis)) for axis in ("ctx", "tp")), 16
+        )
+        vector_sums, bias_sums = small_sums[:vector_count], small_sums[shared_rows:]
+    else:
+        vector_sums = lax.psum(small_sums, ("fsdp", "ctx", "tp"))
+        vector_sums = lax.dynamic_slice_in_dim(vector_sums, lax.axis_index("fsdp") * shard, shard, axis=1)
+        bias_sums = lax.psum(flat_biases, ("fsdp", "ctx"))
+    vector_sums = vector_sums.reshape(6, LAYERS, shard)
+    bias_sums = bias_sums.reshape(-1)[: LAYERS * biases[0].size].reshape(LAYERS, -1)
+
+    def stacked(which):
+        return jnp.stack([grads[layer][which] for layer in range(LAYERS)]).astype(WIDE)
+
+    def turned(start):
+        return jnp.stack([grads[layer][0][start : start + columns].T for layer in range(LAYERS)]).astype(WIDE)
 
     return (
         output.reshape(hidden.shape),
         grad_hidden.reshape(hidden.shape),
-        stacked(0, 0, columns),
-        stacked(0, columns, columns),
-        stacked(0, 2 * columns, columns),
+        turned(0),
+        turned(columns),
+        turned(2 * columns),
         stacked(1),
         stacked(2),
         stacked(3),

time: 695 us -> 664 us (0.955)
  local copies, waits for them, and re-layouts: 46.7 us -> 20.6 us
  Pallas kernels: 510 us -> 495 us
    another operation x13 -> x9, other arithmetic: 20.3 us -> 5.96 us  [the longest x6 14.4 us: stacked(): jnp.stack([grads[layer][which][:, start:start + size] for layer in range(...]
    pallas_call x2, Pallas kernels: 54.6 us -> 42 us  [the longest x1 25.3 us: fetch_first(): pl.pallas_call(functools.partial(fetch_kernel, by_column, len(wides)), ou...]
    convert_element_type x0 -> x6, other arithmetic: none -> 11.6 us  [the longest x3 7.75 us: stacked(): jnp.stack([grads[layer][which] for layer in range(LAYERS)]).astype(WIDE)]
    convert_element_type x3 -> x0, local copies, waits for them, and re-layouts: 10 us -> none  [the longest x2 7.91 us: per_device(): grad_qkv_w = product(normed, grad_qkv, 0, 1).astype(LOW)]
    slice x9 -> x2, local copies, waits for them, and re-layouts: 9.83 us -> 2.22 us  [the longest x1 1.49 us: per_device(): vector_sums[5]]
  transfers between devices with their start and end apart: 5 -> 6, of which waited for: 0 -> 1; matrix products, arithmetic and copies ran while one was open for 9% -> 8% of each run, Pallas kernels for 30% -> 31%
where the time goes in v6:
time: 664 us; the launch traced here: 653 us
  Pallas kernels  495 us (75%)
  matrix products  82.3 us (12%)
  other arithmetic  33.9 us (5%)
  local copies, waits for them, and re-layouts  20.6 us (3%)
  between operations  15.7 us (2%)
    pallas_call x4, Pallas kernels, backward_exchange(): pl.pallas_call(functools.partial(kernel, n, PIECES), out_shape=out_shape,...  216 us
    pallas_call x3, Pallas kernels, forward_exchange(): pl.pallas_call(functools.partial(forward_exchange_kernel, n, PIECES), out...  132 us
    dot_general x24, matrix products, product(): lax.dot_general(left_side, right_side, (((left_axis,), (right_axis,)), ((...  82.3 us
    pallas_call x2, Pallas kernels, attend_back(): pl.pallas_call(functools.partial(attend_back_kernel, scale, own is not No...  56.9 us
    pallas_call x2, Pallas kernels, attend(): pl.pallas_call(functools.partial(attend_kernel, scale), out_shape=(jax.Sh...  47.3 us
    pallas_call x1, Pallas kernels, fetch_first(): pl.pallas_call(functools.partial(fetch_kernel, by_column, len(wides)), ou...  25.3 us
    pallas_call x1, Pallas kernels, sum_all(): pl.pallas_call(functools.partial(sum_all_kernel, axes), out_shape=jax.Sha...  16.7 us
  transfers between devices with their start and end apart: 6, of which 1 were waited for; matrix products, arithmetic and copies ran while one was open for 8% of the time, Pallas kernels for 31%

profile of v6, /device:TPU:0, one launch (start us, length us, event | category | flops | bytes accessed | tf_op | source)
XLA Modules:
  0.0 653.3 jit_solution(12617157418379256711)
XLA Ops:
  17.9 25.3 %fetch_first.1 = (bf16[960,1280]{1,0:T(8,128)(2,1)S(1)}, bf16[640,1280]{1,0:T(8,128)(2,1)S(1)}, bf16[16,1280]{1,0:T(8,128)(2,1)S(1)}, bf16[640,1280]{1,0:T(8,128...) custom-call(bf16[960,640]{1,0:T(8,128)(2,1)S(1)} %pad_maximum_fusion.refs_0_, ...), custom_call_target="tpu_custom_call" | custom-call | tf_op jit(solution)/shard_map/fetch_first/pallas_call | solution.py:593
  54.2 4.7 add_convert_fusion.2.qkv
  60.7 23.7 %attend.2 = (bf16[320,512]{1,0:T(8,128)(2,1)}, f32[320,512]{1,0:T(8,128)}, f32[8,512]{1,0:T(8,128)}, bf16[3,640,512]{2,1,0:T(8,128)(2,1)}) custom-call(s32[1]{0:T(128)S(6)} %copy.35.length, bf16[960,512]{1,0:T(8,128)(2,1)} %add_convert_fusion.2.qkv), custom_call_target="tpu_custom_call" | custom-call | tf_op jit(solution)/shard_map/attend/pallas_call | solution.py:764
  86.9 45.3 %forward_exchange.3 = (bf16[512,1280]{1,0:T(8,128)(2,1)S(1)}, f32[128,1280]{1,0:T(8,128)S(1)}) custom-call(bf16[512,1280]{1,0:T(8,128)(2,1)S(1)} %convolution_convert_fusion.13.partial, f32[128,1280]{1,0:T(8,128)S(1)} %dynamic-slice_bitcast_fusion.residual.normal_in, f32[1,1280]{1,0:T(1,128)S(1)} %get-tuple-element.158.bias, ...), custom_call_target="tpu_custom_call" | custom-call | tf_op jit(solution)/shard_map/forward_exchange/pallas_call | solution.py:615
  134.8 5.4 multiply_convert_fusion.1
  140.2 4.2 convolution_convert_fusion.12.partial
  144.5 44.6 %forward_exchange.4 = (bf16[512,1280]{1,0:T(8,128)(2,1)S(1)}, f32[128,1280]{1,0:T(8,128)S(1)}) custom-call(bf16[512,1280]{1,0:T(8,128)(2,1)S(1)} %convolution_convert_fusion.12.partial, f32[128,1280]{1,0:T(8,128)S(1)} %get-tuple-element.71.residual.normal_in, f32[1,1280]{1,0:T(1,128)S(1)} %get-tuple-element.155.bias, f32[1,1280]{1,0:T(1,128)S(1)} %get-tuple-element.154.gain, ...), custom_call_target="tpu_custom_call" | custom-call | tf_op jit(solution)/shard_map/forward_exchange/pallas_call | solution.py:615
  190.1 5.0 add_convert_fusion.1.qkv
  195.1 23.6 %attend.3 = (bf16[320,512]{1,0:T(8,128)(2,1)}, f32[320,512]{1,0:T(8,128)}, f32[8,512]{1,0:T(8,128)}, bf16[3,640,512]{2,1,0:T(8,128)(2,1)}) custom-call(s32[1]{0:T(128)S(6)} %copy.35.length, bf16[960,512]{1,0:T(8,128)(2,1)} %add_convert_fusion.1.qkv), custom_call_target="tpu_custom_call" | custom-call | tf_op jit(solution)/shard_map/attend/pallas_call | solution.py:764
  220.6 42.3 %forward_exchange.5 = (bf16[512,1280]{1,0:T(8,128)(2,1)S(1)}, f32[128,1280]{1,0:T(8,128)S(1)}) custom-call(bf16[512,1280]{1,0:T(8,128)(2,1)S(1)} %convolution_convert_fusion.11.partial, f32[128,1280]{1,0:T(8,128)S(1)} %get-tuple-element.74.residual.normal_in, f32[1,1280]{1,0:T(1,128)S(1)} %get-tuple-element.152.bias, f32[1,1280]{1,0:T(1,128)S(1)} %get-tuple-element.151.gain, ...), custom_call_target="tpu_custom_call" | custom-call | tf_op jit(solution)/shard_map/forward_exchange/pallas_call | solution.py:615
  264.8 5.8 multiply_convert_fusion
  270.6 3.9 all-gather.14.cloned.1.call-done
  274.6 6.0 convert_reduce_fusion
  280.6 3.6 convolution_convert_fusion.3.first
  284.2 3.6 convolution_convert_fusion.2.second
  287.8 2.9 convolution_convert_fusion.9.partial
  290.8 59.0 %backward_exchange.4 = (bf16[512,1280]{1,0:T(8,128)(2,1)}, f32[128,1280]{1,0:T(8,128)}, f32[8,1280]{1,0:T(8,128)}, bf16[640,1280]{1,0:T(8,128)(2,1)}, bf16[1280,640]{1,0:T(8,128)(2,1)}) custom-call(bf16[512,1280]{1,0:T(8,128)(2,1)} %convolution_convert_fusion.9.partial, f32[128,1280]{1,0:T(8,128)} %get-tuple-element.119.grad_out, f32[128,1280]{1,0:T(8,128)} %copy-done.1, ...), custom_call_target="tpu_custom_call" | custom-call | tf_op jit(solution)/shard_map/backward_exchange/pallas_call | solution.py:645
  349.8 2.9 convolution_convert_fusion.10
  354.1 25.9 %attend_back.2 = bf16[960,512]{1,0:T(8,128)(2,1)} custom-call(s32[1]{0:T(128)S(6)} %copy.35.length, bf16[960,512]{1,0:T(8,128)(2,1)} %add_convert_fusion.1.qkv, bf16[3,640,512]{2,1,0:T(8,128)(2,1)} %get-tuple-element.81.held, bf16[320,512]{1,0:T(8,128)(2,1)} %convolution_convert_fusion.17.grad, f32[320,512]{1,0:T(8,128)} %get-tuple-element.83.out_wide, ...), custom_call_target="tpu_custom_call" | custom-call | tf_op jit(solution)/shard_map/attend_back/pallas_call | solution.py:991
  383.1 2.9 convolution_convert_fusion.5.first
  389.6 50.5 %backward_exchange.5 = (bf16[512,1280]{1,0:T(8,128)(2,1)}, f32[128,1280]{1,0:T(8,128)}, f32[8,1280]{1,0:T(8,128)}, bf16[960,640]{1,0:T(8,128)(2,1)}, bf16[320,640]{1,0:T(8,128)(2,1)}) custom-call(bf16[512,1280]{1,0:T(8,128)(2,1)} %convolution_convert_fusion.8.partial, f32[128,1280]{1,0:T(8,128)} %get-tuple-element.86.grad_out, f32[128,1280]{1,0:T(8,128)} %copy-done.4, ...), custom_call_target="tpu_custom_call" | custom-call | tf_op jit(solution)/shard_map/backward_exchange/pallas_call | solution.py:645
  440.1 5.1 convolution_convert_fusion.second
  448.1 3.6 convolution_convert_fusion.1.first
  451.7 3.0 convolution_convert_fusion.7.partial
  454.6 57.7 %backward_exchange.6 = (bf16[512,1280]{1,0:T(8,128)(2,1)}, f32[128,1280]{1,0:T(8,128)}, f32[8,1280]{1,0:T(8,128)}, bf16[640,1280]{1,0:T(8,128)(2,1)}, bf16[1280,640]{1,0:T(8,128)(2,1)}) custom-call(bf16[512,1280]{1,0:T(8,128)(2,1)} %convolution_convert_fusion.7.partial, f32[128,1280]{1,0:T(8,128)} %get-tuple-element.88.grad_out, f32[128,1280]{1,0:T(8,128)} %copy-done.3, ...), custom_call_target="tpu_custom_call" | custom-call | tf_op jit(solution)/shard_map/backward_exchange/pallas_call | solution.py:645
  515.9 31.0 %attend_back.3 = (bf16[960,512]{1,0:T(8,128)(2,1)}, bf16[512,1280]{1,0:T(8,128)(2,1)}) custom-call(s32[1]{0:T(128)S(6)} %copy.35.length, bf16[960,512]{1,0:T(8,128)(2,1)} %add_convert_fusion.2.qkv, bf16[3,640,512]{2,1,0:T(8,128)(2,1)} %get-tuple-element.65.held, bf16[320,512]{1,0:T(8,128)(2,1)} %convolution_convert_fusion.16.grad, ...), custom_call_target="tpu_custom_call" | custom-call | tf_op jit(solution)/shard_map/attend_back/pallas_call | solution.py:991
  547.0 4.0 convolution_convert_fusion.6.partial
  552.9 3.1 convolution_convert_fusion.4.first
  558.5 49.2 %backward_exchange.7 = (bf16[512,1280]{1,0:T(8,128)(2,1)}, f32[128,1280]{1,0:T(8,128)}, f32[8,1280]{1,0:T(8,128)}, bf16[960,640]{1,0:T(8,128)(2,1)}, bf16[320,640]{1,0:T(8,128)(2,1)}) custom-call(bf16[512,1280]{1,0:T(8,128)(2,1)} %convolution_convert_fusion.6.partial, f32[128,1280]{1,0:T(8,128)} %get-tuple-element.95.grad_out, f32[128,1280]{1,0:T(8,128)} %copy-done, ...), custom_call_target="tpu_custom_call" | custom-call | tf_op jit(solution)/shard_map/backward_exchange/pallas_call | solution.py:645
  609.5 16.7 %sum_all.1 = f32[24,640]{1,0:T(8,128)} custom-call(f32[16,1280]{1,0:T(8,128)} %pad.13.vectors, f32[8,640]{1,0:T(8,128)} %reshape.103.biases), custom_call_target="tpu_custom_call" | custom-call | tf_op jit(solution)/shard_map/sum_all/pallas_call | solution.py:456
  639.7 3.3 maximum_convert_fusion
  643.0 3.2 maximum_convert_fusion.1
  (192 shorter events, 66.6 us)
Async XLA Ops:
  7.2 6.8 %copy-start.27 = (f32[2,640,320]{1,2,0:T(8,128)S(1)}, f32[2,640,320]{1,2,0:T(8,128)}, u32[]{:S(2)}) copy-start(f32[2,640,320]{1,2,0:T(8,128)} %param.22) | copy-start | bytes 4915204
  7.2 127.6 %all-gather.8.cloned.1.call-start = ((), (), s32[]{:S(2)}) async-start(), calls=%async_computation.2 | async-start | bytes 4915200 | tf_op jit(solution)/shard_map/all_gather | solution.py:1096
  44.4 9.8 %copy-start.8 = (bf16[960,1280]{1,0:T(8,128)(2,1)}, bf16[960,1280]{1,0:T(8,128)(2,1)S(1)}, u32[]{:S(2)}) copy-start(bf16[960,1280]{1,0:T(8,128)(2,1)S(1)} %get-tuple-element.63) | copy-start | bytes 7372804
  44.4 95.8 %all-gather.10.cloned.1.call-start = ((), (), s32[]{:S(2)}) async-start(), calls=%async_computation.3 | async-start | bytes 4915200 | tf_op jit(solution)/shard_map/all_gather | solution.py:1097
  45.2 144.9 %all-gather.6.cloned.1.call-start = ((), (), s32[]{:S(2)}) async-start(), calls=%async_computation.1 | async-start | bytes 3686400 | tf_op jit(solution)/shard_map/all_gather | solution.py:1094
  48.2 216.6 %all-gather.12.cloned.1.call-start = ((), (), s32[]{:S(2)}) async-start(), calls=%async_computation.4 | async-start | bytes 4915200 | tf_op jit(solution)/shard_map/all_gather | solution.py:1096
  48.8 225.7 %all-gather.14.cloned.1.call-start = ((), (), s32[]{:S(2)}) async-start(), calls=%async_computation.5 | async-start | bytes 4915200 | tf_op jit(solution)/shard_map/all_gather | solution.py:1097
  49.4 340.2 %reduce-scatter.2.cloned.1.call-start = ((), (), s32[]{:S(2)}) async-start(), calls=%async_computation.6 | async-start | bytes 1638400 | tf_op jit(solution)/shard_map/reduce_scatter | solution.py:1181
  49.4 4.6 copy-start.44
  49.5 4.6 copy-start.45
  54.2 30.2 %copy-start.11 = (bf16[640,1280]{1,0:T(8,128)(2,1)S(1)}, bf16[640,1280]{1,0:T(8,128)(2,1)}, u32[]{:S(2)}) copy-start(bf16[640,1280]{1,0:T(8,128)(2,1)} %copy-done.10) | copy-start | bytes 4915204
  60.0 72.2 %copy-start = (f32[128,1280]{1,0:T(8,128)}, f32[128,1280]{1,0:T(8,128)S(1)}, u32[]{:S(2)}) copy-start(f32[128,1280]{1,0:T(8,128)S(1)} %dynamic-slice_bitcast_fusion.residual.normal_in) | copy-start | bytes 1966084
  84.4 50.3 %copy-start.43 = (f32[2,1280]{1,0:T(2,128)S(1)}, f32[2,1280]{1,0:T(2,128)}, u32[]{:S(2)}) copy-start(f32[2,1280]{1,0:T(2,128)} %param.29) | copy-start | bytes 30724
  86.9 53.3 %copy-start.5 = (f32[1,1280]{1,0:T(1,128)}, f32[1,1280]{1,0:T(1,128)S(1)}, u32[]{:S(2)}) copy-start(f32[1,1280]{1,0:T(1,128)S(1)} %get-tuple-element.157.gain) | copy-start | bytes 15364
  86.9 57.5 %copy-start.6 = (f32[1,1280]{1,0:T(1,128)}, f32[1,1280]{1,0:T(1,128)S(1)}, u32[]{:S(2)}) copy-start(f32[1,1280]{1,0:T(1,128)S(1)} %get-tuple-element.154.gain) | copy-start | bytes 15364
  86.9 133.6 %copy-start.7 = (f32[1,1280]{1,0:T(1,128)}, f32[1,1280]{1,0:T(1,128)S(1)}, u32[]{:S(2)}) copy-start(f32[1,1280]{1,0:T(1,128)S(1)} %get-tuple-element.151.gain) | copy-start | bytes 15364
  132.2 8.0 %copy-start.13 = (bf16[512,1280]{1,0:T(8,128)(2,1)}, bf16[512,1280]{1,0:T(8,128)(2,1)S(1)}, u32[]{:S(2)}) copy-start(bf16[512,1280]{1,0:T(8,128)(2,1)S(1)} %get-tuple-element.68) | copy-start | bytes 3932164
  132.2 12.2 %copy-start.3 = (f32[128,1280]{1,0:T(8,128)}, f32[128,1280]{1,0:T(8,128)S(1)}, u32[]{:S(2)}) copy-start(f32[128,1280]{1,0:T(8,128)S(1)} %get-tuple-element.71.residual.normal_in) | copy-start | bytes 1966084
  190.1 30.5 %copy-start.4 = (f32[128,1280]{1,0:T(8,128)}, f32[128,1280]{1,0:T(8,128)S(1)}, u32[]{:S(2)}) copy-start(f32[128,1280]{1,0:T(8,128)S(1)} %get-tuple-element.74.residual.normal_in) | copy-start | bytes 1966084
  190.1 28.6 %copy-start.12 = (bf16[640,1280]{1,0:T(8,128)(2,1)S(1)}, bf16[640,1280]{1,0:T(8,128)(2,1)}, u32[]{:S(2)}) copy-start(bf16[640,1280]{1,0:T(8,128)(2,1)} %copy-done.10) | copy-start | bytes 4915204
  270.6 13.5 %copy-start.53 = (bf16[512,1280]{1,0:T(8,128)(2,1)}, bf16[512,1280]{1,0:T(8,128)(2,1)S(1)}, u32[]{:S(2)}) copy-start(bf16[512,1280]{1,0:T(8,128)(2,1)S(1)} %get-tuple-element.165) | copy-start | bytes 3932164
  274.5 6.0 copy-start.18
  290.8 59.0 %copy-start.48 = (bf16[1280,1280]{1,0:T(8,128)(2,1)S(1)}, bf16[1280,1280]{1,0:T(8,128)(2,1)}, u32[]{:S(2)}) copy-start(bf16[1280,1280]{1,0:T(8,128)(2,1)} %all-gather.14.cloned.1.call-done) | copy-start | bytes 9830404
  290.8 59.0 %copy-start.54 = (bf16[512,1280]{1,0:T(8,128)(2,1)S(1)}, bf16[512,1280]{1,0:T(8,128)(2,1)}, u32[]{:S(2)}) copy-start(bf16[512,1280]{1,0:T(8,128)(2,1)} %copy-done.53) | copy-start | bytes 3932164
  354.1 27.5 %copy-start.41 = (bf16[320,512]{1,0:T(8,128)(2,1)S(1)}, bf16[320,512]{1,0:T(8,128)(2,1)}, u32[]{:S(2)}) copy-start(bf16[320,512]{1,0:T(8,128)(2,1)} %get-tuple-element.73) | copy-start | bytes 983044
  389.6 50.5 %copy-start.55 = (bf16[512,1280]{1,0:T(8,128)(2,1)S(1)}, bf16[512,1280]{1,0:T(8,128)(2,1)}, u32[]{:S(2)}) copy-start(bf16[512,1280]{1,0:T(8,128)(2,1)} %get-tuple-element.163) | copy-start | bytes 3932164
  440.1 5.1 copy-start.47
  440.1 5.1 copy-start.51
  440.1 5.1 copy-start.52
  515.9 31.0 %copy-start.9 = (bf16[960,1280]{1,0:T(8,128)(2,1)S(1)}, bf16[960,1280]{1,0:T(8,128)(2,1)}, u32[]{:S(2)}) copy-start(bf16[960,1280]{1,0:T(8,128)(2,1)} %copy-done.8) | copy-start | bytes 7372804
  558.5 71.2 %copy-start.34 = (bf16[960,640]{1,0:T(8,128)(2,1)S(1)}, bf16[960,640]{1,0:T(8,128)(2,1)}, u32[]{:S(2)}) copy-start(bf16[960,640]{1,0:T(8,128)(2,1)} %get-tuple-element.98) | copy-start | bytes 3686404
  607.8 22.1 %copy-start.32 = (bf16[512,1280]{1,0:T(8,128)(2,1)S(1)}, bf16[512,1280]{1,0:T(8,128)(2,1)}, u32[]{:S(2)}) copy-start(bf16[512,1280]{1,0:T(8,128)(2,1)} %get-tuple-element.93) | copy-start | bytes 3932164
  (30 other events, 77.4 us)
Sparse Core Ops, SparseCore 0:
  44.5 47.0 all-gather.7
  93.2 46.3 all-gather.9
  141.7 37.1 all-gather.5
  180.3 46.3 all-gather.11
  228.1 46.3 all-gather.13
  352.8 31.2 reduce-scatter.1

commit v7 on v6

--- a/solution.py
+++ b/solution.py
@@ -226,8 +226,18 @@
     ]
 
 
+def forward_fetch_kernel(
+    n, pieces, partial, residual, bias, gain, shift, shard, gathered, middle, fetched, from_left, from_right, total,
+    rs_send, rs_recv, ag_send, ag_recv, sends, recvs
+):
+    forward_exchange_kernel(
+        n, pieces, partial, residual, bias, gain, shift, gathered, middle, from_left, from_right, total, rs_send, rs_recv,
+        ag_send, ag_recv, side=QuartersSide((shard,), (fetched,), sends, recvs)
+    )
+
+
 def forward_exchange_kernel(
-    n, pieces, partial, residual, bias, gain, shift, gathered, middle, from_left, from_right, total, *sems
+    n, pieces, partial, residual, bias, gain, shift, gathered, middle, from_left, from_right, total, *sems, side=None
 ):
     def finish(rows, value):
         mid = value + residual[rows, :] + bias[...]
@@ -236,7 +246,7 @@
         return (hat * gain[...] + shift[...]).astype(LOW)
 
     line_exchange(
-        n, residual.shape[0], pieces, partial, gathered, from_left, from_right, total, sems, finish
+        n, residual.shape[0], pieces, partial, gathered, from_left, from_right, total, sems, finish, side
     )
 
 
@@ -327,7 +337,7 @@
 
     def start(self):
         def body(chunk, carry):
-            for which in range(2):
+            for which in range(len(self.arrays)):
                 for half in range(2):
                     self.copy(which, 0, chunk, half).start()
             return carry
@@ -341,7 +351,7 @@
 
         @pl.when((since >= 0) & (lax.rem(clipped, 2) == 0) & (chunk < self.chunks))
         def _():
-            for which in range(2):
+            for which in range(len(self.arrays)):
                 action(which, chunk)
 
     def at(self, tick):
@@ -382,7 +392,7 @@
 
     def drain(self):
         def body(chunk, carry):
-            for which in range(2):
+            for which in range(len(self.arrays)):
                 for half in range(2):
                     self.copy(which, 0, chunk, half).wait_send()
                 for stage in range(1, 4):
@@ -393,27 +403,23 @@
 
 
 def gradient_shapes(arrays, by_column):
-    chunks = 10 if arrays[0].shape == arrays[1].shape else 5
+    chunks = 5 if all(by_column) else 10
     outs, landings = (), []
     for array, column in zip(arrays, by_column):
         rows, cols = array.shape
         rows, cols = (rows, cols // 2) if column else (rows // 2, cols)
         outs += (jax.ShapeDtypeStruct((rows, cols), LOW),)
         landings.append(pltpu.VMEM((5, chunks, rows // 2 // chunks, cols), LOW))
-    return outs, landings, pltpu.SemaphoreType.DMA((2, 5, chunks))
-
-
-def backward_gradient_kernel(
-    by_column, n, pieces, partial, grad_out, normal_in, gain, first, second, gathered, grad_in, sums, out_first,
-    out_second, from_left, from_right, total, rs_send, rs_recv, ag_send, ag_recv, landing_first, landing_second,
-    side_send, side_recv
-):
-    side = GradientSum(
-        by_column, (first, second), (out_first, out_second), (landing_first, landing_second), (side_send, side_recv)
-    )
+    return outs, landings, pltpu.SemaphoreType.DMA((len(arrays), 5, chunks))
+
+
+def backward_gradient_kernel(by_column, n, pieces, partial, grad_out, normal_in, gain, *refs):
+    count = len(by_column)
+    arrays, (gathered, grad_in, sums), refs = refs[:count], refs[count : count + 3], refs[count + 3 :]
+    outs, (from_left, from_right, total, *sems), refs = refs[:count], refs[count : count + 7], refs[count + 7 :]
+    side = GradientSum(by_column, arrays, outs, refs[:count], refs[count:])
     backward_exchange_kernel(
-        n, pieces, partial, grad_out, normal_in, gain, gathered, grad_in, sums, from_left, from_right, total,
-        rs_send, rs_recv, ag_send, ag_recv, side=side
+        n, pieces, partial, grad_out, normal_in, gain, gathered, grad_in, sums, from_left, from_right, total, *sems, side=side
     )
 
 
@@ -476,156 +482,220 @@
 CAST_ROWS = 64
 
 
-def fetch_kernel(by_column, casts, *refs):
-    count = len(by_column)
-    shards, small, wides, refs = refs[:count], refs[count], refs[count + 1 : count + 1 + casts], refs[count + 1 + casts :]
-    outs, out_small, refs = refs[:count], refs[count], refs[count + 1 :]
-    lows, refs = refs[: casts * LAYERS], refs[casts * LAYERS :]
-    buffers, (cast_sems, sends, recvs, small_send, small_recv) = refs[:casts], refs[casts:]
-    half = lax.axis_index("fsdp")
-    ctx = lax.axis_index("ctx")
-    pair, across = jnp.bitwise_xor(ctx, 1), jnp.bitwise_xor(ctx, 2)
-    peers = ({"fsdp": 1 - half}, {"ctx": across}, {"ctx": pair}, {"ctx": pair})
-
-    barrier = pltpu.get_barrier_semaphore()
-    for peer in peers[:3]:
-        pl.semaphore_signal(barrier, inc=1, device_id=peer, device_id_type=MESH)
-    pl.semaphore_wait(barrier, 3)
-
-    def rows_of(which, quarter, part, base=0):
-        parts = fetch_parts(shards[which].shape[0])
-        height = shards[which].shape[0] // 4 // parts
-        return pl.ds(pl.multiple_of(base + (quarter * parts + part) * height, 16), height)
-
-    def place(which, side, quarter, part):
-        rows, cols = shards[which].shape
-        if by_column[which]:
-            return outs[which].at[rows_of(which, quarter, part), pl.ds(pl.multiple_of(side * cols, 128), cols)]
-        return outs[which].at[rows_of(which, quarter, part, side * rows)]
-
-    def copy(which, stage, part, arriving=False):
-        quarter = (ctx, ctx, ctx, across)[stage]
-        src = shards[which].at[rows_of(which, quarter, part)]
-        dst = place(which, half, quarter, part)
+class Quarters:
+    def __init__(self, shards, outs, sends, recvs):
+        self.shards, self.outs, self.sends, self.recvs = shards, outs, sends, recvs
+        self.half = lax.axis_index("fsdp")
+        self.ctx = lax.axis_index("ctx")
+        self.pair, self.across = jnp.bitwise_xor(self.ctx, 1), jnp.bitwise_xor(self.ctx, 2)
+        self.targets = ({"fsdp": 1 - self.half}, {"ctx": self.across}, {"ctx": self.pair}, {"ctx": self.pair})
+        self.peers = self.targets[:3]
+        self.each = [
+            (which, part) for which in range(len(shards)) for part in range(fetch_parts(shards[which].shape[0]))
+        ]
+
+    def rows_of(self, which, quarter, part):
+        parts = fetch_parts(self.shards[which].shape[0])
+        height = self.shards[which].shape[0] // 4 // parts
+        return pl.ds(pl.multiple_of((quarter * parts + part) * height, 16), height)
+
+    def place(self, which, side, quarter, part):
+        cols = self.shards[which].shape[1]
+        return self.outs[which].at[
+            self.rows_of(which, quarter, part), pl.ds(pl.multiple_of(side * cols, 128), cols)
+        ]
+
+    def copy(self, stage, item, arriving=False):
+        which, part = item
+        quarter = (self.ctx, self.ctx, self.ctx, self.across)[stage]
+        src = self.shards[which].at[self.rows_of(which, quarter, part)]
+        dst = self.place(which, self.half, quarter, part)
         if stage > 0:
-            src = dst = place(which, 1 - half, quarter, part)
+            src = dst = self.place(which, 1 - self.half, quarter, part)
         if arriving:
-            quarter = (ctx, across, pair, jnp.bitwise_xor(ctx, 3))[stage]
-            dst = place(which, 1 - half, quarter, part)
+            quarter = (self.ctx, self.across, self.pair, jnp.bitwise_xor(self.ctx, 3))[stage]
+            dst = self.place(which, 1 - self.half, quarter, part)
         return pltpu.make_async_remote_copy(
             src_ref=src,
             dst_ref=dst,
-            send_sem=sends.at[which, stage, part],
-            recv_sem=recvs.at[which, stage, part],
-            device_id=peers[stage],
+            send_sem=self.sends.at[which, stage, part],
+            recv_sem=self.recvs.at[which, stage, part],
+            device_id=self.targets[stage],
             device_id_type=MESH,
         )
 
-    def small_copy(side):
+    def begin(self):
+        for item in self.each:
+            self.copy(0, item).start()
+
+    def keep_own(self):
+        for shard, out in zip(self.shards, self.outs):
+            cols = shard.shape[1]
+            out[:, pl.ds(pl.multiple_of(self.half * cols, 128), cols)] = shard[...]
+
+    def crossed(self, item):
+        self.copy(0, item, True).wait_recv()
+        self.copy(1, item).start()
+        self.copy(2, item).start()
+
+    def forwarded(self, item):
+        self.copy(1, item, True).wait_recv()
+        self.copy(3, item).start()
+
+    def finish(self):
+        for stage in (2, 3):
+            for item in self.each:
+                self.copy(stage, item, True).wait_recv()
+        for stage in range(4):
+            for item in self.each:
+                self.copy(stage, item).wait_send()
+
+
+class QuartersSide(Quarters):
+    CROSSED, APART, FORWARDED = 4, 3, 3
+
+    def start(self):
+        self.begin()
+        self.keep_own()
+
+    @property
+    def ticks(self):
+        return self.CROSSED + self.FORWARDED + self.APART * (len(self.each) - 1) + 1
+
+    def at(self, tick):
+        for at, item in enumerate(self.each):
+            due = self.CROSSED + self.APART * at
+
+            @pl.when(tick == due)
+            def _():
+                self.crossed(item)
+
+            @pl.when(tick == due + self.FORWARDED)
+            def _():
+                self.forwarded(item)
+
+    def drain(self):
+        self.finish()
+
+
+def fetch_kernel(counts, jobs, *refs):
+    refs = list(refs)
+
+    def take(count):
+        taken = refs[:count]
+        del refs[:count]
+        return taken
+
+    shard_count, small_count, wide_count, low_count = counts
+    shards, smalls, wides = take(shard_count), take(small_count), take(wide_count)
+    outs, out_smalls, lows = take(shard_count), take(small_count), take(low_count)
+    buffers = take(len(jobs))
+    cast_sems, sends, recvs, small_sends, small_recvs = refs
+    quarters = Quarters(shards, outs, sends, recvs)
+
+    barrier = pltpu.get_barrier_semaphore()
+    for peer in quarters.peers:
+        pl.semaphore_signal(barrier, inc=1, device_id=peer, device_id_type=MESH)
+    pl.semaphore_wait(barrier, 3)
+
+    def small_copy(at, side):
+        cols = smalls[at].shape[1]
+        return pltpu.make_async_remote_copy(
+            src_ref=smalls[at],
+            dst_ref=out_smalls[at].at[:, pl.ds(pl.multiple_of(side * cols, 128), cols)],
+            send_sem=small_sends.at[at],
+            recv_sem=small_recvs.at[at],
+            device_id=quarters.peers[0],
+            device_id_type=MESH,
+        )
+
+    def load(at):
+        which, layer, _, _ = jobs[at]
+        return pltpu.make_async_copy(wides[which].at[layer], buffers[at], cast_sems.at[at])
+
+    quarters.begin()
+    for at in range(small_count):
+        small_copy(at, quarters.half).start()
+    for at in range(len(jobs)):
+        load(at).start()
+    quarters.keep_own()
+    for small, out in zip(smalls, out_smalls):
         cols = small.shape[1]
-        return pltpu.make_async_remote_copy(
-            src_ref=small,
-            dst_ref=out_small.at[:, pl.ds(pl.multiple_of(side * cols, 128), cols)],
-            send_sem=small_send,
-            recv_sem=small_recv,
-            device_id=peers[0],
-            device_id_type=MESH,
-        )
-
-    each = [(which, part) for which in range(count) for part in range(fetch_parts(shards[which].shape[0]))]
-    for which, part in each:
-        copy(which, 0, part).start()
-    small_copy(half).start()
-    to_cast = [(layer, which) for layer in range(LAYERS) for which in range(casts)]
-
-    def load(layer, which):
-        return pltpu.make_async_copy(
-            wides[which].at[layer], buffers[which].at[layer], cast_sems.at[which, layer]
-        )
-
-    for layer, which in to_cast:
-        load(layer, which).start()
-    for shard, out, column in zip((*shards, small), (*outs, out_small), (*by_column, True)):
-        rows, cols = shard.shape
-        if column:
-            out[:, pl.ds(pl.multiple_of(half * cols, 128), cols)] = shard[...]
-        else:
-            out[pl.ds(pl.multiple_of(half * rows, 16), rows), :] = shard[...]
-    for layer, which in to_cast:
-        load(layer, which).wait()
-        low = lows[which * LAYERS + layer]
-
-        def cast(at, carry):
-            rows = pl.ds(pl.multiple_of(at * CAST_ROWS, CAST_ROWS), CAST_ROWS)
-            low[rows, :] = buffers[which][layer, rows, :].astype(LOW)
+        out[:, pl.ds(pl.multiple_of(quarters.half * cols, 128), cols)] = small[...]
+    for at, (_, _, low, first) in enumerate(jobs):
+        load(at).wait()
+
+        def cast(step, carry):
+            start = pl.multiple_of(step * CAST_ROWS, CAST_ROWS)
+            lows[low][pl.ds(first + start, CAST_ROWS), :] = buffers[at][pl.ds(start, CAST_ROWS), :].astype(LOW)
             return carry
 
-        lax.fori_loop(0, low.shape[0] // CAST_ROWS, cast, 0)
-    for at in range(len(each) + 1):
-        if at < len(each):
-            copy(each[at][0], 0, each[at][1], True).wait_recv()
-            copy(each[at][0], 1, each[at][1]).start()
-            copy(each[at][0], 2, each[at][1]).start()
+        lax.fori_loop(0, buffers[at].shape[0] // CAST_ROWS, cast, 0)
+    last = len(quarters.each)
+    for at in range(last + 1):
+        if at < last:
+            quarters.crossed(quarters.each[at])
         if at > 0:
-            copy(each[at - 1][0], 1, each[at - 1][1], True).wait_recv()
-            copy(each[at - 1][0], 3, each[at - 1][1]).start()
-    small_copy(1 - half).wait_recv()
-    for stage in (2, 3):
-        for which, part in each:
-            copy(which, stage, part, True).wait_recv()
-    for stage in range(4):
-        for which, part in each:
-            copy(which, stage, part).wait_send()
-    small_copy(half).wait_send()
-
-
-def fetch_first(shards, by_column, small, wides, collective_id):
-    def whole(shape, column):
-        return (shape[0], 2 * shape[1]) if column else (2 * shape[0], shape[1])
-
-    shapes = [whole(shard.shape, column) for shard, column in zip(shards, by_column)]
-    shapes.append(whole(small.shape, True))
-    gathered = len(shapes)
-    for wide in wides:
-        assert wide.shape[0] == LAYERS and wide.shape[1] % CAST_ROWS == 0
-        shapes += [wide.shape[1:]] * LAYERS
-    sems = pltpu.SemaphoreType.DMA((len(shards), 4, max(fetch_parts(shard.shape[0]) for shard in shards)))
+            quarters.forwarded(quarters.each[at - 1])
+    for at in range(small_count):
+        small_copy(at, 1 - quarters.half).wait_recv()
+    quarters.finish()
+    for at in range(small_count):
+        small_copy(at, quarters.half).wait_send()
+
+
+def quarter_sems(shards):
+    most = max(fetch_parts(shard.shape[0]) for shard in shards)
+    return [pltpu.SemaphoreType.DMA((len(shards), 4, most))] * 2
+
+
+def gathered_shape(shard):
+    return jax.ShapeDtypeStruct((shard.shape[0], 2 * shard.shape[1]), shard.dtype)
+
+
+def fetch_first(shards, smalls, wides, jobs, low_shapes, collective_id):
+    counts = (len(shards), len(smalls), len(wides), len(low_shapes))
+    out_shape = tuple(gathered_shape(array) for array in (*shards, *smalls))
+    out_shape += tuple(jax.ShapeDtypeStruct(shape, LOW) for shape in low_shapes)
     return pl.pallas_call(
-        functools.partial(fetch_kernel, by_column, len(wides)),
-        out_shape=tuple(jax.ShapeDtypeStruct(shape, LOW) for shape in shapes),
-        in_specs=in_vmem(gathered) + [pl.BlockSpec(memory_space=pl.ANY)] * len(wides),
-        out_specs=tuple(in_vmem(len(shapes))),
-        scratch_shapes=[pltpu.VMEM(wide.shape, WIDE) for wide in wides]
-        + [
-            pltpu.SemaphoreType.DMA((len(wides), LAYERS)),
-            sems,
-            sems,
-            pltpu.SemaphoreType.DMA,
-            pltpu.SemaphoreType.DMA,
-        ],
+        functools.partial(fetch_kernel, counts, jobs),
+        out_shape=out_shape,
+        in_specs=in_vmem(len(shards) + len(smalls)) + [pl.BlockSpec(memory_space=pl.ANY)] * len(wides),
+        out_specs=tuple(in_vmem(len(out_shape))),
+        scratch_shapes=[pltpu.VMEM(wides[job[0]].shape[1:], WIDE) for job in jobs]
+        + [pltpu.SemaphoreType.DMA((len(jobs),))]
+        + quarter_sems(shards)
+        + [pltpu.SemaphoreType.DMA((len(smalls),))] * 2,
         compiler_params=pltpu.CompilerParams(
-            collective_id=collective_id, has_side_effects=True, vmem_limit_bytes=40 << 20
+            collective_id=collective_id, has_side_effects=True, vmem_limit_bytes=44 << 20
         ),
         name="fetch_first",
-    )(*shards, small, *wides)
-
-
-def forward_exchange(partial, residual, bias, gain, shift, n, collective_id):
+    )(*shards, *smalls, *wides)
+
+
+def forward_exchange(partial, residual, bias, gain, shift, n, collective_id, shard=None):
     rows, width = partial.shape
+    out_shape = (
+        jax.ShapeDtypeStruct((rows, width), LOW),
+        jax.ShapeDtypeStruct(residual.shape, WIDE),
+    )
+    scratch = exchange_scratch(n, rows, width, PIECES)
+    kernel, extra = forward_exchange_kernel, ()
+    if shard is not None:
+        out_shape += (gathered_shape(shard),)
+        scratch = scratch + quarter_sems((shard,))
+        kernel, extra = forward_fetch_kernel, (shard,)
     return pl.pallas_call(
-        functools.partial(forward_exchange_kernel, n, PIECES),
-        out_shape=(
-            jax.ShapeDtypeStruct((rows, width), LOW),
-            jax.ShapeDtypeStruct(residual.shape, WIDE),
-        ),
-        in_specs=in_vmem(5),
-        out_specs=tuple(in_vmem(2)),
-        scratch_shapes=exchange_scratch(n, rows, width, PIECES),
+        functools.partial(kernel, n, PIECES),
+        out_shape=out_shape,
+        in_specs=in_vmem(5 + len(extra)),
+        out_specs=tuple(in_vmem(len(out_shape))),
+        scratch_shapes=scratch,
         compiler_params=pltpu.CompilerParams(
             collective_id=collective_id, has_side_effects=True, vmem_limit_bytes=40 << 20
         ),
         name="forward_exchange",
-    )(partial, residual, bias[None, :], gain[None, :], shift[None, :])
+    )(partial, residual, bias[None, :], gain[None, :], shift[None, :], *extra)
 
 
 def backward_exchange(partial, grad_out, normal_in, gain, n, collective_id, arrays=(), by_column=()):
@@ -1061,43 +1131,41 @@
     def own_slice(full):
         return lax.dynamic_slice_in_dim(full, own_start, own_rows, axis=0)
 
-    small = jnp.concatenate(
-        [output_bias, outer_bias, first_gain, first_shift, second_gain, second_shift], axis=0
-    ).astype(LOW)
-    small = jnp.pad(small, ((0, -small.shape[0] % 16), (0, 0)))
+    smalls = (output_bias, outer_bias, first_gain, first_shift, second_gain, second_shift)
+    qkv_weights = [jnp.swapaxes(weight, 1, 2) for weight in (query_weight, key_weight, value_weight)]
 
     def qkv_shard(layer):
-        return jnp.concatenate(
-            [query_weight[layer].T, key_weight[layer].T, value_weight[layer].T], axis=0
-        ).astype(LOW)
+        return jnp.concatenate([weight[layer] for weight in qkv_weights], axis=0).astype(LOW)
+
+    def gather(array, axis):
+        return lax.all_gather(array, "fsdp", axis=axis, tiled=True)
 
     projections = output_weight.astype(LOW).reshape(-1, output_weight.shape[2])
-    if lax.axis_size("fsdp") == 2:
-        qkv_first, projections, small, *lows = fetch_first(
-            (qkv_shard(0), projections), (True, True), small, (inner_weight, outer_weight), 17
-        )
-        inner_low, outer_low = lows[:LAYERS], lows[LAYERS:]
+    paired = lax.axis_size("fsdp") == 2
+    if paired:
+        wides = (inner_weight, outer_weight, *qkv_weights)
+        jobs = [(which, layer, which * LAYERS + layer, 0) for layer in range(LAYERS) for which in range(2)]
+        shapes = [wide.shape[1:] for wide in wides[:2] for _ in range(LAYERS)]
+        for layer in range(1, LAYERS):
+            jobs += [(2 + at, layer, len(shapes), at * columns) for at in range(3)]
+            shapes.append((3 * columns, qkv_weights[0].shape[2]))
+        results = fetch_first((qkv_shard(0), projections), smalls, wides, tuple(jobs), shapes, 17)
+        qkv_first, projections, *results = results
+        smalls, lows = results[: len(smalls)], results[len(smalls) :]
+        inner_low, outer_low, qkv_low = lows[:LAYERS], lows[LAYERS : 2 * LAYERS], [None, *lows[2 * LAYERS :]]
     else:
-        qkv_first = lax.all_gather(qkv_shard(0), "fsdp", axis=1, tiled=True)
-        projections = lax.all_gather(projections, "fsdp", axis=1, tiled=True)
-        small = lax.all_gather(small, "fsdp", axis=1, tiled=True)
+        qkv_first, projections = gather(qkv_shard(0), 1), gather(projections, 1)
+        smalls = [gather(small, 1) for small in smalls]
         inner_low, outer_low = inner_weight.astype(LOW), outer_weight.astype(LOW)
-    small = small.astype(WIDE)
+        qkv_low = [qkv_shard(layer) for layer in range(LAYERS)]
     projections = projections.reshape(LAYERS, columns, width)
+    smalls = [lax.reduce_precision(small, 8, 7) for small in smalls]
 
     def vector(kind, layer):
-        return small[kind * LAYERS + layer]
-
-    def fetch(layer):
-        qkv = qkv_first
-        if layer > 0:
-            qkv = lax.all_gather(qkv_shard(layer), "fsdp", axis=1, tiled=True)
-        out = projections[layer]
-        inner = lax.all_gather(inner_low[layer], "fsdp", axis=0, tiled=True)
-        outer = lax.all_gather(outer_low[layer], "fsdp", axis=1, tiled=True)
-        return (qkv, out, inner, outer)
-
-    weights = [fetch(layer) for layer in range(LAYERS)]
+        return smalls[kind][layer]
+
+    w_qkvs = [qkv_first] + [None if paired else gather(qkv_low[layer], 1) for layer in range(1, LAYERS)]
+    feeds = [(gather(inner_low[layer], 0), gather(outer_low[layer], 1)) for layer in range(LAYERS)]
 
     hidden_rows = hidden.reshape(rows, width)
     residual = own_slice(hidden_rows)
@@ -1105,20 +1173,29 @@
     normed = (hat_full * vector(2, 0) + vector(3, 0)).astype(LOW)
     kept = []
     for layer in range(LAYERS):
-        w_qkv, w_out, w_inner, w_outer = weights[layer]
+        w_qkv, w_out, (w_inner, w_outer) = w_qkvs[layer], projections[layer], feeds[layer]
         bias_qkv = jnp.concatenate(
             [query_bias[layer], jnp.zeros_like(query_bias[layer]), value_bias[layer]]
         )
         qkv = (product(w_qkv, normed, 1, 1) + bias_qkv[:, None]).astype(LOW)
         attended, attended_wide, log_total, held = attend(qkv, lengths, scale, 2 * layer)
         branch = product(attended, w_out, 0, 0).astype(LOW)
-        normed_two, middle = forward_exchange(
-            branch, residual, vector(0, layer), vector(4, layer), vector(5, layer), tp_size, 2 * layer + 4
-        )
+        normed_two, middle, *fetched = forward_exchange(
+            branch,
+            residual,
+            vector(0, layer),
+            vector(4, layer),
+            vector(5, layer),
+            tp_size,
+            2 * layer + 4,
+            qkv_low[layer + 1] if paired and layer + 1 < LAYERS else None,
+        )
+        if fetched:
+            w_qkvs[layer + 1] = fetched[0]
         inner_pre = product(normed_two, w_inner, 1, 0) + inner_bias[layer]
-        active = gelu_value(inner_pre).astype(LOW)
+        active, slope = gelu_value(inner_pre).astype(LOW), gelu_slope(inner_pre)
         kept.append(
-            (residual, normed, qkv, attended, attended_wide, log_total, held, middle, normed_two, inner_pre, active)
+            (residual, normed, qkv, attended, attended_wide, log_total, held, middle, normed_two, slope, active)
         )
         branch = product(active, w_outer, 1, 0).astype(LOW)
         if layer + 1 < LAYERS:
@@ -1154,7 +1231,7 @@
     vectors = [None] * LAYERS
     biases = [None] * LAYERS
     for layer in reversed(range(LAYERS)):
-        w_qkv, w_out, w_inner, w_outer = weights[layer]
+        w_qkv, w_out, (w_inner, w_outer) = w_qkvs[layer], projections[layer], feeds[layer]
         (
             residual,
             normed,
@@ -1165,13 +1242,15 @@
             held,
             middle,
             normed_two,
-            inner_pre,
+            slope,
             active,
         ) = kept[layer]
         grad_active = product(grad_low, w_outer, 1, 1)
-        grad_inner = (grad_active * gelu_slope(inner_pre)).astype(LOW)
+        grad_inner = (grad_active * slope).astype(LOW)
         branch = product(grad_inner, w_inner, 1, 1).astype(LOW)
-        grad_outer_w = product(active, grad_low, 0, 0).astype(LOW)
+        split = active.shape[1] // 2
+        grad_outer_w = product(active[:, :split], grad_low, 0, 0).astype(LOW)
+        grad_outer_rest = product(active[:, split:], grad_low, 0, 0).astype(LOW)
         grad_inner_w = product(normed_two, grad_inner, 0, 0).astype(LOW)
         grad_mid_low, grad_middle, sums_two, *summed_two = exchange_back(
             branch, grad_own, middle, vector(4, layer), 2 * layer + 8, (grad_inner_w, grad_outer_w), (False, True)
@@ -1200,7 +1279,7 @@
         if layer == 0:
             output = shared[0].astype(WIDE)
         grad_low, grad_own, sums_one, *summed_one = exchange_back(
-            branch, grad_middle, residual, vector(2, layer), 2 * layer + 9, (grad_qkv_w, grad_output_w), (True, True)
+            branch, grad_middle, residual, vector(2, layer), 2 * layer + 9, (grad_qkv_w, grad_output_w, grad_outer_rest), (True, True, True)
         )
         grads[layer] = (*summed_one, *summed_two)
         vectors[layer] = [
@@ -1237,6 +1316,11 @@
     def stacked(which):
         return jnp.stack([grads[layer][which] for layer in range(LAYERS)]).astype(WIDE)
 
+    def joined(first, second):
+        return jnp.stack(
+            [jnp.concatenate([grads[layer][first], grads[layer][second]]) for layer in range(LAYERS)]
+        ).astype(WIDE)
+
     def turned(start):
         return jnp.stack([grads[layer][0][start : start + columns].T for layer in range(LAYERS)]).astype(WIDE)
 
@@ -1247,8 +1331,8 @@
         turned(columns),
         turned(2 * columns),
         stacked(1),
-        stacked(2),
         stacked(3),
+        joined(4, 2),
         bias_sums[:, :columns],
         bias_sums[:, 2 * columns : 3 * columns],
         bias_sums[:, 3 * columns :],

time: 664 us -> 665 us (level)
  Pallas kernels: 495 us -> 504 us
  other arithmetic: 33.9 us -> 25.8 us
    dot_general x24 -> x26, matrix products: 82.3 us -> 84 us  [product(): lax.dot_general(left_side, right_side, (((left_axis,), (right_axis,)), ((...]
  transfers between devices with their start and end apart: 6 -> 5, of which waited for: 1 -> 1; matrix products, arithmetic and copies ran while one was open for 8% -> 8% of each run, Pallas kernels for 31% -> 32%
where the time goes in v7:
time: 665 us; the launch traced here: 656 us
  Pallas kernels  504 us (76%)
  matrix products  84 us (13%)
  other arithmetic  25.8 us (4%)
  local copies, waits for them, and re-layouts  23.6 us (4%)
  between operations  15.5 us (2%)
    pallas_call x4, Pallas kernels, backward_exchange(): pl.pallas_call(functools.partial(kernel, n, PIECES), out_shape=out_shape,...  222 us
    pallas_call x3, Pallas kernels, forward_exchange(): pl.pallas_call(functools.partial(kernel, n, PIECES), out_shape=out_shape,...  135 us
    dot_general x26, matrix products, product(): lax.dot_general(left_side, right_side, (((left_axis,), (right_axis,)), ((...  84 us
    pallas_call x2, Pallas kernels, attend_back(): pl.pallas_call(functools.partial(attend_back_kernel, scale, own is not No...  57.4 us
    pallas_call x2, Pallas kernels, attend(): pl.pallas_call(functools.partial(attend_kernel, scale), out_shape=(jax.Sh...  47.1 us
    pallas_call x1, Pallas kernels, fetch_first(): pl.pallas_call(functools.partial(fetch_kernel, counts, jobs), out_shape=o...  26.5 us
    pallas_call x1, Pallas kernels, sum_all(): pl.pallas_call(functools.partial(sum_all_kernel, axes), out_shape=jax.Sha...  16.8 us
  transfers between devices with their start and end apart: 5, of which 1 were waited for; matrix products, arithmetic and copies ran while one was open for 8% of the time, Pallas kernels for 32%

profile of v7, /device:TPU:0, one launch (start us, length us, event | category | flops | bytes accessed | tf_op | source)
XLA Modules:
  0.0 655.6 jit_solution(10085215684210404897)
XLA Ops:
  11.7 26.5 %fetch_first.1 = (bf16[960,1280]{1,0:T(8,128)(2,1)}, bf16[640,1280]{1,0:T(8,128)(2,1)S(1)}, f32[2,1280]{1,0:T(2,128)S(1)}, f32[2,1280]{1,0:T(2,128)S(1)}, f32[2,...) custom-call(bf16[960,640]{1,0:T(8,128)(2,1)S(1)} %pad_maximum_fusion, ...), custom_call_target="tpu_custom_call" | custom-call | tf_op jit(solution)/shard_map/fetch_first/pallas_call | solution.py:660
  47.2 5.7 add_convert_fusion.2.qkv
  53.0 23.6 %attend.2 = (bf16[320,512]{1,0:T(8,128)(2,1)}, f32[320,512]{1,0:T(8,128)}, f32[8,512]{1,0:T(8,128)}, bf16[3,640,512]{2,1,0:T(8,128)(2,1)}) custom-call(s32[1]{0:T(128)S(6)} %copy.35.length, bf16[960,512]{1,0:T(8,128)(2,1)} %add_convert_fusion.2.qkv), custom_call_target="tpu_custom_call" | custom-call | tf_op jit(solution)/shard_map/attend/pallas_call | solution.py:834
  79.6 47.1 %forward_exchange.3 = (bf16[512,1280]{1,0:T(8,128)(2,1)S(1)}, f32[128,1280]{1,0:T(8,128)S(1)}, bf16[960,1280]{1,0:T(8,128)(2,1)S(1)}) custom-call(bf16[512,1280]{1,0:T(8,128)(2,1)S(1)} %convolution_convert_fusion.15.partial, f32[128,1280]{1,0:T(8,128)S(1)} %dynamic-slice_bitcast_fusion.residual.normal_in, f32[1,1280]{1,0:T(1,128)S(1)} %get-tuple-element.170.bias, ...), custom_call_target="tpu_custom_call" | custom-call | tf_op jit(solution)/shard_map/forward_exchange/pallas_call | solution.py:688
  131.6 6.2 multiply_convert_fusion.1
  138.2 4.3 convolution_convert_fusion.14.partial
  142.5 45.2 %forward_exchange.4 = (bf16[512,1280]{1,0:T(8,128)(2,1)S(1)}, f32[128,1280]{1,0:T(8,128)S(1)}) custom-call(bf16[512,1280]{1,0:T(8,128)(2,1)S(1)} %convolution_convert_fusion.14.partial, f32[128,1280]{1,0:T(8,128)S(1)} %get-tuple-element.86.residual.normal_in, f32[1,1280]{1,0:T(1,128)S(1)} %get-tuple-element.164.bias, f32[1,1280]{1,0:T(1,128)S(1)} %get-tuple-element.162.gain, ...), custom_call_target="tpu_custom_call" | custom-call | tf_op jit(solution)/shard_map/forward_exchange/pallas_call | solution.py:688
  191.2 23.5 %attend.3 = (bf16[320,512]{1,0:T(8,128)(2,1)}, f32[320,512]{1,0:T(8,128)}, f32[8,512]{1,0:T(8,128)}, bf16[3,640,512]{2,1,0:T(8,128)(2,1)}) custom-call(s32[1]{0:T(128)S(6)} %copy.35.length, bf16[960,512]{1,0:T(8,128)(2,1)} %add_convert_fusion.1.qkv), custom_call_target="tpu_custom_call" | custom-call | tf_op jit(solution)/shard_map/attend/pallas_call | solution.py:834
  216.6 42.2 %forward_exchange.5 = (bf16[512,1280]{1,0:T(8,128)(2,1)S(1)}, f32[128,1280]{1,0:T(8,128)S(1)}) custom-call(bf16[512,1280]{1,0:T(8,128)(2,1)S(1)} %convolution_convert_fusion.13.partial, f32[128,1280]{1,0:T(8,128)S(1)} %get-tuple-element.90.residual.normal_in, f32[1,1280]{1,0:T(1,128)S(1)} %get-tuple-element.169.bias, f32[1,1280]{1,0:T(1,128)S(1)} %get-tuple-element.167.gain, ...), custom_call_target="tpu_custom_call" | custom-call | tf_op jit(solution)/shard_map/forward_exchange/pallas_call | solution.py:688
  259.7 5.3 multiply_convert_fusion
  268.3 5.9 convert_reduce_fusion
  274.2 3.6 convolution_convert_fusion.1.refs_0_
  277.9 3.0 convolution_convert_fusion.11.partial
  280.8 56.3 %backward_exchange.4 = (bf16[512,1280]{1,0:T(8,128)(2,1)}, f32[128,1280]{1,0:T(8,128)}, f32[8,1280]{1,0:T(8,128)}, bf16[640,1280]{1,0:T(8,128)(2,1)}, bf16[640,640]{1,0:T(8,128)(2,1)}) custom-call(bf16[512,1280]{1,0:T(8,128)(2,1)} %convolution_convert_fusion.11.partial, f32[128,1280]{1,0:T(8,128)} %get-tuple-element.134.grad_out, f32[128,1280]{1,0:T(8,128)} %copy-done.1, ...), custom_call_target="tpu_custom_call" | custom-call | tf_op jit(solution)/shard_map/backward_exchange/pallas_call | solution.py:715
  337.1 2.9 convolution_convert_fusion.12
  340.1 2.7 convolution_convert_fusion.19.grad
  342.8 26.2 %attend_back.2 = bf16[960,512]{1,0:T(8,128)(2,1)} custom-call(s32[1]{0:T(128)S(6)} %copy.35.length, bf16[960,512]{1,0:T(8,128)(2,1)} %add_convert_fusion.1.qkv, bf16[3,640,512]{2,1,0:T(8,128)(2,1)} %get-tuple-element.97.held, bf16[320,512]{1,0:T(8,128)(2,1)} %convolution_convert_fusion.19.grad, f32[320,512]{1,0:T(8,128)} %get-tuple-element.99.out_wide, ...), custom_call_target="tpu_custom_call" | custom-call | tf_op jit(solution)/shard_map/attend_back/pallas_call | solution.py:1061
  372.2 2.9 convolution_convert_fusion.3.refs_0_
  380.9 55.7 %backward_exchange.5 = (bf16[512,1280]{1,0:T(8,128)(2,1)}, f32[128,1280]{1,0:T(8,128)}, f32[8,1280]{1,0:T(8,128)}, bf16[960,640]{1,0:T(8,128)(2,1)}, bf16[320,640]{1,0:T(8,128)(2,1)}, /*index=5*/bf16[640,640]{1,0:T(8,128)(2,1)}) custom-call(bf16[512,1280]{1,0:T(8,128)(2,1)} %convolution_convert_fusion.10.partial, f32[128,1280]{1,0:T(8,128)} %get-tuple-element.102.grad_out, ...), custom_call_target="tpu_custom_call" | custom-call | tf_op jit(solution)/shard_map/backward_exchange/pallas_call | solution.py:715
  436.6 3.6 convolution_convert_fusion.4.refs_2_
  443.5 2.8 convert_reduce_fusion.1
  446.4 3.6 convolution_convert_fusion.refs_0_
  450.0 3.0 convolution_convert_fusion.9.partial
  452.9 54.6 %backward_exchange.6 = (bf16[512,1280]{1,0:T(8,128)(2,1)}, f32[128,1280]{1,0:T(8,128)}, f32[8,1280]{1,0:T(8,128)}, bf16[640,1280]{1,0:T(8,128)(2,1)}, bf16[640,640]{1,0:T(8,128)(2,1)}) custom-call(bf16[512,1280]{1,0:T(8,128)(2,1)} %convolution_convert_fusion.9.partial, f32[128,1280]{1,0:T(8,128)} %get-tuple-element.104.grad_out, f32[128,1280]{1,0:T(8,128)} %copy-done.3, ...), custom_call_target="tpu_custom_call" | custom-call | tf_op jit(solution)/shard_map/backward_exchange/pallas_call | solution.py:715
  507.6 2.7 convolution_convert_fusion.18.grad
  511.1 31.2 %attend_back.3 = (bf16[960,512]{1,0:T(8,128)(2,1)}, bf16[512,1280]{1,0:T(8,128)(2,1)}) custom-call(s32[1]{0:T(128)S(6)} %copy.35.length, bf16[960,512]{1,0:T(8,128)(2,1)} %add_convert_fusion.2.qkv, bf16[3,640,512]{2,1,0:T(8,128)(2,1)} %get-tuple-element.75.held, bf16[320,512]{1,0:T(8,128)(2,1)} %convolution_convert_fusion.18.grad, ...), custom_call_target="tpu_custom_call" | custom-call | tf_op jit(solution)/shard_map/attend_back/pallas_call | solution.py:1061
  542.4 4.0 convolution_convert_fusion.8.partial
  548.3 3.1 convolution_convert_fusion.2.refs_0_
  553.9 55.2 %backward_exchange.7 = (bf16[512,1280]{1,0:T(8,128)(2,1)}, f32[128,1280]{1,0:T(8,128)}, f32[8,1280]{1,0:T(8,128)}, bf16[960,640]{1,0:T(8,128)(2,1)}, bf16[320,640]{1,0:T(8,128)(2,1)}, /*index=5*/bf16[640,640]{1,0:T(8,128)(2,1)}) custom-call(bf16[512,1280]{1,0:T(8,128)(2,1)} %convolution_convert_fusion.8.partial, f32[128,1280]{1,0:T(8,128)} %get-tuple-element.111.grad_out, ...), custom_call_target="tpu_custom_call" | custom-call | tf_op jit(solution)/shard_map/backward_exchange/pallas_call | solution.py:715
  610.8 16.8 %sum_all.1 = f32[24,640]{1,0:T(8,128)} custom-call(f32[16,1280]{1,0:T(8,128)} %pad.8.vectors, f32[8,640]{1,0:T(8,128)} %reshape.103.biases), custom_call_target="tpu_custom_call" | custom-call | tf_op jit(solution)/shard_map/sum_all/pallas_call | solution.py:462
  642.4 3.3 maximum_convert_fusion.1
  645.6 3.2 maximum_convert_fusion
  (196 shorter events, 64.1 us)
Async XLA Ops:
  7.2 124.4 %all-gather.5.cloned.1.call-start = ((), (), s32[]{:S(2)}) async-start(), calls=%async_computation.1 | async-start | bytes 4915200 | tf_op jit(solution)/shard_map/all_gather | solution.py:1141
  39.4 98.7 %all-gather.7.cloned.1.call-start = ((), (), s32[]{:S(2)}) async-start(), calls=%async_computation.2 | async-start | bytes 4915200 | tf_op jit(solution)/shard_map/all_gather | solution.py:1141
  40.2 219.5 %all-gather.9.cloned.1.call-start = ((), (), s32[]{:S(2)}) async-start(), calls=%async_computation.3 | async-start | bytes 4915200 | tf_op jit(solution)/shard_map/all_gather | solution.py:1141
  40.9 227.4 %all-gather.11.cloned.1.call-start = ((), (), s32[]{:S(2)}) async-start(), calls=%async_computation.4 | async-start | bytes 4915200 | tf_op jit(solution)/shard_map/all_gather | solution.py:1141
  41.5 339.4 %reduce-scatter.2.cloned.1.call-start = ((), (), s32[]{:S(2)}) async-start(), calls=%async_computation.5 | async-start | bytes 1638400 | tf_op jit(solution)/shard_map/reduce_scatter | solution.py:1260
  42.2 4.9 copy-start.49
  42.2 4.9 copy-start.50
  46.9 95.6 %copy-start.6 = (f32[1,1280]{1,0:T(1,128)}, f32[1,1280]{1,0:T(1,128)S(1)}, u32[]{:S(2)}) copy-start(f32[1,1280]{1,0:T(1,128)S(1)} %get-tuple-element.162.gain) | copy-start | bytes 15364
  47.0 32.6 %copy-start.5 = (f32[1,1280]{1,0:T(1,128)}, f32[1,1280]{1,0:T(1,128)S(1)}, u32[]{:S(2)}) copy-start(f32[1,1280]{1,0:T(1,128)S(1)} %get-tuple-element.168.gain) | copy-start | bytes 15364
  47.0 169.5 %copy-start.7 = (f32[1,1280]{1,0:T(1,128)}, f32[1,1280]{1,0:T(1,128)S(1)}, u32[]{:S(2)}) copy-start(f32[1,1280]{1,0:T(1,128)S(1)} %get-tuple-element.167.gain) | copy-start | bytes 15364
  47.2 29.4 %copy-start.18 = (bf16[640,1280]{1,0:T(8,128)(2,1)S(1)}, bf16[640,1280]{1,0:T(8,128)(2,1)}, u32[]{:S(2)}) copy-start(bf16[640,1280]{1,0:T(8,128)(2,1)} %copy-done.17) | copy-start | bytes 4915204
  79.6 58.2 %copy-start = (f32[128,1280]{1,0:T(8,128)}, f32[128,1280]{1,0:T(8,128)S(1)}, u32[]{:S(2)}) copy-start(f32[128,1280]{1,0:T(8,128)S(1)} %dynamic-slice_bitcast_fusion.residual.normal_in) | copy-start | bytes 1966084
  79.6 51.9 %copy-start.48 = (f32[2,1280]{1,0:T(2,128)S(1)}, f32[2,1280]{1,0:T(2,128)}, u32[]{:S(2)}) copy-start(f32[2,1280]{1,0:T(2,128)} %param.29) | copy-start | bytes 30724
  129.3 13.2 %copy-start.3 = (f32[128,1280]{1,0:T(8,128)}, f32[128,1280]{1,0:T(8,128)S(1)}, u32[]{:S(2)}) copy-start(f32[128,1280]{1,0:T(8,128)S(1)} %get-tuple-element.86.residual.normal_in) | copy-start | bytes 1966084
  138.2 50.6 %copy-start.15 = (bf16[960,1280]{1,0:T(8,128)(2,1)S(1)}, bf16[960,1280]{1,0:T(8,128)(2,1)}, u32[]{:S(2)}) copy-start(bf16[960,1280]{1,0:T(8,128)(2,1)} %copy-done.14) | copy-start | bytes 7372804
  187.8 28.8 %copy-start.4 = (f32[128,1280]{1,0:T(8,128)}, f32[128,1280]{1,0:T(8,128)S(1)}, u32[]{:S(2)}) copy-start(f32[128,1280]{1,0:T(8,128)S(1)} %get-tuple-element.90.residual.normal_in) | copy-start | bytes 1966084
  188.8 25.9 %copy-start.19 = (bf16[640,1280]{1,0:T(8,128)(2,1)S(1)}, bf16[640,1280]{1,0:T(8,128)(2,1)}, u32[]{:S(2)}) copy-start(bf16[640,1280]{1,0:T(8,128)(2,1)} %copy-done.17) | copy-start | bytes 4915204
  259.7 6.4 copy-start.24
  274.2 3.6 copy-start.54
  280.8 56.3 %copy-start.31 = (bf16[512,1280]{1,0:T(8,128)(2,1)S(1)}, bf16[512,1280]{1,0:T(8,128)(2,1)}, u32[]{:S(2)}) copy-start(bf16[512,1280]{1,0:T(8,128)(2,1)} %copy-done.30) | copy-start | bytes 3932164
  280.8 56.3 %copy-start.53 = (bf16[1280,1280]{1,0:T(8,128)(2,1)S(1)}, bf16[1280,1280]{1,0:T(8,128)(2,1)}, u32[]{:S(2)}) copy-start(bf16[1280,1280]{1,0:T(8,128)(2,1)} %all-gather.11.cloned.1.call-done) | copy-start | bytes 9830404
  342.7 27.8 %copy-start.32 = (bf16[512,1280]{1,0:T(8,128)(2,1)S(1)}, bf16[512,1280]{1,0:T(8,128)(2,1)}, u32[]{:S(2)}) copy-start(bf16[512,1280]{1,0:T(8,128)(2,1)} %get-tuple-element.98) | copy-start | bytes 3932164
  342.8 27.8 %copy-start.47 = (bf16[320,512]{1,0:T(8,128)(2,1)S(1)}, bf16[320,512]{1,0:T(8,128)(2,1)}, u32[]{:S(2)}) copy-start(bf16[320,512]{1,0:T(8,128)(2,1)} %get-tuple-element.89) | copy-start | bytes 983044
  380.9 55.7 %copy-start.57 = (bf16[512,1280]{1,0:T(8,128)(2,1)S(1)}, bf16[512,1280]{1,0:T(8,128)(2,1)}, u32[]{:S(2)}) copy-start(bf16[512,1280]{1,0:T(8,128)(2,1)} %get-tuple-element.175) | copy-start | bytes 3932164
  436.6 3.6 copy-start.56
  446.4 3.6 copy-start.51
  511.1 31.2 %copy-start.55 = (bf16[960,1280]{1,0:T(8,128)(2,1)S(1)}, bf16[960,1280]{1,0:T(8,128)(2,1)}, u32[]{:S(2)}) copy-start(bf16[960,1280]{1,0:T(8,128)(2,1)} %get-tuple-element.72) | copy-start | bytes 7372804
  542.3 4.0 copy-start.38
  542.3 4.2 copy-start.33
  542.3 4.2 copy-start.45
  553.9 77.3 %copy-start.36 = (bf16[960,640]{1,0:T(8,128)(2,1)S(1)}, bf16[960,640]{1,0:T(8,128)(2,1)}, u32[]{:S(2)}) copy-start(bf16[960,640]{1,0:T(8,128)(2,1)} %get-tuple-element.114) | copy-start | bytes 3686404
  609.1 22.2 %copy-start.34 = (bf16[512,1280]{1,0:T(8,128)(2,1)S(1)}, bf16[512,1280]{1,0:T(8,128)(2,1)}, u32[]{:S(2)}) copy-start(bf16[512,1280]{1,0:T(8,128)(2,1)} %get-tuple-element.109) | copy-start | bytes 3932164
  (32 other events, 65.4 us)
Sparse Core Ops, SparseCore 0:
  39.5 50.3 all-gather.4
  91.5 46.6 all-gather.6
  139.7 46.3 all-gather.8
  187.5 46.3 all-gather.10
  340.2 29.9 reduce-scatter.1

commit v8 on v7

--- a/solution.py
+++ b/solution.py
@@ -470,7 +470,9 @@
             pltpu.SemaphoreType.DMA((steps,)),
             pltpu.SemaphoreType.DMA((steps,)),
         ],
-        compiler_params=pltpu.CompilerParams(collective_id=collective_id, has_side_effects=True),
+        compiler_params=pltpu.CompilerParams(
+            collective_id=collective_id, has_side_effects=True, vmem_limit_bytes=8 << 20
+        ),
         name="sum_all",
     )(vectors, biases)
 
@@ -692,7 +694,7 @@
         out_specs=tuple(in_vmem(len(out_shape))),
         scratch_shapes=scratch,
         compiler_params=pltpu.CompilerParams(
-            collective_id=collective_id, has_side_effects=True, vmem_limit_bytes=40 << 20
+            collective_id=collective_id, has_side_effects=True, vmem_limit_bytes=14 << 20
         ),
         name="forward_exchange",
     )(partial, residual, bias[None, :], gain[None, :], shift[None, :], *extra)
@@ -719,7 +721,7 @@
         out_specs=tuple(in_vmem(len(out_shape))),
         scratch_shapes=scratch,
         compiler_params=pltpu.CompilerParams(
-            collective_id=collective_id, has_side_effects=True, vmem_limit_bytes=56 << 20
+            collective_id=collective_id, has_side_effects=True, vmem_limit_bytes=24 << 20
         ),
         name="backward_exchange",
     )(partial, grad_out, normal_in, gain[None, :], *extra)
@@ -848,7 +850,7 @@
             pltpu.SemaphoreType.DMA((3, PARTS)),
         ],
         compiler_params=pltpu.CompilerParams(
-            collective_id=collective_id, has_side_effects=True, vmem_limit_bytes=56 << 20
+            collective_id=collective_id, has_side_effects=True, vmem_limit_bytes=18 << 20
         ),
         name="attend",
     )(length, qkv)
@@ -1073,7 +1075,7 @@
             *sems,
         ],
         compiler_params=pltpu.CompilerParams(
-            collective_id=collective_id, has_side_effects=True, vmem_limit_bytes=56 << 20
+            collective_id=collective_id, has_side_effects=True, vmem_limit_bytes=20 << 20
         ),
         name="attend_back",
     )(length, qkv, held, grad, out_wide, log_total, *extra)
@@ -1248,9 +1250,7 @@
         grad_active = product(grad_low, w_outer, 1, 1)
         grad_inner = (grad_active * slope).astype(LOW)
         branch = product(grad_inner, w_inner, 1, 1).astype(LOW)
-        split = active.shape[1] // 2
-        grad_outer_w = product(active[:, :split], grad_low, 0, 0).astype(LOW)
-        grad_outer_rest = product(active[:, split:], grad_low, 0, 0).astype(LOW)
+        grad_outer_w = product(active, grad_low, 0, 0).astype(LOW)
         grad_inner_w = product(normed_two, grad_inner, 0, 0).astype(LOW)
         grad_mid_low, grad_middle, sums_two, *summed_two = exchange_back(
             branch, grad_own, middle, vector(4, layer), 2 * layer + 8, (grad_inner_w, grad_outer_w), (False, True)
@@ -1279,7 +1279,7 @@
         if layer == 0:
             output = shared[0].astype(WIDE)
         grad_low, grad_own, sums_one, *summed_one = exchange_back(
-            branch, grad_middle, residual, vector(2, layer), 2 * layer + 9, (grad_qkv_w, grad_output_w, grad_outer_rest), (True, True, True)
+            branch, grad_middle, residual, vector(2, layer), 2 * layer + 9, (grad_qkv_w, grad_output_w), (True, True)
         )
         grads[layer] = (*summed_one, *summed_two)
         vectors[layer] = [
@@ -1316,11 +1316,6 @@
     def stacked(which):
         return jnp.stack([grads[layer][which] for layer in range(LAYERS)]).astype(WIDE)
 
-    def joined(first, second):
-        return jnp.stack(
-            [jnp.concatenate([grads[layer][first], grads[layer][second]]) for layer in range(LAYERS)]
-        ).astype(WIDE)
-
     def turned(start):
         return jnp.stack([grads[layer][0][start : start + columns].T for layer in range(LAYERS)]).astype(WIDE)
 
@@ -1331,8 +1326,8 @@
         turned(columns),
         turned(2 * columns),
         stacked(1),
+        stacked(2),
         stacked(3),
-        joined(4, 2),
         bias_sums[:, :columns],
         bias_sums[:, 2 * columns : 3 * columns],
         bias_sums[:, 3 * columns :],

time: 665 us -> 625 us (0.940)
  Pallas kernels: 504 us -> 464 us
  matrix products: 84 us -> 64 us
  local copies, waits for them, and re-layouts: 23.6 us -> 39.3 us
    pallas_call x4, Pallas kernels: 222 us -> 196 us  [backward_exchange(): pl.pallas_call(functools.partial(kernel, n, PIECES), out_shape=out_shape,...]
    dot_general x26 -> x24, matrix products: 84 us -> 64 us  [product(): lax.dot_general(left_side, right_side, (((left_axis,), (right_axis,)), ((...]
    unnamed x118 -> x194, local copies, waits for them, and re-layouts: 10.1 us -> 27.4 us
    pallas_call x2, Pallas kernels: 57.4 us -> 50.1 us  [attend_back(): pl.pallas_call(functools.partial(attend_back_kernel, scale, own is not No...]
where the time goes in v8:
time: 625 us; the launch traced here: 615 us
  Pallas kernels  464 us (74%)
  matrix products  64 us (10%)
  local copies, waits for them, and re-layouts  39.3 us (6%)
  other arithmetic  25.5 us (4%)
  between operations  15.8 us (3%)
  waiting for transfers between devices  6.57 us (1%)
    pallas_call x4, Pallas kernels, backward_exchange(): pl.pallas_call(functools.partial(kernel, n, PIECES), out_shape=out_shape,...  196 us
    pallas_call x3, Pallas kernels, forward_exchange(): pl.pallas_call(functools.partial(kernel, n, PIECES), out_shape=out_shape,...  134 us
    dot_general x24, matrix products, product(): lax.dot_general(left_side, right_side, (((left_axis,), (right_axis,)), ((...  64 us
    pallas_call x2, Pallas kernels, attend_back(): pl.pallas_call(functools.partial(attend_back_kernel, scale, own is not No...  50.1 us
    pallas_call x2, Pallas kernels, attend(): pl.pallas_call(functools.partial(attend_kernel, scale), out_shape=(jax.Sh...  41.7 us
    unnamed x194, local copies, waits for them, and re-layouts  27.4 us
    pallas_call x1, Pallas kernels, fetch_first(): pl.pallas_call(functools.partial(fetch_kernel, counts, jobs), out_shape=o...  26.6 us
    pallas_call x1, Pallas kernels, sum_all(): pl.pallas_call(functools.partial(sum_all_kernel, axes), out_shape=jax.Sha...  15.3 us
  transfers between devices with their start and end apart: 5, of which 1 were waited for; matrix products, arithmetic and copies ran while one was open for 8% of the time, Pallas kernels for 32%

profile of v8, /device:TPU:0, one launch (start us, length us, event | category | flops | bytes accessed | tf_op | source)
XLA Modules:
  0.0 615.0 jit_solution(9725711300251743725)
XLA Ops:
  11.7 26.6 %fetch_first.1 = (bf16[960,1280]{1,0:T(8,128)(2,1)}, bf16[640,1280]{1,0:T(8,128)(2,1)S(1)}, f32[2,1280]{1,0:T(2,128)S(1)}, f32[2,1280]{1,0:T(2,128)S(1)}, f32[2,...) custom-call(bf16[960,640]{1,0:T(8,128)(2,1)S(1)} %pad_maximum_fusion, ...), custom_call_target="tpu_custom_call" | custom-call | tf_op jit(solution)/shard_map/fetch_first/pallas_call | solution.py:662
  42.3 1.9 reduce_sum.63
  44.2 2.1 multiply_reduce_fusion
  49.0 4.6 add_convert_fusion.2.qkv
  53.6 20.9 %attend.2 = (bf16[320,512]{1,0:T(8,128)(2,1)S(1)}, f32[320,512]{1,0:T(8,128)S(1)}, f32[8,512]{1,0:T(8,128)S(1)}, bf16[3,640,512]{2,1,0:T(8,128)(2,1)S(1)}) custom-call(s32[1]{0:T(128)S(6)} %copy.35.length, bf16[960,512]{1,0:T(8,128)(2,1)S(1)} %add_convert_fusion.2.qkv), custom_call_target="tpu_custom_call" | custom-call | tf_op jit(solution)/shard_map/attend/pallas_call | solution.py:836
  77.4 47.2 %forward_exchange.3 = (bf16[512,1280]{1,0:T(8,128)(2,1)S(1)}, f32[128,1280]{1,0:T(8,128)S(1)}, bf16[960,1280]{1,0:T(8,128)(2,1)S(1)}) custom-call(bf16[512,1280]{1,0:T(8,128)(2,1)S(1)} %convolution_convert_fusion.13.partial, f32[128,1280]{1,0:T(8,128)S(1)} %dynamic-slice_bitcast_fusion.residual.normal_in, f32[1,1280]{1,0:T(1,128)S(1)} %get-tuple-element.166.bias, ...), custom_call_target="tpu_custom_call" | custom-call | tf_op jit(solution)/shard_map/forward_exchange/pallas_call | solution.py:690
  126.0 3.0 dynamic-slice_reduce_fusion
  129.8 6.2 %multiply_convert_fusion.1 = (bf16[512,1280]{1,0:T(8,128)(2,1)}, f32[512,1280]{1,0:T(8,128)}) fusion(f32[1280]{0:T(1024)S(1)} %get-tuple-element.124, bf16[512,1280]{1,0:T(8,128)(2,1)} %copy-done.61, bf16[1280,1280]{1,0:T(8,128)(2,1)} %all-gather.5.cloned.1.call-done), kind=kOutput, calls=%fused_computation.38 | convolution fusion | flops 1681653760 | bytes 8524800 | tf_op jit(solution)/shard_map/dot_general | solution.py:1095
  136.0 4.6 all-gather.7.cloned.1.call-done
  140.6 4.3 convolution_convert_fusion.12.partial
  144.9 45.2 %forward_exchange.4 = (bf16[512,1280]{1,0:T(8,128)(2,1)S(1)}, f32[128,1280]{1,0:T(8,128)S(1)}) custom-call(bf16[512,1280]{1,0:T(8,128)(2,1)S(1)} %convolution_convert_fusion.12.partial, f32[128,1280]{1,0:T(8,128)S(1)} %get-tuple-element.84.residual.normal_in, f32[1,1280]{1,0:T(1,128)S(1)} %get-tuple-element.160.bias, f32[1,1280]{1,0:T(1,128)S(1)} %get-tuple-element.158.gain, ...), custom_call_target="tpu_custom_call" | custom-call | tf_op jit(solution)/shard_map/forward_exchange/pallas_call | solution.py:690
  191.7 20.8 %attend.3 = (bf16[320,512]{1,0:T(8,128)(2,1)S(1)}, f32[320,512]{1,0:T(8,128)S(1)}, f32[8,512]{1,0:T(8,128)S(1)}, bf16[3,640,512]{2,1,0:T(8,128)(2,1)S(1)}) custom-call(s32[1]{0:T(128)S(6)} %copy.35.length, bf16[960,512]{1,0:T(8,128)(2,1)S(1)} %add_convert_fusion.1.qkv), custom_call_target="tpu_custom_call" | custom-call | tf_op jit(solution)/shard_map/attend/pallas_call | solution.py:836
  214.1 42.0 %forward_exchange.5 = (bf16[512,1280]{1,0:T(8,128)(2,1)S(1)}, f32[128,1280]{1,0:T(8,128)S(1)}) custom-call(bf16[512,1280]{1,0:T(8,128)(2,1)S(1)} %convolution_convert_fusion.11.partial, f32[128,1280]{1,0:T(8,128)S(1)} %get-tuple-element.88.residual.normal_in, f32[1,1280]{1,0:T(1,128)S(1)} %copy-done.43, f32[1,1280]{1,0:T(1,128)S(1)} %get-tuple-element.163.gain, ...), custom_call_target="tpu_custom_call" | custom-call | tf_op jit(solution)/shard_map/forward_exchange/pallas_call | solution.py:690
  257.1 6.2 %multiply_convert_fusion = (bf16[512,1280]{1,0:T(8,128)(2,1)}, f32[512,1280]{1,0:T(8,128)}) fusion(f32[1280]{0:T(1024)S(1)} %copy-done.82, bf16[512,1280]{1,0:T(8,128)(2,1)} %copy-done.65, bf16[1280,1280]{1,0:T(8,128)(2,1)} %all-gather.9.cloned.1.call-done), kind=kOutput, calls=%fused_computation.36 | convolution fusion | flops 1681653760 | bytes 8524800 | tf_op jit(solution)/shard_map/dot_general | solution.py:1095
  263.4 6.6 %convert_reduce_fusion = (f32[1280]{0:T(1024)}, bf16[512,1280]{1,0:T(8,128)(2,1)S(1)}) fusion(f32[512,1280]{1,0:T(8,128)} %get-tuple-element.174, bf16[1280,1280]{1,0:T(8,128)(2,1)} %all-gather.11.cloned.1.call-done, f32[1,512,1280]{2,1,0:T(8,128)} %param.19), kind=kOutput, calls=%fused_computation.34 | convolution fusion | flops 1686240000 | bytes 9835520 | tf_op jit(solution)/shard_map/dot_general | solution.py:1095
  272.1 1.9 convolution_convert_fusion.2.refs_1_
  275.9 52.5 %backward_exchange.4 = (bf16[512,1280]{1,0:T(8,128)(2,1)S(1)}, f32[128,1280]{1,0:T(8,128)S(1)}, f32[8,1280]{1,0:T(8,128)S(1)}, bf16[640,1280]{1,0:T(8,128)(2,1)S(1)}, bf16[1280,640]{1,0:T(8,128)(2,1)S(1)}) custom-call(bf16[512,1280]{1,0:T(8,128)(2,1)S(1)} %convolution_convert_fusion.9.partial, f32[128,1280]{1,0:T(8,128)S(1)} %copy-done.2, ...), custom_call_target="tpu_custom_call" | custom-call | tf_op jit(solution)/shard_map/backward_exchange/pallas_call | solution.py:717
  332.7 3.0 convolution_convert_fusion.10
  336.3 2.3 convolution_convert_fusion.17.grad
  338.7 22.9 %attend_back.2 = bf16[960,512]{1,0:T(8,128)(2,1)S(1)} custom-call(s32[1]{0:T(128)S(6)} %copy.35.length, bf16[960,512]{1,0:T(8,128)(2,1)S(1)} %add_convert_fusion.1.qkv, bf16[3,640,512]{2,1,0:T(8,128)(2,1)S(1)} %copy-done.10, bf16[320,512]{1,0:T(8,128)(2,1)S(1)} %convolution_convert_fusion.17.grad, f32[320,512]{1,0:T(8,128)S(1)} %copy-done.31, ...), custom_call_target="tpu_custom_call" | custom-call | tf_op jit(solution)/shard_map/attend_back/pallas_call | solution.py:1063
  363.1 2.9 convolution_convert_fusion.5.refs_0_
  365.9 2.6 convolution_convert_fusion.8.partial
  374.4 45.8 %backward_exchange.5 = (bf16[512,1280]{1,0:T(8,128)(2,1)S(1)}, f32[128,1280]{1,0:T(8,128)S(1)}, f32[8,1280]{1,0:T(8,128)S(1)}, bf16[960,640]{1,0:T(8,128)(2,1)S(1)}, bf16[320,640]{1,0:T(8,128)(2,1)S(1)}) custom-call(bf16[512,1280]{1,0:T(8,128)(2,1)S(1)} %copy-done.24, f32[128,1280]{1,0:T(8,128)S(1)} %copy-done.35, f32[128,1280]{1,0:T(8,128)S(1)} %copy-done.4, ...), custom_call_target="tpu_custom_call" | custom-call | tf_op jit(solution)/shard_map/backward_exchange/pallas_call | solution.py:717
  424.0 2.8 convert_reduce_fusion.1
  430.7 51.7 %backward_exchange.6 = (bf16[512,1280]{1,0:T(8,128)(2,1)S(1)}, f32[128,1280]{1,0:T(8,128)S(1)}, f32[8,1280]{1,0:T(8,128)S(1)}, bf16[640,1280]{1,0:T(8,128)(2,1)S(1)}, bf16[1280,640]{1,0:T(8,128)(2,1)S(1)}) custom-call(bf16[512,1280]{1,0:T(8,128)(2,1)S(1)} %convolution_convert_fusion.7.partial, f32[128,1280]{1,0:T(8,128)S(1)} %get-tuple-element.102.grad_out, ...), custom_call_target="tpu_custom_call" | custom-call | tf_op jit(solution)/shard_map/backward_exchange/pallas_call | solution.py:717
  485.6 27.2 %attend_back.3 = (bf16[960,512]{1,0:T(8,128)(2,1)S(1)}, bf16[512,1280]{1,0:T(8,128)(2,1)S(1)}) custom-call(s32[1]{0:T(128)S(6)} %copy.35.length, bf16[960,512]{1,0:T(8,128)(2,1)S(1)} %add_convert_fusion.2.qkv, bf16[3,640,512]{2,1,0:T(8,128)(2,1)S(1)} %copy-done.8, bf16[320,512]{1,0:T(8,128)(2,1)S(1)} %convolution_convert_fusion.16.grad, ...), custom_call_target="tpu_custom_call" | custom-call | tf_op jit(solution)/shard_map/attend_back/pallas_call | solution.py:1063
  512.9 2.6 convolution_convert_fusion.6.partial
  517.3 3.1 convolution_convert_fusion.4.refs_0_
  524.7 45.6 %backward_exchange.7 = (bf16[512,1280]{1,0:T(8,128)(2,1)S(1)}, f32[128,1280]{1,0:T(8,128)}, f32[8,1280]{1,0:T(8,128)S(1)}, bf16[960,640]{1,0:T(8,128)(2,1)S(1)}, bf16[320,640]{1,0:T(8,128)(2,1)S(1)}) custom-call(bf16[512,1280]{1,0:T(8,128)(2,1)S(1)} %copy-done.23, f32[128,1280]{1,0:T(8,128)S(1)} %copy-done.33, ...), custom_call_target="tpu_custom_call" | custom-call | tf_op jit(solution)/shard_map/backward_exchange/pallas_call | solution.py:717
  573.3 15.3 %sum_all.1 = f32[24,640]{1,0:T(8,128)S(1)} custom-call(f32[16,1280]{1,0:T(8,128)S(1)} %pad.8.vectors, f32[8,640]{1,0:T(8,128)S(1)} %reshape.103.biases), custom_call_target="tpu_custom_call" | custom-call | tf_op jit(solution)/shard_map/sum_all/pallas_call | solution.py:462
  601.7 3.3 maximum_convert_fusion
  605.0 3.2 maximum_convert_fusion.1
  (268 shorter events, 68.1 us)
Async XLA Ops:
  7.2 122.6 %all-gather.5.cloned.1.call-start = ((), (), s32[]{:S(2)}) async-start(), calls=%async_computation.1 | async-start | bytes 4915200 | tf_op jit(solution)/shard_map/all_gather | solution.py:1143
  39.5 101.1 %all-gather.7.cloned.1.call-start = ((), (), s32[]{:S(2)}) async-start(), calls=%async_computation.2 | async-start | bytes 4915200 | tf_op jit(solution)/shard_map/all_gather | solution.py:1143
  40.2 216.9 %all-gather.9.cloned.1.call-start = ((), (), s32[]{:S(2)}) async-start(), calls=%async_computation.3 | async-start | bytes 4915200 | tf_op jit(solution)/shard_map/all_gather | solution.py:1143
  41.0 222.4 %all-gather.11.cloned.1.call-start = ((), (), s32[]{:S(2)}) async-start(), calls=%async_computation.4 | async-start | bytes 4915200 | tf_op jit(solution)/shard_map/all_gather | solution.py:1143
  41.5 327.6 %reduce-scatter.2.cloned.1.call-start = ((), (), s32[]{:S(2)}) async-start(), calls=%async_computation.5 | async-start | bytes 1638400 | tf_op jit(solution)/shard_map/reduce_scatter | solution.py:1260
  46.4 7.2 %copy-start.87 = (f32[512]{0:T(512)}, f32[512]{0:T(512)S(1)}, u32[]{:S(2)}) copy-start(f32[512]{0:T(512)S(1)} %add_rsqrt_fusion) | copy-start | bytes 6148
  47.0 6.6 %copy-start.78 = (f32[1280]{0:T(1024)}, f32[1280]{0:T(1024)S(1)}, u32[]{:S(2)}) copy-start(f32[1280]{0:T(1024)S(1)} %get-tuple-element.157) | copy-start | bytes 15364
  47.6 6.0 copy-start.80
  49.0 25.7 %copy-start.58 = (bf16[640,1280]{1,0:T(8,128)(2,1)S(1)}, bf16[640,1280]{1,0:T(8,128)(2,1)}, u32[]{:S(2)}) copy-start(bf16[640,1280]{1,0:T(8,128)(2,1)} %copy-done.57) | copy-start | bytes 4915204
  74.6 50.0 %copy-start.38 = (bf16[320,512]{1,0:T(8,128)(2,1)}, bf16[320,512]{1,0:T(8,128)(2,1)S(1)}, u32[]{:S(2)}) copy-start(bf16[320,512]{1,0:T(8,128)(2,1)S(1)} %get-tuple-element.75) | copy-start | bytes 983044
  76.7 52.3 %copy-start.75 = (f32[2,1280]{1,0:T(2,128)S(1)}, f32[2,1280]{1,0:T(2,128)}, u32[]{:S(2)}) copy-start(f32[2,1280]{1,0:T(2,128)} %param.29) | copy-start | bytes 30724
  126.0 18.9 %copy-start = (f32[128,1280]{1,0:T(8,128)}, f32[128,1280]{1,0:T(8,128)S(1)}, u32[]{:S(2)}) copy-start(f32[128,1280]{1,0:T(8,128)S(1)} %get-tuple-element.84.residual.normal_in) | copy-start | bytes 1966084
  140.6 49.6 %copy-start.55 = (bf16[960,1280]{1,0:T(8,128)(2,1)S(1)}, bf16[960,1280]{1,0:T(8,128)(2,1)}, u32[]{:S(2)}) copy-start(bf16[960,1280]{1,0:T(8,128)(2,1)} %copy-done.54) | copy-start | bytes 7372804
  140.6 49.6 %copy-start.84 = (f32[960]{0:T(1024)S(1)}, f32[960]{0:T(1024)}, u32[]{:S(2)}) copy-start(f32[960]{0:T(1024)} %get-tuple-element.169) | copy-start | bytes 11524
  190.1 23.8 %copy-start.3 = (f32[128,1280]{1,0:T(8,128)}, f32[128,1280]{1,0:T(8,128)S(1)}, u32[]{:S(2)}) copy-start(f32[128,1280]{1,0:T(8,128)S(1)} %get-tuple-element.88.residual.normal_in) | copy-start | bytes 1966084
  190.2 22.3 %copy-start.59 = (bf16[640,1280]{1,0:T(8,128)(2,1)S(1)}, bf16[640,1280]{1,0:T(8,128)(2,1)}, u32[]{:S(2)}) copy-start(bf16[640,1280]{1,0:T(8,128)(2,1)} %copy-done.57) | copy-start | bytes 4915204
  191.7 22.4 %copy-start.43 = (f32[1,1280]{1,0:T(1,128)S(1)}, f32[1,1280]{1,0:T(1,128)}, u32[]{:S(2)}) copy-start(f32[1,1280]{1,0:T(1,128)} %get-tuple-element.165.bias) | copy-start | bytes 15364
  191.7 22.4 %copy-start.44 = (f32[1,1280]{1,0:T(1,128)S(1)}, f32[1,1280]{1,0:T(1,128)}, u32[]{:S(2)}) copy-start(f32[1,1280]{1,0:T(1,128)} %get-tuple-element.161.shift) | copy-start | bytes 15364
  212.5 44.6 %copy-start.82 = (f32[1280]{0:T(1024)S(1)}, f32[1280]{0:T(1024)}, u32[]{:S(2)}) copy-start(f32[1280]{0:T(1024)} %get-tuple-element.123) | copy-start | bytes 15364
  263.4 6.6 %copy-start.66 = (bf16[512,1280]{1,0:T(8,128)(2,1)S(1)}, bf16[512,1280]{1,0:T(8,128)(2,1)}, u32[]{:S(2)}) copy-start(bf16[512,1280]{1,0:T(8,128)(2,1)} %copy-done.65) | copy-start | bytes 3932164
  275.9 56.8 %copy-start.91 = (bf16[1280,1280]{1,0:T(8,128)(2,1)S(1)}, bf16[1280,1280]{1,0:T(8,128)(2,1)}, u32[]{:S(2)}) copy-start(bf16[1280,1280]{1,0:T(8,128)(2,1)} %all-gather.11.cloned.1.call-done) | copy-start | bytes 9830404
  338.7 23.7 %copy-start.20 = (bf16[512,1280]{1,0:T(8,128)(2,1)S(1)}, bf16[512,1280]{1,0:T(8,128)(2,1)}, u32[]{:S(2)}) copy-start(bf16[512,1280]{1,0:T(8,128)(2,1)} %copy-done.19) | copy-start | bytes 3932164
  338.7 23.7 %copy-start.41 = (bf16[320,512]{1,0:T(8,128)(2,1)S(1)}, bf16[320,512]{1,0:T(8,128)(2,1)}, u32[]{:S(2)}) copy-start(bf16[320,512]{1,0:T(8,128)(2,1)} %copy-done.40) | copy-start | bytes 983044
  374.4 46.9 %copy-start.96 = (bf16[512,1280]{1,0:T(8,128)(2,1)S(1)}, bf16[512,1280]{1,0:T(8,128)(2,1)}, u32[]{:S(2)}) copy-start(bf16[512,1280]{1,0:T(8,128)(2,1)} %get-tuple-element.171) | copy-start | bytes 3932164
  430.7 51.8 %copy-start.60 = (bf16[640,1280]{1,0:T(8,128)(2,1)S(1)}, bf16[640,1280]{1,0:T(8,128)(2,1)}, u32[]{:S(2)}) copy-start(bf16[640,1280]{1,0:T(8,128)(2,1)} %copy-done.57) | copy-start | bytes 4915204
  482.4 30.4 %copy-start.15 = (bf16[1280,640]{1,0:T(8,128)(2,1)}, bf16[1280,640]{1,0:T(8,128)(2,1)S(1)}, u32[]{:S(2)}) copy-start(bf16[1280,640]{1,0:T(8,128)(2,1)S(1)} %get-tuple-element.117) | copy-start | bytes 4915204
  482.4 30.4 %copy-start.17 = (bf16[640,1280]{1,0:T(8,128)(2,1)}, bf16[640,1280]{1,0:T(8,128)(2,1)S(1)}, u32[]{:S(2)}) copy-start(bf16[640,1280]{1,0:T(8,128)(2,1)S(1)} %get-tuple-element.115) | copy-start | bytes 4915204
  482.4 30.4 %copy-start.32 = (f32[128,1280]{1,0:T(8,128)}, f32[128,1280]{1,0:T(8,128)S(1)}, u32[]{:S(2)}) copy-start(f32[128,1280]{1,0:T(8,128)S(1)} %get-tuple-element.109.grad_out) | copy-start | bytes 1966084
  483.8 29.1 %copy-start.93 = (bf16[960,1280]{1,0:T(8,128)(2,1)S(1)}, bf16[960,1280]{1,0:T(8,128)(2,1)}, u32[]{:S(2)}) copy-start(bf16[960,1280]{1,0:T(8,128)(2,1)} %get-tuple-element.70) | copy-start | bytes 7372804
  524.7 48.4 %copy-start.71 = (f32[1,1280]{1,0:T(1,128)S(1)}, f32[1,1280]{1,0:T(1,128)}, u32[]{:S(2)}) copy-start(f32[1,1280]{1,0:T(1,128)} %stack.78) | copy-start | bytes 15364
  524.7 48.5 %copy-start.72 = (f32[1,1280]{1,0:T(1,128)S(1)}, f32[1,1280]{1,0:T(1,128)}, u32[]{:S(2)}) copy-start(f32[1,1280]{1,0:T(1,128)} %get-tuple-element.144) | copy-start | bytes 15364
  524.7 48.5 %copy-start.73 = (f32[1,1280]{1,0:T(1,128)S(1)}, f32[1,1280]{1,0:T(1,128)}, u32[]{:S(2)}) copy-start(f32[1,1280]{1,0:T(1,128)} %get-tuple-element.145) | copy-start | bytes 15364
  (70 other events, 152.7 us)
Sparse Core Ops, SparseCore 0:
  39.6 52.7 all-gather.4
  94.0 46.5 all-gather.6
  142.1 46.3 all-gather.8
  189.9 46.3 all-gather.10
  335.8 31.1 reduce-scatter.1

commit v9 on v8

--- a/solution.py
+++ b/solution.py
@@ -482,6 +482,7 @@
 
 
 CAST_ROWS = 64
+FIRST_GAIN, FIRST_SHIFT = 2, 3
 
 
 class Quarters:
@@ -554,7 +555,7 @@
 
 
 class QuartersSide(Quarters):
-    CROSSED, APART, FORWARDED = 4, 3, 3
+    CROSSED, APART, FORWARDED = 6, 5, 4
 
     def start(self):
         self.begin()
@@ -589,9 +590,9 @@
         return taken
 
     shard_count, small_count, wide_count, low_count = counts
-    shards, smalls, wides = take(shard_count), take(small_count), take(wide_count)
-    outs, out_smalls, lows = take(shard_count), take(small_count), take(low_count)
-    buffers = take(len(jobs))
+    shards, smalls, wides, (frames,) = take(shard_count), take(small_count), take(wide_count), take(1)
+    outs, out_smalls, lows, (normed,) = take(shard_count), take(small_count), take(low_count), take(1)
+    buffers, (frame_buffer,) = take(len(jobs)), take(1)
     cast_sems, sends, recvs, small_sends, small_recvs = refs
     quarters = Quarters(shards, outs, sends, recvs)
 
@@ -615,11 +616,20 @@
         which, layer, _, _ = jobs[at]
         return pltpu.make_async_copy(wides[which].at[layer], buffers[at], cast_sems.at[at])
 
-    quarters.begin()
+    frame_load = pltpu.make_async_copy(frames, frame_buffer, cast_sems.at[len(jobs)])
+
+    def norm(step, carry):
+        rows = pl.ds(pl.multiple_of(step * CAST_ROWS, CAST_ROWS), CAST_ROWS)
+        hat, _ = norm_parts(frame_buffer[rows, :])
+        normed[rows, :] = (hat * out_smalls[FIRST_GAIN][0:1, :] + out_smalls[FIRST_SHIFT][0:1, :]).astype(LOW)
+        return carry
+
     for at in range(small_count):
         small_copy(at, quarters.half).start()
+    quarters.begin()
     for at in range(len(jobs)):
         load(at).start()
+    frame_load.start()
     quarters.keep_own()
     for small, out in zip(smalls, out_smalls):
         cols = small.shape[1]
@@ -633,14 +643,18 @@
             return carry
 
         lax.fori_loop(0, buffers[at].shape[0] // CAST_ROWS, cast, 0)
+    for at in range(small_count):
+        small_copy(at, 1 - quarters.half).wait_recv()
+        out_smalls[at][...] = out_smalls[at][...].astype(LOW).astype(WIDE)
     last = len(quarters.each)
     for at in range(last + 1):
         if at < last:
             quarters.crossed(quarters.each[at])
         if at > 0:
             quarters.forwarded(quarters.each[at - 1])
-    for at in range(small_count):
-        small_copy(at, 1 - quarters.half).wait_recv()
+        if at == fetch_parts(shards[0].shape[0]):
+            frame_load.wait()
+            lax.fori_loop(0, normed.shape[0] // CAST_ROWS, norm, 0)
     quarters.finish()
     for at in range(small_count):
         small_copy(at, quarters.half).wait_send()
@@ -655,24 +669,24 @@
     return jax.ShapeDtypeStruct((shard.shape[0], 2 * shard.shape[1]), shard.dtype)
 
 
-def fetch_first(shards, smalls, wides, jobs, low_shapes, collective_id):
+def fetch_first(shards, smalls, wides, frames, jobs, low_shapes, collective_id):
     counts = (len(shards), len(smalls), len(wides), len(low_shapes))
     out_shape = tuple(gathered_shape(array) for array in (*shards, *smalls))
-    out_shape += tuple(jax.ShapeDtypeStruct(shape, LOW) for shape in low_shapes)
+    out_shape += tuple(jax.ShapeDtypeStruct(shape, LOW) for shape in (*low_shapes, frames.shape))
     return pl.pallas_call(
         functools.partial(fetch_kernel, counts, jobs),
         out_shape=out_shape,
-        in_specs=in_vmem(len(shards) + len(smalls)) + [pl.BlockSpec(memory_space=pl.ANY)] * len(wides),
+        in_specs=in_vmem(len(shards) + len(smalls)) + [pl.BlockSpec(memory_space=pl.ANY)] * (len(wides) + 1),
         out_specs=tuple(in_vmem(len(out_shape))),
         scratch_shapes=[pltpu.VMEM(wides[job[0]].shape[1:], WIDE) for job in jobs]
-        + [pltpu.SemaphoreType.DMA((len(jobs),))]
+        + [pltpu.VMEM(frames.shape, WIDE), pltpu.SemaphoreType.DMA((len(jobs) + 1,))]
         + quarter_sems(shards)
         + [pltpu.SemaphoreType.DMA((len(smalls),))] * 2,
         compiler_params=pltpu.CompilerParams(
-            collective_id=collective_id, has_side_effects=True, vmem_limit_bytes=44 << 20
+            collective_id=collective_id, has_side_effects=True, vmem_limit_bytes=42 << 20
         ),
         name="fetch_first",
-    )(*shards, *smalls, *wides)
+    )(*shards, *smalls, *wides, frames)
 
 
 def forward_exchange(partial, residual, bias, gain, shift, n, collective_id, shard=None):
@@ -694,7 +708,7 @@
         out_specs=tuple(in_vmem(len(out_shape))),
         scratch_shapes=scratch,
         compiler_params=pltpu.CompilerParams(
-            collective_id=collective_id, has_side_effects=True, vmem_limit_bytes=14 << 20
+            collective_id=collective_id, has_side_effects=True, vmem_limit_bytes=12 << 20
         ),
         name="forward_exchange",
     )(partial, residual, bias[None, :], gain[None, :], shift[None, :], *extra)
@@ -721,7 +735,7 @@
         out_specs=tuple(in_vmem(len(out_shape))),
         scratch_shapes=scratch,
         compiler_params=pltpu.CompilerParams(
-            collective_id=collective_id, has_side_effects=True, vmem_limit_bytes=24 << 20
+            collective_id=collective_id, has_side_effects=True, vmem_limit_bytes=20 << 20
         ),
         name="backward_exchange",
     )(partial, grad_out, normal_in, gain[None, :], *extra)
@@ -850,7 +864,7 @@
             pltpu.SemaphoreType.DMA((3, PARTS)),
         ],
         compiler_params=pltpu.CompilerParams(
-            collective_id=collective_id, has_side_effects=True, vmem_limit_bytes=18 << 20
+            collective_id=collective_id, has_side_effects=True, vmem_limit_bytes=16 << 20
         ),
         name="attend",
     )(length, qkv)
@@ -1075,7 +1089,7 @@
             *sems,
         ],
         compiler_params=pltpu.CompilerParams(
-            collective_id=collective_id, has_side_effects=True, vmem_limit_bytes=20 << 20
+            collective_id=collective_id, has_side_effects=True, vmem_limit_bytes=18 << 20
         ),
         name="attend_back",
     )(length, qkv, held, grad, out_wide, log_total, *extra)
@@ -1133,6 +1147,7 @@
     def own_slice(full):
         return lax.dynamic_slice_in_dim(full, own_start, own_rows, axis=0)
 
+    hidden_rows = hidden.reshape(rows, width)
     smalls = (output_bias, outer_bias, first_gain, first_shift, second_gain, second_shift)
     qkv_weights = [jnp.swapaxes(weight, 1, 2) for weight in (query_weight, key_weight, value_weight)]
 
@@ -1151,8 +1166,8 @@
         for layer in range(1, LAYERS):
             jobs += [(2 + at, layer, len(shapes), at * columns) for at in range(3)]
             shapes.append((3 * columns, qkv_weights[0].shape[2]))
-        results = fetch_first((qkv_shard(0), projections), smalls, wides, tuple(jobs), shapes, 17)
-        qkv_first, projections, *results = results
+        results = fetch_first((qkv_shard(0), projections), smalls, wides, hidden_rows, tuple(jobs), shapes, 17)
+        qkv_first, projections, *results, normed = results
         smalls, lows = results[: len(smalls)], results[len(smalls) :]
         inner_low, outer_low, qkv_low = lows[:LAYERS], lows[LAYERS : 2 * LAYERS], [None, *lows[2 * LAYERS :]]
     else:
@@ -1160,22 +1175,23 @@
         smalls = [gather(small, 1) for small in smalls]
         inner_low, outer_low = inner_weight.astype(LOW), outer_weight.astype(LOW)
         qkv_low = [qkv_shard(layer) for layer in range(LAYERS)]
+        smalls = [lax.reduce_precision(small, 8, 7) for small in smalls]
+        hat_full, _ = norm_parts(hidden_rows)
+        normed = (hat_full * smalls[FIRST_GAIN][0] + smalls[FIRST_SHIFT][0]).astype(LOW)
     projections = projections.reshape(LAYERS, columns, width)
-    smalls = [lax.reduce_precision(small, 8, 7) for small in smalls]
 
     def vector(kind, layer):
         return smalls[kind][layer]
 
-    w_qkvs = [qkv_first] + [None if paired else gather(qkv_low[layer], 1) for layer in range(1, LAYERS)]
-    feeds = [(gather(inner_low[layer], 0), gather(outer_low[layer], 1)) for layer in range(LAYERS)]
-
-    hidden_rows = hidden.reshape(rows, width)
+    w_qkvs = [qkv_first] + [gather(qkv_low[layer], 1) for layer in range(1, LAYERS)]
+    w_inners = [gather(inner_low[layer], 0) for layer in range(LAYERS)]
+    carried = paired and tp_size == 4
+    w_outers = [None if carried and layer == 0 else gather(outer_low[layer], 1) for layer in range(LAYERS)]
+
     residual = own_slice(hidden_rows)
-    hat_full, _ = norm_parts(hidden_rows)
-    normed = (hat_full * vector(2, 0) + vector(3, 0)).astype(LOW)
     kept = []
     for layer in range(LAYERS):
-        w_qkv, w_out, (w_inner, w_outer) = w_qkvs[layer], projections[layer], feeds[layer]
+        w_qkv, w_out, w_inner = w_qkvs[layer], projections[layer], w_inners[layer]
         bias_qkv = jnp.concatenate(
             [query_bias[layer], jnp.zeros_like(query_bias[layer]), value_bias[layer]]
         )
@@ -1190,16 +1206,16 @@
             vector(5, layer),
             tp_size,
             2 * layer + 4,
-            qkv_low[layer + 1] if paired and layer + 1 < LAYERS else None,
+            outer_low[layer] if carried and layer == 0 else None,
         )
         if fetched:
-            w_qkvs[layer + 1] = fetched[0]
+            w_outers[layer] = fetched[0]
         inner_pre = product(normed_two, w_inner, 1, 0) + inner_bias[layer]
         active, slope = gelu_value(inner_pre).astype(LOW), gelu_slope(inner_pre)
         kept.append(
             (residual, normed, qkv, attended, attended_wide, log_total, held, middle, normed_two, slope, active)
         )
-        branch = product(active, w_outer, 1, 0).astype(LOW)
+        branch = product(active, w_outers[layer], 1, 0).astype(LOW)
         if layer + 1 < LAYERS:
             normed, residual = forward_exchange(
                 branch,
@@ -1233,7 +1249,7 @@
     vectors = [None] * LAYERS
     biases = [None] * LAYERS
     for layer in reversed(range(LAYERS)):
-        w_qkv, w_out, (w_inner, w_outer) = w_qkvs[layer], projections[layer], feeds[layer]
+        w_qkv, w_out, w_inner, w_outer = w_qkvs[layer], projections[layer], w_inners[layer], w_outers[layer]
         (
             residual,
             normed,

time: 625 us -> 613 us (0.981)
    unnamed x194 -> x174, local copies, waits for them, and re-layouts: 27.4 us -> 30.7 us
  transfers between devices with their start and end apart: 5 -> 5, of which waited for: 1 -> 0; matrix products, arithmetic and copies ran while one was open for 8% -> 6% of each run, Pallas kernels for 32% -> 33%
where the time goes in v9:
time: 613 us; the launch traced here: 605 us
  Pallas kernels  465 us (76%)
  matrix products  62.1 us (10%)
  local copies, waits for them, and re-layouts  40.1 us (7%)
  other arithmetic  19.9 us (3%)
  between operations  15.7 us (3%)
    pallas_call x4, Pallas kernels, backward_exchange(): pl.pallas_call(functools.partial(kernel, n, PIECES), out_shape=out_shape,...  194 us
    pallas_call x3, Pallas kernels, forward_exchange(): pl.pallas_call(functools.partial(kernel, n, PIECES), out_shape=out_shape,...  135 us
    dot_general x24, matrix products, product(): lax.dot_general(left_side, right_side, (((left_axis,), (right_axis,)), ((...  62.1 us
    pallas_call x2, Pallas kernels, attend_back(): pl.pallas_call(functools.partial(attend_back_kernel, scale, own is not No...  50.5 us
    pallas_call x2, Pallas kernels, attend(): pl.pallas_call(functools.partial(attend_kernel, scale), out_shape=(jax.Sh...  41.6 us
    unnamed x174, local copies, waits for them, and re-layouts  30.7 us
    pallas_call x1, Pallas kernels, fetch_first(): pl.pallas_call(functools.partial(fetch_kernel, counts, jobs), out_shape=o...  28.4 us
    pallas_call x1, Pallas kernels, sum_all(): pl.pallas_call(functools.partial(sum_all_kernel, axes), out_shape=jax.Sha...  15.6 us
  transfers between devices with their start and end apart: 5, of which 0 were waited for; matrix products, arithmetic and copies ran while one was open for 6% of the time, Pallas kernels for 33%

profile of v9, /device:TPU:0, one launch (start us, length us, event | category | flops | bytes accessed | tf_op | source)
XLA Modules:
  0.0 604.6 jit_solution(13732249226158534131)
XLA Ops:
  11.7 28.4 %fetch_first.1 = (bf16[960,1280]{1,0:T(8,128)(2,1)}, bf16[640,1280]{1,0:T(8,128)(2,1)S(1)}, f32[2,1280]{1,0:T(2,128)S(1)}, f32[2,1280]{1,0:T(2,128)S(1)}, f32[2,...) custom-call(bf16[960,640]{1,0:T(8,128)(2,1)S(1)} %pad_maximum_fusion, ...), custom_call_target="tpu_custom_call" | custom-call | tf_op jit(solution)/shard_map/fetch_first/pallas_call | solution.py:676
  45.3 3.5 add_convert_fusion.1.qkv
  48.9 20.9 %attend.2 = (bf16[320,512]{1,0:T(8,128)(2,1)S(1)}, f32[320,512]{1,0:T(8,128)S(1)}, f32[8,512]{1,0:T(8,128)S(1)}, bf16[3,640,512]{2,1,0:T(8,128)(2,1)S(1)}) custom-call(s32[1]{0:T(128)S(6)} %copy.35.length, bf16[960,512]{1,0:T(8,128)(2,1)S(1)} %add_convert_fusion.1.qkv), custom_call_target="tpu_custom_call" | custom-call | tf_op jit(solution)/shard_map/attend/pallas_call | solution.py:850
  73.1 47.0 %forward_exchange.3 = (bf16[512,1280]{1,0:T(8,128)(2,1)S(1)}, f32[128,1280]{1,0:T(8,128)S(1)}, bf16[1280,1280]{1,0:T(8,128)(2,1)S(1)}) custom-call(bf16[512,1280]{1,0:T(8,128)(2,1)S(1)} %convolution_convert_fusion.13.partial, f32[128,1280]{1,0:T(8,128)S(1)} %dynamic-slice_bitcast_fusion.residual.normal_in, f32[1,1280]{1,0:T(1,128)S(1)} %get-tuple-element.167.bias, ...), custom_call_target="tpu_custom_call" | custom-call | tf_op jit(solution)/shard_map/forward_exchange/pallas_call | solution.py:704
  122.9 2.2 dynamic-slice_reduce_fusion
  125.2 5.9 multiply_convert_fusion.1
  133.0 43.1 %forward_exchange.4 = (bf16[512,1280]{1,0:T(8,128)(2,1)S(1)}, f32[128,1280]{1,0:T(8,128)S(1)}) custom-call(bf16[512,1280]{1,0:T(8,128)(2,1)S(1)} %convolution_convert_fusion.12.partial, f32[128,1280]{1,0:T(8,128)S(1)} %get-tuple-element.84.residual.normal_in, f32[1,1280]{1,0:T(1,128)S(1)} %get-tuple-element.161.bias, f32[1,1280]{1,0:T(1,128)S(1)} %get-tuple-element.159.gain, ...), custom_call_target="tpu_custom_call" | custom-call | tf_op jit(solution)/shard_map/forward_exchange/pallas_call | solution.py:704
  178.1 3.6 add_convert_fusion.qkv
  181.8 20.7 %attend.3 = (bf16[320,512]{1,0:T(8,128)(2,1)S(1)}, f32[320,512]{1,0:T(8,128)S(1)}, f32[8,512]{1,0:T(8,128)S(1)}, bf16[3,640,512]{2,1,0:T(8,128)(2,1)S(1)}) custom-call(s32[1]{0:T(128)S(6)} %copy.35.length, bf16[960,512]{1,0:T(8,128)(2,1)S(1)} %add_convert_fusion.qkv), custom_call_target="tpu_custom_call" | custom-call | tf_op jit(solution)/shard_map/attend/pallas_call | solution.py:850
  204.1 44.8 %forward_exchange.5 = (bf16[512,1280]{1,0:T(8,128)(2,1)S(1)}, f32[128,1280]{1,0:T(8,128)S(1)}) custom-call(bf16[512,1280]{1,0:T(8,128)(2,1)S(1)} %convolution_convert_fusion.11.partial, f32[128,1280]{1,0:T(8,128)S(1)} %copy-done.4, f32[1,1280]{1,0:T(1,128)S(1)} %get-tuple-element.166.bias, f32[1,1280]{1,0:T(1,128)S(1)} %get-tuple-element.164.gain, ...), custom_call_target="tpu_custom_call" | custom-call | tf_op jit(solution)/shard_map/forward_exchange/pallas_call | solution.py:704
  250.0 6.3 %multiply_convert_fusion = (bf16[512,1280]{1,0:T(8,128)(2,1)}, f32[512,1280]{1,0:T(8,128)}) fusion(f32[1280]{0:T(1024)S(1)} %get-tuple-element.125, bf16[512,1280]{1,0:T(8,128)(2,1)} %copy-done.65, bf16[1280,1280]{1,0:T(8,128)(2,1)} %all-gather.9.cloned.1.call-done), kind=kOutput, calls=%fused_computation.35 | convolution fusion | flops 1681653760 | bytes 8524800 | tf_op jit(solution)/shard_map/dot_general | solution.py:1109
  256.2 6.6 %convert_reduce_fusion = (f32[1280]{0:T(1024)}, bf16[512,1280]{1,0:T(8,128)(2,1)S(1)}) fusion(f32[512,1280]{1,0:T(8,128)} %get-tuple-element.173, bf16[1280,1280]{1,0:T(8,128)(2,1)} %all-gather.11.cloned.1.call-done, f32[1,512,1280]{2,1,0:T(8,128)} %param.19), kind=kOutput, calls=%fused_computation.33 | convolution fusion | flops 1686240000 | bytes 9835520 | tf_op jit(solution)/shard_map/dot_general | solution.py:1109
  262.8 1.9 convolution_convert_fusion.3.refs_0_
  264.9 1.9 convolution_convert_fusion.2.refs_1_
  268.8 52.2 %backward_exchange.4 = (bf16[512,1280]{1,0:T(8,128)(2,1)S(1)}, f32[128,1280]{1,0:T(8,128)S(1)}, f32[8,1280]{1,0:T(8,128)S(1)}, bf16[640,1280]{1,0:T(8,128)(2,1)S(1)}, bf16[1280,640]{1,0:T(8,128)(2,1)S(1)}) custom-call(bf16[512,1280]{1,0:T(8,128)(2,1)S(1)} %convolution_convert_fusion.9.partial, f32[128,1280]{1,0:T(8,128)S(1)} %copy-done.2, ...), custom_call_target="tpu_custom_call" | custom-call | tf_op jit(solution)/shard_map/backward_exchange/pallas_call | solution.py:731
  325.3 3.0 convolution_convert_fusion.10
  328.9 2.4 convolution_convert_fusion.17.grad
  331.4 22.9 %attend_back.2 = bf16[960,512]{1,0:T(8,128)(2,1)S(1)} custom-call(s32[1]{0:T(128)S(6)} %copy.35.length, bf16[960,512]{1,0:T(8,128)(2,1)S(1)} %add_convert_fusion.qkv, bf16[3,640,512]{2,1,0:T(8,128)(2,1)S(1)} %copy-done.11, bf16[320,512]{1,0:T(8,128)(2,1)S(1)} %convolution_convert_fusion.17.grad, f32[320,512]{1,0:T(8,128)S(1)} %copy-done.34, ...), custom_call_target="tpu_custom_call" | custom-call | tf_op jit(solution)/shard_map/attend_back/pallas_call | solution.py:1077
  355.7 2.9 convolution_convert_fusion.5.refs_0_
  358.6 2.6 convolution_convert_fusion.8.partial
  367.0 44.4 %backward_exchange.5 = (bf16[512,1280]{1,0:T(8,128)(2,1)S(1)}, f32[128,1280]{1,0:T(8,128)S(1)}, f32[8,1280]{1,0:T(8,128)S(1)}, bf16[960,640]{1,0:T(8,128)(2,1)S(1)}, bf16[320,640]{1,0:T(8,128)(2,1)S(1)}) custom-call(bf16[512,1280]{1,0:T(8,128)(2,1)S(1)} %copy-done.27, f32[128,1280]{1,0:T(8,128)S(1)} %copy-done.38, f32[128,1280]{1,0:T(8,128)S(1)} %copy-done.5, ...), custom_call_target="tpu_custom_call" | custom-call | tf_op jit(solution)/shard_map/backward_exchange/pallas_call | solution.py:731
  411.5 1.9 convolution_convert_fusion.refs_1_
  414.6 2.8 convert_reduce_fusion.1
  417.4 1.9 convolution_convert_fusion.1.refs_0_
  421.3 51.8 %backward_exchange.6 = (bf16[512,1280]{1,0:T(8,128)(2,1)S(1)}, f32[128,1280]{1,0:T(8,128)S(1)}, f32[8,1280]{1,0:T(8,128)S(1)}, bf16[640,1280]{1,0:T(8,128)(2,1)S(1)}, bf16[1280,640]{1,0:T(8,128)(2,1)S(1)}) custom-call(bf16[512,1280]{1,0:T(8,128)(2,1)S(1)} %convolution_convert_fusion.7.partial, f32[128,1280]{1,0:T(8,128)S(1)} %get-tuple-element.104.grad_out, ...), custom_call_target="tpu_custom_call" | custom-call | tf_op jit(solution)/shard_map/backward_exchange/pallas_call | solution.py:731
  476.3 27.6 %attend_back.3 = (bf16[960,512]{1,0:T(8,128)(2,1)S(1)}, bf16[512,1280]{1,0:T(8,128)(2,1)S(1)}) custom-call(s32[1]{0:T(128)S(6)} %copy.35.length, bf16[960,512]{1,0:T(8,128)(2,1)S(1)} %add_convert_fusion.1.qkv, bf16[3,640,512]{2,1,0:T(8,128)(2,1)S(1)} %copy-done.9, bf16[320,512]{1,0:T(8,128)(2,1)S(1)} %convolution_convert_fusion.16.grad, ...), custom_call_target="tpu_custom_call" | custom-call | tf_op jit(solution)/shard_map/attend_back/pallas_call | solution.py:1077
  503.9 2.6 convolution_convert_fusion.6.partial
  506.8 3.1 convolution_convert_fusion.4.refs_0_
  514.8 45.4 %backward_exchange.7 = (bf16[512,1280]{1,0:T(8,128)(2,1)S(1)}, f32[128,1280]{1,0:T(8,128)}, f32[8,1280]{1,0:T(8,128)S(1)}, bf16[960,640]{1,0:T(8,128)(2,1)S(1)}, bf16[320,640]{1,0:T(8,128)(2,1)S(1)}) custom-call(bf16[512,1280]{1,0:T(8,128)(2,1)S(1)} %copy-done.26, f32[128,1280]{1,0:T(8,128)S(1)} %copy-done.36, ...), custom_call_target="tpu_custom_call" | custom-call | tf_op jit(solution)/shard_map/backward_exchange/pallas_call | solution.py:731
  563.2 15.6 %sum_all.1 = f32[24,640]{1,0:T(8,128)S(1)} custom-call(f32[16,1280]{1,0:T(8,128)S(1)} %pad.8.vectors, f32[8,640]{1,0:T(8,128)S(1)} %reshape.91.biases), custom_call_target="tpu_custom_call" | custom-call | tf_op jit(solution)/shard_map/sum_all/pallas_call | solution.py:462
  591.4 3.3 maximum_convert_fusion
  594.6 3.2 maximum_convert_fusion.1
  (238 shorter events, 62.7 us)
Async XLA Ops:
  7.2 118.0 %all-gather.7.cloned.1.call-start = ((), (), s32[]{:S(2)}) async-start(), calls=%async_computation.2 | async-start | bytes 4915200 | tf_op jit(solution)/shard_map/all_gather | solution.py:1158
  42.3 28.3 %copy-start.56 = (bf16[640,1280]{1,0:T(8,128)(2,1)}, bf16[640,1280]{1,0:T(8,128)(2,1)S(1)}, u32[]{:S(2)}) copy-start(bf16[640,1280]{1,0:T(8,128)(2,1)S(1)} %get-tuple-element.74) | copy-start | bytes 4915204
  42.3 135.8 %all-gather.5.cloned.1.call-start = ((), (), s32[]{:S(2)}) async-start(), calls=%async_computation.1 | async-start | bytes 3686400 | tf_op jit(solution)/shard_map/all_gather | solution.py:1158
  43.1 206.9 %all-gather.9.cloned.1.call-start = ((), (), s32[]{:S(2)}) async-start(), calls=%async_computation.3 | async-start | bytes 4915200 | tf_op jit(solution)/shard_map/all_gather | solution.py:1158
  43.8 212.4 %all-gather.11.cloned.1.call-start = ((), (), s32[]{:S(2)}) async-start(), calls=%async_computation.4 | async-start | bytes 4915200 | tf_op jit(solution)/shard_map/all_gather | solution.py:1158
  44.4 317.4 %reduce-scatter.2.cloned.1.call-start = ((), (), s32[]{:S(2)}) async-start(), calls=%async_computation.5 | async-start | bytes 1638400 | tf_op jit(solution)/shard_map/reduce_scatter | solution.py:1276
  73.1 52.0 %copy-start.74 = (f32[2,1280]{1,0:T(2,128)S(1)}, f32[2,1280]{1,0:T(2,128)}, u32[]{:S(2)}) copy-start(f32[2,1280]{1,0:T(2,128)} %param.29) | copy-start | bytes 30724
  122.9 10.2 %copy-start = (f32[128,1280]{1,0:T(8,128)}, f32[128,1280]{1,0:T(8,128)S(1)}, u32[]{:S(2)}) copy-start(f32[128,1280]{1,0:T(8,128)S(1)} %get-tuple-element.84.residual.normal_in) | copy-start | bytes 1966084
  125.2 6.0 copy-start.54
  178.1 24.4 %copy-start.57 = (bf16[640,1280]{1,0:T(8,128)(2,1)S(1)}, bf16[640,1280]{1,0:T(8,128)(2,1)}, u32[]{:S(2)}) copy-start(bf16[640,1280]{1,0:T(8,128)(2,1)} %copy-done.56) | copy-start | bytes 4915204
  181.8 22.3 %copy-start.4 = (f32[128,1280]{1,0:T(8,128)S(1)}, f32[128,1280]{1,0:T(8,128)}, u32[]{:S(2)}) copy-start(f32[128,1280]{1,0:T(8,128)} %copy-done.3) | copy-start | bytes 1966084
  256.2 6.6 %copy-start.66 = (bf16[512,1280]{1,0:T(8,128)(2,1)S(1)}, bf16[512,1280]{1,0:T(8,128)(2,1)}, u32[]{:S(2)}) copy-start(bf16[512,1280]{1,0:T(8,128)(2,1)} %copy-done.65) | copy-start | bytes 3932164
  268.8 56.6 %copy-start.79 = (bf16[1280,1280]{1,0:T(8,128)(2,1)S(1)}, bf16[1280,1280]{1,0:T(8,128)(2,1)}, u32[]{:S(2)}) copy-start(bf16[1280,1280]{1,0:T(8,128)(2,1)} %all-gather.11.cloned.1.call-done) | copy-start | bytes 9830404
  328.3 3.0 copy-start.11
  328.3 3.0 copy-start.34
  331.3 23.7 %copy-start.23 = (bf16[512,1280]{1,0:T(8,128)(2,1)S(1)}, bf16[512,1280]{1,0:T(8,128)(2,1)}, u32[]{:S(2)}) copy-start(bf16[512,1280]{1,0:T(8,128)(2,1)} %copy-done.22) | copy-start | bytes 3932164
  331.3 23.7 %copy-start.44 = (bf16[320,512]{1,0:T(8,128)(2,1)S(1)}, bf16[320,512]{1,0:T(8,128)(2,1)}, u32[]{:S(2)}) copy-start(bf16[320,512]{1,0:T(8,128)(2,1)} %copy-done.43) | copy-start | bytes 983044
  367.0 44.4 %copy-start.86 = (bf16[512,1280]{1,0:T(8,128)(2,1)S(1)}, bf16[512,1280]{1,0:T(8,128)(2,1)}, u32[]{:S(2)}) copy-start(bf16[512,1280]{1,0:T(8,128)(2,1)} %copy-done.85) | copy-start | bytes 3932164
  411.5 3.2 copy-start.83
  421.3 51.9 %copy-start.58 = (bf16[640,1280]{1,0:T(8,128)(2,1)S(1)}, bf16[640,1280]{1,0:T(8,128)(2,1)}, u32[]{:S(2)}) copy-start(bf16[640,1280]{1,0:T(8,128)(2,1)} %copy-done.56) | copy-start | bytes 4915204
  473.1 3.0 copy-start.9
  473.2 3.2 copy-start.32
  473.2 3.1 copy-start.46
  476.3 27.6 %copy-start.81 = (bf16[960,1280]{1,0:T(8,128)(2,1)S(1)}, bf16[960,1280]{1,0:T(8,128)(2,1)}, u32[]{:S(2)}) copy-start(bf16[960,1280]{1,0:T(8,128)(2,1)} %get-tuple-element.71) | copy-start | bytes 7372804
  506.8 3.1 copy-start.42
  514.8 48.3 %copy-start.69 = (f32[1,1280]{1,0:T(1,128)S(1)}, f32[1,1280]{1,0:T(1,128)}, u32[]{:S(2)}) copy-start(f32[1,1280]{1,0:T(1,128)} %stack.78) | copy-start | bytes 15364
  514.8 48.3 %copy-start.70 = (f32[1,1280]{1,0:T(1,128)S(1)}, f32[1,1280]{1,0:T(1,128)}, u32[]{:S(2)}) copy-start(f32[1,1280]{1,0:T(1,128)} %get-tuple-element.145) | copy-start | bytes 15364
  514.8 48.3 %copy-start.71 = (f32[1,1280]{1,0:T(1,128)S(1)}, f32[1,1280]{1,0:T(1,128)}, u32[]{:S(2)}) copy-start(f32[1,1280]{1,0:T(1,128)} %get-tuple-element.146) | copy-start | bytes 15364
  514.8 48.3 %copy-start.72 = (f32[1,1280]{1,0:T(1,128)S(1)}, f32[1,1280]{1,0:T(1,128)}, u32[]{:S(2)}) copy-start(f32[1,1280]{1,0:T(1,128)} %get-tuple-element.147) | copy-start | bytes 15364
  563.1 19.2 %copy-start.30 = (bf16[960,640]{1,0:T(8,128)(2,1)S(1)}, bf16[960,640]{1,0:T(8,128)(2,1)}, u32[]{:S(2)}) copy-start(bf16[960,640]{1,0:T(8,128)(2,1)} %copy-done.29) | copy-start | bytes 3686404
  591.4 3.3 copy-start.13
  591.4 3.3 copy-start.17
  (60 other events, 98.4 us)
Sparse Core Ops, SparseCore 0:
  42.4 55.6 all-gather.6
  99.7 37.1 all-gather.4
  138.4 46.3 all-gather.8
  186.2 46.3 all-gather.10
  328.4 29.5 reduce-scatter.1

commit v10 on v9

--- a/solution.py
+++ b/solution.py
@@ -280,7 +280,7 @@
         self.by_column = by_column
         self.chunks = landings[0].shape[1]
         self.arrays, self.outs, self.landings = arrays, outs, landings
-        self.sends, self.recvs = sems
+        self.sends, self.recvs, self.stores = sems
         self.half = lax.axis_index("fsdp")
         self.ctx = lax.axis_index("ctx")
         self.core = lax.rem(self.ctx, 2)
@@ -310,6 +310,14 @@
         part = self.outs[which].shape[0] // 2
         height = part // self.chunks
         return pl.ds(pl.multiple_of(core * part + chunk * height, 16), height)
+
+    def store(self, which, whose, chunk):
+        core = self.core if whose == 0 else 1 - self.core
+        return pltpu.make_async_copy(
+            self.landings[which].at[3 + whose, chunk],
+            self.outs[which].at[self.out_rows(which, core, chunk)],
+            self.stores.at[which, whose, chunk],
+        )
 
     def copy(self, which, stage, chunk, half=0):
         pair, across, other = self.peers
@@ -378,14 +386,12 @@
             self.copy(which, 2, chunk).wait_recv()
             low = (landing[2, chunk].astype(WIDE) + landing[3, chunk].astype(WIDE)).astype(LOW)
             landing[3, chunk] = low
-            self.outs[which][self.out_rows(which, self.core, chunk), :] = low
             self.copy(which, 3, chunk).start()
+            self.store(which, 0, chunk).start()
 
         def shared(which, chunk):
             self.copy(which, 3, chunk).wait_recv()
-            self.outs[which][self.out_rows(which, 1 - self.core, chunk), :] = self.landings[which][
-                4, chunk
-            ]
+            self.store(which, 1, chunk).start()
 
         for lag, action in zip(self.LAGS, (joined, crossed, summed, shared)):
             self.when_due(tick, lag, action)
@@ -397,6 +403,8 @@
                     self.copy(which, 0, chunk, half).wait_send()
                 for stage in range(1, 4):
                     self.copy(which, stage, chunk).wait_send()
+                for whose in range(2):
+                    self.store(which, whose, chunk).wait()
             return carry
 
         lax.fori_loop(0, self.chunks, body, 0)
@@ -408,9 +416,10 @@
     for array, column in zip(arrays, by_column):
         rows, cols = array.shape
         rows, cols = (rows, cols // 2) if column else (rows // 2, cols)
-        outs += (jax.ShapeDtypeStruct((rows, cols), LOW),)
+        outs += (pltpu.HBM((rows, cols), LOW),)
         landings.append(pltpu.VMEM((5, chunks, rows // 2 // chunks, cols), LOW))
-    return outs, landings, pltpu.SemaphoreType.DMA((len(arrays), 5, chunks))
+    sems = [pltpu.SemaphoreType.DMA((len(arrays), 5, chunks))] * 2
+    return outs, landings, sems + [pltpu.SemaphoreType.DMA((len(arrays), 2, chunks))]
 
 
 def backward_gradient_kernel(by_column, n, pieces, partial, grad_out, normal_in, gain, *refs):
@@ -726,13 +735,13 @@
     if arrays:
         outs, landings, sems = gradient_shapes(arrays, by_column)
         out_shape = out_shape + outs
-        scratch = scratch + landings + [sems] * 2
+        scratch = scratch + landings + sems
         kernel, extra = functools.partial(backward_gradient_kernel, by_column), arrays
     return pl.pallas_call(
         functools.partial(kernel, n, PIECES),
         out_shape=out_shape,
         in_specs=in_vmem(4 + len(extra)),
-        out_specs=tuple(in_vmem(len(out_shape))),
+        out_specs=tuple(in_vmem(3) + [pl.BlockSpec(memory_space=pltpu.HBM)] * len(extra)),
         scratch_shapes=scratch,
         compiler_params=pltpu.CompilerParams(
             collective_id=collective_id, has_side_effects=True, vmem_limit_bytes=20 << 20
@@ -1166,15 +1175,20 @@
         for layer in range(1, LAYERS):
             jobs += [(2 + at, layer, len(shapes), at * columns) for at in range(3)]
             shapes.append((3 * columns, qkv_weights[0].shape[2]))
+        wides += (cotangent,)
+        jobs.append((len(wides) - 1, 0, len(shapes), 0))
+        shapes.append(cotangent.shape[1:])
         results = fetch_first((qkv_shard(0), projections), smalls, wides, hidden_rows, tuple(jobs), shapes, 17)
         qkv_first, projections, *results, normed = results
         smalls, lows = results[: len(smalls)], results[len(smalls) :]
+        *lows, grad_low = lows
         inner_low, outer_low, qkv_low = lows[:LAYERS], lows[LAYERS : 2 * LAYERS], [None, *lows[2 * LAYERS :]]
     else:
         qkv_first, projections = gather(qkv_shard(0), 1), gather(projections, 1)
         smalls = [gather(small, 1) for small in smalls]
         inner_low, outer_low = inner_weight.astype(LOW), outer_weight.astype(LOW)
         qkv_low = [qkv_shard(layer) for layer in range(LAYERS)]
+        grad_low = cotangent.reshape(rows, width).astype(LOW)
         smalls = [lax.reduce_precision(small, 8, 7) for small in smalls]
         hat_full, _ = norm_parts(hidden_rows)
         normed = (hat_full * smalls[FIRST_GAIN][0] + smalls[FIRST_SHIFT][0]).astype(LOW)
@@ -1243,7 +1257,6 @@
 
     grad_rows = cotangent.reshape(rows, width)
     grad_own = own_slice(grad_rows)
-    grad_low = grad_rows.astype(LOW)
     outer_bias_sum = jnp.sum(grad_own, axis=0)
     grads = [None] * LAYERS
     vectors = [None] * LAYERS

time: 613 us -> 611 us (level)
    unnamed x174 -> x152, local copies, waits for them, and re-layouts: 30.7 us -> 27 us
where the time goes in v10:
time: 611 us; the launch traced here: 602 us
  Pallas kernels  468 us (77%)
  matrix products  62.6 us (10%)
  local copies, waits for them, and re-layouts  34.8 us (6%)
  other arithmetic  19.3 us (3%)
  between operations  15.7 us (3%)
    pallas_call x4, Pallas kernels, backward_exchange(): pl.pallas_call(functools.partial(kernel, n, PIECES), out_shape=out_shape,...  195 us
    pallas_call x3, Pallas kernels, forward_exchange(): pl.pallas_call(functools.partial(kernel, n, PIECES), out_shape=out_shape,...  135 us
    dot_general x24, matrix products, product(): lax.dot_general(left_side, right_side, (((left_axis,), (right_axis,)), ((...  62.6 us
    pallas_call x2, Pallas kernels, attend_back(): pl.pallas_call(functools.partial(attend_back_kernel, scale, own is not No...  50.2 us
    pallas_call x2, Pallas kernels, attend(): pl.pallas_call(functools.partial(attend_kernel, scale), out_shape=(jax.Sh...  41.3 us
    pallas_call x1, Pallas kernels, fetch_first(): pl.pallas_call(functools.partial(fetch_kernel, counts, jobs), out_shape=o...  29.8 us
    unnamed x152, local copies, waits for them, and re-layouts  27 us
    pallas_call x1, Pallas kernels, sum_all(): pl.pallas_call(functools.partial(sum_all_kernel, axes), out_shape=jax.Sha...  15.5 us
  transfers between devices with their start and end apart: 5, of which 0 were waited for; matrix products, arithmetic and copies ran while one was open for 6% of the time, Pallas kernels for 33%

profile of v10, /device:TPU:0, one launch (start us, length us, event | category | flops | bytes accessed | tf_op | source)
XLA Modules:
  0.0 602.1 jit_solution(3708088048061098593)
XLA Ops:
  11.7 29.8 %fetch_first.1 = (bf16[960,1280]{1,0:T(8,128)(2,1)}, bf16[640,1280]{1,0:T(8,128)(2,1)S(1)}, f32[2,1280]{1,0:T(2,128)S(1)}, f32[2,1280]{1,0:T(2,128)S(1)}, f32[2,...) custom-call(bf16[960,640]{1,0:T(8,128)(2,1)S(1)} %pad_maximum_fusion, ...), custom_call_target="tpu_custom_call" | custom-call | tf_op jit(solution)/shard_map/fetch_first/pallas_call | solution.py:685
  49.0 3.6 add_convert_fusion.1.qkv
  52.7 20.9 %attend.2 = (bf16[320,512]{1,0:T(8,128)(2,1)S(1)}, f32[320,512]{1,0:T(8,128)S(1)}, f32[8,512]{1,0:T(8,128)S(1)}, bf16[3,640,512]{2,1,0:T(8,128)(2,1)S(1)}) custom-call(s32[1]{0:T(128)S(6)} %copy.35.length, bf16[960,512]{1,0:T(8,128)(2,1)S(1)} %add_convert_fusion.1.qkv), custom_call_target="tpu_custom_call" | custom-call | tf_op jit(solution)/shard_map/attend/pallas_call | solution.py:859
  75.1 46.8 %forward_exchange.3 = (bf16[512,1280]{1,0:T(8,128)(2,1)S(1)}, f32[128,1280]{1,0:T(8,128)S(1)}, bf16[1280,1280]{1,0:T(8,128)(2,1)S(1)}) custom-call(bf16[512,1280]{1,0:T(8,128)(2,1)S(1)} %convolution_convert_fusion.13.partial, f32[128,1280]{1,0:T(8,128)S(1)} %dynamic-slice_bitcast_fusion.residual.normal_in, f32[1,1280]{1,0:T(1,128)S(1)} %get-tuple-element.169.bias, ...), custom_call_target="tpu_custom_call" | custom-call | tf_op jit(solution)/shard_map/forward_exchange/pallas_call | solution.py:713
  124.7 2.2 dynamic-slice_reduce_fusion
  127.0 5.9 multiply_convert_fusion.1
  134.8 43.5 %forward_exchange.4 = (bf16[512,1280]{1,0:T(8,128)(2,1)S(1)}, f32[128,1280]{1,0:T(8,128)S(1)}) custom-call(bf16[512,1280]{1,0:T(8,128)(2,1)S(1)} %convolution_convert_fusion.12.partial, f32[128,1280]{1,0:T(8,128)S(1)} %get-tuple-element.85.residual.normal_in, f32[1,1280]{1,0:T(1,128)S(1)} %get-tuple-element.163.bias, f32[1,1280]{1,0:T(1,128)S(1)} %get-tuple-element.161.gain, ...), custom_call_target="tpu_custom_call" | custom-call | tf_op jit(solution)/shard_map/forward_exchange/pallas_call | solution.py:713
  180.2 3.6 add_convert_fusion.qkv
  183.9 20.4 %attend.3 = (bf16[320,512]{1,0:T(8,128)(2,1)S(1)}, f32[320,512]{1,0:T(8,128)S(1)}, f32[8,512]{1,0:T(8,128)S(1)}, bf16[3,640,512]{2,1,0:T(8,128)(2,1)S(1)}) custom-call(s32[1]{0:T(128)S(6)} %copy.35.length, bf16[960,512]{1,0:T(8,128)(2,1)S(1)} %add_convert_fusion.qkv), custom_call_target="tpu_custom_call" | custom-call | tf_op jit(solution)/shard_map/attend/pallas_call | solution.py:859
  205.9 44.9 %forward_exchange.5 = (bf16[512,1280]{1,0:T(8,128)(2,1)S(1)}, f32[128,1280]{1,0:T(8,128)S(1)}) custom-call(bf16[512,1280]{1,0:T(8,128)(2,1)S(1)} %convolution_convert_fusion.11.partial, f32[128,1280]{1,0:T(8,128)S(1)} %copy-done.5, f32[1,1280]{1,0:T(1,128)S(1)} %get-tuple-element.168.bias, f32[1,1280]{1,0:T(1,128)S(1)} %get-tuple-element.166.gain, ...), custom_call_target="tpu_custom_call" | custom-call | tf_op jit(solution)/shard_map/forward_exchange/pallas_call | solution.py:713
  251.9 5.9 multiply_convert_fusion
  258.9 3.6 convolution_convert_fusion.2.refs_1_
  262.5 5.6 convert_reduce_fusion
  268.2 1.9 convolution_convert_fusion.3.refs_0_
  272.2 52.7 %backward_exchange.4 = (bf16[512,1280]{1,0:T(8,128)(2,1)S(1)}, f32[128,1280]{1,0:T(8,128)S(1)}, f32[8,1280]{1,0:T(8,128)S(1)}, bf16[640,1280]{1,0:T(8,128)(2,1)}, bf16[1280,640]{1,0:T(8,128)(2,1)}) custom-call(bf16[512,1280]{1,0:T(8,128)(2,1)S(1)} %convolution_convert_fusion.9.partial, f32[128,1280]{1,0:T(8,128)S(1)} %copy-done.3, ...), custom_call_target="tpu_custom_call" | custom-call | tf_op jit(solution)/shard_map/backward_exchange/pallas_call | solution.py:740
  326.8 2.9 convolution_convert_fusion.10
  329.8 2.3 convolution_convert_fusion.17.grad
  332.2 22.9 %attend_back.2 = bf16[960,512]{1,0:T(8,128)(2,1)S(1)} custom-call(s32[1]{0:T(128)S(6)} %copy.35.length, bf16[960,512]{1,0:T(8,128)(2,1)S(1)} %add_convert_fusion.qkv, bf16[3,640,512]{2,1,0:T(8,128)(2,1)S(1)} %copy-done.12, bf16[320,512]{1,0:T(8,128)(2,1)S(1)} %convolution_convert_fusion.17.grad, f32[320,512]{1,0:T(8,128)S(1)} %copy-done.23, ...), custom_call_target="tpu_custom_call" | custom-call | tf_op jit(solution)/shard_map/attend_back/pallas_call | solution.py:1086
  356.4 2.9 convolution_convert_fusion.5.refs_0_
  359.3 2.6 convolution_convert_fusion.8.partial
  367.1 44.7 %backward_exchange.5 = (bf16[512,1280]{1,0:T(8,128)(2,1)S(1)}, f32[128,1280]{1,0:T(8,128)S(1)}, f32[8,1280]{1,0:T(8,128)S(1)}, bf16[960,640]{1,0:T(8,128)(2,1)}, bf16[320,640]{1,0:T(8,128)(2,1)}) custom-call(bf16[512,1280]{1,0:T(8,128)(2,1)S(1)} %copy-done.19, f32[128,1280]{1,0:T(8,128)S(1)} %copy-done.27, f32[128,1280]{1,0:T(8,128)S(1)} %copy-done.6, ...), custom_call_target="tpu_custom_call" | custom-call | tf_op jit(solution)/shard_map/backward_exchange/pallas_call | solution.py:740
  411.8 1.9 convolution_convert_fusion.refs_1_
  414.5 2.8 convert_reduce_fusion.1
  417.4 1.9 convolution_convert_fusion.1.refs_0_
  421.3 52.6 %backward_exchange.6 = (bf16[512,1280]{1,0:T(8,128)(2,1)S(1)}, f32[128,1280]{1,0:T(8,128)S(1)}, f32[8,1280]{1,0:T(8,128)S(1)}, bf16[640,1280]{1,0:T(8,128)(2,1)}, bf16[1280,640]{1,0:T(8,128)(2,1)}) custom-call(bf16[512,1280]{1,0:T(8,128)(2,1)S(1)} %convolution_convert_fusion.7.partial, f32[128,1280]{1,0:T(8,128)S(1)} %get-tuple-element.106.grad_out, ...), custom_call_target="tpu_custom_call" | custom-call | tf_op jit(solution)/shard_map/backward_exchange/pallas_call | solution.py:740
  475.9 27.4 %attend_back.3 = (bf16[960,512]{1,0:T(8,128)(2,1)S(1)}, bf16[512,1280]{1,0:T(8,128)(2,1)S(1)}) custom-call(s32[1]{0:T(128)S(6)} %copy.35.length, bf16[960,512]{1,0:T(8,128)(2,1)S(1)} %add_convert_fusion.1.qkv, bf16[3,640,512]{2,1,0:T(8,128)(2,1)S(1)} %copy-done.10, bf16[320,512]{1,0:T(8,128)(2,1)S(1)} %convolution_convert_fusion.16.grad, ...), custom_call_target="tpu_custom_call" | custom-call | tf_op jit(solution)/shard_map/attend_back/pallas_call | solution.py:1086
  503.3 2.6 convolution_convert_fusion.6.partial
  506.1 3.1 convolution_convert_fusion.4.refs_0_
  514.1 45.5 %backward_exchange.7 = (bf16[512,1280]{1,0:T(8,128)(2,1)S(1)}, f32[128,1280]{1,0:T(8,128)}, f32[8,1280]{1,0:T(8,128)S(1)}, bf16[960,640]{1,0:T(8,128)(2,1)}, bf16[320,640]{1,0:T(8,128)(2,1)}) custom-call(bf16[512,1280]{1,0:T(8,128)(2,1)S(1)} %copy-done.18, f32[128,1280]{1,0:T(8,128)S(1)} %copy-done.25, ...), custom_call_target="tpu_custom_call" | custom-call | tf_op jit(solution)/shard_map/backward_exchange/pallas_call | solution.py:740
  560.8 15.5 %sum_all.1 = f32[24,640]{1,0:T(8,128)S(1)} custom-call(f32[16,1280]{1,0:T(8,128)S(1)} %pad.8.vectors, f32[8,640]{1,0:T(8,128)S(1)} %reshape.90.biases), custom_call_target="tpu_custom_call" | custom-call | tf_op jit(solution)/shard_map/sum_all/pallas_call | solution.py:471
  588.8 3.3 maximum_convert_fusion
  592.1 3.2 maximum_convert_fusion.1
  (216 shorter events, 56.8 us)
Async XLA Ops:
  7.2 119.8 %all-gather.7.cloned.1.call-start = ((), (), s32[]{:S(2)}) async-start(), calls=%async_computation.2 | async-start | bytes 4915200 | tf_op jit(solution)/shard_map/all_gather | solution.py:1167
  44.9 135.3 %all-gather.5.cloned.1.call-start = ((), (), s32[]{:S(2)}) async-start(), calls=%async_computation.1 | async-start | bytes 3686400 | tf_op jit(solution)/shard_map/all_gather | solution.py:1167
  45.6 206.3 %all-gather.9.cloned.1.call-start = ((), (), s32[]{:S(2)}) async-start(), calls=%async_computation.3 | async-start | bytes 4915200 | tf_op jit(solution)/shard_map/all_gather | solution.py:1167
  45.7 3.2 copy-start.64
  45.7 3.2 copy-start.65
  46.4 216.2 %all-gather.11.cloned.1.call-start = ((), (), s32[]{:S(2)}) async-start(), calls=%async_computation.4 | async-start | bytes 4915200 | tf_op jit(solution)/shard_map/all_gather | solution.py:1167
  46.9 315.0 %reduce-scatter.2.cloned.1.call-start = ((), (), s32[]{:S(2)}) async-start(), calls=%async_computation.5 | async-start | bytes 1638400 | tf_op jit(solution)/shard_map/reduce_scatter | solution.py:1289
  49.0 24.6 %copy-start.42 = (bf16[640,1280]{1,0:T(8,128)(2,1)S(1)}, bf16[640,1280]{1,0:T(8,128)(2,1)}, u32[]{:S(2)}) copy-start(bf16[640,1280]{1,0:T(8,128)(2,1)} %copy-done.41) | copy-start | bytes 4915204
  52.7 21.8 %copy-start.63 = (f32[2,1280]{1,0:T(2,128)S(1)}, f32[2,1280]{1,0:T(2,128)}, u32[]{:S(2)}) copy-start(f32[2,1280]{1,0:T(2,128)} %param.29) | copy-start | bytes 30724
  52.7 22.4 %copy-start.13 = (bf16[1280,640]{1,0:T(8,128)(2,1)S(1)}, bf16[1280,640]{1,0:T(8,128)(2,1)}, u32[]{:S(2)}) copy-start(bf16[1280,640]{1,0:T(8,128)(2,1)} %get-tuple-element.81.shard) | copy-start | bytes 4915204
  73.6 48.3 %copy-start.28 = (bf16[320,512]{1,0:T(8,128)(2,1)}, bf16[320,512]{1,0:T(8,128)(2,1)S(1)}, u32[]{:S(2)}) copy-start(bf16[320,512]{1,0:T(8,128)(2,1)S(1)} %get-tuple-element.77) | copy-start | bytes 983044
  124.7 10.1 %copy-start.1 = (f32[128,1280]{1,0:T(8,128)}, f32[128,1280]{1,0:T(8,128)S(1)}, u32[]{:S(2)}) copy-start(f32[128,1280]{1,0:T(8,128)S(1)} %get-tuple-element.85.residual.normal_in) | copy-start | bytes 1966084
  126.9 6.0 copy-start.39
  180.2 24.1 %copy-start.43 = (bf16[640,1280]{1,0:T(8,128)(2,1)S(1)}, bf16[640,1280]{1,0:T(8,128)(2,1)}, u32[]{:S(2)}) copy-start(bf16[640,1280]{1,0:T(8,128)(2,1)} %copy-done.41) | copy-start | bytes 4915204
  183.9 22.0 %copy-start.5 = (f32[128,1280]{1,0:T(8,128)S(1)}, f32[128,1280]{1,0:T(8,128)}, u32[]{:S(2)}) copy-start(f32[128,1280]{1,0:T(8,128)} %copy-done.4) | copy-start | bytes 1966084
  251.9 7.0 %copy-start.48 = (bf16[512,1280]{1,0:T(8,128)(2,1)S(1)}, bf16[512,1280]{1,0:T(8,128)(2,1)}, u32[]{:S(2)}) copy-start(bf16[512,1280]{1,0:T(8,128)(2,1)} %copy-done.47) | copy-start | bytes 3932164
  262.5 5.6 copy-start.54
  272.2 54.6 %copy-start.67 = (bf16[1280,1280]{1,0:T(8,128)(2,1)S(1)}, bf16[1280,1280]{1,0:T(8,128)(2,1)}, u32[]{:S(2)}) copy-start(bf16[1280,1280]{1,0:T(8,128)(2,1)} %all-gather.11.cloned.1.call-done) | copy-start | bytes 9830404
  272.2 54.6 %copy-start.75 = (bf16[512,1280]{1,0:T(8,128)(2,1)S(1)}, bf16[512,1280]{1,0:T(8,128)(2,1)}, u32[]{:S(2)}) copy-start(bf16[512,1280]{1,0:T(8,128)(2,1)} %copy-done.74) | copy-start | bytes 3932164
  332.2 23.1 %copy-start.15 = (bf16[512,1280]{1,0:T(8,128)(2,1)S(1)}, bf16[512,1280]{1,0:T(8,128)(2,1)}, u32[]{:S(2)}) copy-start(bf16[512,1280]{1,0:T(8,128)(2,1)} %copy-done.14) | copy-start | bytes 3932164
  332.2 23.1 %copy-start.31 = (bf16[320,512]{1,0:T(8,128)(2,1)S(1)}, bf16[320,512]{1,0:T(8,128)(2,1)}, u32[]{:S(2)}) copy-start(bf16[320,512]{1,0:T(8,128)(2,1)} %copy-done.30) | copy-start | bytes 983044
  356.4 2.9 copy-start.70
  367.1 44.7 %copy-start.73 = (bf16[512,1280]{1,0:T(8,128)(2,1)S(1)}, bf16[512,1280]{1,0:T(8,128)(2,1)}, u32[]{:S(2)}) copy-start(bf16[512,1280]{1,0:T(8,128)(2,1)} %copy-done.72) | copy-start | bytes 3932164
  414.5 2.8 copy-start.50
  421.2 52.6 %copy-start.44 = (bf16[640,1280]{1,0:T(8,128)(2,1)S(1)}, bf16[640,1280]{1,0:T(8,128)(2,1)}, u32[]{:S(2)}) copy-start(bf16[640,1280]{1,0:T(8,128)(2,1)} %copy-done.41) | copy-start | bytes 4915204
  475.8 27.4 %copy-start.69 = (bf16[960,1280]{1,0:T(8,128)(2,1)S(1)}, bf16[960,1280]{1,0:T(8,128)(2,1)}, u32[]{:S(2)}) copy-start(bf16[960,1280]{1,0:T(8,128)(2,1)} %get-tuple-element.72) | copy-start | bytes 7372804
  503.3 2.9 copy-start.46
  506.1 3.1 copy-start.29
  576.9 2.8 copy-start.59
  585.9 3.0 copy-start.58
  588.8 3.3 copy-start.55
  588.8 3.3 copy-start.57
  (49 other events, 76.1 us)
Sparse Core Ops, SparseCore 0:
  45.0 55.6 all-gather.6
  102.3 37.1 all-gather.4
  141.0 46.3 all-gather.8
  188.8 46.3 all-gather.10
  329.9 29.4 reduce-scatter.1

commit v11 on v10

--- a/solution.py
+++ b/solution.py
@@ -601,8 +601,8 @@
     shard_count, small_count, wide_count, low_count = counts
     shards, smalls, wides, (frames,) = take(shard_count), take(small_count), take(wide_count), take(1)
     outs, out_smalls, lows, (normed,) = take(shard_count), take(small_count), take(low_count), take(1)
-    buffers, (frame_buffer,) = take(len(jobs)), take(1)
-    cast_sems, sends, recvs, small_sends, small_recvs = refs
+    buffers, (frame_buffer,), stages = take(len(jobs)), take(1), take(low_count)
+    store_sems, cast_sems, sends, recvs, small_sends, small_recvs = refs
     quarters = Quarters(shards, outs, sends, recvs)
 
     barrier = pltpu.get_barrier_semaphore()
@@ -620,6 +620,9 @@
             device_id=quarters.peers[0],
             device_id_type=MESH,
         )
+
+    def store(low):
+        return pltpu.make_async_copy(stages[low], lows[low], store_sems.at[low])
 
     def load(at):
         which, layer, _, _ = jobs[at]
@@ -648,10 +651,12 @@
 
         def cast(step, carry):
             start = pl.multiple_of(step * CAST_ROWS, CAST_ROWS)
-            lows[low][pl.ds(first + start, CAST_ROWS), :] = buffers[at][pl.ds(start, CAST_ROWS), :].astype(LOW)
+            stages[low][pl.ds(first + start, CAST_ROWS), :] = buffers[at][pl.ds(start, CAST_ROWS), :].astype(LOW)
             return carry
 
         lax.fori_loop(0, buffers[at].shape[0] // CAST_ROWS, cast, 0)
+        if first + buffers[at].shape[0] == lows[low].shape[0]:
+            store(low).start()
     for at in range(small_count):
         small_copy(at, 1 - quarters.half).wait_recv()
         out_smalls[at][...] = out_smalls[at][...].astype(LOW).astype(WIDE)
@@ -667,6 +672,8 @@
     quarters.finish()
     for at in range(small_count):
         small_copy(at, quarters.half).wait_send()
+    for low in range(low_count):
+        store(low).wait()
 
 
 def quarter_sems(shards):
@@ -681,18 +688,24 @@
 def fetch_first(shards, smalls, wides, frames, jobs, low_shapes, collective_id):
     counts = (len(shards), len(smalls), len(wides), len(low_shapes))
     out_shape = tuple(gathered_shape(array) for array in (*shards, *smalls))
-    out_shape += tuple(jax.ShapeDtypeStruct(shape, LOW) for shape in (*low_shapes, frames.shape))
+    gathered = len(out_shape)
+    out_shape += tuple(pltpu.HBM(shape, LOW) for shape in low_shapes)
+    out_shape += (jax.ShapeDtypeStruct(frames.shape, LOW),)
     return pl.pallas_call(
         functools.partial(fetch_kernel, counts, jobs),
         out_shape=out_shape,
         in_specs=in_vmem(len(shards) + len(smalls)) + [pl.BlockSpec(memory_space=pl.ANY)] * (len(wides) + 1),
-        out_specs=tuple(in_vmem(len(out_shape))),
+        out_specs=tuple(
+            in_vmem(gathered) + [pl.BlockSpec(memory_space=pltpu.HBM)] * len(low_shapes) + in_vmem(1)
+        ),
         scratch_shapes=[pltpu.VMEM(wides[job[0]].shape[1:], WIDE) for job in jobs]
-        + [pltpu.VMEM(frames.shape, WIDE), pltpu.SemaphoreType.DMA((len(jobs) + 1,))]
+        + [pltpu.VMEM(frames.shape, WIDE)]
+        + [pltpu.VMEM(shape, LOW) for shape in low_shapes]
+        + [pltpu.SemaphoreType.DMA((len(low_shapes),)), pltpu.SemaphoreType.DMA((len(jobs) + 1,))]
         + quarter_sems(shards)
         + [pltpu.SemaphoreType.DMA((len(smalls),))] * 2,
         compiler_params=pltpu.CompilerParams(
-            collective_id=collective_id, has_side_effects=True, vmem_limit_bytes=42 << 20
+            collective_id=collective_id, has_side_effects=True, vmem_limit_bytes=40 << 20
         ),
         name="fetch_first",
     )(*shards, *smalls, *wides, frames)

time: 611 us -> 609 us (level)
    unnamed x152 -> x158, local copies, waits for them, and re-layouts: 27 us -> 28.6 us
where the time goes in v11:
time: 609 us; the launch traced here: 600 us
  Pallas kernels  465 us (76%)
  matrix products  62.5 us (10%)
  local copies, waits for them, and re-layouts  35.1 us (6%)
  other arithmetic  19.3 us (3%)
  between operations  15.7 us (3%)
    pallas_call x4, Pallas kernels, backward_exchange(): pl.pallas_call(functools.partial(kernel, n, PIECES), out_shape=out_shape,...  196 us
    pallas_call x3, Pallas kernels, forward_exchange(): pl.pallas_call(functools.partial(kernel, n, PIECES), out_shape=out_shape,...  135 us
    dot_general x24, matrix products, product(): lax.dot_general(left_side, right_side, (((left_axis,), (right_axis,)), ((...  62.5 us
    pallas_call x2, Pallas kernels, attend_back(): pl.pallas_call(functools.partial(attend_back_kernel, scale, own is not No...  50.3 us
    pallas_call x2, Pallas kernels, attend(): pl.pallas_call(functools.partial(attend_kernel, scale), out_shape=(jax.Sh...  41.3 us
    unnamed x158, local copies, waits for them, and re-layouts  28.6 us
    pallas_call x1, Pallas kernels, fetch_first(): pl.pallas_call(functools.partial(fetch_kernel, counts, jobs), out_shape=o...  27.3 us
    pallas_call x1, Pallas kernels, sum_all(): pl.pallas_call(functools.partial(sum_all_kernel, axes), out_shape=jax.Sha...  15.5 us
  transfers between devices with their start and end apart: 5, of which 0 were waited for; matrix products, arithmetic and copies ran while one was open for 6% of the time, Pallas kernels for 33%

profile of v11, /device:TPU:0, one launch (start us, length us, event | category | flops | bytes accessed | tf_op | source)
XLA Modules:
  0.0 599.9 jit_solution(14126092099163802218)
XLA Ops:
  11.6 27.3 %fetch_first.1 = (bf16[960,1280]{1,0:T(8,128)(2,1)S(1)}, bf16[640,1280]{1,0:T(8,128)(2,1)S(1)}, f32[2,1280]{1,0:T(2,128)S(1)}, f32[2,1280]{1,0:T(2,128)S(1)}, f3...) custom-call(bf16[960,640]{1,0:T(8,128)(2,1)S(1)} %pad_maximum_fusion, ...), custom_call_target="tpu_custom_call" | custom-call | tf_op jit(solution)/shard_map/fetch_first/pallas_call | solution.py:694
  46.8 3.6 add_convert_fusion.1.qkv
  50.5 20.9 %attend.2 = (bf16[320,512]{1,0:T(8,128)(2,1)S(1)}, f32[320,512]{1,0:T(8,128)S(1)}, f32[8,512]{1,0:T(8,128)S(1)}, bf16[3,640,512]{2,1,0:T(8,128)(2,1)S(1)}) custom-call(s32[1]{0:T(128)S(6)} %copy.35.length, bf16[960,512]{1,0:T(8,128)(2,1)S(1)} %add_convert_fusion.1.qkv), custom_call_target="tpu_custom_call" | custom-call | tf_op jit(solution)/shard_map/attend/pallas_call | solution.py:872
  72.9 46.8 %forward_exchange.3 = (bf16[512,1280]{1,0:T(8,128)(2,1)S(1)}, f32[128,1280]{1,0:T(8,128)S(1)}, bf16[1280,1280]{1,0:T(8,128)(2,1)S(1)}) custom-call(bf16[512,1280]{1,0:T(8,128)(2,1)S(1)} %convolution_convert_fusion.13.partial, f32[128,1280]{1,0:T(8,128)S(1)} %dynamic-slice_bitcast_fusion.residual.normal_in, f32[1,1280]{1,0:T(1,128)S(1)} %get-tuple-element.169.bias, ...), custom_call_target="tpu_custom_call" | custom-call | tf_op jit(solution)/shard_map/forward_exchange/pallas_call | solution.py:726
  122.5 2.2 dynamic-slice_reduce_fusion
  124.8 5.9 multiply_convert_fusion.1
  132.6 43.5 %forward_exchange.4 = (bf16[512,1280]{1,0:T(8,128)(2,1)S(1)}, f32[128,1280]{1,0:T(8,128)S(1)}) custom-call(bf16[512,1280]{1,0:T(8,128)(2,1)S(1)} %convolution_convert_fusion.12.partial, f32[128,1280]{1,0:T(8,128)S(1)} %get-tuple-element.85.residual.normal_in, f32[1,1280]{1,0:T(1,128)S(1)} %get-tuple-element.163.bias, f32[1,1280]{1,0:T(1,128)S(1)} %get-tuple-element.161.gain, ...), custom_call_target="tpu_custom_call" | custom-call | tf_op jit(solution)/shard_map/forward_exchange/pallas_call | solution.py:726
  178.0 3.6 add_convert_fusion.qkv
  181.7 20.4 %attend.3 = (bf16[320,512]{1,0:T(8,128)(2,1)S(1)}, f32[320,512]{1,0:T(8,128)S(1)}, f32[8,512]{1,0:T(8,128)S(1)}, bf16[3,640,512]{2,1,0:T(8,128)(2,1)S(1)}) custom-call(s32[1]{0:T(128)S(6)} %copy.35.length, bf16[960,512]{1,0:T(8,128)(2,1)S(1)} %add_convert_fusion.qkv), custom_call_target="tpu_custom_call" | custom-call | tf_op jit(solution)/shard_map/attend/pallas_call | solution.py:872
  203.7 44.9 %forward_exchange.5 = (bf16[512,1280]{1,0:T(8,128)(2,1)S(1)}, f32[128,1280]{1,0:T(8,128)S(1)}) custom-call(bf16[512,1280]{1,0:T(8,128)(2,1)S(1)} %convolution_convert_fusion.11.partial, f32[128,1280]{1,0:T(8,128)S(1)} %copy-done.5, f32[1,1280]{1,0:T(1,128)S(1)} %get-tuple-element.168.bias, f32[1,1280]{1,0:T(1,128)S(1)} %get-tuple-element.166.gain, ...), custom_call_target="tpu_custom_call" | custom-call | tf_op jit(solution)/shard_map/forward_exchange/pallas_call | solution.py:726
  249.7 5.9 multiply_convert_fusion
  256.7 3.6 convolution_convert_fusion.2.refs_1_
  260.3 5.6 convert_reduce_fusion
  265.9 1.9 convolution_convert_fusion.3.refs_0_
  269.9 52.8 %backward_exchange.4 = (bf16[512,1280]{1,0:T(8,128)(2,1)S(1)}, f32[128,1280]{1,0:T(8,128)S(1)}, f32[8,1280]{1,0:T(8,128)S(1)}, bf16[640,1280]{1,0:T(8,128)(2,1)}, bf16[1280,640]{1,0:T(8,128)(2,1)}) custom-call(bf16[512,1280]{1,0:T(8,128)(2,1)S(1)} %convolution_convert_fusion.9.partial, f32[128,1280]{1,0:T(8,128)S(1)} %copy-done.3, ...), custom_call_target="tpu_custom_call" | custom-call | tf_op jit(solution)/shard_map/backward_exchange/pallas_call | solution.py:753
  324.6 2.9 convolution_convert_fusion.10
  327.6 2.3 convolution_convert_fusion.17.grad
  330.0 22.9 %attend_back.2 = bf16[960,512]{1,0:T(8,128)(2,1)S(1)} custom-call(s32[1]{0:T(128)S(6)} %copy.35.length, bf16[960,512]{1,0:T(8,128)(2,1)S(1)} %add_convert_fusion.qkv, bf16[3,640,512]{2,1,0:T(8,128)(2,1)S(1)} %copy-done.15, bf16[320,512]{1,0:T(8,128)(2,1)S(1)} %convolution_convert_fusion.17.grad, f32[320,512]{1,0:T(8,128)S(1)} %copy-done.26, ...), custom_call_target="tpu_custom_call" | custom-call | tf_op jit(solution)/shard_map/attend_back/pallas_call | solution.py:1099
  354.2 2.9 convolution_convert_fusion.5.refs_0_
  357.1 2.6 convolution_convert_fusion.8.partial
  364.9 44.7 %backward_exchange.5 = (bf16[512,1280]{1,0:T(8,128)(2,1)S(1)}, f32[128,1280]{1,0:T(8,128)S(1)}, f32[8,1280]{1,0:T(8,128)S(1)}, bf16[960,640]{1,0:T(8,128)(2,1)}, bf16[320,640]{1,0:T(8,128)(2,1)}) custom-call(bf16[512,1280]{1,0:T(8,128)(2,1)S(1)} %copy-done.22, f32[128,1280]{1,0:T(8,128)S(1)} %copy-done.30, f32[128,1280]{1,0:T(8,128)S(1)} %copy-done.6, ...), custom_call_target="tpu_custom_call" | custom-call | tf_op jit(solution)/shard_map/backward_exchange/pallas_call | solution.py:753
  409.6 1.9 convolution_convert_fusion.refs_1_
  412.4 2.8 convert_reduce_fusion.1
  415.2 1.9 convolution_convert_fusion.1.refs_0_
  419.0 52.6 %backward_exchange.6 = (bf16[512,1280]{1,0:T(8,128)(2,1)S(1)}, f32[128,1280]{1,0:T(8,128)S(1)}, f32[8,1280]{1,0:T(8,128)S(1)}, bf16[640,1280]{1,0:T(8,128)(2,1)}, bf16[1280,640]{1,0:T(8,128)(2,1)}) custom-call(bf16[512,1280]{1,0:T(8,128)(2,1)S(1)} %convolution_convert_fusion.7.partial, f32[128,1280]{1,0:T(8,128)S(1)} %get-tuple-element.106.grad_out, ...), custom_call_target="tpu_custom_call" | custom-call | tf_op jit(solution)/shard_map/backward_exchange/pallas_call | solution.py:753
  473.6 27.4 %attend_back.3 = (bf16[960,512]{1,0:T(8,128)(2,1)S(1)}, bf16[512,1280]{1,0:T(8,128)(2,1)S(1)}) custom-call(s32[1]{0:T(128)S(6)} %copy.35.length, bf16[960,512]{1,0:T(8,128)(2,1)S(1)} %add_convert_fusion.1.qkv, bf16[3,640,512]{2,1,0:T(8,128)(2,1)S(1)} %copy-done.13, bf16[320,512]{1,0:T(8,128)(2,1)S(1)} %convolution_convert_fusion.16.grad, ...), custom_call_target="tpu_custom_call" | custom-call | tf_op jit(solution)/shard_map/attend_back/pallas_call | solution.py:1099
  501.1 2.6 convolution_convert_fusion.6.partial
  503.9 3.1 convolution_convert_fusion.4.refs_0_
  511.9 45.5 %backward_exchange.7 = (bf16[512,1280]{1,0:T(8,128)(2,1)S(1)}, f32[128,1280]{1,0:T(8,128)}, f32[8,1280]{1,0:T(8,128)S(1)}, bf16[960,640]{1,0:T(8,128)(2,1)}, bf16[320,640]{1,0:T(8,128)(2,1)}) custom-call(bf16[512,1280]{1,0:T(8,128)(2,1)S(1)} %copy-done.21, f32[128,1280]{1,0:T(8,128)S(1)} %copy-done.28, ...), custom_call_target="tpu_custom_call" | custom-call | tf_op jit(solution)/shard_map/backward_exchange/pallas_call | solution.py:753
  558.6 15.5 %sum_all.1 = f32[24,640]{1,0:T(8,128)S(1)} custom-call(f32[16,1280]{1,0:T(8,128)S(1)} %pad.8.vectors, f32[8,640]{1,0:T(8,128)S(1)} %reshape.90.biases), custom_call_target="tpu_custom_call" | custom-call | tf_op jit(solution)/shard_map/sum_all/pallas_call | solution.py:471
  586.6 3.3 maximum_convert_fusion
  589.9 3.2 maximum_convert_fusion.1
  (222 shorter events, 57.1 us)
Async XLA Ops:
  7.2 2.9 copy-start.9
  7.2 2.9 copy-start.8
  7.2 117.5 %all-gather.7.cloned.1.call-start = ((), (), s32[]{:S(2)}) async-start(), calls=%async_computation.2 | async-start | bytes 4915200 | tf_op jit(solution)/shard_map/all_gather | solution.py:1180
  42.7 135.3 %all-gather.5.cloned.1.call-start = ((), (), s32[]{:S(2)}) async-start(), calls=%async_computation.1 | async-start | bytes 3686400 | tf_op jit(solution)/shard_map/all_gather | solution.py:1180
  43.4 206.3 %all-gather.9.cloned.1.call-start = ((), (), s32[]{:S(2)}) async-start(), calls=%async_computation.3 | async-start | bytes 4915200 | tf_op jit(solution)/shard_map/all_gather | solution.py:1180
  43.5 3.2 copy-start.67
  43.5 3.2 copy-start.68
  44.2 216.1 %all-gather.11.cloned.1.call-start = ((), (), s32[]{:S(2)}) async-start(), calls=%async_computation.4 | async-start | bytes 4915200 | tf_op jit(solution)/shard_map/all_gather | solution.py:1180
  44.8 315.0 %reduce-scatter.2.cloned.1.call-start = ((), (), s32[]{:S(2)}) async-start(), calls=%async_computation.5 | async-start | bytes 1638400 | tf_op jit(solution)/shard_map/reduce_scatter | solution.py:1302
  46.8 24.6 %copy-start.47 = (bf16[640,1280]{1,0:T(8,128)(2,1)S(1)}, bf16[640,1280]{1,0:T(8,128)(2,1)}, u32[]{:S(2)}) copy-start(bf16[640,1280]{1,0:T(8,128)(2,1)} %copy-done.46) | copy-start | bytes 4915204
  50.5 21.8 %copy-start.66 = (f32[2,1280]{1,0:T(2,128)S(1)}, f32[2,1280]{1,0:T(2,128)}, u32[]{:S(2)}) copy-start(f32[2,1280]{1,0:T(2,128)} %param.29) | copy-start | bytes 30724
  50.5 22.4 %copy-start.16 = (bf16[1280,640]{1,0:T(8,128)(2,1)S(1)}, bf16[1280,640]{1,0:T(8,128)(2,1)}, u32[]{:S(2)}) copy-start(bf16[1280,640]{1,0:T(8,128)(2,1)} %get-tuple-element.81.shard) | copy-start | bytes 4915204
  71.4 48.3 %copy-start.31 = (bf16[320,512]{1,0:T(8,128)(2,1)}, bf16[320,512]{1,0:T(8,128)(2,1)S(1)}, u32[]{:S(2)}) copy-start(bf16[320,512]{1,0:T(8,128)(2,1)S(1)} %get-tuple-element.77) | copy-start | bytes 983044
  122.5 10.1 %copy-start.1 = (f32[128,1280]{1,0:T(8,128)}, f32[128,1280]{1,0:T(8,128)S(1)}, u32[]{:S(2)}) copy-start(f32[128,1280]{1,0:T(8,128)S(1)} %get-tuple-element.85.residual.normal_in) | copy-start | bytes 1966084
  124.7 6.0 copy-start.42
  178.0 24.1 %copy-start.48 = (bf16[640,1280]{1,0:T(8,128)(2,1)S(1)}, bf16[640,1280]{1,0:T(8,128)(2,1)}, u32[]{:S(2)}) copy-start(bf16[640,1280]{1,0:T(8,128)(2,1)} %copy-done.46) | copy-start | bytes 4915204
  181.7 22.0 %copy-start.5 = (f32[128,1280]{1,0:T(8,128)S(1)}, f32[128,1280]{1,0:T(8,128)}, u32[]{:S(2)}) copy-start(f32[128,1280]{1,0:T(8,128)} %copy-done.4) | copy-start | bytes 1966084
  249.7 7.0 %copy-start.73 = (bf16[512,1280]{1,0:T(8,128)(2,1)S(1)}, bf16[512,1280]{1,0:T(8,128)(2,1)}, u32[]{:S(2)}) copy-start(bf16[512,1280]{1,0:T(8,128)(2,1)} %get-tuple-element.95) | copy-start | bytes 3932164
  260.3 5.6 copy-start.57
  269.9 54.7 %copy-start.70 = (bf16[1280,1280]{1,0:T(8,128)(2,1)S(1)}, bf16[1280,1280]{1,0:T(8,128)(2,1)}, u32[]{:S(2)}) copy-start(bf16[1280,1280]{1,0:T(8,128)(2,1)} %all-gather.11.cloned.1.call-done) | copy-start | bytes 9830404
  269.9 54.7 %copy-start.78 = (bf16[512,1280]{1,0:T(8,128)(2,1)S(1)}, bf16[512,1280]{1,0:T(8,128)(2,1)}, u32[]{:S(2)}) copy-start(bf16[512,1280]{1,0:T(8,128)(2,1)} %copy-done.77) | copy-start | bytes 3932164
  330.0 23.1 %copy-start.18 = (bf16[512,1280]{1,0:T(8,128)(2,1)S(1)}, bf16[512,1280]{1,0:T(8,128)(2,1)}, u32[]{:S(2)}) copy-start(bf16[512,1280]{1,0:T(8,128)(2,1)} %copy-done.17) | copy-start | bytes 3932164
  330.0 23.1 %copy-start.34 = (bf16[320,512]{1,0:T(8,128)(2,1)S(1)}, bf16[320,512]{1,0:T(8,128)(2,1)}, u32[]{:S(2)}) copy-start(bf16[320,512]{1,0:T(8,128)(2,1)} %copy-done.33) | copy-start | bytes 983044
  354.2 2.9 copy-start.72
  364.9 44.7 %copy-start.76 = (bf16[512,1280]{1,0:T(8,128)(2,1)S(1)}, bf16[512,1280]{1,0:T(8,128)(2,1)}, u32[]{:S(2)}) copy-start(bf16[512,1280]{1,0:T(8,128)(2,1)} %copy-done.75) | copy-start | bytes 3932164
  419.0 52.6 %copy-start.49 = (bf16[640,1280]{1,0:T(8,128)(2,1)S(1)}, bf16[640,1280]{1,0:T(8,128)(2,1)}, u32[]{:S(2)}) copy-start(bf16[640,1280]{1,0:T(8,128)(2,1)} %copy-done.46) | copy-start | bytes 4915204
  473.6 27.4 %copy-start.45 = (bf16[960,1280]{1,0:T(8,128)(2,1)S(1)}, bf16[960,1280]{1,0:T(8,128)(2,1)}, u32[]{:S(2)}) copy-start(bf16[960,1280]{1,0:T(8,128)(2,1)} %copy-done.44) | copy-start | bytes 7372804
  503.9 3.1 copy-start.32
  558.5 19.1 %copy-start.62 = (bf16[960,640]{1,0:T(8,128)(2,1)S(1)}, bf16[960,640]{1,0:T(8,128)(2,1)}, u32[]{:S(2)}) copy-start(bf16[960,640]{1,0:T(8,128)(2,1)} %get-tuple-element.115) | copy-start | bytes 3686404
  583.7 3.0 copy-start.61
  586.6 3.3 copy-start.58
  586.6 3.3 copy-start.60
  (52 other events, 81.8 us)
Sparse Core Ops, SparseCore 0:
  42.8 55.6 all-gather.6
  100.1 37.1 all-gather.4
  138.8 46.4 all-gather.8
  186.7 46.2 all-gather.10
  327.7 29.4 reduce-scatter.1

commit v12 on v11

--- a/solution.py
+++ b/solution.py
@@ -18,7 +18,7 @@
 ROOT_HALF = 1.0 / math.sqrt(2.0)
 DENSITY = 1.0 / math.sqrt(2.0 * math.pi)
 REDUCE_LAG = 2
-GATHER_LAG = 3
+GATHER_LAG = 2
 
 
 def norm_parts(values):

time: 609 us -> 613 us (level)
    pallas_call x4, Pallas kernels: 196 us -> 204 us  [backward_exchange(): pl.pallas_call(functools.partial(kernel, n, PIECES), out_shape=out_shape,...]
  transfers between devices with their start and end apart: 5 -> 5, of which waited for: 0 -> 0; matrix products, arithmetic and copies ran while one was open for 6% -> 6% of each run, Pallas kernels for 33% -> 32%
where the time goes in v12:
time: 613 us; the launch traced here: 604 us
  Pallas kernels  470 us (77%)
  matrix products  62.5 us (10%)
  local copies, waits for them, and re-layouts  35.1 us (6%)
  other arithmetic  19.3 us (3%)
  between operations  15.7 us (3%)
    pallas_call x4, Pallas kernels, backward_exchange(): pl.pallas_call(functools.partial(kernel, n, PIECES), out_shape=out_shape,...  204 us
    pallas_call x3, Pallas kernels, forward_exchange(): pl.pallas_call(functools.partial(kernel, n, PIECES), out_shape=out_shape,...  130 us
    dot_general x24, matrix products, product(): lax.dot_general(left_side, right_side, (((left_axis,), (right_axis,)), ((...  62.5 us
    pallas_call x2, Pallas kernels, attend_back(): pl.pallas_call(functools.partial(attend_back_kernel, scale, own is not No...  50.5 us
    pallas_call x2, Pallas kernels, attend(): pl.pallas_call(functools.partial(attend_kernel, scale), out_shape=(jax.Sh...  42.1 us
    unnamed x158, local copies, waits for them, and re-layouts  28.6 us
    pallas_call x1, Pallas kernels, fetch_first(): pl.pallas_call(functools.partial(fetch_kernel, counts, jobs), out_shape=o...  27.3 us
    pallas_call x1, Pallas kernels, sum_all(): pl.pallas_call(functools.partial(sum_all_kernel, axes), out_shape=jax.Sha...  15.4 us
  transfers between devices with their start and end apart: 5, of which 0 were waited for; matrix products, arithmetic and copies ran while one was open for 6% of the time, Pallas kernels for 32%

profile of v12, /device:TPU:0, one launch (start us, length us, event | category | flops | bytes accessed | tf_op | source)
XLA Modules:
  0.0 604.3 jit_solution(15326125342597321713)
XLA Ops:
  11.6 27.3 %fetch_first.1 = (bf16[960,1280]{1,0:T(8,128)(2,1)S(1)}, bf16[640,1280]{1,0:T(8,128)(2,1)S(1)}, f32[2,1280]{1,0:T(2,128)S(1)}, f32[2,1280]{1,0:T(2,128)S(1)}, f3...) custom-call(bf16[960,640]{1,0:T(8,128)(2,1)S(1)} %pad_maximum_fusion, ...), custom_call_target="tpu_custom_call" | custom-call | tf_op jit(solution)/shard_map/fetch_first/pallas_call | solution.py:694
  46.8 3.6 add_convert_fusion.1.qkv
  50.5 20.9 %attend.2 = (bf16[320,512]{1,0:T(8,128)(2,1)S(1)}, f32[320,512]{1,0:T(8,128)S(1)}, f32[8,512]{1,0:T(8,128)S(1)}, bf16[3,640,512]{2,1,0:T(8,128)(2,1)S(1)}) custom-call(s32[1]{0:T(128)S(6)} %copy.35.length, bf16[960,512]{1,0:T(8,128)(2,1)S(1)} %add_convert_fusion.1.qkv), custom_call_target="tpu_custom_call" | custom-call | tf_op jit(solution)/shard_map/attend/pallas_call | solution.py:872
  72.9 45.9 %forward_exchange.3 = (bf16[512,1280]{1,0:T(8,128)(2,1)S(1)}, f32[128,1280]{1,0:T(8,128)S(1)}, bf16[1280,1280]{1,0:T(8,128)(2,1)S(1)}) custom-call(bf16[512,1280]{1,0:T(8,128)(2,1)S(1)} %convolution_convert_fusion.13.partial, f32[128,1280]{1,0:T(8,128)S(1)} %dynamic-slice_bitcast_fusion.residual.normal_in, f32[1,1280]{1,0:T(1,128)S(1)} %get-tuple-element.169.bias, ...), custom_call_target="tpu_custom_call" | custom-call | tf_op jit(solution)/shard_map/forward_exchange/pallas_call | solution.py:726
  121.6 2.2 dynamic-slice_reduce_fusion
  123.8 5.9 multiply_convert_fusion.1
  131.7 41.9 %forward_exchange.4 = (bf16[512,1280]{1,0:T(8,128)(2,1)S(1)}, f32[128,1280]{1,0:T(8,128)S(1)}) custom-call(bf16[512,1280]{1,0:T(8,128)(2,1)S(1)} %convolution_convert_fusion.12.partial, f32[128,1280]{1,0:T(8,128)S(1)} %get-tuple-element.85.residual.normal_in, f32[1,1280]{1,0:T(1,128)S(1)} %get-tuple-element.163.bias, f32[1,1280]{1,0:T(1,128)S(1)} %get-tuple-element.161.gain, ...), custom_call_target="tpu_custom_call" | custom-call | tf_op jit(solution)/shard_map/forward_exchange/pallas_call | solution.py:726
  175.5 3.6 add_convert_fusion.qkv
  179.2 21.2 %attend.3 = (bf16[320,512]{1,0:T(8,128)(2,1)S(1)}, f32[320,512]{1,0:T(8,128)S(1)}, f32[8,512]{1,0:T(8,128)S(1)}, bf16[3,640,512]{2,1,0:T(8,128)(2,1)S(1)}) custom-call(s32[1]{0:T(128)S(6)} %copy.35.length, bf16[960,512]{1,0:T(8,128)(2,1)S(1)} %add_convert_fusion.qkv), custom_call_target="tpu_custom_call" | custom-call | tf_op jit(solution)/shard_map/attend/pallas_call | solution.py:872
  202.0 42.1 %forward_exchange.5 = (bf16[512,1280]{1,0:T(8,128)(2,1)S(1)}, f32[128,1280]{1,0:T(8,128)S(1)}) custom-call(bf16[512,1280]{1,0:T(8,128)(2,1)S(1)} %convolution_convert_fusion.11.partial, f32[128,1280]{1,0:T(8,128)S(1)} %copy-done.5, f32[1,1280]{1,0:T(1,128)S(1)} %get-tuple-element.168.bias, f32[1,1280]{1,0:T(1,128)S(1)} %get-tuple-element.166.gain, ...), custom_call_target="tpu_custom_call" | custom-call | tf_op jit(solution)/shard_map/forward_exchange/pallas_call | solution.py:726
  245.1 5.9 multiply_convert_fusion
  252.1 3.6 convolution_convert_fusion.2.refs_1_
  255.7 5.6 convert_reduce_fusion
  261.4 1.9 convolution_convert_fusion.3.refs_0_
  265.4 56.1 %backward_exchange.4 = (bf16[512,1280]{1,0:T(8,128)(2,1)S(1)}, f32[128,1280]{1,0:T(8,128)S(1)}, f32[8,1280]{1,0:T(8,128)S(1)}, bf16[640,1280]{1,0:T(8,128)(2,1)}, bf16[1280,640]{1,0:T(8,128)(2,1)}) custom-call(bf16[512,1280]{1,0:T(8,128)(2,1)S(1)} %convolution_convert_fusion.9.partial, f32[128,1280]{1,0:T(8,128)S(1)} %copy-done.3, ...), custom_call_target="tpu_custom_call" | custom-call | tf_op jit(solution)/shard_map/backward_exchange/pallas_call | solution.py:753
  323.4 2.9 convolution_convert_fusion.10
  326.4 2.3 convolution_convert_fusion.17.grad
  328.8 22.9 %attend_back.2 = bf16[960,512]{1,0:T(8,128)(2,1)S(1)} custom-call(s32[1]{0:T(128)S(6)} %copy.35.length, bf16[960,512]{1,0:T(8,128)(2,1)S(1)} %add_convert_fusion.qkv, bf16[3,640,512]{2,1,0:T(8,128)(2,1)S(1)} %copy-done.15, bf16[320,512]{1,0:T(8,128)(2,1)S(1)} %convolution_convert_fusion.17.grad, f32[320,512]{1,0:T(8,128)S(1)} %copy-done.26, ...), custom_call_target="tpu_custom_call" | custom-call | tf_op jit(solution)/shard_map/attend_back/pallas_call | solution.py:1099
  353.0 2.9 convolution_convert_fusion.5.refs_0_
  355.9 2.6 convolution_convert_fusion.8.partial
  363.7 46.6 %backward_exchange.5 = (bf16[512,1280]{1,0:T(8,128)(2,1)S(1)}, f32[128,1280]{1,0:T(8,128)S(1)}, f32[8,1280]{1,0:T(8,128)S(1)}, bf16[960,640]{1,0:T(8,128)(2,1)}, bf16[320,640]{1,0:T(8,128)(2,1)}) custom-call(bf16[512,1280]{1,0:T(8,128)(2,1)S(1)} %copy-done.22, f32[128,1280]{1,0:T(8,128)S(1)} %copy-done.30, f32[128,1280]{1,0:T(8,128)S(1)} %copy-done.6, ...), custom_call_target="tpu_custom_call" | custom-call | tf_op jit(solution)/shard_map/backward_exchange/pallas_call | solution.py:753
  410.4 1.9 convolution_convert_fusion.refs_1_
  413.1 2.8 convert_reduce_fusion.1
  415.9 1.9 convolution_convert_fusion.1.refs_0_
  419.8 54.4 %backward_exchange.6 = (bf16[512,1280]{1,0:T(8,128)(2,1)S(1)}, f32[128,1280]{1,0:T(8,128)S(1)}, f32[8,1280]{1,0:T(8,128)S(1)}, bf16[640,1280]{1,0:T(8,128)(2,1)}, bf16[1280,640]{1,0:T(8,128)(2,1)}) custom-call(bf16[512,1280]{1,0:T(8,128)(2,1)S(1)} %convolution_convert_fusion.7.partial, f32[128,1280]{1,0:T(8,128)S(1)} %get-tuple-element.106.grad_out, ...), custom_call_target="tpu_custom_call" | custom-call | tf_op jit(solution)/shard_map/backward_exchange/pallas_call | solution.py:753
  476.2 27.6 %attend_back.3 = (bf16[960,512]{1,0:T(8,128)(2,1)S(1)}, bf16[512,1280]{1,0:T(8,128)(2,1)S(1)}) custom-call(s32[1]{0:T(128)S(6)} %copy.35.length, bf16[960,512]{1,0:T(8,128)(2,1)S(1)} %add_convert_fusion.1.qkv, bf16[3,640,512]{2,1,0:T(8,128)(2,1)S(1)} %copy-done.13, bf16[320,512]{1,0:T(8,128)(2,1)S(1)} %convolution_convert_fusion.16.grad, ...), custom_call_target="tpu_custom_call" | custom-call | tf_op jit(solution)/shard_map/attend_back/pallas_call | solution.py:1099
  503.9 2.6 convolution_convert_fusion.6.partial
  506.7 3.1 convolution_convert_fusion.4.refs_0_
  514.6 47.3 %backward_exchange.7 = (bf16[512,1280]{1,0:T(8,128)(2,1)S(1)}, f32[128,1280]{1,0:T(8,128)}, f32[8,1280]{1,0:T(8,128)S(1)}, bf16[960,640]{1,0:T(8,128)(2,1)}, bf16[320,640]{1,0:T(8,128)(2,1)}) custom-call(bf16[512,1280]{1,0:T(8,128)(2,1)S(1)} %copy-done.21, f32[128,1280]{1,0:T(8,128)S(1)} %copy-done.28, ...), custom_call_target="tpu_custom_call" | custom-call | tf_op jit(solution)/shard_map/backward_exchange/pallas_call | solution.py:753
  563.1 15.4 %sum_all.1 = f32[24,640]{1,0:T(8,128)S(1)} custom-call(f32[16,1280]{1,0:T(8,128)S(1)} %pad.8.vectors, f32[8,640]{1,0:T(8,128)S(1)} %reshape.90.biases), custom_call_target="tpu_custom_call" | custom-call | tf_op jit(solution)/shard_map/sum_all/pallas_call | solution.py:471
  591.0 3.3 maximum_convert_fusion
  594.3 3.2 maximum_convert_fusion.1
  (222 shorter events, 57.1 us)
Async XLA Ops:
  7.2 2.9 copy-start.9
  7.2 2.9 copy-start.8
  7.2 116.6 %all-gather.7.cloned.1.call-start = ((), (), s32[]{:S(2)}) async-start(), calls=%async_computation.2 | async-start | bytes 4915200 | tf_op jit(solution)/shard_map/all_gather | solution.py:1180
  42.7 132.8 %all-gather.5.cloned.1.call-start = ((), (), s32[]{:S(2)}) async-start(), calls=%async_computation.1 | async-start | bytes 3686400 | tf_op jit(solution)/shard_map/all_gather | solution.py:1180
  43.4 201.7 %all-gather.9.cloned.1.call-start = ((), (), s32[]{:S(2)}) async-start(), calls=%async_computation.3 | async-start | bytes 4915200 | tf_op jit(solution)/shard_map/all_gather | solution.py:1180
  43.5 3.2 copy-start.67
  43.5 3.2 copy-start.68
  44.2 211.6 %all-gather.11.cloned.1.call-start = ((), (), s32[]{:S(2)}) async-start(), calls=%async_computation.4 | async-start | bytes 4915200 | tf_op jit(solution)/shard_map/all_gather | solution.py:1180
  44.8 313.8 %reduce-scatter.2.cloned.1.call-start = ((), (), s32[]{:S(2)}) async-start(), calls=%async_computation.5 | async-start | bytes 1638400 | tf_op jit(solution)/shard_map/reduce_scatter | solution.py:1302
  46.8 24.6 %copy-start.47 = (bf16[640,1280]{1,0:T(8,128)(2,1)S(1)}, bf16[640,1280]{1,0:T(8,128)(2,1)}, u32[]{:S(2)}) copy-start(bf16[640,1280]{1,0:T(8,128)(2,1)} %copy-done.46) | copy-start | bytes 4915204
  50.5 21.8 %copy-start.66 = (f32[2,1280]{1,0:T(2,128)S(1)}, f32[2,1280]{1,0:T(2,128)}, u32[]{:S(2)}) copy-start(f32[2,1280]{1,0:T(2,128)} %param.29) | copy-start | bytes 30724
  50.5 22.4 %copy-start.16 = (bf16[1280,640]{1,0:T(8,128)(2,1)S(1)}, bf16[1280,640]{1,0:T(8,128)(2,1)}, u32[]{:S(2)}) copy-start(bf16[1280,640]{1,0:T(8,128)(2,1)} %get-tuple-element.81.shard) | copy-start | bytes 4915204
  71.4 47.4 %copy-start.31 = (bf16[320,512]{1,0:T(8,128)(2,1)}, bf16[320,512]{1,0:T(8,128)(2,1)S(1)}, u32[]{:S(2)}) copy-start(bf16[320,512]{1,0:T(8,128)(2,1)S(1)} %get-tuple-element.77) | copy-start | bytes 983044
  121.6 10.1 %copy-start.1 = (f32[128,1280]{1,0:T(8,128)}, f32[128,1280]{1,0:T(8,128)S(1)}, u32[]{:S(2)}) copy-start(f32[128,1280]{1,0:T(8,128)S(1)} %get-tuple-element.85.residual.normal_in) | copy-start | bytes 1966084
  123.8 6.0 copy-start.42
  175.5 24.9 %copy-start.48 = (bf16[640,1280]{1,0:T(8,128)(2,1)S(1)}, bf16[640,1280]{1,0:T(8,128)(2,1)}, u32[]{:S(2)}) copy-start(bf16[640,1280]{1,0:T(8,128)(2,1)} %copy-done.46) | copy-start | bytes 4915204
  179.1 22.8 %copy-start.5 = (f32[128,1280]{1,0:T(8,128)S(1)}, f32[128,1280]{1,0:T(8,128)}, u32[]{:S(2)}) copy-start(f32[128,1280]{1,0:T(8,128)} %copy-done.4) | copy-start | bytes 1966084
  245.1 7.0 %copy-start.73 = (bf16[512,1280]{1,0:T(8,128)(2,1)S(1)}, bf16[512,1280]{1,0:T(8,128)(2,1)}, u32[]{:S(2)}) copy-start(bf16[512,1280]{1,0:T(8,128)(2,1)} %get-tuple-element.95) | copy-start | bytes 3932164
  255.7 5.6 copy-start.57
  265.4 58.0 %copy-start.70 = (bf16[1280,1280]{1,0:T(8,128)(2,1)S(1)}, bf16[1280,1280]{1,0:T(8,128)(2,1)}, u32[]{:S(2)}) copy-start(bf16[1280,1280]{1,0:T(8,128)(2,1)} %all-gather.11.cloned.1.call-done) | copy-start | bytes 9830404
  265.4 58.0 %copy-start.78 = (bf16[512,1280]{1,0:T(8,128)(2,1)S(1)}, bf16[512,1280]{1,0:T(8,128)(2,1)}, u32[]{:S(2)}) copy-start(bf16[512,1280]{1,0:T(8,128)(2,1)} %copy-done.77) | copy-start | bytes 3932164
  328.8 23.1 %copy-start.18 = (bf16[512,1280]{1,0:T(8,128)(2,1)S(1)}, bf16[512,1280]{1,0:T(8,128)(2,1)}, u32[]{:S(2)}) copy-start(bf16[512,1280]{1,0:T(8,128)(2,1)} %copy-done.17) | copy-start | bytes 3932164
  328.8 23.1 %copy-start.34 = (bf16[320,512]{1,0:T(8,128)(2,1)S(1)}, bf16[320,512]{1,0:T(8,128)(2,1)}, u32[]{:S(2)}) copy-start(bf16[320,512]{1,0:T(8,128)(2,1)} %copy-done.33) | copy-start | bytes 983044
  353.0 2.9 copy-start.72
  363.7 46.6 %copy-start.76 = (bf16[512,1280]{1,0:T(8,128)(2,1)S(1)}, bf16[512,1280]{1,0:T(8,128)(2,1)}, u32[]{:S(2)}) copy-start(bf16[512,1280]{1,0:T(8,128)(2,1)} %copy-done.75) | copy-start | bytes 3932164
  419.7 54.5 %copy-start.49 = (bf16[640,1280]{1,0:T(8,128)(2,1)S(1)}, bf16[640,1280]{1,0:T(8,128)(2,1)}, u32[]{:S(2)}) copy-start(bf16[640,1280]{1,0:T(8,128)(2,1)} %copy-done.46) | copy-start | bytes 4915204
  476.2 27.6 %copy-start.45 = (bf16[960,1280]{1,0:T(8,128)(2,1)S(1)}, bf16[960,1280]{1,0:T(8,128)(2,1)}, u32[]{:S(2)}) copy-start(bf16[960,1280]{1,0:T(8,128)(2,1)} %copy-done.44) | copy-start | bytes 7372804
  506.7 3.1 copy-start.32
  563.0 19.0 %copy-start.62 = (bf16[960,640]{1,0:T(8,128)(2,1)S(1)}, bf16[960,640]{1,0:T(8,128)(2,1)}, u32[]{:S(2)}) copy-start(bf16[960,640]{1,0:T(8,128)(2,1)} %get-tuple-element.115) | copy-start | bytes 3686404
  588.1 3.0 copy-start.61
  591.0 3.3 copy-start.58
  591.0 3.3 copy-start.60
  (52 other events, 81.8 us)
Sparse Core Ops, SparseCore 0:
  42.8 55.6 all-gather.6
  100.1 37.1 all-gather.4
  138.8 46.3 all-gather.8
  186.6 46.3 all-gather.10
  326.5 30.0 reduce-scatter.1
